TPU v7x, 32 devices: a whole 2x2x4 slice. The times are simulated.
32 devices in a mesh: slot: 4 (over y, x), seq: 2 (over core), blk: 4 (over z).
Axes of the slice: x: 2, y: 2, z: 4, core: 2. Of those that a mesh axis runs over, the one named last changes fastest.
Arguments:
- tokens: bfloat16 [4, 1024, 2048], P('slot', ('blk', 'seq')), may hold values from -6 to 6
- out_grad: bfloat16 [4, 1024, 2048], P('slot', ('blk', 'seq')), may hold values from -6 to 6
- lengths: int32 [4], P('slot'), may hold values from 256 to 1024, as said below
- attn_gain: bfloat16 [2048], P(('slot', 'blk')), may hold values from 0.099609375 to 1.8984375
- w_query: bfloat16 [2048, 2048], P(('slot', 'blk'), 'seq'), may hold values from -0.125 to 0.125
- w_key: bfloat16 [2048, 2048], P(('slot', 'blk'), 'seq'), may hold values from -0.125 to 0.125
- w_value: bfloat16 [2048, 2048], P(('slot', 'blk'), 'seq'), may hold values from -0.125 to 0.125
- output_weight: bfloat16 [2048, 2048], P(('slot', 'blk'), 'seq'), may hold values from -1 to 1
- mlp_gain: bfloat16 [2048], P(('slot', 'blk')), may hold values from 0.099609375 to 1.8984375
- gate_weight: bfloat16 [2048, 8192], P(('slot', 'blk'), 'seq'), may hold values from -0.125 to 0.125
- up_weight: bfloat16 [2048, 8192], P(('slot', 'blk'), 'seq'), may hold values from -0.125 to 0.125
- down_weight: bfloat16 [2048, 8192], P(('slot', 'blk'), 'seq'), may hold values from -0.0625 to 0.0625
Outputs:
- layer_out: bfloat16 [4, 1024, 2048], P('slot', ('blk', 'seq'))
- grad_tokens: float32 [4, 1024, 2048], P('slot', ('blk', 'seq'))
- grad_attn_gain: float32 [2048], P(('slot', 'blk'))
- grad_w_query: float32 [2048, 2048], P(('slot', 'blk'), 'seq')
- grad_w_key: float32 [2048, 2048], P(('slot', 'blk'), 'seq')
- grad_w_value: float32 [2048, 2048], P(('slot', 'blk'), 'seq')
- grad_w_output: float32 [2048, 2048], P(('slot', 'blk'), 'seq')
- grad_mlp_gain: float32 [2048], P(('slot', 'blk'))
- grad_w_gate: float32 [2048, 8192], P(('slot', 'blk'), 'seq')
- grad_w_up: float32 [2048, 8192], P(('slot', 'blk'), 'seq')
- grad_w_down: float32 [2048, 8192], P(('slot', 'blk'), 'seq')
Inputs may be any that keep to these rules, and one draw needn't show every extreme that they name: `lengths`: the valid tokens of a slot are its first ones; at least one slot is full.
All inputs are finite; a program needn't handle non-finite values.
Results may differ from a plain program's by a relative error of at most 0.025.
Values may be sent and summed in bfloat16 or wider, within the bound.
No kernel may reach another device: no remote copies, remote signals or barrier semaphores. Data moves between devices by JAX's collectives and lax.ppermute only.
A program may use at most 192 MiB of HBM per device.

v0:
```python
from functools import partial

import jax
import jax.numpy as jnp
from jax import lax
from jax.sharding import PartitionSpec as P

HEADS = 32
HEAD_DIM = 64


EPSILON = 1e-05
ROPE_BASE = 130000.0


def from_behind(value, axis, steps):
    count = lax.axis_size(axis)
    first, last = (max(0, -steps), min(count, count - steps))
    return lax.ppermute(value, axis, [(source, source + steps) for source in range(first, last)])


def from_behind_2(array, axis, by):
    peers = lax.axis_size(axis)
    return lax.ppermute(array, axis, [(i, (i + by) % peers) for i in range(peers)])


def rope_tables(positions, head_size):
    half_size = head_size // 2
    frequency = ROPE_BASE ** (-jnp.arange(half_size, dtype=jnp.float32) * 2.0 / head_size)
    angles = positions.astype(jnp.float32)[:, None] * frequency[None, :]
    return (jnp.cos(angles), jnp.sin(angles))


def rotate(vectors, cosine, sine_tab):
    half_size = vectors.shape[-1] // 2
    first_half = vectors[..., :half_size]
    second_half = vectors[..., half_size:]
    cos_wide = cosine[:, None, :]
    sin_wide = sine_tab[:, None, :]
    return jnp.concatenate(
        [
            first_half * cos_wide - second_half * sin_wide,
            second_half * cos_wide + first_half * sin_wide,
        ],
        axis=-1,
    )


def norm_rows(input_rows_packed, gain_row):
    inverse = lax.rsqrt(
        jnp.mean(input_rows_packed * input_rows_packed, axis=-1, keepdims=True) + EPSILON
    )
    return (input_rows_packed * inverse * gain_row, inverse)


def norm_back(input_rows_packed, inverse, gain_row, upstream):
    scaled = upstream * gain_row
    normed = input_rows_packed * inverse
    grad_in = inverse * (scaled - normed * jnp.mean(scaled * normed, axis=-1, keepdims=True))
    return (grad_in, jnp.sum(upstream * normed, axis=0))


def matmul(left, right):
    return jnp.dot(left, right, preferred_element_type=jnp.float32)


def over_rows(left, right):
    return lax.dot_general(
        left, right, (((0,), (0,)), ((), ())), preferred_element_type=jnp.float32
    )


def over_cols(left, right):
    return lax.dot_general(
        left, right, (((1,), (1,)), ((), ())), preferred_element_type=jnp.float32
    )


def block_scores(queries, key_rows, query_pos, key_first, length, score_scale):
    key_pos = key_first + jnp.arange(key_rows.shape[0], dtype=jnp.int32)
    allowed = (key_pos[None, :] <= query_pos[:, None]) & (key_pos[None, :] < length)
    scores = (
        jnp.einsum("qhd,khd->hqk", queries, key_rows, preferred_element_type=jnp.float32)
        * score_scale
    )
    return jnp.where(allowed[None, :, :], scores, -jnp.inf)


def attend_tile(tile_item, key_rows, val_rows, key_first, length, score_scale):
    queries, query_pos, run_max, run_sum, run_out = tile_item
    scores = block_scores(queries, key_rows, query_pos, key_first, length, score_scale)
    new_max = jnp.maximum(run_max, jnp.max(scores, axis=2))
    factor = jnp.exp(run_max - new_max)
    exp_weights = jnp.exp(scores - new_max[:, :, None])
    run_sum = run_sum * factor + jnp.sum(exp_weights, axis=2)
    mixed_out = jnp.einsum(
        "hqk,khd->qhd",
        exp_weights.astype(jnp.bfloat16),
        val_rows,
        preferred_element_type=jnp.float32,
    )
    run_out = run_out * jnp.transpose(factor)[:, :, None] + mixed_out
    return (new_max, run_sum, run_out)


def back_tile(carried, tile_item, key_rows, val_rows, key_first, length, score_scale):
    grad_keys, grad_vals = carried
    queries, query_pos, out_cot, log_sum, row_dot, grad_query = tile_item
    scores = block_scores(queries, key_rows, query_pos, key_first, length, score_scale)
    probs = jnp.exp(scores - log_sum[:, :, None])
    grad_vals = grad_vals + jnp.einsum(
        "hqk,qhd->khd", probs.astype(jnp.bfloat16), out_cot, preferred_element_type=jnp.float32
    )
    grad_weight = jnp.einsum("qhd,khd->hqk", out_cot, val_rows, preferred_element_type=jnp.float32)
    grad_scores = (probs * (grad_weight - row_dot[:, :, None])).astype(jnp.bfloat16)
    grad_query = (
        grad_query
        + jnp.einsum("hqk,khd->qhd", grad_scores, key_rows, preferred_element_type=jnp.float32)
        * score_scale
    )
    grad_keys = (
        grad_keys
        + jnp.einsum("hqk,qhd->khd", grad_scores, queries, preferred_element_type=jnp.float32)
        * score_scale
    )
    return ((grad_keys, grad_vals), grad_query)


def sum_mlp(term_gate, term_up, term_down):
    return (
        lax.psum_scatter(
            term_gate.astype(jnp.bfloat16), ("slot", "blk"), scatter_dimension=0, tiled=True
        ).astype(jnp.float32),
        lax.psum_scatter(
            term_up.astype(jnp.bfloat16), ("slot", "blk"), scatter_dimension=0, tiled=True
        ).astype(jnp.float32),
        lax.psum_scatter(
            term_down.astype(jnp.bfloat16), ("slot", "blk"), scatter_dimension=0, tiled=True
        ).astype(jnp.float32),
    )


def shards(
    tokens,
    out_grad,
    lengths,
    attn_gain,
    w_query,
    w_key,
    w_value,
    output_weight,
    mlp_gain,
    gate_weight,
    up_weight,
    down_weight,
):
    seq_count = lax.axis_size("seq")
    blk_count = lax.axis_size("blk")
    seq_rank = lax.axis_index("seq")
    blk_rank = lax.axis_index("blk")
    tok_rows = tokens.shape[1]
    block_len = tok_rows * seq_count
    local_heads = HEADS // seq_count
    local_width = local_heads * HEAD_DIM
    score_scale = HEAD_DIM ** (-0.5)
    length = lengths[0]
    block_pos = blk_rank * block_len + jnp.arange(block_len, dtype=jnp.int32)
    positions = blk_rank * block_len + seq_rank * tok_rows + jnp.arange(tok_rows, dtype=jnp.int32)
    live_rows = (positions < length)[:, None]
    input_rows_packed = tokens[0].astype(jnp.float32)
    cosine, sine_tab = rope_tables(block_pos, HEAD_DIM)
    head_shape = (block_len, local_heads, HEAD_DIM)
    tile_rows = min(512, block_len)
    tile_count = block_len // tile_rows
    tiled_shape = (tile_count, tile_rows, local_heads, HEAD_DIM)
    pos_tiles = block_pos.reshape(tile_count, tile_rows)
    (
        gain_attn,
        gain_mlp,
        full_query,
        full_key,
        full_value,
        full_output,
        full_gate,
        full_up,
        full_down,
    ) = (
        lax.all_gather(attn_gain, ("slot", "blk"), axis=0, tiled=True),
        lax.all_gather(mlp_gain, ("slot", "blk"), axis=0, tiled=True),
        lax.all_gather(w_query, ("slot", "blk"), axis=0, tiled=True),
        lax.all_gather(w_key, ("slot", "blk"), axis=0, tiled=True),
        lax.all_gather(w_value, ("slot", "blk"), axis=0, tiled=True),
        lax.all_gather(output_weight, ("slot", "blk"), axis=0, tiled=True),
        lax.all_gather(gate_weight, ("slot", "blk"), axis=0, tiled=True),
        lax.all_gather(up_weight, ("slot", "blk"), axis=0, tiled=True),
        lax.all_gather(down_weight, ("slot", "blk"), axis=0, tiled=True),
    )
    gain_attn_f = gain_attn.astype(jnp.float32)
    gain_mlp_f = gain_mlp.astype(jnp.float32)
    normed_attn, inverse_attn = norm_rows(input_rows_packed, gain_attn_f)
    hidden_after_attention = normed_attn.astype(jnp.bfloat16)
    hidden_block = lax.all_gather(hidden_after_attention, "seq", axis=0, tiled=True)
    queries = rotate(matmul(hidden_block, full_query).reshape(head_shape), cosine, sine_tab).astype(
        jnp.bfloat16
    )
    key_rows = rotate(matmul(hidden_block, full_key).reshape(head_shape), cosine, sine_tab).astype(
        jnp.bfloat16
    )
    val_rows = matmul(hidden_block, full_value).astype(jnp.bfloat16).reshape(head_shape)
    query_tiles = queries.reshape(tiled_shape)
    run_max = jnp.full((tile_count, local_heads, tile_rows), -1e30, jnp.float32)
    run_sum = jnp.zeros((tile_count, local_heads, tile_rows), jnp.float32)
    run_out = jnp.zeros(tiled_shape, jnp.float32)
    kept_blocks = []
    moving_keys, moving_vals = (key_rows, val_rows)
    for cycle_step in range(blk_count):
        key_first = (blk_rank - cycle_step) % blk_count * block_len
        kept_blocks.append((moving_keys, moving_vals, key_first))
        step_fn = partial(
            attend_tile,
            key_rows=moving_keys,
            val_rows=moving_vals,
            key_first=key_first,
            length=length,
            score_scale=score_scale,
        )
        run_max, run_sum, run_out = lax.map(
            step_fn, (query_tiles, pos_tiles, run_max, run_sum, run_out)
        )
        if cycle_step + 1 < blk_count:
            moving_keys, moving_vals = from_behind((moving_keys, moving_vals), "blk", 1)
    log_sum = run_max + jnp.log(run_sum)
    attended_tiles = (run_out / jnp.transpose(run_sum, (0, 2, 1))[:, :, :, None]).astype(
        jnp.bfloat16
    )
    attention_mixed = attended_tiles.reshape(block_len, local_width)
    residual_stream = input_rows_packed + lax.psum_scatter(
        over_cols(attention_mixed, full_output).astype(jnp.bfloat16),
        "seq",
        scatter_dimension=0,
        tiled=True,
    ).astype(jnp.float32)
    normed_mlp, inverse_mlp = norm_rows(residual_stream, gain_mlp_f)
    hidden_after_feedforward = normed_mlp.astype(jnp.bfloat16)
    mlp_block = lax.all_gather(hidden_after_feedforward, "seq", axis=0, tiled=True)
    gate_logits = matmul(mlp_block, full_gate)
    up_logits = matmul(mlp_block, full_up)
    sigmoid_gate = jax.nn.sigmoid(gate_logits)
    swiglu_product = (gate_logits * sigmoid_gate * up_logits).astype(jnp.bfloat16)
    mlp_proj = lax.psum_scatter(
        over_cols(swiglu_product, full_down).astype(jnp.bfloat16),
        "seq",
        scatter_dimension=0,
        tiled=True,
    ).astype(jnp.float32)
    block_out = jnp.where(live_rows, residual_stream + mlp_proj, 0.0)
    out_cot = jnp.where(live_rows, out_grad[0].astype(jnp.float32), 0.0)
    cot_block = lax.all_gather(out_cot.astype(jnp.bfloat16), "seq", axis=0, tiled=True)
    grad_down_term = over_rows(cot_block, swiglu_product)
    grad_act = matmul(cot_block, full_down)
    grad_gate = (
        grad_act * up_logits * sigmoid_gate * (1.0 + gate_logits * (1.0 - sigmoid_gate))
    ).astype(jnp.bfloat16)
    grad_up = (grad_act * gate_logits * sigmoid_gate).astype(jnp.bfloat16)
    grad_gate_term = over_rows(mlp_block, grad_gate)
    grad_up_term = over_rows(mlp_block, grad_up)
    grad_hidden_mlp = lax.psum_scatter(
        (over_cols(grad_gate, full_gate) + over_cols(grad_up, full_up)).astype(jnp.bfloat16),
        "seq",
        scatter_dimension=0,
        tiled=True,
    ).astype(jnp.float32)
    grad_resid_part, gain_mlp_term = norm_back(
        residual_stream, inverse_mlp, gain_mlp_f, grad_hidden_mlp
    )
    grad_resid = out_cot + grad_resid_part
    resid_block = lax.all_gather(grad_resid.astype(jnp.bfloat16), "seq", axis=0, tiled=True)
    grad_wout_term = over_rows(resid_block, attention_mixed)
    grad_attended = matmul(resid_block, full_output).astype(jnp.bfloat16)
    cot_tiles = grad_attended.reshape(tiled_shape)
    row_dot = jnp.transpose(
        jnp.sum(cot_tiles.astype(jnp.float32) * attended_tiles.astype(jnp.float32), axis=-1),
        (0, 2, 1),
    )
    grad_query = jnp.zeros(tiled_shape, jnp.float32)
    moving_grads = (jnp.zeros(head_shape, jnp.float32), jnp.zeros(head_shape, jnp.float32))
    for kept_keys, kept_vals, key_first in kept_blocks:
        back_fn = partial(
            back_tile,
            key_rows=kept_keys,
            val_rows=kept_vals,
            key_first=key_first,
            length=length,
            score_scale=score_scale,
        )
        moving_grads, grad_query = lax.scan(
            back_fn, moving_grads, (query_tiles, pos_tiles, cot_tiles, log_sum, row_dot, grad_query)
        )
        moving_grads = (
            from_behind_2(moving_grads[0].astype(jnp.bfloat16), "blk", 1).astype(jnp.float32),
            from_behind_2(moving_grads[1].astype(jnp.bfloat16), "blk", 1).astype(jnp.float32),
        )
    grad_keys, grad_vals = moving_grads
    grad_query_low = grad_query.reshape(head_shape).astype(jnp.bfloat16).astype(jnp.float32)
    grad_keys_low = grad_keys.astype(jnp.bfloat16).astype(jnp.float32)
    grad_query_pre = (
        rotate(grad_query_low, cosine, -sine_tab)
        .astype(jnp.bfloat16)
        .reshape(block_len, local_width)
    )
    grad_key_pre = (
        rotate(grad_keys_low, cosine, -sine_tab)
        .astype(jnp.bfloat16)
        .reshape(block_len, local_width)
    )
    grad_value_low = grad_vals.astype(jnp.bfloat16).reshape(block_len, local_width)
    grad_hidden_attn = lax.psum_scatter(
        (
            over_cols(grad_query_pre, full_query)
            + over_cols(grad_key_pre, full_key)
            + over_cols(grad_value_low, full_value)
        ).astype(jnp.bfloat16),
        "seq",
        scatter_dimension=0,
        tiled=True,
    ).astype(jnp.float32)
    grad_in_part, gain_attn_term = norm_back(
        input_rows_packed, inverse_attn, gain_attn_f, grad_hidden_attn
    )
    grad_wgate, grad_wup, grad_wdown = sum_mlp(grad_gate_term, grad_up_term, grad_down_term)
    grad_wquery, grad_wkey, grad_wvalue, grad_woutput, gain_attn_part, gain_mlp_part = (
        lax.psum_scatter(
            over_rows(hidden_block, grad_query_pre).astype(jnp.bfloat16),
            ("slot", "blk"),
            scatter_dimension=0,
            tiled=True,
        ).astype(jnp.float32),
        lax.psum_scatter(
            over_rows(hidden_block, grad_key_pre).astype(jnp.bfloat16),
            ("slot", "blk"),
            scatter_dimension=0,
            tiled=True,
        ).astype(jnp.float32),
        lax.psum_scatter(
            over_rows(hidden_block, grad_value_low).astype(jnp.bfloat16),
            ("slot", "blk"),
            scatter_dimension=0,
            tiled=True,
        ).astype(jnp.float32),
        lax.psum_scatter(
            grad_wout_term.astype(jnp.bfloat16), ("slot", "blk"), scatter_dimension=0, tiled=True
        ).astype(jnp.float32),
        lax.psum_scatter(
            gain_attn_term.astype(jnp.bfloat16), ("slot", "blk"), scatter_dimension=0, tiled=True
        ).astype(jnp.float32),
        lax.psum_scatter(
            gain_mlp_term.astype(jnp.bfloat16), ("slot", "blk"), scatter_dimension=0, tiled=True
        ).astype(jnp.float32),
    )
    grad_gattn, grad_gmlp = lax.psum((gain_attn_part, gain_mlp_part), "seq")
    grad_inputs = grad_resid + grad_in_part
    return (
        block_out.astype(jnp.bfloat16)[None],
        grad_inputs[None],
        grad_gattn,
        grad_wquery,
        grad_wkey,
        grad_wvalue,
        grad_woutput,
        grad_gmlp,
        grad_wgate,
        grad_wup,
        grad_wdown,
    )


def solution(mesh):
    placed = (
        P("slot", ("blk", "seq"), None),
        P("slot", ("blk", "seq"), None),
        P("slot"),
        P(("slot", "blk")),
        P(("slot", "blk"), "seq"),
        P(("slot", "blk"), "seq"),
        P(("slot", "blk"), "seq"),
        P(("slot", "blk"), "seq"),
        P(("slot", "blk")),
        P(("slot", "blk"), "seq"),
        P(("slot", "blk"), "seq"),
        P(("slot", "blk"), "seq"),
    )
    return jax.shard_map(
        shards,
        mesh=mesh,
        in_specs=placed,
        out_specs=(
            P("slot", ("blk", "seq"), None),
            P("slot", ("blk", "seq"), None),
            P(("slot", "blk")),
            P(("slot", "blk"), "seq"),
            P(("slot", "blk"), "seq"),
            P(("slot", "blk"), "seq"),
            P(("slot", "blk"), "seq"),
            P(("slot", "blk")),
            P(("slot", "blk"), "seq"),
            P(("slot", "blk"), "seq"),
            P(("slot", "blk"), "seq"),
        ),
        check_vma=False,
    )
```

profile of v0, /device:TPU:0, one launch (start us, length us, event | category | flops | bytes accessed | tf_op | source)
XLA Modules:
  0.0 2703.4 jit_solution(6175386488568458087)
XLA Ops:
  8.5 42.4 %all-gather = bf16[16,1,128]{2,1,0:T(2,128)(2,1)S(1)} all-gather(bf16[1,1,128]{2,1,0:T(2,128)(2,1)} %bitcast.279), channel_id=1, replica_groups=mesh['slot'=4,'seq'=2,'blk'=4] {'slot','blk'}, dimensions={0}, use_global_device_ids=true | all-gather | bytes 4352 | tf_op jit(solution)/shard_map/all_gather | solution.py:188
  58.4 79.9 %all-gather.18.cloned.1.call-done = bf16[2048,1024]{1,0:T(8,128)(2,1)} async-done(((bf16[128,1024]{1,0:T(8,128)(2,1)}), bf16[2048,1024]{1,0:T(8,128)(2,1)}) %all-gather.18.cloned.1.call-update) | async-done | bytes 4194320 | tf_op jit(solution)/shard_map/all_gather | solution.py:191
  138.2 4.2 fusion.189
  142.5 73.0 %all-gather.16.cloned.1.call-done = bf16[2048,1024]{1,0:T(8,128)(2,1)} async-done(((bf16[128,1024]{1,0:T(8,128)(2,1)}), bf16[2048,1024]{1,0:T(8,128)(2,1)}) %all-gather.16.cloned.1.call-update) | async-done | bytes 4194320 | tf_op jit(solution)/shard_map/all_gather | solution.py:190
  223.3 71.0 %all-gather.20.cloned.1.call-done = bf16[2048,1024]{1,0:T(8,128)(2,1)} async-done(((bf16[128,1024]{1,0:T(8,128)(2,1)}), bf16[2048,1024]{1,0:T(8,128)(2,1)}) %all-gather.20.cloned.1.call-update) | async-done | bytes 4194320 | tf_op jit(solution)/shard_map/all_gather | solution.py:192
  307.3 14.4 collective-permute-done.1
  321.8 4.3 collective-permute-start.3
  326.9 15.0 collective-permute-done.2
  341.9 4.7 collective-permute-start.4
  347.5 10.7 collective-permute-done.3
  358.2 5.2 collective-permute-start.5
  364.3 16.4 collective-permute-done.4
  389.7 8.9 collective-permute-done.5
  401.2 4.5 convolution_convert_fusion.8
  405.8 40.4 %all-gather.1 = bf16[16,1,128]{2,1,0:T(2,128)(2,1)S(1)} all-gather(bf16[1,1,128]{2,1,0:T(2,128)(2,1)S(1)} %bitcast.280), channel_id=1, replica_groups=mesh['slot'=4,'seq'=2,'blk'=4] {'slot','blk'}, dimensions={0}, use_global_device_ids=true | all-gather | bytes 4352 | tf_op jit(solution)/shard_map/all_gather | solution.py:189
  456.0 195.9 %all-gather.28.cloned.1.call-done = bf16[2048,4096]{1,0:T(8,128)(2,1)} async-done(((bf16[128,4096]{1,0:T(8,128)(2,1)}), bf16[2048,4096]{1,0:T(8,128)(2,1)}) %all-gather.28.cloned.1.call-update) | async-done | bytes 16777232 | tf_op jit(solution)/shard_map/all_gather | solution.py:195
  652.0 12.6 fusion.191
  664.6 180.4 %all-gather.26.cloned.1.call-done = bf16[2048,4096]{1,0:T(8,128)(2,1)} async-done(((bf16[128,4096]{1,0:T(8,128)(2,1)}), bf16[2048,4096]{1,0:T(8,128)(2,1)}) %all-gather.26.cloned.1.call-update) | async-done | bytes 16777232 | tf_op jit(solution)/shard_map/all_gather | solution.py:194
  844.9 10.2 fusion.190
  855.1 195.1 %all-gather.30.cloned.1.call-done = bf16[2048,4096]{1,0:T(8,128)(2,1)} async-done(((bf16[128,4096]{1,0:T(8,128)(2,1)}), bf16[2048,4096]{1,0:T(8,128)(2,1)}) %all-gather.30.cloned.1.call-update) | async-done | bytes 16777232 | tf_op jit(solution)/shard_map/all_gather | solution.py:196
  1050.2 13.6 multiply_convert_fusion.4
  1063.8 12.3 fusion.192
  1076.1 12.5 fusion.12
  1088.7 6.8 reduce-scatter.16.cloned.1.call-done
  1102.2 8.7 all-gather.34.cloned.1.call-done
  1110.8 4.6 convolution_convert_fusion.9
  1138.9 7.5 collective-permute-done.6
  1148.2 9.4 collective-permute-done.10
  1158.8 10.1 collective-permute-done.7
  1169.9 10.2 collective-permute-done.11
  1180.3 11.0 collective-permute-done.8
  1192.1 10.5 collective-permute-done.12
  1202.8 11.0 collective-permute-done.9
  1218.0 6.4 collective-permute-done.13
  1227.6 12.3 convolution_convert_fusion.7
  1240.4 4.7 convolution_convert_fusion.3
  1245.1 4.3 convolution_convert_fusion.4
  1258.5 9.8 convolution_convert_fusion.1
  1268.4 9.9 convolution_convert_fusion.2
  1279.5 9.9 convolution_convert_fusion
  1292.8 43.6 %all-reduce.3 = (bf16[2048]{0:T(1024)(128)(2,1)S(1)}, bf16[2048]{0:T(1024)(128)(2,1)S(1)}) all-reduce(bf16[2048]{0:T(1024)(128)(2,1)S(1)} %get-tuple-element.228, bf16[2048]{0:T(1024)(128)(2,1)S(1)} %copy-done.53), channel_id=6, replica_groups=mesh['slot'=4,'seq'=2,'blk'=4] {'slot','blk'}, use_global_device_ids=true, to_apply=%region_18.19.clone | all-reduce | flops 4096 | bytes 16384
  1342.9 7.1 reduce-scatter.26.cloned.1.call-done
  1351.7 95.0 %reduce-scatter.24.cloned.1.call-done = bf16[128,1024]{1,0:T(8,128)(2,1)} async-done(((bf16[2048,1024]{1,0:T(8,128)(2,1)}), bf16[128,1024]{1,0:T(8,128)(2,1)}) %reduce-scatter.24.cloned.1.call-update) | async-done | bytes 262160 | tf_op jit(solution)/shard_map/reduce_scatter | solution.py:344
  1448.5 95.0 %reduce-scatter.22.cloned.1.call-done = bf16[128,1024]{1,0:T(8,128)(2,1)} async-done(((bf16[2048,1024]{1,0:T(8,128)(2,1)}), bf16[128,1024]{1,0:T(8,128)(2,1)}) %reduce-scatter.22.cloned.1.call-update) | async-done | bytes 262160 | tf_op jit(solution)/shard_map/reduce_scatter | solution.py:338
  1545.3 95.2 %reduce-scatter.20.cloned.1.call-done = bf16[128,1024]{1,0:T(8,128)(2,1)} async-done(((bf16[2048,1024]{1,0:T(8,128)(2,1)}), bf16[128,1024]{1,0:T(8,128)(2,1)}) %reduce-scatter.20.cloned.1.call-update) | async-done | bytes 262160 | tf_op jit(solution)/shard_map/reduce_scatter | solution.py:332
  1642.3 348.7 %reduce-scatter.30.cloned.1.call-done = bf16[128,4096]{1,0:T(8,128)(2,1)} async-done(((bf16[2048,4096]{1,0:T(8,128)(2,1)}), bf16[128,4096]{1,0:T(8,128)(2,1)}) %reduce-scatter.30.cloned.1.call-update) | async-done | bytes 1048592 | tf_op jit(solution)/shard_map/reduce_scatter | solution.py:134
  1993.8 348.5 %reduce-scatter.28.cloned.1.call-done = bf16[128,4096]{1,0:T(8,128)(2,1)} async-done(((bf16[2048,4096]{1,0:T(8,128)(2,1)}), bf16[128,4096]{1,0:T(8,128)(2,1)}) %reduce-scatter.28.cloned.1.call-update) | async-done | bytes 1048592 | tf_op jit(solution)/shard_map/reduce_scatter | solution.py:131
  2345.1 348.5 %reduce-scatter.32.cloned.1.call-done = bf16[128,4096]{1,0:T(8,128)(2,1)} async-done(((bf16[2048,4096]{1,0:T(8,128)(2,1)}), bf16[128,4096]{1,0:T(8,128)(2,1)}) %reduce-scatter.32.cloned.1.call-update) | async-done | bytes 1048592 | tf_op jit(solution)/shard_map/reduce_scatter | solution.py:137
  (288 shorter events, 130.1 us)
Async XLA Ops:
  7.2 51.2 %all-gather.14.cloned.1.call-start = ((), (), s32[]{:S(2)}) async-start(), calls=%async_computation.11 | async-start | bytes 1572864 | tf_op jit(solution)/shard_map/all_gather | solution.py:202
  52.9 85.3 %all-gather.18.cloned.1.call-start = ((), (), s32[]{:S(2)}) async-start(), calls=%async_computation.13 | async-start | bytes 4456448 | tf_op jit(solution)/shard_map/all_gather | solution.py:191
  53.7 161.9 %all-gather.16.cloned.1.call-start = ((), (), s32[]{:S(2)}) async-start(), calls=%async_computation.12 | async-start | bytes 4456448 | tf_op jit(solution)/shard_map/all_gather | solution.py:190
  54.4 239.9 %all-gather.20.cloned.1.call-start = ((), (), s32[]{:S(2)}) async-start(), calls=%async_computation.14 | async-start | bytes 4456448 | tf_op jit(solution)/shard_map/all_gather | solution.py:192
  55.0 345.5 %all-gather.22.cloned.1.call-start = ((), (), s32[]{:S(2)}) async-start(), calls=%async_computation.15 | async-start | bytes 4456448 | tf_op jit(solution)/shard_map/all_gather | solution.py:193
  55.6 390.7 %reduce-scatter.12.cloned.1.call-start = ((), (), s32[]{:S(2)}) async-start(), calls=%async_computation.16 | async-start | bytes 1572864 | tf_op jit(solution)/shard_map/reduce_scatter | solution.py:237
  57.2 162.3 %copy-start.37 = (f32[256,32]{0,1:T(8,128)}, f32[256,32]{0,1:T(8,128)S(1)}, u32[]{:S(2)}) copy-start(f32[256,32]{0,1:T(8,128)S(1)} %get-tuple-element.288) | copy-start | bytes 98308
  58.4 157.2 %copy-start.5 = (bf16[256,2048]{1,0:T(8,128)(2,1)S(1)}, bf16[256,2048]{1,0:T(8,128)(2,1)}, u32[]{:S(2)}) copy-start(bf16[256,2048]{1,0:T(8,128)(2,1)} %all-gather.14.cloned.1.call-done) | copy-start | bytes 3145732
  219.8 106.2 %copy-start.17 = (bf16[256,16,32]{0,2,1:T(8,128)(2,1)}, bf16[256,16,32]{0,2,1:T(8,128)(2,1)S(1)}, u32[]{:S(2)}) copy-start(bf16[256,16,32]{0,2,1:T(8,128)(2,1)S(1)} %get-tuple-element.280) | copy-start | bytes 786436
  219.9 84.1 %collective-permute-start = (bf16[256,16,64]{0,2,1:T(8,128)(2,1)S(1)}, bf16[256,16,64]{0,2,1:T(8,128)(2,1)S(1)}, u32[]{:S(2)}, u32[]{:S(2)}) collective-permute-start(bf16[256,16,64]{0,2,1:T(8,128)(2,1)S(1)} %pad_maximum_fusion.1), channel_id=1, source_target_pairs={{0,1},{1,2},{2,3},{4,5},{5,6},{6,7},{8,9},{9,10},{10,11},{12,13},{... | collective-permute-start | bytes 1572872 | tf_op jit(solution)/shard_map/ppermute | solution.py:19
  300.5 21.2 collective-permute-start.1
  304.0 37.9 %collective-permute-start.2 = (bf16[256,16,64]{0,2,1:T(8,128)(2,1)S(1)}, bf16[256,16,64]{0,2,1:T(8,128)(2,1)S(1)}, u32[]{:S(2)}, u32[]{:S(2)}) collective-permute-start(bf16[256,16,64]{0,2,1:T(8,128)(2,1)S(1)} %collective-permute-done), channel_id=1, source_target_pairs={{0,1},{1,2},{2,3},{4,5},{5,6},{6,7},{8,9},{9,10},{10,11},{12,13},{... | collective-permute-start | bytes 1572872 | tf_op jit(solution)/shard_map/ppermute | solution.py:19
  307.3 77.8 %copy-start.39 = (pred[256,256]{0,1:T(8,128)(4,1)}, pred[256,256]{0,1:T(8,128)(4,1)S(1)}, u32[]{:S(2)}) copy-start(pred[256,256]{0,1:T(8,128)(4,1)S(1)} %get-tuple-element.306) | copy-start | bytes 196612
  307.3 91.2 %copy-start.30 = (pred[256,256]{0,1:T(8,128)(4,1)}, pred[256,256]{0,1:T(8,128)(4,1)S(1)}, u32[]{:S(2)}) copy-start(pred[256,256]{0,1:T(8,128)(4,1)S(1)} %get-tuple-element.304) | copy-start | bytes 196612
  321.8 65.5 %copy-start.33 = (bf16[256,16,64]{0,2,1:T(8,128)(2,1)}, bf16[256,16,64]{0,2,1:T(8,128)(2,1)S(1)}, u32[]{:S(2)}) copy-start(bf16[256,16,64]{0,2,1:T(8,128)(2,1)S(1)} %collective-permute-done.1) | copy-start | bytes 1572868
  321.8 36.4 %collective-permute-start.3 = (bf16[256,16,64]{0,2,1:T(8,128)(2,1)S(1)}, bf16[256,16,64]{0,2,1:T(8,128)(2,1)S(1)}, u32[]{:S(2)}, u32[]{:S(2)}) collective-permute-start(bf16[256,16,64]{0,2,1:T(8,128)(2,1)S(1)} %collective-permute-done.1), channel_id=1, source_target_pairs={{0,1},{1,2},{2,3},{4,5},{5,6},{6,7},{8,9},{9,10},{10,11},{12,13},{... | collective-permute-start | bytes 1572872 | tf_op jit(solution)/shard_map/ppermute | solution.py:19
  326.9 58.2 %copy-start.15 = (f32[16,256,256]{1,2,0:T(8,128)}, f32[16,256,256]{1,2,0:T(8,128)S(1)}, u32[]{:S(2)}) copy-start(f32[16,256,256]{1,2,0:T(8,128)S(1)} %get-tuple-element.314) | copy-start | bytes 12582916
  326.9 61.5 %copy-start.42 = (f32[16,256]{1,0:T(8,128)}, f32[16,256]{1,0:T(8,128)S(1)}, u32[]{:S(2)}) copy-start(f32[16,256]{1,0:T(8,128)S(1)} %get-tuple-element.313) | copy-start | bytes 49156
  341.9 38.7 %collective-permute-start.4 = (bf16[256,16,64]{0,2,1:T(8,128)(2,1)S(1)}, bf16[256,16,64]{0,2,1:T(8,128)(2,1)S(1)}, u32[]{:S(2)}, u32[]{:S(2)}) collective-permute-start(bf16[256,16,64]{0,2,1:T(8,128)(2,1)S(1)} %collective-permute-done.2), channel_id=1, source_target_pairs={{0,1},{1,2},{2,3},{4,5},{5,6},{6,7},{8,9},{9,10},{10,11},{12,13},{... | collective-permute-start | bytes 1572872 | tf_op jit(solution)/shard_map/ppermute | solution.py:19
  358.2 40.3 %collective-permute-start.5 = (bf16[256,16,64]{0,2,1:T(8,128)(2,1)S(1)}, bf16[256,16,64]{0,2,1:T(8,128)(2,1)S(1)}, u32[]{:S(2)}, u32[]{:S(2)}) collective-permute-start(bf16[256,16,64]{0,2,1:T(8,128)(2,1)S(1)} %collective-permute-done.3), channel_id=1, source_target_pairs={{0,1},{1,2},{2,3},{4,5},{5,6},{6,7},{8,9},{9,10},{10,11},{12,13},{... | collective-permute-start | bytes 1572872 | tf_op jit(solution)/shard_map/ppermute | solution.py:19
  405.7 50.3 %all-gather.24.cloned.1.call-start = ((), (), s32[]{:S(2)}) async-start(), calls=%async_computation.17 | async-start | bytes 1572864 | tf_op jit(solution)/shard_map/all_gather | solution.py:245
  449.6 202.3 %all-gather.28.cloned.1.call-start = ((), (), s32[]{:S(2)}) async-start(), calls=%async_computation.19 | async-start | bytes 17825792 | tf_op jit(solution)/shard_map/all_gather | solution.py:195
  450.4 394.6 %all-gather.26.cloned.1.call-start = ((), (), s32[]{:S(2)}) async-start(), calls=%async_computation.18 | async-start | bytes 17825792 | tf_op jit(solution)/shard_map/all_gather | solution.py:194
  451.1 404.0 %all-gather.32.cloned.1.call-start = ((), (), s32[]{:S(2)}) async-start(), calls=%async_computation.22 | async-start | bytes 1572864 | tf_op jit(solution)/shard_map/all_gather | solution.py:258
  452.2 598.0 %all-gather.30.cloned.1.call-start = ((), (), s32[]{:S(2)}) async-start(), calls=%async_computation.20 | async-start | bytes 17825792 | tf_op jit(solution)/shard_map/all_gather | solution.py:196
  452.9 642.6 %reduce-scatter.16.cloned.1.call-start = ((), (), s32[]{:S(2)}) async-start(), calls=%async_computation.23 | async-start | bytes 1572864 | tf_op jit(solution)/shard_map/reduce_scatter | solution.py:267
  456.0 388.9 %copy-start.9 = (bf16[256,2048]{1,0:T(8,128)(2,1)S(1)}, bf16[256,2048]{1,0:T(8,128)(2,1)}, u32[]{:S(2)}) copy-start(bf16[256,2048]{1,0:T(8,128)(2,1)} %all-gather.24.cloned.1.call-done) | copy-start | bytes 3145732
  1088.6 22.2 all-gather.34.cloned.1.call-start
  1100.5 190.8 %reduce-scatter.18.cloned.1.call-start = ((), (), s32[]{:S(2)}) async-start(), calls=%async_computation.25 | async-start | bytes 1572864 | tf_op jit(solution)/shard_map/reduce_scatter | solution.py:317
  1129.8 16.6 collective-permute-start.6
  1131.6 26.0 collective-permute-start.10
  1147.2 21.7 collective-permute-start.7
  1158.7 21.4 collective-permute-start.11
  1169.0 22.3 collective-permute-start.8
  1180.3 22.3 collective-permute-start.12
  1191.5 22.3 collective-permute-start.9
  1202.7 21.7 collective-permute-start.13
  1227.6 112.0 %reduce-scatter.14.cloned.1.call-start = ((), (), s32[]{:S(2)}) async-start(), calls=%async_computation.21 | async-start | bytes 1572864 | tf_op jit(solution)/shard_map/reduce_scatter | solution.py:250
  1239.9 110.0 %reduce-scatter.26.cloned.1.call-start = ((), (), s32[]{:S(2)}) async-start(), calls=%async_computation.29 | async-start | bytes 4456448 | tf_op jit(solution)/shard_map/reduce_scatter | solution.py:350
  1245.1 201.6 %reduce-scatter.24.cloned.1.call-start = ((), (), s32[]{:S(2)}) async-start(), calls=%async_computation.28 | async-start | bytes 4456448 | tf_op jit(solution)/shard_map/reduce_scatter | solution.py:344
  1249.5 294.1 %reduce-scatter.22.cloned.1.call-start = ((), (), s32[]{:S(2)}) async-start(), calls=%async_computation.27 | async-start | bytes 4456448 | tf_op jit(solution)/shard_map/reduce_scatter | solution.py:338
  1253.0 387.6 %reduce-scatter.20.cloned.1.call-start = ((), (), s32[]{:S(2)}) async-start(), calls=%async_computation.26 | async-start | bytes 4456448 | tf_op jit(solution)/shard_map/reduce_scatter | solution.py:332
  1257.3 733.8 %reduce-scatter.30.cloned.1.call-start = ((), (), s32[]{:S(2)}) async-start(), calls=%async_computation.31 | async-start | bytes 17825792 | tf_op jit(solution)/shard_map/reduce_scatter | solution.py:134
  1268.3 1074.0 %reduce-scatter.28.cloned.1.call-start = ((), (), s32[]{:S(2)}) async-start(), calls=%async_computation.30 | async-start | bytes 17825792 | tf_op jit(solution)/shard_map/reduce_scatter | solution.py:131
  1278.3 1415.3 %reduce-scatter.32.cloned.1.call-start = ((), (), s32[]{:S(2)}) async-start(), calls=%async_computation.32 | async-start | bytes 17825792 | tf_op jit(solution)/shard_map/reduce_scatter | solution.py:137
  1289.4 50.2 %copy-start.13 = (bf16[128,2048]{1,0:T(8,128)(2,1)S(1)}, bf16[128,2048]{1,0:T(8,128)(2,1)}, u32[]{:S(2)}) copy-start(bf16[128,2048]{1,0:T(8,128)(2,1)} %reduce-scatter.16.cloned.1.call-done) | copy-start | bytes 1572868
  1289.4 50.2 %copy-start.44 = (f32[16,1,128]{2,1,0:T(1,128)S(1)}, f32[16,1,128]{2,1,0:T(1,128)}, u32[]{:S(2)}) copy-start(f32[16,1,128]{2,1,0:T(1,128)} %copy-done.43) | copy-start | bytes 24580
  1289.4 50.1 %copy-start.56 = (f32[128]{0:T(128)S(1)}, f32[128]{0:T(128)}, u32[]{:S(2)}) copy-start(f32[128]{0:T(128)} %copy-done.55) | copy-start | bytes 1540
  (57 other events, 705.7 us)
Sparse Core Ops, SparseCore 0:
  53.0 5.3 all-gather.13
  61.1 77.0 all-gather.17
  141.0 74.4 all-gather.15
  218.1 76.0 all-gather.19
  296.9 100.4 all-gather.21
  405.9 9.3 reduce-scatter.11
  449.7 6.2 all-gather.23
  459.2 192.7 all-gather.27
  655.1 189.7 all-gather.25
  847.0 7.2 all-gather.31
  857.4 192.7 all-gather.29
  1088.7 6.7 reduce-scatter.15
  1100.6 10.1 all-gather.33
  1227.7 7.8 reduce-scatter.17
  1240.0 7.5 reduce-scatter.13
  1249.7 100.1 reduce-scatter.25
  1352.1 94.6 reduce-scatter.23
  1448.9 94.6 reduce-scatter.21
  1545.8 94.6 reduce-scatter.19
  1642.7 348.3 reduce-scatter.29
  1993.4 348.9 reduce-scatter.27
  2344.6 348.9 reduce-scatter.31
where the time goes:
time: 2710 us; the launch traced here: 2700 us
  waiting for transfers between devices  2300 us (85%)
  matrix products  172 us (6%)
  blocking collectives  129 us (5%)
  other arithmetic  41.5 us (2%)
  starting transfers between devices  29.7 us (1%)
    reduce_scatter x1, waiting for transfers between devices, sum_mlp(): lax.psum_scatter(term_up.astype(jnp.bfloat16), ('slot', 'blk'), scatter_d...  349 us
    reduce_scatter x1, waiting for transfers between devices, sum_mlp(): lax.psum_scatter(term_gate.astype(jnp.bfloat16), ('slot', 'blk'), scatter...  349 us
    reduce_scatter x1, waiting for transfers between devices, sum_mlp(): lax.psum_scatter(term_down.astype(jnp.bfloat16), ('slot', 'blk'), scatter...  349 us
    all_gather x1, waiting for transfers between devices, shards(): lax.all_gather(up_weight, ('slot', 'blk'), axis=0, tiled=True)  196 us
    all_gather x1, waiting for transfers between devices, shards(): lax.all_gather(down_weight, ('slot', 'blk'), axis=0, tiled=True)  195 us
    all_gather x1, waiting for transfers between devices, shards(): lax.all_gather(gate_weight, ('slot', 'blk'), axis=0, tiled=True)  180 us
    reduce_scatter x1, waiting for transfers between devices, shards(): lax.psum_scatter(over_rows(hidden_block, grad_query_pre).astype(jnp.bfloa...  95.2 us
    reduce_scatter x1, waiting for transfers between devices, shards(): lax.psum_scatter(over_rows(hidden_block, grad_key_pre).astype(jnp.bfloat1...  95 us
  transfers between devices with their start and end apart: 36, of which 30 were waited for; matrix products, arithmetic and copies ran while one was open for 5% of the time, Pallas kernels for 0%

commit v1 on v0

v1 whole, which is shorter than its diff:
```python
from functools import partial

import jax
import jax.numpy as jnp
from jax import lax
from jax.experimental import pallas as pl
from jax.experimental.pallas import tpu as pltpu
from jax.sharding import PartitionSpec as P

HEADS = 32
HEAD_DIM = 64
EPSILON = 1e-05
ROPE_BASE = 130000.0
LOW = jnp.bfloat16
WIDE = jnp.float32


def turn(value, axis, by):
    count = lax.axis_size(axis)
    return lax.ppermute(value, axis, [(i, (i + by) % count) for i in range(count)])


def swap(value, axis, mask):
    count = lax.axis_size(axis)
    return lax.ppermute(value, axis, [(i, i ^ mask) for i in range(count)])


def after(value, *others):
    return lax.optimization_barrier((value, *others))[0]


def matmul(left, right):
    return jnp.dot(left, right, preferred_element_type=WIDE)


def over_rows(left, right):
    return lax.dot_general(left, right, (((0,), (0,)), ((), ())), preferred_element_type=WIDE)


def over_cols(left, right):
    return lax.dot_general(left, right, (((1,), (1,)), ((), ())), preferred_element_type=WIDE)


def slot_order(array):
    rank = lax.axis_index("slot")
    count = lax.axis_size("slot")
    parts = jnp.split(array, count, axis=-1)
    bit = 1
    while bit < count:
        flip = (rank & bit) != 0
        parts = [jnp.where(flip, parts[i ^ bit], parts[i]) for i in range(count)]
        bit *= 2
    return jnp.concatenate(parts, axis=-1)


def seq_gather(rows):
    count = lax.axis_size("seq")
    held = [rows]
    bit = 1
    while bit < count:
        held = held + [swap(part, "seq", bit) for part in held]
        bit *= 2
    return held


def seq_reduce(parts):
    bit = lax.axis_size("seq") // 2
    while bit >= 1:
        sent = [swap(part.astype(LOW), "seq", bit) for part in parts[bit:]]
        parts = [a.astype(WIDE) + b.astype(WIDE) for a, b in zip(parts[:bit], sent)]
        bit //= 2
    return parts[0]


def gather_rows(rows):
    moving = rows
    blocks = seq_gather(moving)
    for _ in range(lax.axis_size("blk") - 1):
        moving = turn(moving, "blk", 1)
        blocks = blocks + seq_gather(moving)
    return jnp.concatenate(blocks, axis=0)


def scatter_rows(terms):
    blks, seqs = lax.axis_size("blk"), lax.axis_size("seq")
    size = terms.shape[0] // (blks * seqs)

    def block(k):
        first = k * seqs
        return seq_reduce([terms[(first + m) * size : (first + m + 1) * size] for m in range(seqs)])

    moving = block(1 % blks)
    for step in range(1, blks):
        here = block((1 + step) % blks)
        moving = turn(moving.astype(LOW), "blk", 1).astype(WIDE) + here
    return moving


def columns_of(array, owner, parts):
    width = array.shape[1] // parts
    return lax.dynamic_slice(array, (0, owner * width), (array.shape[0], width))


def blk_weights(arrays):
    blks, rank = lax.axis_size("blk"), lax.axis_index("blk")

    def piece(owner):
        return jnp.concatenate([columns_of(a, owner, blks) for a in arrays], axis=1)

    own = piece(rank)
    rows = own.shape[0]
    full = jnp.zeros((blks * rows, own.shape[1]), own.dtype)
    full = lax.dynamic_update_slice(full, own, (rank * rows, 0))
    for k in range(1, blks):
        got = turn(piece((rank + k) % blks), "blk", k)
        full = lax.dynamic_update_slice(full, got, ((rank - k) % blks * rows, 0))
    return full


def slot_weights(own, first):
    near = [swap(own, "slot", 1), swap(own, "slot", 2)]
    far = swap(near[first - 1], "slot", 3 - first)
    return jnp.concatenate([own, near[0], near[1], far], axis=0)


def slot_sum(terms, first):
    far = swap(terms[3].astype(LOW), "slot", first)
    second = 3 - first
    relay = (terms[second].astype(WIDE) + far.astype(WIDE)).astype(LOW)
    one = swap(relay, "slot", second)
    two = swap(terms[first].astype(LOW), "slot", first)
    return terms[0].astype(WIDE) + one.astype(WIDE) + two.astype(WIDE)


def blk_grads(summed, widths):
    blks, rank = lax.axis_size("blk"), lax.axis_index("blk")
    rows = summed.shape[0] // blks
    low = summed.astype(LOW)

    def piece(owner):
        return lax.dynamic_slice(low, (owner * rows, 0), (rows, low.shape[1]))

    got = [(rank, piece(rank))]
    for k in range(1, blks):
        got.append(((rank - k) % blks, turn(piece((rank + k) % blks), "blk", k)))
    outs, at = [], 0
    for width in widths:
        out = jnp.zeros((rows, blks * width), WIDE)
        for owner, part in got:
            out = lax.dynamic_update_slice(out, part[:, at : at + width].astype(WIDE), (0, owner * width))
        outs.append(out)
        at += width
    return outs


def norm_rows(rows, gain_row):
    inverse = lax.rsqrt(jnp.mean(rows * rows, axis=-1, keepdims=True) + EPSILON)
    return rows * inverse * gain_row, inverse


def norm_back(rows, inverse, gain_row, upstream):
    scaled = upstream * gain_row
    normed = rows * inverse
    grad_in = inverse * (scaled - normed * jnp.mean(scaled * normed, axis=-1, keepdims=True))
    return grad_in, jnp.sum(upstream * normed, axis=0)


def row_positions(index, blk_rank, seq_rank, blks, seqs, size):
    sub = index // size
    k, m = sub // seqs, sub % seqs
    return ((blk_rank - k + blks) % blks * seqs + (seq_rank ^ m)) * size + index % size


def partner(vectors, lanes):
    half = HEAD_DIM // 2
    width = vectors.shape[1]
    if width % 128 == 0:
        ahead = pltpu.roll(vectors, width - half, 1)
        behind = pltpu.roll(vectors, half, 1)
        return jnp.where(lanes % HEAD_DIM < half, ahead, behind)
    parts = []
    for head in range(width // HEAD_DIM):
        first = head * HEAD_DIM
        parts += [vectors[:, first + half : first + HEAD_DIM], vectors[:, first : first + half]]
    return jnp.concatenate(parts, axis=1)


def attend_kernel(dims, place_ref, qkv_ref, kv_ref, cos_ref, sin_ref, allcos_ref, allsin_ref, q_ref, k_ref, v_ref, out_ref, lse_ref):
    heads, width, rows, total, blks, seqs, size, scale = dims
    step = pl.program_id(0)
    lanes = lax.broadcasted_iota(jnp.int32, (1, width), 1)

    @pl.when(step == 0)
    def _():
        pre = kv_ref[:, width : 2 * width]
        k_ref[...] = (pre * allcos_ref[...] + partner(pre, lanes) * allsin_ref[...]).astype(LOW)
        v_ref[...] = kv_ref[:, 2 * width :].astype(LOW)

    pre = qkv_ref[:, :width]
    queries = (pre * cos_ref[...] + partner(pre, lanes) * sin_ref[...]).astype(LOW)
    q_ref[...] = queries
    blk_rank, seq_rank, length = place_ref[0], place_ref[1], place_ref[2]
    q_index = step * rows + lax.broadcasted_iota(jnp.int32, (rows, 1), 0)
    k_index = lax.broadcasted_iota(jnp.int32, (1, total), 1)
    q_pos = row_positions(q_index, blk_rank, seq_rank, blks, seqs, size)
    k_pos = row_positions(k_index, blk_rank, seq_rank, blks, seqs, size)
    k_pos = jnp.where(k_pos < length, k_pos, jnp.int32(1 << 30))
    allowed = k_pos <= q_pos
    lse_lanes = lax.broadcasted_iota(jnp.int32, (1, 128), 1)

    def one_head(head, carried):
        out, lse = carried
        mine = lanes // HEAD_DIM == head
        picked = jnp.where(mine, queries.astype(WIDE) * scale, 0.0).astype(LOW)
        scores = over_cols(picked, k_ref[...])
        scores = jnp.where(allowed, scores, -1e30)
        top = jnp.max(scores, axis=1, keepdims=True)
        weights = jnp.exp(scores - top)
        total_weight = jnp.sum(weights, axis=1, keepdims=True)
        mixed = matmul(weights.astype(LOW), v_ref[...]) / total_weight
        out = jnp.where(mine, mixed, out)
        lse = jnp.where(lse_lanes == head, top + jnp.log(total_weight), lse)
        return out, lse

    out, lse = lax.fori_loop(
        0, heads, one_head, (jnp.zeros((rows, width), WIDE), jnp.zeros((rows, 128), WIDE))
    )
    out_ref[...] = out.astype(LOW)
    lse_ref[...] = lse


def attend_back_kernel(
    dims, place_ref, q_ref, k_ref, v_ref, out_ref, cot_ref, lse_ref, cos_ref, sin_ref, allcos_ref, allsin_ref, grad_ref, gk_acc, gv_acc
):
    heads, width, rows, total, blks, seqs, size, scale = dims
    step = pl.program_id(0)
    lanes = lax.broadcasted_iota(jnp.int32, (1, width), 1)

    @pl.when(step == 0)
    def _():
        gk_acc[...] = jnp.zeros_like(gk_acc)
        gv_acc[...] = jnp.zeros_like(gv_acc)

    queries = q_ref[...]
    blk_rank, seq_rank, length = place_ref[0], place_ref[1], place_ref[2]
    q_index = step * rows + lax.broadcasted_iota(jnp.int32, (rows, 1), 0)
    k_index = lax.broadcasted_iota(jnp.int32, (1, total), 1)
    q_pos = row_positions(q_index, blk_rank, seq_rank, blks, seqs, size)
    k_pos = row_positions(k_index, blk_rank, seq_rank, blks, seqs, size)
    k_pos = jnp.where(k_pos < length, k_pos, jnp.int32(1 << 30))
    allowed = k_pos <= q_pos
    lse_lanes = lax.broadcasted_iota(jnp.int32, (1, 128), 1)
    cot = cot_ref[...].astype(WIDE)
    dots = cot * out_ref[...].astype(WIDE)

    def one_head(head, grad_q):
        mine = lanes // HEAD_DIM == head
        picked = jnp.where(mine, queries.astype(WIDE) * scale, 0.0).astype(LOW)
        cot_head = jnp.where(mine, cot, 0.0).astype(LOW)
        row_dot = jnp.sum(jnp.where(mine, dots, 0.0), axis=1, keepdims=True)
        lse = jnp.sum(jnp.where(lse_lanes == head, lse_ref[...], 0.0), axis=1, keepdims=True)
        scores = over_cols(picked, k_ref[...])
        probs = jnp.exp(jnp.where(allowed, scores, -1e30) - lse)
        gv_acc[...] += over_rows(probs.astype(LOW), cot_head)
        grad_probs = over_cols(cot_head, v_ref[...])
        grad_scores = (probs * (grad_probs - row_dot)).astype(LOW)
        gk_acc[...] += over_rows(grad_scores, picked)
        return jnp.where(mine, matmul(grad_scores, k_ref[...]) * scale, grad_q)

    grad_q = lax.fori_loop(0, heads, one_head, jnp.zeros((rows, width), WIDE))
    low = grad_q.astype(LOW).astype(WIDE)
    turned = low * cos_ref[...] - partner(low, lanes) * sin_ref[...]
    here = pl.ds(pl.multiple_of(step * rows, rows), rows)
    grad_ref[here, :width] = turned.astype(LOW)

    @pl.when(step == pl.num_programs(0) - 1)
    def _():
        low_k = gk_acc[...].astype(LOW).astype(WIDE)
        turned_k = low_k * allcos_ref[...] - partner(low_k, lanes) * allsin_ref[...]
        grad_ref[:, width : 2 * width] = turned_k.astype(LOW)
        grad_ref[:, 2 * width :] = gv_acc[...].astype(LOW)


def attention_dims(total, width, size, rows):
    return (
        width // HEAD_DIM, width, rows, total, lax.axis_size("blk"), lax.axis_size("seq"), size, HEAD_DIM**-0.5,
    )


def attend(qkv, place, cos, sin, size):
    total, width = qkv.shape[0], qkv.shape[1] // 3
    rows = min(256, total)
    dims = attention_dims(total, width, size, rows)
    by_rows = lambda wide: pl.BlockSpec((rows, wide), lambda i, place: (i, 0))
    whole = lambda wide: pl.BlockSpec((total, wide), lambda i, place: (0, 0))
    return pl.pallas_call(
        partial(attend_kernel, dims),
        grid_spec=pltpu.PrefetchScalarGridSpec(
            num_scalar_prefetch=1,
            grid=(total // rows,),
            in_specs=[
                by_rows(3 * width), whole(3 * width), by_rows(width), by_rows(width), whole(width), whole(width),
            ],
            out_specs=[by_rows(width), whole(width), whole(width), by_rows(width), by_rows(128)],
        ),
        out_shape=[
            jax.ShapeDtypeStruct((total, width), LOW),
            jax.ShapeDtypeStruct((total, width), LOW),
            jax.ShapeDtypeStruct((total, width), LOW),
            jax.ShapeDtypeStruct((total, width), LOW),
            jax.ShapeDtypeStruct((total, 128), WIDE),
        ],
        compiler_params=pltpu.CompilerParams(vmem_limit_bytes=48 << 20),
        cost_estimate=pl.CostEstimate(
            flops=4 * total * total * width * dims[0], bytes_accessed=total * width * 30,
            transcendentals=total * total * dims[0],
        ),
        name="attend",
    )(place, qkv, qkv, cos, sin, cos, sin)


def attend_back(queries, key_rows, val_rows, attended, cot, lse, place, cos, sin, size):
    total, width = queries.shape
    rows = min(256, total)
    dims = attention_dims(total, width, size, rows)
    by_rows = lambda wide: pl.BlockSpec((rows, wide), lambda i, place: (i, 0))
    whole = lambda wide: pl.BlockSpec((total, wide), lambda i, place: (0, 0))
    return pl.pallas_call(
        partial(attend_back_kernel, dims),
        grid_spec=pltpu.PrefetchScalarGridSpec(
            num_scalar_prefetch=1,
            grid=(total // rows,),
            in_specs=[
                by_rows(width), whole(width), whole(width), by_rows(width), by_rows(width), by_rows(128),
                by_rows(width), by_rows(width), whole(width), whole(width),
            ],
            out_specs=whole(3 * width),
            scratch_shapes=[pltpu.VMEM((total, width), WIDE), pltpu.VMEM((total, width), WIDE)],
        ),
        out_shape=jax.ShapeDtypeStruct((total, 3 * width), LOW),
        compiler_params=pltpu.CompilerParams(vmem_limit_bytes=48 << 20),
        cost_estimate=pl.CostEstimate(
            flops=10 * total * total * width * dims[0], bytes_accessed=total * width * 30,
            transcendentals=total * total * dims[0],
        ),
        name="attend_back",
    )(place, queries, key_rows, val_rows, attended, cot, lse, cos, sin, cos, sin)


def gather_gains(gains):
    blks, rank = lax.axis_size("blk"), lax.axis_index("blk")
    width = gains.shape[1]
    full = jnp.zeros((2, blks * width), gains.dtype)
    full = lax.dynamic_update_slice(full, gains, (0, rank * width))
    for k in range(1, blks):
        full = lax.dynamic_update_slice(full, turn(gains, "blk", k), (0, (rank - k) % blks * width))
    near = [swap(full, "slot", 1), swap(full, "slot", 2)]
    return jnp.concatenate([full, near[0], near[1], swap(near[0], "slot", 2)], axis=1)


def sum_gain(term):
    blks, rank = lax.axis_size("blk"), lax.axis_index("blk")
    term = term[None]
    bit = 1
    while bit < lax.axis_size("seq"):
        term = term + swap(term, "seq", bit)
        bit *= 2
    width = term.shape[1] // lax.axis_size("slot")
    parts = [term[:, i * width : (i + 1) * width] for i in range(4)]
    relay = parts[2] + swap(parts[3], "slot", 1)
    mine = parts[0] + swap(parts[1], "slot", 1) + swap(relay, "slot", 2)
    total = mine
    for k in range(1, blks):
        total = total + turn(mine, "blk", k)
    shard = width // blks
    return lax.dynamic_slice(total, (0, rank * shard), (1, shard))[0]


def shards(
    tokens, out_grad, lengths, attn_gain, w_query, w_key, w_value, output_weight, mlp_gain, gate_weight, up_weight, down_weight
):
    seqs, blks = lax.axis_size("seq"), lax.axis_size("blk")
    seq_rank, blk_rank = lax.axis_index("seq"), lax.axis_index("blk")
    size, model = tokens.shape[1], tokens.shape[2]
    total = size * seqs * blks
    length = lengths[0]
    width = w_query.shape[1] // blks
    hidden = gate_weight.shape[1] // blks
    positions = (blk_rank * seqs + seq_rank) * size + jnp.arange(size, dtype=jnp.int32)
    live_rows = (positions < length)[:, None]
    place = jnp.stack([blk_rank, seq_rank, length]).astype(jnp.int32)

    all_pos = row_positions(jnp.arange(total, dtype=jnp.int32), blk_rank, seq_rank, blks, seqs, size)
    half = HEAD_DIM // 2
    frequency = ROPE_BASE ** (-jnp.arange(half, dtype=WIDE) * 2.0 / HEAD_DIM)
    angles = all_pos.astype(WIDE)[:, None] * frequency[None, :]
    cos_tab, sin_tab = jnp.cos(angles), jnp.sin(angles)
    cos_wide = jnp.tile(cos_tab, (1, width // half))
    sin_wide = jnp.tile(jnp.concatenate([-sin_tab, sin_tab], axis=1), (1, width // HEAD_DIM))

    own_tokens = slot_order(tokens[0])
    own_cot = jnp.where(live_rows, slot_order(out_grad[0]), 0)
    gains = gather_gains(jnp.stack([attn_gain, mlp_gain])).astype(WIDE)
    gain_attn, gain_mlp = gains[0], gains[1]

    all_tokens = gather_rows(own_tokens)
    part_qkv = blk_weights([w_query, w_key, w_value])
    full_qkv = slot_weights(part_qkv, 2)
    rest = after((output_weight, gate_weight, up_weight, down_weight), part_qkv, all_tokens)
    part_output = blk_weights([rest[0]])
    full_output = slot_weights(part_output, 1)
    part_gate = blk_weights([rest[1]])
    full_gate = slot_weights(part_gate, 1)
    part_up = blk_weights([rest[2]])
    full_up = slot_weights(part_up, 2)
    part_down = blk_weights([rest[3]])
    full_down = slot_weights(part_down, 1)
    all_cot = gather_rows(after(own_cot, part_down))

    normed_attn, inverse_all = norm_rows(all_tokens.astype(WIDE), gain_attn)
    hidden_attn = normed_attn.astype(LOW)
    qkv_pre = matmul(hidden_attn, full_qkv)
    queries, key_rows, val_rows, attended, lse = attend(qkv_pre, place, cos_wide, sin_wide, size)
    rows_f = own_tokens.astype(WIDE)
    resid = rows_f + scatter_rows(over_cols(attended, full_output).astype(LOW))
    normed_mlp, inverse_mlp = norm_rows(resid, gain_mlp)
    hidden_mlp = gather_rows(normed_mlp.astype(LOW))
    gate_pre = matmul(hidden_mlp, full_gate)
    up_pre = matmul(hidden_mlp, full_up)
    sigmoid_gate = jax.nn.sigmoid(gate_pre)
    activation = (gate_pre * sigmoid_gate * up_pre).astype(LOW)

    grad_act = matmul(all_cot, full_down)
    grad_gate = (grad_act * up_pre * sigmoid_gate * (1.0 + gate_pre * (1.0 - sigmoid_gate))).astype(LOW)
    grad_up = (grad_act * gate_pre * sigmoid_gate).astype(LOW)
    grad_hidden_mlp = scatter_rows((over_cols(grad_gate, full_gate) + over_cols(grad_up, full_up)).astype(LOW))
    grad_resid_part, gain_mlp_term = norm_back(resid, inverse_mlp, gain_mlp, grad_hidden_mlp)
    grad_resid = own_cot.astype(WIDE) + grad_resid_part
    resid_low = gather_rows(grad_resid.astype(LOW))

    def groups(left, right):
        step = model // 4
        return [over_rows(left[:, i * step : (i + 1) * step], right).astype(LOW) for i in range(4)]

    sum_down = slot_sum(groups(all_cot, activation), 1)
    sum_gate = slot_sum(groups(hidden_mlp, grad_gate), 1)
    sum_up = slot_sum(groups(hidden_mlp, grad_up), 2)

    grad_attended = matmul(resid_low, full_output).astype(LOW)
    sum_output = slot_sum(groups(resid_low, attended), 1)
    grad_qkv = attend_back(
        queries, key_rows, val_rows, attended, grad_attended, lse, place, cos_wide, sin_wide, size
    )
    mlp_out = scatter_rows(over_cols(activation, full_down).astype(LOW))
    layer_out = jnp.where(live_rows, resid + mlp_out, 0.0)

    grad_hidden_attn = scatter_rows(over_cols(grad_qkv, full_qkv).astype(LOW))
    sum_qkv = slot_sum(groups(hidden_attn, grad_qkv), 2)
    inverse_attn = lax.rsqrt(jnp.mean(rows_f * rows_f, axis=-1, keepdims=True) + EPSILON)
    grad_in_part, gain_attn_term = norm_back(rows_f, inverse_attn, gain_attn, grad_hidden_attn)
    (grad_wdown,) = blk_grads(sum_down, [hidden])
    (grad_wgate,) = blk_grads(sum_gate, [hidden])
    (grad_wup,) = blk_grads(sum_up, [hidden])
    (grad_woutput,) = blk_grads(sum_output, [width])
    grad_wquery, grad_wkey, grad_wvalue = blk_grads(sum_qkv, [width] * 3)
    return (
        slot_order(layer_out).astype(LOW)[None],
        slot_order(grad_resid + grad_in_part)[None],
        sum_gain(gain_attn_term),
        grad_wquery,
        grad_wkey,
        grad_wvalue,
        grad_woutput,
        sum_gain(gain_mlp_term),
        grad_wgate,
        grad_wup,
        grad_wdown,
    )


def solution(mesh):
    rows = P("slot", ("blk", "seq"), None)
    gain = P(("slot", "blk"))
    weight = P(("slot", "blk"), "seq")
    return jax.shard_map(
        shards,
        mesh=mesh,
        in_specs=(rows, rows, P("slot"), gain, weight, weight, weight, weight, gain, weight, weight, weight),
        out_specs=(rows, rows, gain, weight, weight, weight, weight, gain, weight, weight, weight),
        check_vma=False,
    )
```

time: 2710 us -> 789 us (0.29)
  waiting for transfers between devices: 2300 us -> 407 us
  starting transfers between devices: 29.7 us -> 176 us
  blocking collectives: 129 us -> 0 us
  matrix products: 172 us -> 97.1 us
  Pallas kernels: 0 us -> 45 us
    reduce_scatter x11 -> x0, waiting for transfers between devices: 1340 us -> none  [the longest x1 349 us: sum_mlp(): lax.psum_scatter(term_up.astype(jnp.bfloat16), ('slot', 'blk'), scatter_d...]
    all_gather x11 -> x0, waiting for transfers between devices: 808 us -> none  [the longest x1 196 us: shards(): lax.all_gather(up_weight, ('slot', 'blk'), axis=0, tiled=True)]
    ppermute x14 -> x136, waiting for transfers between devices: 141 us -> 407 us  [the longest x63 254 us: turn(): lax.ppermute(value, axis, [(i, (i + by) % count) for i in range(count)])]
    ppermute x14 -> x136, starting transfers between devices: 27.8 us -> 176 us  [the longest x63 128 us: turn(): lax.ppermute(value, axis, [(i, (i + by) % count) for i in range(count)])]
    all_gather x2 -> x0, blocking collectives: 82.8 us -> none  [the longest x1 42.4 us: shards(): lax.all_gather(attn_gain, ('slot', 'blk'), axis=0, tiled=True)]
    dot_general x31 -> x5, matrix products: 80.7 us -> 28.1 us  [matmul(): return jnp.dot(left, right, preferred_element_type=WIDE)]
    pallas_call x0 -> x2, Pallas kernels: none -> 45 us  [the longest x1 22.8 us: attend_back(): pl.pallas_call(partial(attend_back_kernel, dims), grid_spec=pltpu.Prefetc...]
    unnamed x1 -> x0, blocking collectives: 43.6 us -> none
  transfers between devices with their start and end apart: 36 -> 136, of which waited for: 30 -> 59; matrix products, arithmetic and copies ran while one was open for 5% -> 13% of each run, Pallas kernels for 0% -> 3%
where the time goes in v1:
time: 789 us; the launch traced here: 783 us
  waiting for transfers between devices  407 us (52%)
  starting transfers between devices  176 us (22%)
  matrix products  97.1 us (12%)
  Pallas kernels  45 us (6%)
  local copies, waits for them, and re-layouts  28.3 us (4%)
  other arithmetic  25.6 us (3%)
    ppermute x63, waiting for transfers between devices, turn(): lax.ppermute(value, axis, [(i, (i + by) % count) for i in range(count)])  254 us
    ppermute x73, waiting for transfers between devices, swap(): return lax.ppermute(value, axis, [(i, i ^ mask) for i in range(count)])  152 us
    ppermute x63, starting transfers between devices, turn(): lax.ppermute(value, axis, [(i, (i + by) % count) for i in range(count)])  128 us
    ppermute x73, starting transfers between devices, swap(): return lax.ppermute(value, axis, [(i, i ^ mask) for i in range(count)])  47.9 us
    dot_general x5, matrix products, over_cols(): lax.dot_general(left, right, (((1,), (1,)), ((), ())), preferred_element_...  34.8 us
    dot_general x20, matrix products, over_rows(): lax.dot_general(left, right, (((0,), (0,)), ((), ())), preferred_element_...  34.2 us
    dot_general x5, matrix products, matmul(): return jnp.dot(left, right, preferred_element_type=WIDE)  28.1 us
    pallas_call x1, Pallas kernels, attend_back(): pl.pallas_call(partial(attend_back_kernel, dims), grid_spec=pltpu.Prefetc...  22.8 us
  transfers between devices with their start and end apart: 136, of which 59 were waited for; matrix products, arithmetic and copies ran while one was open for 13% of the time, Pallas kernels for 3%

profile of v1, /device:TPU:0, one launch (start us, length us, event | category | flops | bytes accessed | tf_op | source)
XLA Modules:
  0.0 782.9 jit_solution(980948461639418543)
XLA Ops:
  34.0 6.3 collective-permute-done.14
  46.7 12.2 %collective-permute-done.3 = bf16[128,2048]{1,0:T(8,128)(2,1)S(1)} collective-permute-done((bf16[128,2048]{1,0:T(8,128)(2,1)}, bf16[128,2048]{1,0:T(8,128)(2,1)S(1)}, u32[]{:S(2)}, u32[]{:S(2)}) %collective-permute-start.3) | collective-permute-done | bytes 524320 | tf_op jit(solution)/shard_map/ppermute | solution.py:20
  66.3 7.7 collective-permute-done.5
  91.3 5.1 fusion.43.qkv_ref.kv_ref
  98.5 22.2 %attend.1 = (bf16[1024,256]{1,0:T(8,128)(2,1)S(1)}, bf16[1024,256]{1,0:T(8,128)(2,1)S(1)}, bf16[1024,256]{1,0:T(8,128)(2,1)S(1)}, bf16[1024,256]{1,0:T(8,128)(2,1)S(1)}, f32[1024,128]{1,0:T(8,128)S(1)}) custom-call(s32[3]{0:T(128)S(1)} %pad_add_fusion.place_ref, f32[1024,768]{1,0:T(8,128)} %fusion.43.qkv_ref.kv_ref, f32[1024,768]{1,0:T(8,128)} %fusion.43.qkv_ref.kv_ref, ...), custom_call_target="tpu_custom_call" | custom-call | flops 4294967296 | bytes 7864320 | tf_op jit(solution)/shard_map/attend/pallas_call | solution.py:296
  132.8 6.9 collective-permute-done.53
  142.3 9.8 %collective-permute-done.40 = bf16[128,1024]{1,0:T(8,128)(2,1)S(1)} collective-permute-done((bf16[128,1024]{1,0:T(8,128)(2,1)S(1)}, bf16[128,1024]{1,0:T(8,128)(2,1)S(1)}, u32[]{:S(2)}, u32[]{:S(2)}) %collective-permute-start.40) | collective-permute-done | bytes 262176 | tf_op jit(solution)/shard_map/ppermute | solution.py:20
  156.7 27.4 %collective-permute-start.46 = (bf16[128,1024]{1,0:T(8,128)(2,1)S(1)}, bf16[128,1024]{1,0:T(8,128)(2,1)S(1)}, u32[]{:S(2)}, u32[]{:S(2)}) collective-permute-start(bf16[128,1024]{1,0:T(8,128)(2,1)S(1)} %get-tuple-element.88), channel_id=1, source_target_pairs={{0,2},{1,3},{2,0},{3,1},{4,6},{5,7},{6,4},{7,5},{8,10},{9,11},{10,... | collective-permute-start | bytes 786440 | tf_op jit(solution)/shard_map/ppermute | solution.py:20
  187.6 9.2 %collective-permute-done.46 = bf16[128,1024]{1,0:T(8,128)(2,1)S(1)} collective-permute-done((bf16[128,1024]{1,0:T(8,128)(2,1)S(1)}, bf16[128,1024]{1,0:T(8,128)(2,1)S(1)}, u32[]{:S(2)}, u32[]{:S(2)}) %collective-permute-start.46) | collective-permute-done | bytes 262176 | tf_op jit(solution)/shard_map/ppermute | solution.py:20
  198.0 5.6 collective-permute-start.67
  204.7 14.4 %collective-permute-done.67 = bf16[128,2048]{1,0:T(8,128)(2,1)S(1)} collective-permute-done((bf16[128,2048]{1,0:T(8,128)(2,1)S(1)}, bf16[128,2048]{1,0:T(8,128)(2,1)S(1)}, u32[]{:S(2)}, u32[]{:S(2)}) %collective-permute-start.67) | collective-permute-done | bytes 524320 | tf_op jit(solution)/shard_map/ppermute | solution.py:20
  219.1 11.2 %collective-permute-done.28 = bf16[128,2048]{1,0:T(8,128)(2,1)S(1)} collective-permute-done((bf16[128,2048]{1,0:T(8,128)(2,1)S(1)}, bf16[128,2048]{1,0:T(8,128)(2,1)S(1)}, u32[]{:S(2)}, u32[]{:S(2)}) %collective-permute-start.28) | collective-permute-done | bytes 524320 | tf_op jit(solution)/shard_map/ppermute | solution.py:20
  233.0 8.6 %collective-permute-done.69 = bf16[128,2048]{1,0:T(8,128)(2,1)S(1)} collective-permute-done((bf16[128,2048]{1,0:T(8,128)(2,1)S(1)}, bf16[128,2048]{1,0:T(8,128)(2,1)S(1)}, u32[]{:S(2)}, u32[]{:S(2)}) %collective-permute-start.69) | collective-permute-done | bytes 524320 | tf_op jit(solution)/shard_map/ppermute | solution.py:20
  243.0 9.4 %collective-permute-done.30 = bf16[128,2048]{1,0:T(8,128)(2,1)S(1)} collective-permute-done((bf16[128,2048]{1,0:T(8,128)(2,1)S(1)}, bf16[128,2048]{1,0:T(8,128)(2,1)S(1)}, u32[]{:S(2)}, u32[]{:S(2)}) %collective-permute-start.30) | collective-permute-done | bytes 524320 | tf_op jit(solution)/shard_map/ppermute | solution.py:20
  256.8 12.5 %collective-permute-done.33 = bf16[128,2048]{1,0:T(8,128)(2,1)S(1)} collective-permute-done((bf16[128,2048]{1,0:T(8,128)(2,1)S(1)}, bf16[128,2048]{1,0:T(8,128)(2,1)S(1)}, u32[]{:S(2)}, u32[]{:S(2)}) %collective-permute-start.33) | collective-permute-done | bytes 524320 | tf_op jit(solution)/shard_map/ppermute | solution.py:20
  269.3 10.0 %collective-permute-done.56 = bf16[512,1024]{1,0:T(8,128)(2,1)S(1)} collective-permute-done((bf16[512,1024]{1,0:T(8,128)(2,1)S(1)}, bf16[512,1024]{1,0:T(8,128)(2,1)S(1)}, u32[]{:S(2)}, u32[]{:S(2)}) %collective-permute-start.56) | collective-permute-done | bytes 1048608 | tf_op jit(solution)/shard_map/ppermute | solution.py:25
  280.2 6.0 fusion.39
  286.2 5.9 collective-permute-done.35
  292.2 8.0 %collective-permute-done.49 = bf16[512,1024]{1,0:T(8,128)(2,1)S(1)} collective-permute-done((bf16[512,1024]{1,0:T(8,128)(2,1)S(1)}, bf16[512,1024]{1,0:T(8,128)(2,1)S(1)}, u32[]{:S(2)}, u32[]{:S(2)}) %collective-permute-start.49) | collective-permute-done | bytes 1048608 | tf_op jit(solution)/shard_map/ppermute | solution.py:25
  306.1 20.2 %collective-permute-done.48 = bf16[512,1024]{1,0:T(8,128)(2,1)S(1)} collective-permute-done((bf16[512,1024]{1,0:T(8,128)(2,1)S(1)}, bf16[512,1024]{1,0:T(8,128)(2,1)S(1)}, u32[]{:S(2)}, u32[]{:S(2)}) %collective-permute-start.48) | collective-permute-done | bytes 1048608 | tf_op jit(solution)/shard_map/ppermute | solution.py:25
  326.3 20.0 %collective-permute-done.50 = bf16[512,1024]{1,0:T(8,128)(2,1)S(1)} collective-permute-done((bf16[512,1024]{1,0:T(8,128)(2,1)S(1)}, bf16[512,1024]{1,0:T(8,128)(2,1)S(1)}, u32[]{:S(2)}, u32[]{:S(2)}) %collective-permute-start.50) | collective-permute-done | bytes 1048608 | tf_op jit(solution)/shard_map/ppermute | solution.py:25
  346.3 6.0 fusion.41
  353.3 9.6 %multiply_convert_fusion.1 = (bf16[1024,1024]{1,0:T(8,128)(2,1)S(1)}, bf16[1024,1024]{1,0:T(8,128)(2,1)S(1)}, bf16[1024,1024]{1,0:T(8,128)(2,1)S(1)}) fusion(f32[1024,1024]{1,0:T(8,128)} %fusion.39, f32[1024,1024]{1,0:T(8,128)} %fusion.41, bf16[1024,2048]{1,0:T(8,128)(2,1)S(1)} %constant_dynamic-update-slice_fusion.8, ...), kind=kOutput, calls=%fused_computation.10 | convolution fusion | flops 4328521728 | bytes 23068672 | tf_op jit(solution)/shard_map/dot_general | solution.py:33
  389.4 10.1 %fusion.40 = f32[1024,2048]{1,0:T(8,128)} fusion(bf16[1024,1024]{1,0:T(8,128)(2,1)S(1)} %get-tuple-element.48, bf16[512,1024]{1,0:T(8,128)(2,1)S(1)} %copy-done.61, bf16[512,1024]{1,0:T(8,128)(2,1)S(1)} %copy-done.57, bf16[512,1024]{1,0:T(8,128)(2,1)S(1)} %copy-done.59, bf16[512,1024]{1,0:T(8,128)(2,1)S(1)} %constant_dynamic-update-slice_fusion.35), kind=kOutput, calls=%fused_computation.108 | convolution fusion | flops 4311744512 | bytes 14680064 | tf_op jit(solution)/shard_map/dot_general | solution.py:41
  399.6 11.3 %add_convert_fusion = bf16[1024,2048]{1,0:T(8,128)(2,1)} fusion(f32[1024,2048]{1,0:T(8,128)} %fusion.40, bf16[1024,1024]{1,0:T(8,128)(2,1)S(1)} %get-tuple-element.46, bf16[512,1024]{1,0:T(8,128)(2,1)} %collective-permute-done.44, bf16[512,1024]{1,0:T(8,128)(2,1)} %copy-done.62, bf16[512,1024]{1,0:T(8,128)(2,1)} %copy-done.55, bf16[512,1024]{1,0:T(8,128)(2,1)} %copy-done.23), kind=kOutput, calls=%fused_computation.5 | convolution fusion | flops 4315938816 | bytes 18874368 | tf_op jit(solution)/shard_map/dot_general | solution.py:41
  413.9 5.8 convolution_convert_fusion.2
  428.5 18.4 %collective-permute-done.124 = bf16[512,1024]{1,0:T(8,128)(2,1)S(1)} collective-permute-done((bf16[512,1024]{1,0:T(8,128)(2,1)S(1)}, bf16[512,1024]{1,0:T(8,128)(2,1)S(1)}, u32[]{:S(2)}, u32[]{:S(2)}) %collective-permute-start.124) | collective-permute-done | bytes 1048608 | tf_op jit(solution)/shard_map/ppermute | solution.py:25
  449.1 12.6 %collective-permute-done.58 = bf16[128,2048]{1,0:T(8,128)(2,1)S(1)} collective-permute-done((bf16[128,2048]{1,0:T(8,128)(2,1)S(1)}, bf16[128,2048]{1,0:T(8,128)(2,1)S(1)}, u32[]{:S(2)}, u32[]{:S(2)}) %collective-permute-start.58) | collective-permute-done | bytes 524320 | tf_op jit(solution)/shard_map/ppermute | solution.py:20
  464.9 13.5 %collective-permute-done.74 = bf16[128,2048]{1,0:T(8,128)(2,1)S(1)} collective-permute-done((bf16[128,2048]{1,0:T(8,128)(2,1)S(1)}, bf16[128,2048]{1,0:T(8,128)(2,1)S(1)}, u32[]{:S(2)}, u32[]{:S(2)}) %collective-permute-start.74) | collective-permute-done | bytes 524320 | tf_op jit(solution)/shard_map/ppermute | solution.py:20
  480.8 6.1 collective-permute-done.60
  488.9 21.7 %collective-permute-done.126 = bf16[512,1024]{1,0:T(8,128)(2,1)S(1)} collective-permute-done((bf16[512,1024]{1,0:T(8,128)(2,1)S(1)}, bf16[512,1024]{1,0:T(8,128)(2,1)S(1)}, u32[]{:S(2)}, u32[]{:S(2)}) %collective-permute-start.126) | collective-permute-done | bytes 1048608 | tf_op jit(solution)/shard_map/ppermute | solution.py:25
  511.4 9.1 %collective-permute-done.120 = bf16[512,1024]{1,0:T(8,128)(2,1)S(1)} collective-permute-done((bf16[512,1024]{1,0:T(8,128)(2,1)S(1)}, bf16[512,1024]{1,0:T(8,128)(2,1)S(1)}, u32[]{:S(2)}, u32[]{:S(2)}) %collective-permute-start.120) | collective-permute-done | bytes 1048608 | tf_op jit(solution)/shard_map/ppermute | solution.py:25
  520.5 9.9 %collective-permute-done.119 = bf16[512,1024]{1,0:T(8,128)(2,1)S(1)} collective-permute-done((bf16[512,1024]{1,0:T(8,128)(2,1)S(1)}, bf16[512,1024]{1,0:T(8,128)(2,1)S(1)}, u32[]{:S(2)}, u32[]{:S(2)}) %collective-permute-start.119) | collective-permute-done | bytes 1048608 | tf_op jit(solution)/shard_map/ppermute | solution.py:25
  564.4 10.9 %collective-permute-done.127 = bf16[128,1024]{1,0:T(8,128)(2,1)S(1)} collective-permute-done((bf16[128,1024]{1,0:T(8,128)(2,1)S(1)}, bf16[128,1024]{1,0:T(8,128)(2,1)S(1)}, u32[]{:S(2)}, u32[]{:S(2)}) %collective-permute-start.127) | collective-permute-done | bytes 262176 | tf_op jit(solution)/shard_map/ppermute | solution.py:20
  581.6 5.0 collective-permute-done.128
  593.9 15.1 %collective-permute-done.79 = bf16[128,2048]{1,0:T(8,128)(2,1)S(1)} collective-permute-done((bf16[128,2048]{1,0:T(8,128)(2,1)S(1)}, bf16[128,2048]{1,0:T(8,128)(2,1)S(1)}, u32[]{:S(2)}, u32[]{:S(2)}) %collective-permute-start.79) | collective-permute-done | bytes 524320 | tf_op jit(solution)/shard_map/ppermute | solution.py:20
  609.0 8.2 %collective-permute-start.81 = (bf16[128,2048]{1,0:T(8,128)(2,1)S(1)}, bf16[128,2048]{1,0:T(8,128)(2,1)S(1)}, u32[]{:S(2)}, u32[]{:S(2)}) collective-permute-start(bf16[128,2048]{1,0:T(8,128)(2,1)S(1)} %collective-permute-done.79), channel_id=1, source_target_pairs={{0,1},{1,2},{2,3},{3,0},{4,5},{5,6},{6,7},{7,4},{8,9},{9,10},{10,1... | collective-permute-start | bytes 1572872 | tf_op jit(solution)/shard_map/ppermute | solution.py:20
  617.3 12.6 %collective-permute-done.122 = bf16[128,1024]{1,0:T(8,128)(2,1)S(1)} collective-permute-done((bf16[128,1024]{1,0:T(8,128)(2,1)S(1)}, bf16[128,1024]{1,0:T(8,128)(2,1)S(1)}, u32[]{:S(2)}, u32[]{:S(2)}) %collective-permute-start.122) | collective-permute-done | bytes 262176 | tf_op jit(solution)/shard_map/ppermute | solution.py:20
  630.1 4.8 collective-permute-start.83
  635.1 11.2 %collective-permute-done.83 = bf16[128,2048]{1,0:T(8,128)(2,1)S(1)} collective-permute-done((bf16[128,2048]{1,0:T(8,128)(2,1)S(1)}, bf16[128,2048]{1,0:T(8,128)(2,1)S(1)}, u32[]{:S(2)}, u32[]{:S(2)}) %collective-permute-start.83) | collective-permute-done | bytes 524320 | tf_op jit(solution)/shard_map/ppermute | solution.py:20
  650.5 22.8 %attend_back.1 = bf16[1024,768]{1,0:T(8,128)(2,1)} custom-call(s32[3]{0:T(128)S(1)} %pad_add_fusion.place_ref, bf16[1024,256]{1,0:T(8,128)(2,1)S(1)} %get-tuple-element.27.q_ref, bf16[1024,256]{1,0:T(8,128)(2,1)S(1)} %get-tuple-element.28.k_ref, bf16[1024,256]{1,0:T(8,128)(2,1)S(1)} %get-tuple-element.29.v_ref, ...), custom_call_target="tpu_custom_call" | custom-call | flops 10737418240 | bytes 7864320 | tf_op jit(solution)/shard_map/attend_back/pallas_call | solution.py:328
  679.2 6.3 convolution_convert_fusion.1
  692.5 5.2 collective-permute-done.106
  699.7 4.8 collective-permute-done.108
  704.5 10.0 %collective-permute-done.99 = bf16[512,768]{1,0:T(8,128)(2,1)S(1)} collective-permute-done((bf16[512,768]{1,0:T(8,128)(2,1)S(1)}, bf16[512,768]{1,0:T(8,128)(2,1)S(1)}, u32[]{:S(2)}, u32[]{:S(2)}) %collective-permute-start.99) | collective-permute-done | bytes 786464 | tf_op jit(solution)/shard_map/ppermute | solution.py:25
  717.8 9.8 %collective-permute-done.86 = bf16[128,2048]{1,0:T(8,128)(2,1)S(1)} collective-permute-done((bf16[128,2048]{1,0:T(8,128)(2,1)S(1)}, bf16[128,2048]{1,0:T(8,128)(2,1)S(1)}, u32[]{:S(2)}, u32[]{:S(2)}) %collective-permute-start.86) | collective-permute-done | bytes 524320 | tf_op jit(solution)/shard_map/ppermute | solution.py:20
  737.1 7.6 collective-permute-done.88
  749.0 14.9 %collective-permute-done.103 = bf16[128,768]{1,0:T(8,128)(2,1)S(1)} collective-permute-done((bf16[128,768]{1,0:T(8,128)(2,1)S(1)}, bf16[128,768]{1,0:T(8,128)(2,1)S(1)}, u32[]{:S(2)}, u32[]{:S(2)}) %collective-permute-start.103) | collective-permute-done | bytes 196640 | tf_op jit(solution)/shard_map/ppermute | solution.py:20
  (574 shorter events, 257.1 us)
Async XLA Ops:
  2.1 56.8 %collective-permute-start = (bf16[128,2048]{1,0:T(8,128)(2,1)S(1)}, bf16[128,2048]{1,0:T(8,128)(2,1)}, u32[]{:S(2)}, u32[]{:S(2)}) collective-permute-start(bf16[128,2048]{1,0:T(8,128)(2,1)S(1)} %get-tuple-element.39), channel_id=1, source_target_pairs={{0,4},{4,0},{1,5},{5,1},{2,6},{6,2},{3,7},{7,3},{8,12},{12,8},{9,1... | collective-permute-start | bytes 1572872 | tf_op jit(solution)/shard_map/ppermute | solution.py:25
  2.6 38.4 %collective-permute-start.1 = (bf16[128,2048]{1,0:T(8,128)(2,1)S(1)}, bf16[128,2048]{1,0:T(8,128)(2,1)}, u32[]{:S(2)}, u32[]{:S(2)}) collective-permute-start(bf16[128,2048]{1,0:T(8,128)(2,1)S(1)} %get-tuple-element.39), channel_id=1, source_target_pairs={{0,1},{1,2},{2,3},{3,0},{4,5},{5,6},{6,7},{7,4},{8,9},{9,10},{10,1... | collective-permute-start | bytes 1572872 | tf_op jit(solution)/shard_map/ppermute | solution.py:20
  45.2 46.0 %collective-permute-start.16 = (bf16[512,768]{1,0:T(8,128)(2,1)}, bf16[512,768]{1,0:T(8,128)(2,1)S(1)}, u32[]{:S(2)}, u32[]{:S(2)}) collective-permute-start(bf16[512,768]{1,0:T(8,128)(2,1)} %constant_dynamic-update-slice_fusion.44), channel_id=1, source_target_pairs={{0,8},{8,0},{16,24},{24,16},{1,9},{9,1},{17,25},{25,17},{2,10},{10... | collective-permute-start | bytes 2359304 | tf_op jit(solution)/shard_map/ppermute | solution.py:25
  64.0 27.3 %collective-permute-start.18 = (bf16[512,768]{1,0:T(8,128)(2,1)S(1)}, bf16[512,768]{1,0:T(8,128)(2,1)S(1)}, u32[]{:S(2)}, u32[]{:S(2)}) collective-permute-start(bf16[512,768]{1,0:T(8,128)(2,1)S(1)} %collective-permute-done.17), channel_id=1, source_target_pairs={{0,8},{8,0},{16,24},{24,16},{1,9},{9,1},{17,25},{25,17},{2,10},{10... | collective-permute-start | bytes 2359304 | tf_op jit(solution)/shard_map/ppermute | solution.py:25
  87.5 40.7 %collective-permute-start.51 = (bf16[128,1024]{1,0:T(8,128)(2,1)}, bf16[128,1024]{1,0:T(8,128)(2,1)S(1)}, u32[]{:S(2)}, u32[]{:S(2)}) collective-permute-start(bf16[128,1024]{1,0:T(8,128)(2,1)} %get-tuple-element.81), channel_id=1, source_target_pairs={{0,1},{1,2},{2,3},{3,0},{4,5},{5,6},{6,7},{7,4},{8,9},{9,10},{10,1... | collective-permute-start | bytes 786440 | tf_op jit(solution)/shard_map/ppermute | solution.py:20
  89.4 39.8 %collective-permute-start.52 = (bf16[128,1024]{1,0:T(8,128)(2,1)}, bf16[128,1024]{1,0:T(8,128)(2,1)}, u32[]{:S(2)}, u32[]{:S(2)}) collective-permute-start(bf16[128,1024]{1,0:T(8,128)(2,1)} %get-tuple-element.80), channel_id=1, source_target_pairs={{0,2},{1,3},{2,0},{3,1},{4,6},{5,7},{6,4},{7,5},{8,10},{9,11},{10,... | collective-permute-start | bytes 786440 | tf_op jit(solution)/shard_map/ppermute | solution.py:20
  129.2 27.4 %collective-permute-start.41 = (bf16[128,1024]{1,0:T(8,128)(2,1)S(1)}, bf16[128,1024]{1,0:T(8,128)(2,1)S(1)}, u32[]{:S(2)}, u32[]{:S(2)}) collective-permute-start(bf16[128,1024]{1,0:T(8,128)(2,1)S(1)} %get-tuple-element.83), channel_id=1, source_target_pairs={{0,3},{1,0},{2,1},{3,2},{4,7},{5,4},{6,5},{7,6},{8,11},{9,8},{10,9... | collective-permute-start | bytes 786440 | tf_op jit(solution)/shard_map/ppermute | solution.py:20
  139.7 44.4 %collective-permute-start.45 = (bf16[128,1024]{1,0:T(8,128)(2,1)S(1)}, bf16[128,1024]{1,0:T(8,128)(2,1)S(1)}, u32[]{:S(2)}, u32[]{:S(2)}) collective-permute-start(bf16[128,1024]{1,0:T(8,128)(2,1)S(1)} %get-tuple-element.89), channel_id=1, source_target_pairs={{0,1},{1,2},{2,3},{3,0},{4,5},{5,6},{6,7},{7,4},{8,9},{9,10},{10,1... | collective-permute-start | bytes 786440 | tf_op jit(solution)/shard_map/ppermute | solution.py:20
  141.5 55.3 %collective-permute-start.65 = (bf16[128,2048]{1,0:T(8,128)(2,1)S(1)}, bf16[128,2048]{1,0:T(8,128)(2,1)S(1)}, u32[]{:S(2)}, u32[]{:S(2)}) collective-permute-start(bf16[128,2048]{1,0:T(8,128)(2,1)S(1)} %maximum_select_fusion), channel_id=1, source_target_pairs={{0,1},{1,2},{2,3},{3,0},{4,5},{5,6},{6,7},{7,4},{8,9},{9,10},{10,1... | collective-permute-start | bytes 1572872 | tf_op jit(solution)/shard_map/ppermute | solution.py:20
  142.2 55.5 %collective-permute-start.27 = (bf16[128,2048]{1,0:T(8,128)(2,1)S(1)}, bf16[128,2048]{1,0:T(8,128)(2,1)S(1)}, u32[]{:S(2)}, u32[]{:S(2)}) collective-permute-start(bf16[128,2048]{1,0:T(8,128)(2,1)S(1)} %get-tuple-element.64), channel_id=1, source_target_pairs={{0,4},{4,0},{1,5},{5,1},{2,6},{6,2},{3,7},{7,3},{8,12},{12,8},{9,1... | collective-permute-start | bytes 1572872 | tf_op jit(solution)/shard_map/ppermute | solution.py:25
  152.2 45.8 %collective-permute-start.26 = (bf16[128,2048]{1,0:T(8,128)(2,1)S(1)}, bf16[128,2048]{1,0:T(8,128)(2,1)S(1)}, u32[]{:S(2)}, u32[]{:S(2)}) collective-permute-start(bf16[128,2048]{1,0:T(8,128)(2,1)S(1)} %add_convert_fusion.20), channel_id=1, source_target_pairs={{0,1},{1,2},{2,3},{3,0},{4,5},{5,6},{6,7},{7,4},{8,9},{9,10},{10,1... | collective-permute-start | bytes 1572872 | tf_op jit(solution)/shard_map/ppermute | solution.py:20
  156.7 40.1 %collective-permute-start.46 = (bf16[128,1024]{1,0:T(8,128)(2,1)S(1)}, bf16[128,1024]{1,0:T(8,128)(2,1)S(1)}, u32[]{:S(2)}, u32[]{:S(2)}) collective-permute-start(bf16[128,1024]{1,0:T(8,128)(2,1)S(1)} %get-tuple-element.88), channel_id=1, source_target_pairs={{0,2},{1,3},{2,0},{3,1},{4,6},{5,7},{6,4},{7,5},{8,10},{9,11},{10,... | collective-permute-start | bytes 786440 | tf_op jit(solution)/shard_map/ppermute | solution.py:20
  196.8 36.1 %collective-permute-start.54 = (bf16[512,1024]{1,0:T(8,128)(2,1)S(1)}, bf16[512,1024]{1,0:T(8,128)(2,1)S(1)}, u32[]{:S(2)}, u32[]{:S(2)}) collective-permute-start(bf16[512,1024]{1,0:T(8,128)(2,1)S(1)} %constant_dynamic-update-slice_fusion.32), channel_id=1, source_target_pairs={{0,8},{8,0},{16,24},{24,16},{1,9},{9,1},{17,25},{25,17},{2,10},{10... | collective-permute-start | bytes 3145736 | tf_op jit(solution)/shard_map/ppermute | solution.py:25
  203.8 26.5 %collective-permute-start.28 = (bf16[128,2048]{1,0:T(8,128)(2,1)S(1)}, bf16[128,2048]{1,0:T(8,128)(2,1)S(1)}, u32[]{:S(2)}, u32[]{:S(2)}) collective-permute-start(bf16[128,2048]{1,0:T(8,128)(2,1)S(1)} %add_convert_fusion.19), channel_id=1, source_target_pairs={{0,1},{1,2},{2,3},{3,0},{4,5},{5,6},{6,7},{7,4},{8,9},{9,10},{10,1... | collective-permute-start | bytes 1572872 | tf_op jit(solution)/shard_map/ppermute | solution.py:20
  204.0 28.4 %collective-permute-start.31 = (bf16[128,2048]{1,0:T(8,128)(2,1)S(1)}, bf16[128,2048]{1,0:T(8,128)(2,1)S(1)}, u32[]{:S(2)}, u32[]{:S(2)}) collective-permute-start(bf16[128,2048]{1,0:T(8,128)(2,1)S(1)} %get-tuple-element.62), channel_id=1, source_target_pairs={{0,4},{4,0},{1,5},{5,1},{2,6},{6,2},{3,7},{7,3},{8,12},{12,8},{9,1... | collective-permute-start | bytes 1572872 | tf_op jit(solution)/shard_map/ppermute | solution.py:25
  204.1 26.5 %collective-permute-start.66 = (bf16[128,2048]{1,0:T(8,128)(2,1)S(1)}, bf16[128,2048]{1,0:T(8,128)(2,1)S(1)}, u32[]{:S(2)}, u32[]{:S(2)}) collective-permute-start(bf16[128,2048]{1,0:T(8,128)(2,1)S(1)} %collective-permute-done.65), channel_id=1, source_target_pairs={{0,4},{4,0},{1,5},{5,1},{2,6},{6,2},{3,7},{7,3},{8,12},{12,8},{9,1... | collective-permute-start | bytes 1572872 | tf_op jit(solution)/shard_map/ppermute | solution.py:25
  230.7 26.2 %collective-permute-start.55 = (bf16[512,1024]{1,0:T(8,128)(2,1)S(1)}, bf16[512,1024]{1,0:T(8,128)(2,1)S(1)}, u32[]{:S(2)}, u32[]{:S(2)}) collective-permute-start(bf16[512,1024]{1,0:T(8,128)(2,1)S(1)} %constant_dynamic-update-slice_fusion.32), channel_id=1, source_target_pairs={{0,16},{8,24},{16,0},{24,8},{1,17},{9,25},{17,1},{25,9},{2,18},{10... | collective-permute-start | bytes 3145736 | tf_op jit(solution)/shard_map/ppermute | solution.py:25
  232.4 71.5 %collective-permute-start.42 = (bf16[512,1024]{1,0:T(8,128)(2,1)S(1)}, bf16[512,1024]{1,0:T(8,128)(2,1)S(1)}, u32[]{:S(2)}, u32[]{:S(2)}) collective-permute-start(bf16[512,1024]{1,0:T(8,128)(2,1)S(1)} %constant_dynamic-update-slice_fusion.38), channel_id=1, source_target_pairs={{0,8},{8,0},{16,24},{24,16},{1,9},{9,1},{17,25},{25,17},{2,10},{10... | collective-permute-start | bytes 3145736 | tf_op jit(solution)/shard_map/ppermute | solution.py:25
  241.5 37.8 %collective-permute-start.56 = (bf16[512,1024]{1,0:T(8,128)(2,1)S(1)}, bf16[512,1024]{1,0:T(8,128)(2,1)S(1)}, u32[]{:S(2)}, u32[]{:S(2)}) collective-permute-start(bf16[512,1024]{1,0:T(8,128)(2,1)S(1)} %collective-permute-done.54), channel_id=1, source_target_pairs={{0,16},{8,24},{16,0},{24,8},{1,17},{9,25},{17,1},{25,9},{2,18},{10... | collective-permute-start | bytes 3145736 | tf_op jit(solution)/shard_map/ppermute | solution.py:25
  254.4 45.9 %collective-permute-start.49 = (bf16[512,1024]{1,0:T(8,128)(2,1)S(1)}, bf16[512,1024]{1,0:T(8,128)(2,1)S(1)}, u32[]{:S(2)}, u32[]{:S(2)}) collective-permute-start(bf16[512,1024]{1,0:T(8,128)(2,1)S(1)} %constant_dynamic-update-slice_fusion.35), channel_id=1, source_target_pairs={{0,16},{8,24},{16,0},{24,8},{1,17},{9,25},{17,1},{25,9},{2,18},{10... | collective-permute-start | bytes 3145736 | tf_op jit(solution)/shard_map/ppermute | solution.py:25
  256.8 35.2 %collective-permute-start.32 = (bf16[128,2048]{1,0:T(8,128)(2,1)S(1)}, bf16[128,2048]{1,0:T(8,128)(2,1)S(1)}, u32[]{:S(2)}, u32[]{:S(2)}) collective-permute-start(bf16[128,2048]{1,0:T(8,128)(2,1)S(1)} %get-tuple-element.41), channel_id=1, source_target_pairs={{0,4},{4,0},{1,5},{5,1},{2,6},{6,2},{3,7},{7,3},{8,12},{12,8},{9,1... | collective-permute-start | bytes 1572872 | tf_op jit(solution)/shard_map/ppermute | solution.py:25
  269.3 32.1 %collective-permute-start.34 = (bf16[128,2048]{1,0:T(8,128)(2,1)S(1)}, bf16[128,2048]{1,0:T(8,128)(2,1)S(1)}, u32[]{:S(2)}, u32[]{:S(2)}) collective-permute-start(bf16[128,2048]{1,0:T(8,128)(2,1)S(1)} %collective-permute-done.33), channel_id=1, source_target_pairs={{0,4},{4,0},{1,5},{5,1},{2,6},{6,2},{3,7},{7,3},{8,12},{12,8},{9,1... | collective-permute-start | bytes 1572872 | tf_op jit(solution)/shard_map/ppermute | solution.py:25
  301.4 44.9 %collective-permute-start.50 = (bf16[512,1024]{1,0:T(8,128)(2,1)S(1)}, bf16[512,1024]{1,0:T(8,128)(2,1)S(1)}, u32[]{:S(2)}, u32[]{:S(2)}) collective-permute-start(bf16[512,1024]{1,0:T(8,128)(2,1)S(1)} %collective-permute-done.49), channel_id=1, source_target_pairs={{0,8},{8,0},{16,24},{24,16},{1,9},{9,1},{17,25},{25,17},{2,10},{10... | collective-permute-start | bytes 3145736 | tf_op jit(solution)/shard_map/ppermute | solution.py:25
  303.9 48.5 %collective-permute-start.43 = (bf16[512,1024]{1,0:T(8,128)(2,1)S(1)}, bf16[512,1024]{1,0:T(8,128)(2,1)S(1)}, u32[]{:S(2)}, u32[]{:S(2)}) collective-permute-start(bf16[512,1024]{1,0:T(8,128)(2,1)S(1)} %constant_dynamic-update-slice_fusion.38), channel_id=1, source_target_pairs={{0,16},{8,24},{16,0},{24,8},{1,17},{9,25},{17,1},{25,9},{2,18},{10... | collective-permute-start | bytes 3145736 | tf_op jit(solution)/shard_map/ppermute | solution.py:25
  305.4 47.9 %collective-permute-start.44 = (bf16[512,1024]{1,0:T(8,128)(2,1)S(1)}, bf16[512,1024]{1,0:T(8,128)(2,1)}, u32[]{:S(2)}, u32[]{:S(2)}) collective-permute-start(bf16[512,1024]{1,0:T(8,128)(2,1)S(1)} %collective-permute-done.42), channel_id=1, source_target_pairs={{0,16},{8,24},{16,0},{24,8},{1,17},{9,25},{17,1},{25,9},{2,18},{10... | collective-permute-start | bytes 3145736 | tf_op jit(solution)/shard_map/ppermute | solution.py:25
  388.2 38.7 %collective-permute-start.130 = (bf16[512,1024]{1,0:T(8,128)(2,1)}, bf16[512,1024]{1,0:T(8,128)(2,1)}, u32[]{:S(2)}, u32[]{:S(2)}) collective-permute-start(bf16[512,1024]{1,0:T(8,128)(2,1)} %convolution_convert_fusion.4), channel_id=1, source_target_pairs={{0,8},{8,0},{16,24},{24,16},{1,9},{9,1},{17,25},{25,17},{2,10},{10... | collective-permute-start | bytes 3145736 | tf_op jit(solution)/shard_map/ppermute | solution.py:25
  422.7 40.2 %collective-permute-start.118 = (bf16[512,1024]{1,0:T(8,128)(2,1)S(1)}, bf16[512,1024]{1,0:T(8,128)(2,1)S(1)}, u32[]{:S(2)}, u32[]{:S(2)}) collective-permute-start(bf16[512,1024]{1,0:T(8,128)(2,1)S(1)} %copy-done.26), channel_id=1, source_target_pairs={{0,8},{8,0},{16,24},{24,16},{1,9},{9,1},{17,25},{25,17},{2,10},{10... | collective-permute-start | bytes 3145736 | tf_op jit(solution)/shard_map/ppermute | solution.py:25
  447.4 32.1 %collective-permute-start.132 = (bf16[512,1024]{1,0:T(8,128)(2,1)S(1)}, bf16[512,1024]{1,0:T(8,128)(2,1)S(1)}, u32[]{:S(2)}, u32[]{:S(2)}) collective-permute-start(bf16[512,1024]{1,0:T(8,128)(2,1)S(1)} %copy-done.25), channel_id=1, source_target_pairs={{0,8},{8,0},{16,24},{24,16},{1,9},{9,1},{17,25},{25,17},{2,10},{10... | collective-permute-start | bytes 3145736 | tf_op jit(solution)/shard_map/ppermute | solution.py:25
  462.0 26.2 %collective-permute-start.131 = (bf16[512,1024]{1,0:T(8,128)(2,1)S(1)}, bf16[512,1024]{1,0:T(8,128)(2,1)S(1)}, u32[]{:S(2)}, u32[]{:S(2)}) collective-permute-start(bf16[512,1024]{1,0:T(8,128)(2,1)S(1)} %add_convert_fusion.2), channel_id=1, source_target_pairs={{0,16},{8,24},{16,0},{24,8},{1,17},{9,25},{17,1},{25,9},{2,18},{10... | collective-permute-start | bytes 3145736 | tf_op jit(solution)/shard_map/ppermute | solution.py:25
  463.6 47.0 %collective-permute-start.126 = (bf16[512,1024]{1,0:T(8,128)(2,1)S(1)}, bf16[512,1024]{1,0:T(8,128)(2,1)S(1)}, u32[]{:S(2)}, u32[]{:S(2)}) collective-permute-start(bf16[512,1024]{1,0:T(8,128)(2,1)S(1)} %copy-done.24), channel_id=1, source_target_pairs={{0,16},{8,24},{16,0},{24,8},{1,17},{9,25},{17,1},{25,9},{2,18},{10... | collective-permute-start | bytes 3145736 | tf_op jit(solution)/shard_map/ppermute | solution.py:25
  478.4 32.3 %collective-permute-start.125 = (bf16[512,1024]{1,0:T(8,128)(2,1)S(1)}, bf16[512,1024]{1,0:T(8,128)(2,1)S(1)}, u32[]{:S(2)}, u32[]{:S(2)}) collective-permute-start(bf16[512,1024]{1,0:T(8,128)(2,1)S(1)} %add_convert_fusion.4), channel_id=1, source_target_pairs={{0,8},{8,0},{16,24},{24,16},{1,9},{9,1},{17,25},{25,17},{2,10},{10... | collective-permute-start | bytes 3145736 | tf_op jit(solution)/shard_map/ppermute | solution.py:25
  479.5 41.0 %collective-permute-start.120 = (bf16[512,1024]{1,0:T(8,128)(2,1)S(1)}, bf16[512,1024]{1,0:T(8,128)(2,1)S(1)}, u32[]{:S(2)}, u32[]{:S(2)}) collective-permute-start(bf16[512,1024]{1,0:T(8,128)(2,1)S(1)} %convolution_convert_fusion.11), channel_id=1, source_target_pairs={{0,8},{8,0},{16,24},{24,16},{1,9},{9,1},{17,25},{25,17},{2,10},{10... | collective-permute-start | bytes 3145736 | tf_op jit(solution)/shard_map/ppermute | solution.py:25
  486.9 43.5 %collective-permute-start.119 = (bf16[512,1024]{1,0:T(8,128)(2,1)S(1)}, bf16[512,1024]{1,0:T(8,128)(2,1)S(1)}, u32[]{:S(2)}, u32[]{:S(2)}) collective-permute-start(bf16[512,1024]{1,0:T(8,128)(2,1)S(1)} %add_convert_fusion.6), channel_id=1, source_target_pairs={{0,16},{8,24},{16,0},{24,8},{1,17},{9,25},{17,1},{25,9},{2,18},{10... | collective-permute-start | bytes 3145736 | tf_op jit(solution)/shard_map/ppermute | solution.py:25
  488.2 43.7 %collective-permute-start.77 = (bf16[128,2048]{1,0:T(8,128)(2,1)S(1)}, bf16[128,2048]{1,0:T(8,128)(2,1)S(1)}, u32[]{:S(2)}, u32[]{:S(2)}) collective-permute-start(bf16[128,2048]{1,0:T(8,128)(2,1)S(1)} %copy-done.36), channel_id=1, source_target_pairs={{0,4},{4,0},{1,5},{5,1},{2,6},{6,2},{3,7},{7,3},{8,12},{12,8},{9,1... | collective-permute-start | bytes 1572872 | tf_op jit(solution)/shard_map/ppermute | solution.py:25
  510.7 28.1 %collective-permute-start.63 = (bf16[128,2048]{1,0:T(8,128)(2,1)S(1)}, bf16[128,2048]{1,0:T(8,128)(2,1)S(1)}, u32[]{:S(2)}, u32[]{:S(2)}) collective-permute-start(bf16[128,2048]{1,0:T(8,128)(2,1)S(1)} %get-tuple-element.58), channel_id=1, source_target_pairs={{0,4},{4,0},{1,5},{5,1},{2,6},{6,2},{3,7},{7,3},{8,12},{12,8},{9,1... | collective-permute-start | bytes 1572872 | tf_op jit(solution)/shard_map/ppermute | solution.py:25
  530.3 33.1 %collective-permute-start.133 = (bf16[128,1024]{1,0:T(8,128)(2,1)S(1)}, bf16[128,1024]{1,0:T(8,128)(2,1)S(1)}, u32[]{:S(2)}, u32[]{:S(2)}) collective-permute-start(bf16[128,1024]{1,0:T(8,128)(2,1)S(1)} %get-tuple-element.67), channel_id=1, source_target_pairs={{0,1},{1,2},{2,3},{3,0},{4,5},{5,6},{6,7},{7,4},{8,9},{9,10},{10,1... | collective-permute-start | bytes 786440 | tf_op jit(solution)/shard_map/ppermute | solution.py:20
  531.9 47.6 %collective-permute-start.134 = (bf16[128,1024]{1,0:T(8,128)(2,1)S(1)}, bf16[128,1024]{1,0:T(8,128)(2,1)S(1)}, u32[]{:S(2)}, u32[]{:S(2)}) collective-permute-start(bf16[128,1024]{1,0:T(8,128)(2,1)S(1)} %get-tuple-element.66), channel_id=1, source_target_pairs={{0,2},{1,3},{2,0},{3,1},{4,6},{5,7},{6,4},{7,5},{8,10},{9,11},{10,... | collective-permute-start | bytes 786440 | tf_op jit(solution)/shard_map/ppermute | solution.py:20
  550.6 39.9 %collective-permute-start.135 = (bf16[128,1024]{1,0:T(8,128)(2,1)S(1)}, bf16[128,1024]{1,0:T(8,128)(2,1)S(1)}, u32[]{:S(2)}, u32[]{:S(2)}) collective-permute-start(bf16[128,1024]{1,0:T(8,128)(2,1)S(1)} %get-tuple-element.65), channel_id=1, source_target_pairs={{0,3},{1,0},{2,1},{3,2},{4,7},{5,4},{6,5},{7,6},{8,11},{9,8},{10,9... | collective-permute-start | bytes 786440 | tf_op jit(solution)/shard_map/ppermute | solution.py:20
  559.0 27.6 %collective-permute-start.128 = (bf16[128,1024]{1,0:T(8,128)(2,1)S(1)}, bf16[128,1024]{1,0:T(8,128)(2,1)S(1)}, u32[]{:S(2)}, u32[]{:S(2)}) collective-permute-start(bf16[128,1024]{1,0:T(8,128)(2,1)S(1)} %get-tuple-element.69), channel_id=1, source_target_pairs={{0,2},{1,3},{2,0},{3,1},{4,6},{5,7},{6,4},{7,5},{8,10},{9,11},{10,... | collective-permute-start | bytes 786440 | tf_op jit(solution)/shard_map/ppermute | solution.py:20
  563.4 30.3 %collective-permute-start.129 = (bf16[128,1024]{1,0:T(8,128)(2,1)S(1)}, bf16[128,1024]{1,0:T(8,128)(2,1)S(1)}, u32[]{:S(2)}, u32[]{:S(2)}) collective-permute-start(bf16[128,1024]{1,0:T(8,128)(2,1)S(1)} %get-tuple-element.68), channel_id=1, source_target_pairs={{0,3},{1,0},{2,1},{3,2},{4,7},{5,4},{6,5},{7,6},{8,11},{9,8},{10,9... | collective-permute-start | bytes 786440 | tf_op jit(solution)/shard_map/ppermute | solution.py:20
  575.3 42.0 %collective-permute-start.121 = (bf16[128,1024]{1,0:T(8,128)(2,1)S(1)}, bf16[128,1024]{1,0:T(8,128)(2,1)S(1)}, u32[]{:S(2)}, u32[]{:S(2)}) collective-permute-start(bf16[128,1024]{1,0:T(8,128)(2,1)S(1)} %get-tuple-element.73), channel_id=1, source_target_pairs={{0,1},{1,2},{2,3},{3,0},{4,5},{5,6},{6,7},{7,4},{8,9},{9,10},{10,1... | collective-permute-start | bytes 786440 | tf_op jit(solution)/shard_map/ppermute | solution.py:20
  579.5 50.3 %collective-permute-start.122 = (bf16[128,1024]{1,0:T(8,128)(2,1)S(1)}, bf16[128,1024]{1,0:T(8,128)(2,1)S(1)}, u32[]{:S(2)}, u32[]{:S(2)}) collective-permute-start(bf16[128,1024]{1,0:T(8,128)(2,1)S(1)} %get-tuple-element.72), channel_id=1, source_target_pairs={{0,2},{1,3},{2,0},{3,1},{4,6},{5,7},{6,4},{7,5},{8,10},{9,11},{10,... | collective-permute-start | bytes 786440 | tf_op jit(solution)/shard_map/ppermute | solution.py:20
  590.5 39.5 %collective-permute-start.123 = (bf16[128,1024]{1,0:T(8,128)(2,1)S(1)}, bf16[128,1024]{1,0:T(8,128)(2,1)S(1)}, u32[]{:S(2)}, u32[]{:S(2)}) collective-permute-start(bf16[128,1024]{1,0:T(8,128)(2,1)S(1)} %get-tuple-element.71), channel_id=1, source_target_pairs={{0,3},{1,0},{2,1},{3,2},{4,7},{5,4},{6,5},{7,6},{8,11},{9,8},{10,9... | collective-permute-start | bytes 786440 | tf_op jit(solution)/shard_map/ppermute | solution.py:20
  593.8 41.1 %collective-permute-start.78 = (bf16[128,2048]{1,0:T(8,128)(2,1)S(1)}, bf16[128,2048]{1,0:T(8,128)(2,1)S(1)}, u32[]{:S(2)}, u32[]{:S(2)}) collective-permute-start(bf16[128,2048]{1,0:T(8,128)(2,1)S(1)} %get-tuple-element.36), channel_id=1, source_target_pairs={{0,4},{4,0},{1,5},{5,1},{2,6},{6,2},{3,7},{7,3},{8,12},{12,8},{9,1... | collective-permute-start | bytes 1572872 | tf_op jit(solution)/shard_map/ppermute | solution.py:25
  691.6 38.3 %collective-permute-start.101 = (bf16[512,768]{1,0:T(8,128)(2,1)S(1)}, bf16[512,768]{1,0:T(8,128)(2,1)S(1)}, u32[]{:S(2)}, u32[]{:S(2)}) collective-permute-start(bf16[512,768]{1,0:T(8,128)(2,1)S(1)} %convolution_convert_fusion.15), channel_id=1, source_target_pairs={{0,16},{8,24},{16,0},{24,8},{1,17},{9,25},{17,1},{25,9},{2,18},{10... | collective-permute-start | bytes 2359304 | tf_op jit(solution)/shard_map/ppermute | solution.py:25
  717.3 46.7 %collective-permute-start.91 = (bf16[128,2048]{1,0:T(8,128)(2,1)S(1)}, bf16[128,2048]{1,0:T(8,128)(2,1)S(1)}, u32[]{:S(2)}, u32[]{:S(2)}) collective-permute-start(bf16[128,2048]{1,0:T(8,128)(2,1)S(1)} %get-tuple-element.50), channel_id=1, source_target_pairs={{0,4},{4,0},{1,5},{5,1},{2,6},{6,2},{3,7},{7,3},{8,12},{12,8},{9,1... | collective-permute-start | bytes 1572872 | tf_op jit(solution)/shard_map/ppermute | solution.py:25
  733.4 30.4 %collective-permute-start.103 = (bf16[128,768]{1,0:T(8,128)(2,1)S(1)}, bf16[128,768]{1,0:T(8,128)(2,1)S(1)}, u32[]{:S(2)}, u32[]{:S(2)}) collective-permute-start(bf16[128,768]{1,0:T(8,128)(2,1)S(1)} %get-tuple-element.92), channel_id=1, source_target_pairs={{0,2},{1,3},{2,0},{3,1},{4,6},{5,7},{6,4},{7,5},{8,10},{9,11},{10,... | collective-permute-start | bytes 589832 | tf_op jit(solution)/shard_map/ppermute | solution.py:20
  736.3 27.5 %collective-permute-start.104 = (bf16[128,768]{1,0:T(8,128)(2,1)S(1)}, bf16[128,768]{1,0:T(8,128)(2,1)S(1)}, u32[]{:S(2)}, u32[]{:S(2)}) collective-permute-start(bf16[128,768]{1,0:T(8,128)(2,1)S(1)} %get-tuple-element.91), channel_id=1, source_target_pairs={{0,3},{1,0},{2,1},{3,2},{4,7},{5,4},{6,5},{7,6},{8,11},{9,8},{10,9... | collective-permute-start | bytes 589832 | tf_op jit(solution)/shard_map/ppermute | solution.py:20
  (164 other events, 2758.2 us)

commit v2 on v1

v2 whole, which is shorter than its diff:
```python
from functools import partial

import jax
import jax.numpy as jnp
from jax import lax
from jax.experimental import pallas as pl
from jax.experimental.pallas import tpu as pltpu
from jax.sharding import PartitionSpec as P

HEADS = 32
HEAD_DIM = 64
HALF = HEAD_DIM // 2
EPSILON = 1e-05
ROPE_BASE = 130000.0
LOW = jnp.bfloat16
WIDE = jnp.float32
GROUPS = 4
ANY = pl.BlockSpec(memory_space=pl.ANY)


def turn(value, axis, by):
    count = lax.axis_size(axis)
    return lax.ppermute(value, axis, [(i, (i + by) % count) for i in range(count)])


def swap(value, axis, mask):
    count = lax.axis_size(axis)
    return lax.ppermute(value, axis, [(i, i ^ mask) for i in range(count)])


def after(value, *others):
    return lax.optimization_barrier((value, *others))[0]


def matmul(left, right):
    return jnp.dot(left, right, preferred_element_type=WIDE)


def over_rows(left, right):
    return lax.dot_general(left, right, (((0,), (0,)), ((), ())), preferred_element_type=WIDE)


def over_cols(left, right):
    return lax.dot_general(left, right, (((1,), (1,)), ((), ())), preferred_element_type=WIDE)


def slot_order(array):
    rank = lax.axis_index("slot")
    parts = jnp.split(array, GROUPS, axis=-1)
    for bit in (1, 2):
        flip = (rank & bit) != 0
        parts = [jnp.where(flip, parts[i ^ bit], parts[i]) for i in range(GROUPS)]
    return jnp.concatenate(parts, axis=-1)


def seq_gather(rows):
    count = lax.axis_size("seq")
    held = [rows]
    bit = 1
    while bit < count:
        held = held + [swap(part, "seq", bit) for part in held]
        bit *= 2
    return held


def seq_reduce(parts):
    bit = lax.axis_size("seq") // 2
    parts = [[part] for part in parts]
    while bit >= 1:
        kept = parts[:bit]
        for mine, other in zip(kept, parts[bit:]):
            mine.append(swap(add_up(other).astype(LOW), "seq", bit))
        parts = kept
        bit //= 2
    return parts[0]


def add_up(summands):
    total = summands[0]
    for summand in summands[1:]:
        total = total.astype(WIDE) + summand.astype(WIDE)
    return total


class Phases:
    def __init__(self):
        self.ended = ()

    def take(self, *values):
        values = tuple(values)
        if self.ended:
            values = lax.optimization_barrier((values, self.ended))[0]
        return values[0] if len(values) == 1 else values

    def end(self, *values):
        self.ended = values


class Exchange:
    def __init__(self, pieces):
        self.pieces = pieces
        self.got = {0: pieces[0]}

    def send(self, *steps):
        for k in steps:
            self.got[k] = turn(self.pieces[k], "blk", k)
        return [self.got[k] for k in steps]

    def by_rank(self):
        blks, rank = lax.axis_size("blk"), lax.axis_index("blk")
        rows, cols = self.got[0].shape
        full = jnp.zeros((blks * rows, cols), self.got[0].dtype)
        for k in range(blks):
            full = lax.dynamic_update_slice(full, self.got[k], ((rank - k) % blks * rows, 0))
        return full


def column_pieces(arrays, parts=1):
    blks, rank = lax.axis_size("blk"), lax.axis_index("blk")

    def cut(array, owner, part):
        width = array.shape[1] // (blks * parts)
        return lax.dynamic_slice(array, (0, (owner * parts + part) * width), (array.shape[0], width))

    return [
        jnp.concatenate([cut(a, (rank + k) % blks, part) for part in range(parts) for a in arrays], axis=1)
        for k in range(blks)
    ]


def row_pieces(summands):
    blks, rank = lax.axis_size("blk"), lax.axis_index("blk")
    rows = summands[0].shape[0] // blks

    def cut(owner):
        parts = [lax.dynamic_slice(s, (owner * rows, 0), (rows, s.shape[1])) for s in summands]
        return add_up(parts).astype(LOW)

    return [cut((rank + k) % blks) for k in range(blks)]


def join_owners(exchanged, cuts, scale):
    blks, rank = lax.axis_size("blk"), lax.axis_index("blk")
    wide = sum(width for _, width in cuts)
    out = jnp.zeros((exchanged.got[0].shape[0], blks * wide), WIDE)
    for k in range(blks):
        first = (rank - k) % blks * wide
        for at, width in cuts:
            part = exchanged.got[k][:, at : at + width].astype(WIDE) * scale
            out = lax.dynamic_update_slice(out, part, (0, first))
            first = first + width
    return out


def norm_rows(rows):
    inverse = lax.rsqrt(jnp.mean(rows * rows, axis=-1, keepdims=True) + EPSILON)
    return rows * inverse, inverse


def norm_back(normed, inverse, upstream):
    product = upstream * normed
    return inverse * (upstream - normed * jnp.mean(product, axis=-1, keepdims=True)), product


def vmem(shape):
    return pl.BlockSpec(shape, lambda *_: (0,) * len(shape))


def params(mebibytes):
    return pltpu.CompilerParams(vmem_limit_bytes=mebibytes << 20)


def cost():
    return pl.CostEstimate(flops=1, bytes_accessed=1, transcendentals=0)


def partner(vectors):
    width = vectors.shape[1]
    if width % 128 == 0:
        lanes = lax.broadcasted_iota(jnp.int32, (1, width), 1)
        ahead = pltpu.roll(vectors, width - HALF, 1)
        behind = pltpu.roll(vectors, HALF, 1)
        return jnp.where(lanes % HEAD_DIM < HALF, ahead, behind)
    parts = []
    for first in range(0, width, HEAD_DIM):
        parts += [vectors[:, first + HALF : first + HEAD_DIM], vectors[:, first : first + HALF]]
    return jnp.concatenate(parts, axis=1)


def widen(table, width):
    return table if table.shape[1] == width else jnp.concatenate([table] * (width // table.shape[1]), axis=1)


def qkv_kernel(width, *refs):
    parts, weights, (cos_ref, sin_ref) = refs[:-10], refs[-10:-6], refs[-6:-4]
    h_ref, q_ref, k_ref, v_ref = refs[-4:]
    size, model = parts[0].shape
    step = model // GROUPS
    for n, part in enumerate(parts):
        normed, _ = norm_rows(part[...].astype(WIDE))
        h_ref[n * size : (n + 1) * size, :] = normed.astype(LOW)
    total = h_ref.shape[0]
    rows = min(512, total)

    def some(first):
        here = slice(first, first + rows)
        pre = matmul(h_ref[here, :step], weights[0][:, : 3 * width])
        for i in range(1, GROUPS):
            pre += matmul(h_ref[here, i * step : (i + 1) * step], weights[i][:, : 3 * width])
        cos, sin = widen(cos_ref[here, :], width), widen(sin_ref[here, :], width)
        for at, out_ref in ((0, q_ref), (1, k_ref)):
            half = pre[:, at * width : (at + 1) * width]
            out_ref[here, :] = (half * cos + partner(half) * sin).astype(LOW)
        v_ref[here, :] = pre[:, 2 * width :].astype(LOW)

    for first in range(0, total, rows):
        some(first)


def project_qkv(parts, weights, cos, sin, width):
    size, model = parts[0].shape
    total = size * len(parts)
    return pl.pallas_call(
        partial(qkv_kernel, width),
        grid=(1,),
        in_specs=[vmem((size, model))] * len(parts) + [vmem(w.shape) for w in weights] + [vmem(cos.shape)] * 2,
        out_specs=[vmem((total, model))] + [vmem((total, width))] * 3,
        out_shape=[jax.ShapeDtypeStruct((total, model), LOW)] + [jax.ShapeDtypeStruct((total, width), LOW)] * 3,
        compiler_params=params(60),
        cost_estimate=cost(),
        name="project_qkv",
    )(*parts, *weights, cos, sin)


def row_positions(index, blk_rank, seq_rank, blks, seqs, size):
    sub = index // size
    k, m = sub // seqs, sub % seqs
    return ((blk_rank - k + blks) % blks * seqs + (seq_rank ^ m)) * size + index % size


def allowed_pairs(dims, place_ref, firsts, rows):
    total, blks, seqs, size = dims
    blk_rank, seq_rank, length = place_ref[0], place_ref[1], place_ref[2]
    k_index = lax.broadcasted_iota(jnp.int32, (1, total), 1)
    k_pos = row_positions(k_index, blk_rank, seq_rank, blks, seqs, size)
    k_pos = jnp.where(k_pos < length, k_pos, jnp.int32(1 << 30))
    index = lax.broadcasted_iota(jnp.int32, (rows, 1), 0)
    q_pos = [row_positions(first + index, blk_rank, seq_rank, blks, seqs, size) for first in firsts]
    return k_pos <= jnp.concatenate(q_pos, axis=0)


def tiles_of(count, block):
    if count * block <= 512:
        return [[(g, 0, block) for g in range(count)]]
    rows = min(256, block)
    return [[(g, first, rows)] for g in range(count) for first in range(0, block, rows)]


def rows_of(refs, tile):
    return jnp.concatenate([refs[g][first : first + rows, :] for g, first, rows in tile], axis=0)


def put_rows(refs, tile, value):
    at = 0
    for g, first, rows in tile:
        refs[g][first : first + rows, :] = value[at : at + rows]
        at += rows


def put_parts(terms, size, column, value):
    seqs = len(terms)
    for n in range(value.shape[0] // size):
        g, m = n // seqs, n % seqs
        terms[m][g * size : (g + 1) * size, column : column + value.shape[1]] = value[n * size : (n + 1) * size]


def attend_kernel(dims, ks, width, place_ref, *refs):
    count, seqs = len(ks), dims[2]
    q_refs, (k_ref, v_ref), weights = refs[:count], refs[count : count + 2], refs[count + 2 : count + 6]
    out_refs, lse_refs, terms = refs[count + 6 : 2 * count + 6], refs[2 * count + 6 : 3 * count + 6], refs[3 * count + 6 :]
    block = q_refs[0].shape[0]
    lanes = lax.broadcasted_iota(jnp.int32, (1, width), 1)
    lse_lanes = lax.broadcasted_iota(jnp.int32, (1, 128), 1)
    for tile in tiles_of(count, block):
        rows = tile[0][2]
        allowed = allowed_pairs(dims, place_ref, [ks[g] * block + first for g, first, _ in tile], rows)
        queries = rows_of(q_refs, tile).astype(WIDE) * HEAD_DIM**-0.5
        wide = rows * len(tile)

        def one_head(head, carried):
            out, lse = carried
            mine = lanes // HEAD_DIM == head
            picked = jnp.where(mine, queries, 0.0).astype(LOW)
            scores = jnp.where(allowed, over_cols(picked, k_ref[...]), -1e30)
            top = jnp.max(scores, axis=1, keepdims=True)
            probs = jnp.exp(scores - top)
            weight = jnp.sum(probs, axis=1, keepdims=True)
            mixed = matmul(probs.astype(LOW), v_ref[...]) / weight
            return jnp.where(mine, mixed, out), jnp.where(lse_lanes == head, top + jnp.log(weight), lse)

        out, lse = lax.fori_loop(
            0, width // HEAD_DIM, one_head, (jnp.zeros((wide, width), WIDE), jnp.zeros((wide, 128), WIDE))
        )
        put_rows(out_refs, tile, out.astype(LOW))
        put_rows(lse_refs, tile, lse)
    attended = jnp.concatenate([ref[...] for ref in out_refs], axis=0)
    for i, weight in enumerate(weights):
        step = weight.shape[0]
        put_parts(terms, block // seqs, i * step, over_cols(attended, weight[:, 3 * width :]).astype(LOW))


def attend_blocks(ks, place, queries, key_rows, val_rows, weights, size, model):
    total, width = queries.shape
    blks, seqs, count = lax.axis_size("blk"), lax.axis_size("seq"), len(ks)
    block = total // blks
    rows_at = lambda k, wide: pl.BlockSpec((block, wide), lambda *_: (k, 0))
    got = pl.pallas_call(
        partial(attend_kernel, (total, blks, seqs, size), ks, width),
        grid_spec=pltpu.PrefetchScalarGridSpec(
            num_scalar_prefetch=1,
            grid=(1,),
            in_specs=[rows_at(k, width) for k in ks] + [vmem((total, width))] * 2 + [vmem(w.shape) for w in weights],
            out_specs=[vmem((block, width))] * count + [vmem((block, 128))] * count + [vmem((count * size, model))] * seqs,
        ),
        out_shape=[jax.ShapeDtypeStruct((block, width), LOW)] * count
        + [jax.ShapeDtypeStruct((block, 128), WIDE)] * count
        + [jax.ShapeDtypeStruct((count * size, model), LOW)] * seqs,
        compiler_params=params(56),
        cost_estimate=cost(),
        name="attend_blocks",
    )(place, *[queries] * count, key_rows, val_rows, *weights)
    return got[:count], got[count : 2 * count], got[2 * count :]


def mlp_kernel(count, seqs, place_ref, *refs):
    parts, pairs, down = refs[:count], (refs[count : count + 4], refs[count + 4 : count + 8]), refs[count + 8 : count + 12]
    grad_acc, out_acc, h_rel = refs[-3:]
    outs = refs[-3 - 4 - 2 * seqs : -3]
    h_ref, c_ref, act_ref, pair_ref = outs[:4]
    grad_terms, out_terms = outs[4 : 4 + seqs], outs[4 + seqs :]
    size, model = parts[0].shape[0], h_ref.shape[1]
    step, hidden = model // GROUPS, down[0].shape[1]
    j = pl.program_id(0)
    groups = [slice(i * step, (i + 1) * step) for i in range(GROUPS)]

    @pl.when(j == 0)
    def _():
        for m in range(count):
            rows = slice(m * size, (m + 1) * size)
            h_rel[rows, :] = parts[m][:, :model]
            c_ref[rows, :] = parts[m][:, model:]
            for i in range(GROUPS):
                there = pl.multiple_of((place_ref[3] ^ i) * step, step)
                h_ref[rows, pl.ds(there, step)] = parts[m][:, groups[i]]

    def pair_weight(i):
        return jnp.where(j == 0, pairs[0][i][...], pairs[1][i][...])

    both = matmul(h_rel[:, groups[0]], pair_weight(0))
    grad_act = matmul(c_ref[:, groups[0]], down[0][...])
    for i in range(1, GROUPS):
        both += matmul(h_rel[:, groups[i]], pair_weight(i))
        grad_act += matmul(c_ref[:, groups[i]], down[i][...])
    gate, up = both[:, :hidden], both[:, hidden:]
    sig = jax.nn.sigmoid(gate)
    act_ref[...] = (gate * sig * up).astype(LOW)
    pair_ref[:, :hidden] = (grad_act * up * sig * (1.0 + gate * (1.0 - sig))).astype(LOW)
    pair_ref[:, hidden:] = (grad_act * gate * sig).astype(LOW)
    for i, here in enumerate(groups):
        grad = over_cols(pair_ref[...], pair_weight(i))
        out = over_cols(act_ref[...], down[i][...])

        @pl.when(j == 0)
        def _():
            grad_acc[:, here] = grad
            out_acc[:, here] = out

        @pl.when(j == 1)
        def _():
            grad_sum, out_sum = grad_acc[:, here] + grad, out_acc[:, here] + out
            put_parts(grad_terms, size, i * step, grad_sum.astype(LOW))
            put_parts(out_terms, size, i * step, out_sum.astype(LOW))


def mlp_blocks(at, seqs, place, parts, pairs, down, held, total):
    count, (size, model) = len(parts), (parts[0].shape[0], parts[0].shape[1] // 2)
    step, hidden = model // GROUPS, down[0].shape[1] // 2
    rows = count * size
    old = [] if held is None else list(held)
    mine = lambda wide: pl.BlockSpec((rows, wide), lambda j, place: (at, 0))
    mine_half = lambda wide: pl.BlockSpec((rows, wide), lambda j, place: (at, j))
    half = lambda wide: pl.BlockSpec((step, wide), lambda j, place: (0, j))
    got = pl.pallas_call(
        partial(mlp_kernel, count, seqs),
        grid_spec=pltpu.PrefetchScalarGridSpec(
            num_scalar_prefetch=1,
            grid=(2,),
            in_specs=[vmem((size, 2 * model))] * count
            + [vmem((step, 2 * hidden))] * 8
            + [half(hidden)] * 4
            + [ANY] * len(old),
            out_specs=[mine(model), mine(model), mine_half(hidden), mine_half(2 * hidden)]
            + [vmem((rows // seqs, model))] * (2 * seqs),
            scratch_shapes=[pltpu.VMEM((rows, model), WIDE)] * 2 + [pltpu.VMEM((rows, model), LOW)],
        ),
        out_shape=[jax.ShapeDtypeStruct((total, model), LOW)] * 2
        + [jax.ShapeDtypeStruct((total, 2 * hidden), LOW), jax.ShapeDtypeStruct((total, 4 * hidden), LOW)]
        + [jax.ShapeDtypeStruct((rows // seqs, model), LOW)] * (2 * seqs),
        input_output_aliases={count + 13 + i: i for i in range(4)} if old else {},
        compiler_params=params(60),
        cost_estimate=cost(),
        name="mlp_blocks",
    )(place, *parts, *pairs[0], *pairs[1], *down, *old)
    return got[:4], got[4 : 4 + seqs], got[4 + seqs :]


def attend_back_kernel(dims, ks, width, fresh, place_ref, *refs):
    count, seqs = len(ks), dims[2]

    def some(number):
        nonlocal refs
        taken, refs = refs[:number], refs[number:]
        return taken

    q_refs, (k_ref, v_ref), out_refs, lse_refs = some(count), some(2), some(count), some(count)
    cos_refs, sin_refs, weights, parts = some(count), some(count), some(4), some(count * seqs)
    old = [] if fresh else some(3)
    (r_ref, gk_ref, gv_ref), gq_refs, (cot_ref,) = some(3), some(count), some(1)
    block = q_refs[0].shape[0]
    size = block // seqs
    lanes = lax.broadcasted_iota(jnp.int32, (1, width), 1)
    lse_lanes = lax.broadcasted_iota(jnp.int32, (1, 128), 1)
    gk_ref[...] = jnp.zeros_like(gk_ref) if fresh else old[1][...]
    gv_ref[...] = jnp.zeros_like(gv_ref) if fresh else old[2][...]
    for n, part in enumerate(parts):
        r_ref[n * size : (n + 1) * size, :] = part[...]
    step = weights[0].shape[0]
    cot = matmul(r_ref[:, :step], weights[0][:, 3 * width :])
    for i in range(1, GROUPS):
        cot += matmul(r_ref[:, i * step : (i + 1) * step], weights[i][:, 3 * width :])
    cot_ref[...] = cot.astype(LOW).astype(WIDE)
    for tile in tiles_of(count, block):
        rows = tile[0][2]
        allowed = allowed_pairs(dims, place_ref, [ks[g] * block + first for g, first, _ in tile], rows)
        queries = rows_of(q_refs, tile).astype(WIDE) * HEAD_DIM**-0.5
        tile_cot = jnp.concatenate([cot_ref[g * block + first : g * block + first + n, :] for g, first, n in tile], axis=0)
        dots = tile_cot * rows_of(out_refs, tile).astype(WIDE)
        tile_lse = rows_of(lse_refs, tile)
        wide = rows * len(tile)

        def one_head(head, grad_q):
            mine = lanes // HEAD_DIM == head
            picked = jnp.where(mine, queries, 0.0).astype(LOW)
            cot_head = jnp.where(mine, tile_cot, 0.0).astype(LOW)
            row_dot = jnp.sum(jnp.where(mine, dots, 0.0), axis=1, keepdims=True)
            lse = jnp.sum(jnp.where(lse_lanes == head, tile_lse, 0.0), axis=1, keepdims=True)
            scores = jnp.where(allowed, over_cols(picked, k_ref[...]), -1e30)
            probs = jnp.exp(scores - lse)
            gv_ref[...] += over_rows(probs.astype(LOW), cot_head)
            grad_probs = over_cols(cot_head, v_ref[...])
            grad_scores = (probs * (grad_probs - row_dot)).astype(LOW)
            gk_ref[...] += over_rows(grad_scores, picked)
            return jnp.where(mine, matmul(grad_scores, k_ref[...]) * HEAD_DIM**-0.5, grad_q)

        grad_q = lax.fori_loop(0, width // HEAD_DIM, one_head, jnp.zeros((wide, width), WIDE))
        low = grad_q.astype(LOW).astype(WIDE)
        cos, sin = widen(rows_of(cos_refs, tile), width), widen(rows_of(sin_refs, tile), width)
        put_rows(gq_refs, tile, (low * cos - partner(low) * sin).astype(LOW))


def attend_back_blocks(at, ks, place, queries, key_rows, val_rows, attended, lse, cos, sin, weights, parts, held):
    total, width = queries.shape
    blks, seqs, count = lax.axis_size("blk"), lax.axis_size("seq"), len(ks)
    size, model = parts[0].shape
    block = total // blks
    rows_at = lambda k, wide: pl.BlockSpec((block, wide), lambda *_: (k, 0))
    whole = vmem((total, width))
    old = [] if held is None else list(held)
    first_old = 1 + count + 2 + 2 * count + 2 * count + 4 + count * seqs
    tables = [rows_at(k, cos.shape[1]) for k in ks]
    got = pl.pallas_call(
        partial(attend_back_kernel, (total, blks, seqs, size), ks, width, held is None),
        grid_spec=pltpu.PrefetchScalarGridSpec(
            num_scalar_prefetch=1,
            grid=(1,),
            in_specs=[rows_at(k, width) for k in ks]
            + [whole] * 2
            + [vmem((block, width))] * count
            + [vmem((block, 128))] * count
            + tables * 2
            + [vmem(w.shape) for w in weights]
            + [vmem((size, model))] * (count * seqs)
            + ([ANY, whole, whole] if old else []),
            out_specs=[pl.BlockSpec((count * block, model), lambda *_: (at, 0)), whole, whole] + [vmem((block, width))] * count,
            scratch_shapes=[pltpu.VMEM((count * block, width), WIDE)],
        ),
        out_shape=[jax.ShapeDtypeStruct((total, model), LOW)]
        + [jax.ShapeDtypeStruct((total, width), WIDE)] * 2
        + [jax.ShapeDtypeStruct((block, width), LOW)] * count,
        input_output_aliases={first_old + i: i for i in range(3)} if old else {},
        compiler_params=params(60),
        cost_estimate=cost(),
        name="attend_back_blocks",
    )(
        place, *[queries] * count, key_rows, val_rows, *[attended[k] for k in ks], *[lse[k] for k in ks],
        *[cos] * count, *[sin] * count, *weights, *parts, *old,
    )
    return got[:3], got[3:]


def finish_kernel(width, count, seqs, *refs):
    def some(number):
        nonlocal refs
        taken, refs = refs[:number], refs[number:]
        return taken

    gq_refs, gk_refs, gv_refs, cos_refs, sin_refs = (some(count) for _ in range(5))
    weights, parts = some(4), some(count * seqs)
    outs, (gain_ref,), terms = some(count), some(1), some(seqs)
    size = parts[0].shape[0]
    step = weights[0].shape[0]
    for g, out_ref in enumerate(outs):
        low_k = gk_refs[g][...].astype(LOW).astype(WIDE)
        cos, sin = widen(cos_refs[g][...], width), widen(sin_refs[g][...], width)
        out_ref[:, :width] = gq_refs[g][...]
        out_ref[:, width : 2 * width] = (low_k * cos - partner(low_k) * sin).astype(LOW)
        out_ref[:, 2 * width :] = gv_refs[g][...].astype(LOW)
    grads = jnp.concatenate([ref[...] for ref in outs], axis=0)
    inverses = []
    for part in parts:
        rows = part[...].astype(WIDE)
        inverses.append(lax.rsqrt(jnp.mean(rows * rows, axis=-1, keepdims=True) + EPSILON))
    for i in range(GROUPS):
        here = slice(i * step, (i + 1) * step)
        grad = over_cols(grads, weights[i][:, : 3 * width])
        put_parts(terms, size, i * step, grad.astype(LOW))
        gain = 0.0
        for n, part in enumerate(parts):
            mine = grad[n * size : (n + 1) * size]
            gain += jnp.sum(mine * (part[:, here].astype(WIDE) * inverses[n]), axis=0, keepdims=True)
        gain_ref[:, here] = gain


def finish_blocks(ks, grad_q, grad_k, grad_v, cos, sin, weights, parts):
    count = len(ks)
    total, width = grad_k.shape
    seqs, (size, model) = len(parts) // count, parts[0].shape
    block = size * seqs
    rows_at = lambda k, wide: pl.BlockSpec((block, wide), lambda _: (k, 0))
    tables = [rows_at(k, cos.shape[1]) for k in ks]
    got = pl.pallas_call(
        partial(finish_kernel, width, count, seqs),
        grid=(1,),
        in_specs=[vmem((block, width))] * count
        + [rows_at(k, width) for k in ks] * 2
        + tables * 2
        + [vmem(w.shape) for w in weights]
        + [vmem((size, model))] * (count * seqs),
        out_specs=[vmem((block, 3 * width))] * count + [vmem((1, model))] + [vmem((count * size, model))] * seqs,
        out_shape=[jax.ShapeDtypeStruct((block, 3 * width), LOW)] * count
        + [jax.ShapeDtypeStruct((1, model), WIDE)]
        + [jax.ShapeDtypeStruct((count * size, model), LOW)] * seqs,
        compiler_params=params(56),
        cost_estimate=cost(),
        name="finish_blocks",
    )(*[grad_q[k] for k in ks], *[grad_k] * count, *[grad_v] * count, *[cos] * count, *[sin] * count, *weights, *parts)
    return got[:count], got[count], got[count + 1 :]


def weight_kernel(counts, *refs):
    outs = refs[-GROUPS:]
    step = outs[0].shape[0]
    for i, out_ref in enumerate(outs):
        at, column = 0, 0
        for count in counts:
            left_ref, rights = refs[at], refs[at + 1 : at + 1 + count]
            rows, wide = rights[0].shape
            here = slice(i * step, (i + 1) * step)
            total = over_rows(left_ref[:rows, here], rights[0][...])
            for g in range(1, count):
                total += over_rows(left_ref[g * rows : (g + 1) * rows, here], rights[g][...])
            out_ref[:, column : column + wide] = total.astype(LOW)
            at, column = at + 1 + count, column + wide


def weight_terms(*pairs):
    step = pairs[0][0].shape[1] // GROUPS
    cols = sum(rights[0].shape[1] for _, rights in pairs)
    arrays = [a for left, rights in pairs for a in (left, *rights)]
    return pl.pallas_call(
        partial(weight_kernel, [len(rights) for _, rights in pairs]),
        grid=(1,),
        in_specs=[vmem(a.shape) for a in arrays],
        out_specs=[vmem((step, cols))] * GROUPS,
        out_shape=[jax.ShapeDtypeStruct((step, cols), LOW)] * GROUPS,
        compiler_params=params(60),
        cost_estimate=cost(),
        name="weight_terms",
    )(*arrays)


def pair_kernel(left_ref, right_ref, out_ref):
    out_ref[...] = over_rows(left_ref[...], right_ref[...]).astype(LOW)


def pair_term(left, right):
    (total, model), cols = left.shape, right.shape[1]
    tall, wide = min(model, 1024), min(cols, 1024)
    return pl.pallas_call(
        pair_kernel,
        grid=(model // tall, cols // wide),
        in_specs=[pl.BlockSpec((total, tall), lambda i, j: (0, i)), pl.BlockSpec((total, wide), lambda i, j: (0, j))],
        out_specs=pl.BlockSpec((tall, wide), lambda i, j: (i, j)),
        out_shape=jax.ShapeDtypeStruct((model, cols), LOW),
        compiler_params=params(60),
        cost_estimate=cost(),
        name="pair_term",
    )(left, right)


def shards(
    tokens, out_grad, lengths, attn_gain, w_query, w_key, w_value, output_weight, mlp_gain, gate_weight, up_weight, down_weight
):
    seqs, blks = lax.axis_size("seq"), lax.axis_size("blk")
    seq_rank, blk_rank = lax.axis_index("seq"), lax.axis_index("blk")
    size, model = tokens.shape[1], tokens.shape[2]
    block = size * seqs
    total = block * blks
    length = lengths[0]
    width = w_query.shape[1] // blks
    hidden = gate_weight.shape[1] // blks
    positions = (blk_rank * seqs + seq_rank) * size + jnp.arange(size, dtype=jnp.int32)
    live_rows = (positions < length)[:, None]
    place = jnp.stack([blk_rank, seq_rank, length, lax.axis_index("slot")]).astype(jnp.int32)

    all_pos = row_positions(jnp.arange(total, dtype=jnp.int32), blk_rank, seq_rank, blks, seqs, size)
    frequency = ROPE_BASE ** (-jnp.arange(HALF, dtype=WIDE) * 2.0 / HEAD_DIM)
    angles = all_pos.astype(WIDE)[:, None] * frequency[None, :]
    cos_tab, sin_tab = jnp.cos(angles), jnp.sin(angles)
    table = min(width, 128)
    cos_wide = jnp.tile(cos_tab, (1, table // HALF))
    sin_wide = jnp.tile(jnp.concatenate([-sin_tab, sin_tab], axis=1), (1, table // HEAD_DIM))

    own_tokens = slot_order(tokens[0])
    own_cot = jnp.where(live_rows, slot_order(out_grad[0]), 0)
    gain_attn, gain_mlp = attn_gain.astype(WIDE)[:, None], mlp_gain.astype(WIDE)[:, None]
    rows_f = own_tokens.astype(WIDE)

    def scaled(weight, gain):
        return (weight.astype(WIDE) * gain).astype(LOW)

    attn_out = Exchange(
        column_pieces([scaled(w, gain_attn) for w in (w_query, w_key, w_value)] + [output_weight])
    )
    pair_out = Exchange(column_pieces([scaled(gate_weight, gain_mlp), scaled(up_weight, gain_mlp)], 2))
    down_out = Exchange(column_pieces([down_weight]))
    phase = Phases()
    flat = lambda lists: [item for items in lists for item in items]
    in_order, in_turn = [[0, 1], [2, 3]], [[1, 2], [3, 0]]

    def calls(ks):
        return [ks] if block * len(ks) <= 512 else [[k] for k in ks]

    def reduced(ks, parts):
        summands = seq_reduce(parts)
        return [[s[g * size : (g + 1) * size] for s in summands] for g in range(len(ks))]

    def reduce_calls(got):
        for ks, parts in got:
            for k, summands in zip(ks, reduced(ks, parts)):
                terms[k] = summands

    token_blocks = [None] * blks
    ahead = turn(own_tokens, "blk", 1)
    attn_out.send(1, 2, 3)
    token_blocks[0] = seq_gather(own_tokens)
    part_attn = attn_out.by_rank()
    phase.end(ahead, part_attn, token_blocks[0], cos_wide, sin_wide, place)

    moving, part_attn, down_out.pieces = phase.take(ahead, part_attn, down_out.pieces)
    ahead = turn(moving, "blk", 1)
    near_x, near_y = swap(part_attn, "slot", 1), swap(part_attn, "slot", 2)
    down_out.send(1, 3)
    phase.end(ahead, near_x, near_y, down_out.got)

    second, moving, near_x, down_out.pieces = phase.take(moving, ahead, near_x, down_out.pieces)
    ahead = turn(moving, "blk", 1)
    far = swap(near_x, "slot", 2)
    down_out.send(2)
    token_blocks[1], token_blocks[2] = seq_gather(second), seq_gather(moving)
    full_attn = [part_attn, near_x, near_y, far]
    part_down = down_out.by_rank()
    phase.end(ahead, far, token_blocks[1:3], part_down)

    moving, part_down, pair_out.pieces = phase.take(ahead, part_down, pair_out.pieces)
    token_blocks[3] = seq_gather(moving)
    near_x, near_y = swap(part_down, "slot", 1), swap(part_down, "slot", 2)
    pair_out.send(1, 3)
    got = []
    for ks in [list(range(blks))] if total <= 1024 else [[k] for k in range(blks)]:
        here = slice(ks[0] * block, (ks[-1] + 1) * block)
        got.append(project_qkv(flat([token_blocks[k] for k in ks]), full_attn, cos_wide[here], sin_wide[here], width))
    hidden_attn, queries, key_rows, val_rows = (
        parts[0] if len(parts) == 1 else jnp.concatenate(parts, axis=0) for parts in zip(*got)
    )
    attended, lse, terms = [None] * blks, [None] * blks, [None] * blks

    def attend(ks, queries):
        got = []
        for some in calls(ks):
            outs, lses, parts = attend_blocks(some, place, queries, key_rows, val_rows, full_attn, size, model)
            got.append((some, parts))
            for k, out, log in zip(some, outs, lses):
                attended[k], lse[k] = out, log
        return [ks for ks, _ in got], [parts for _, parts in got]

    takers, parts = attend(in_turn[0], queries)
    phase.end(near_x, near_y, pair_out.got, parts)

    queries, near_y, pair_out.pieces, parts = phase.take(queries, near_y, pair_out.pieces, parts)
    pair_out.send(2)
    full_down = [part_down, near_x, near_y, swap(near_y, "slot", 1)]
    reduce_calls(zip(takers, parts))
    takers, parts = attend(in_turn[1], queries)
    part_pair = pair_out.by_rank()
    phase.end(part_pair, full_down, parts, terms[1], terms[2])

    moving, part_pair, parts = phase.take(add_up(terms[1]).astype(LOW), part_pair, parts)
    halves = [part_pair[:, :hidden], part_pair[:, hidden:]]
    near_x, near_y = [swap(halves[0], "slot", 1)], [swap(halves[0], "slot", 2)]
    reduce_calls(zip(takers, parts))
    moving = turn(moving, "blk", 1)
    phase.end(moving, terms)
    moving, half_b = phase.take(add_up([moving, *terms[2]]).astype(LOW), halves[1])
    near_x, near_y = near_x + [swap(half_b, "slot", 1)], near_y + [swap(half_b, "slot", 2)]
    moving = turn(moving, "blk", 1)
    phase.end(moving, near_x[0], near_y[0])
    moving, far = phase.take(add_up([moving, *terms[3]]).astype(LOW), near_x[0])
    far_a = swap(far, "slot", 2)
    moving = turn(moving, "blk", 1)
    phase.end(moving, near_x, near_y)
    resid = rows_f + add_up([moving, *terms[0]])
    normed_mlp, inverse_mlp = norm_rows(resid)

    def feed(ks, held):
        got = []
        for some in calls(ks):
            held, grads, outs = mlp_blocks(
                some[0] // len(some), seqs, place, flat([blocks[k] for k in some]), full_pair, full_down, held, total
            )
            got.append([grads, outs])
        return held, calls(ks), got

    def reduce_pairs(takers, got):
        for ks, (grads, outs) in zip(takers, got):
            for k, grad, out in zip(ks, reduced(ks, grads), reduced(ks, outs)):
                terms[k] = [grad, out]

    def join_pair(moving, pair):
        sums = pair if moving is None else [[moving[:, i * model : (i + 1) * model], *part] for i, part in enumerate(pair)]
        return jnp.concatenate([add_up(part).astype(LOW) for part in sums], axis=1)

    blocks, terms = [None] * blks, [None] * blks
    moving, far = phase.take(jnp.concatenate([normed_mlp.astype(LOW), own_cot], axis=1), near_y[1])
    far_b = swap(far, "slot", 1)
    full_pair = [[halves[0], near_x[0], near_y[0], far_a], [halves[1], near_x[1], near_y[1], far_b]]
    ahead = turn(moving, "blk", 1)
    blocks[0] = seq_gather(moving)
    phase.end(ahead, far_a, far_b, blocks[0])

    moving, blocks[0] = phase.take(ahead, blocks[0])
    ahead = turn(moving, "blk", 1)
    blocks[1] = seq_gather(moving)
    held, takers, got = feed(in_order[0], None)
    phase.end(ahead, blocks[1], held)

    moving, got = phase.take(ahead, got)
    ahead = turn(moving, "blk", 1)
    blocks[2] = seq_gather(moving)
    reduce_pairs(takers, got)
    phase.end(ahead, blocks[2], terms[1])

    moving, summed, blocks[2] = phase.take(ahead, join_pair(None, terms[1]), blocks[2])
    blocks[3] = seq_gather(moving)
    moving = turn(summed, "blk", 1)
    held, takers, got = feed(in_order[1], held)
    phase.end(moving, held)
    hidden_mlp, all_cot, activation, grad_pair = held

    moving, got, grad_pair, activation = phase.take(moving, got, grad_pair, activation)
    reduce_pairs(takers, got)
    moving = turn(join_pair(moving, terms[2]), "blk", 1)
    term = pair_term(hidden_mlp, grad_pair)
    down_terms = weight_terms((all_cot, [activation]))
    phase.end(moving, terms, term, down_terms)

    moving, far, term = phase.take(join_pair(moving, terms[3]), down_terms[3], term)
    sum_pair = lax.psum_scatter(term, "slot", scatter_dimension=0, tiled=True)
    moving = turn(moving, "blk", 1)
    far = swap(far, "slot", 1)
    phase.end(moving, far)
    grad_part, out_part = (add_up([moving[:, i * model : (i + 1) * model], *terms[0][i]]) for i in range(2))
    layer_out = jnp.where(live_rows, resid + out_part, 0.0)
    grad_resid_part, gain_mlp_term = norm_back(normed_mlp, inverse_mlp, grad_part)
    grad_resid = own_cot.astype(WIDE) + grad_resid_part

    moving, relay, near_term = phase.take(
        grad_resid.astype(LOW), add_up([down_terms[2], far]).astype(LOW), down_terms[1]
    )
    ahead = turn(moving, "blk", 1)
    one, two = swap(relay, "slot", 2), swap(near_term, "slot", 1)
    blocks = [seq_gather(moving), None, None, None]
    phase.end(ahead, blocks[0])

    grad_q = [None] * blks

    def attend_back(ks, held):
        for some in calls(ks):
            held, grads = attend_back_blocks(
                some[0] // len(some), some, place, queries, key_rows, val_rows, attended, lse, cos_wide, sin_wide,
                full_attn, flat([blocks[k] for k in some]), held,
            )
            for k, grad in zip(some, grads):
                grad_q[k] = grad
        return held

    moving, blocks[0] = phase.take(ahead, blocks[0])
    ahead = turn(moving, "blk", 1)
    blocks[1] = seq_gather(moving)
    held = attend_back(in_order[0], None)
    phase.end(ahead, blocks[1], held)

    moving = phase.take(ahead)
    ahead = turn(moving, "blk", 1)
    blocks[2] = seq_gather(moving)
    phase.end(ahead, blocks[2], one, two)

    down_back = Exchange(row_pieces([down_terms[0], one, two]))
    moving, blocks[2], down_back.pieces = phase.take(ahead, blocks[2], down_back.pieces)
    blocks[3] = seq_gather(moving)
    down_back.send(1, 3)
    held = attend_back(in_order[1], held)
    all_resid, grad_k, grad_v = held
    phase.end(held)

    grad_qkv, terms, gain_terms = [None] * blks, [None] * blks, []

    def finish(ks, grad_k):
        got = []
        for some in calls(ks):
            outs, gain_term, parts = finish_blocks(
                some, grad_q, grad_k, grad_v, cos_wide, sin_wide, full_attn, flat([token_blocks[k] for k in some])
            )
            gain_terms.append(gain_term)
            got.append(parts)
            for k, out in zip(some, outs):
                grad_qkv[k] = out
        return calls(ks), got

    grad_k = phase.take(grad_k)
    takers, parts = finish(in_turn[0], grad_k)
    phase.end(parts, down_back.got)

    parts, grad_k, down_back.pieces = phase.take(parts, grad_k, down_back.pieces)
    reduce_calls(zip(takers, parts))
    moving = turn(add_up(terms[1]).astype(LOW), "blk", 1)
    down_back.send(2)
    takers, parts = finish(in_turn[1], grad_k)
    last_terms = weight_terms((hidden_attn, grad_qkv), (all_resid, attended))
    gain_terms = jnp.concatenate([add_up(gain_terms), jnp.sum(gain_mlp_term, axis=0, keepdims=True)], axis=0)
    phase.end(moving, terms[1], terms[2], parts, gain_terms, last_terms, down_back.got, sum_pair)

    pair_back = Exchange(row_pieces([sum_pair]))
    moving, parts, gain_terms, far, pair_back.pieces = phase.take(
        add_up([moving, *terms[2]]).astype(LOW), parts, gain_terms, last_terms[3], pair_back.pieces
    )
    moving = turn(moving, "blk", 1)
    far = swap(far, "slot", 2)
    pair_back.send(1)
    bit = 1
    while bit < seqs:
        gain_terms = gain_terms + swap(gain_terms, "seq", bit)
        bit *= 2
    reduce_calls(zip(takers, parts))
    phase.end(moving, far, terms, gain_terms, pair_back.got)

    gain_parts = jnp.split(gain_terms, GROUPS, axis=1)
    moving, relay, near_term, gain_far, gain_two, pair_back.pieces = phase.take(
        add_up([moving, *terms[3]]).astype(LOW), add_up([last_terms[1], far]).astype(LOW), last_terms[2],
        gain_parts[3], gain_parts[1], pair_back.pieces,
    )
    gain_far, gain_two = swap(gain_far, "slot", 1), swap(gain_two, "slot", 1)
    moving = turn(moving, "blk", 1)
    one, two = swap(relay, "slot", 1), swap(near_term, "slot", 2)
    pair_back.send(3)
    phase.end(moving, one, two, pair_back.got, gain_far, gain_two)

    last_back = Exchange(row_pieces([last_terms[0], one, two]))
    gain_relay, last_back.pieces, pair_back.pieces = phase.take(
        gain_parts[2] + gain_far, last_back.pieces, pair_back.pieces
    )
    gain_one = swap(gain_relay, "slot", 2)
    gain_sum = gain_parts[0] + gain_two + gain_one
    pair_back.send(2)
    last_back.send(1, 2, 3)
    gain_sums = [gain_sum] + [turn(gain_sum, "blk", k) for k in range(1, blks)]

    grad_hidden_attn = add_up([moving, *terms[0]])
    normed_attn, inverse_attn = norm_rows(rows_f)
    grad_in_part, _ = norm_back(normed_attn, inverse_attn, grad_hidden_attn)
    shard = attn_gain.shape[0]
    gain_grads = lax.dynamic_slice(add_up(gain_sums), (0, blk_rank * shard), (2, shard))
    half = hidden // 2
    return (
        slot_order(layer_out).astype(LOW)[None],
        slot_order(grad_resid + grad_in_part)[None],
        gain_grads[0] / gain_attn[:, 0],
        join_owners(last_back, [(0, width)], gain_attn),
        join_owners(last_back, [(width, width)], gain_attn),
        join_owners(last_back, [(2 * width, width)], gain_attn),
        join_owners(last_back, [(3 * width, width)], 1.0),
        gain_grads[1] / gain_mlp[:, 0],
        join_owners(pair_back, [(0, half), (hidden, half)], gain_mlp),
        join_owners(pair_back, [(half, half), (hidden + half, half)], gain_mlp),
        join_owners(down_back, [(0, hidden)], 1.0),
    )


def solution(mesh):
    rows = P("slot", ("blk", "seq"), None)
    gain = P(("slot", "blk"))
    weight = P(("slot", "blk"), "seq")
    return jax.shard_map(
        shards,
        mesh=mesh,
        in_specs=(rows, rows, P("slot"), gain, weight, weight, weight, weight, gain, weight, weight, weight),
        out_specs=(rows, rows, gain, weight, weight, weight, weight, gain, weight, weight, weight),
        check_vma=False,
    )
```

time: 789 us -> 663 us (0.84)
  Pallas kernels: 45 us -> 166 us
  starting transfers between devices: 176 us -> 78.2 us
  matrix products: 97.1 us -> 0 us
  waiting for transfers between devices: 407 us -> 319 us
  other arithmetic: 25.6 us -> 49.8 us
  between operations: 4.07 us -> 16.5 us
    pallas_call x2 -> x12, Pallas kernels: 45 us -> 166 us  [the longest x2 54.4 us: mlp_blocks(): pl.pallas_call(partial(mlp_kernel, count, seqs), grid_spec=pltpu.Prefetch...]
    dot_general x30 -> x0, matrix products: 97.1 us -> none  [the longest x5 34.8 us: over_cols(): lax.dot_general(left, right, (((1,), (1,)), ((), ())), preferred_element_...]
    ppermute x63 -> x39, starting transfers between devices: 128 us -> 49.9 us  [turn(): lax.ppermute(value, axis, [(i, (i + by) % count) for i in range(count)])]
    ppermute x73 -> x42, waiting for transfers between devices: 152 us -> 104 us  [swap(): return lax.ppermute(value, axis, [(i, i ^ mask) for i in range(count)])]
    ppermute x63 -> x39, waiting for transfers between devices: 254 us -> 216 us  [turn(): lax.ppermute(value, axis, [(i, (i + by) % count) for i in range(count)])]
    ppermute x73 -> x42, starting transfers between devices: 47.9 us -> 28.3 us  [swap(): return lax.ppermute(value, axis, [(i, i ^ mask) for i in range(count)])]
    convert_element_type x22 -> x20, other arithmetic: 9.3 us -> 24.7 us  [the longest x4 7.61 us: join_pair(): return jnp.concatenate([add_up(part).astype(LOW) for part in sums], axis=1)]
  transfers between devices with their start and end apart: 136 -> 82, of which waited for: 59 -> 35; matrix products, arithmetic and copies ran while one was open for 13% -> 9% of each run, Pallas kernels for 3% -> 25%
where the time goes in v2:
time: 663 us; the launch traced here: 657 us
  waiting for transfers between devices  319 us (48%)
  Pallas kernels  166 us (25%)
  starting transfers between devices  78.2 us (12%)
  other arithmetic  49.8 us (8%)
  local copies, waits for them, and re-layouts  27.5 us (4%)
  between operations  16.5 us (2%)
    ppermute x39, waiting for transfers between devices, turn(): lax.ppermute(value, axis, [(i, (i + by) % count) for i in range(count)])  216 us
    ppermute x42, waiting for transfers between devices, swap(): return lax.ppermute(value, axis, [(i, i ^ mask) for i in range(count)])  104 us
    pallas_call x2, Pallas kernels, mlp_blocks(): pl.pallas_call(partial(mlp_kernel, count, seqs), grid_spec=pltpu.Prefetch...  54.4 us
    ppermute x39, starting transfers between devices, turn(): lax.ppermute(value, axis, [(i, (i + by) % count) for i in range(count)])  49.9 us
    pallas_call x2, Pallas kernels, attend_back_blocks(): pl.pallas_call(partial(attend_back_kernel, (total, blks, seqs, size), ks,...  30.1 us
    ppermute x42, starting transfers between devices, swap(): return lax.ppermute(value, axis, [(i, i ^ mask) for i in range(count)])  28.3 us
    pallas_call x2, Pallas kernels, attend_blocks(): pl.pallas_call(partial(attend_kernel, (total, blks, seqs, size), ks, widt...  25 us
    pallas_call x2, Pallas kernels, weight_terms(): pl.pallas_call(partial(weight_kernel, [len(rights) for _, rights in pairs...  18 us
  transfers between devices with their start and end apart: 82, of which 35 were waited for; matrix products, arithmetic and copies ran while one was open for 9% of the time, Pallas kernels for 25%

profile of v2, /device:TPU:0, one launch (start us, length us, event | category | flops | bytes accessed | tf_op | source)
XLA Modules:
  0.0 657.5 jit_solution(10641824897553374107)
XLA Ops:
  9.2 2.6 collective-permute-start.1
  17.3 2.8 collective-permute-start.4
  24.9 7.5 %collective-permute-done.2 = bf16[128,1024]{1,0:T(8,128)(2,1)S(1)} collective-permute-done((bf16[128,1024]{1,0:T(8,128)(2,1)}, bf16[128,1024]{1,0:T(8,128)(2,1)S(1)}, u32[]{:S(2)}, u32[]{:S(2)}) %collective-permute-start.2) | collective-permute-done | bytes 262176 | tf_op jit(solution)/shard_map/ppermute | solution.py:23
  32.4 11.1 %collective-permute-done.3 = bf16[128,1024]{1,0:T(8,128)(2,1)} collective-permute-done((bf16[128,1024]{1,0:T(8,128)(2,1)}, bf16[128,1024]{1,0:T(8,128)(2,1)}, u32[]{:S(2)}, u32[]{:S(2)}) %collective-permute-start.3) | collective-permute-done | bytes 262176 | tf_op jit(solution)/shard_map/ppermute | solution.py:23
  50.3 5.1 collective-permute-start.5
  57.3 3.8 collective-permute-start.9
  63.7 12.4 %collective-permute-done.8 = bf16[128,1024]{1,0:T(8,128)(2,1)S(1)} collective-permute-done((bf16[128,1024]{1,0:T(8,128)(2,1)}, bf16[128,1024]{1,0:T(8,128)(2,1)S(1)}, u32[]{:S(2)}, u32[]{:S(2)}) %collective-permute-start.8) | collective-permute-done | bytes 262176 | tf_op jit(solution)/shard_map/ppermute | solution.py:23
  76.2 3.9 collective-permute-done.9
  86.2 22.8 %collective-permute-done.13 = bf16[128,1024]{1,0:T(8,128)(2,1)S(1)} collective-permute-done((bf16[128,1024]{1,0:T(8,128)(2,1)S(1)}, bf16[128,1024]{1,0:T(8,128)(2,1)S(1)}, u32[]{:S(2)}, u32[]{:S(2)}) %collective-permute-start.13) | collective-permute-done | bytes 262176 | tf_op jit(solution)/shard_map/ppermute | solution.py:23
  112.7 4.0 collective-permute-start.19
  120.8 10.9 %project_qkv.1 = (bf16[1024,2048]{1,0:T(8,128)(2,1)}, bf16[1024,256]{1,0:T(8,128)(2,1)}, bf16[1024,256]{1,0:T(8,128)(2,1)}, bf16[1024,256]{1,0:T(8,128)(2,1)}) custom-call(bf16[128,2048]{1,0:T(8,128)(2,1)} %copy-done.4, bf16[128,2048]{1,0:T(8,128)(2,1)} %copy-done.24, bf16[128,2048]{1,0:T(8,128)(2,1)} %copy-done.25, bf16[128,2048]{1,0:T(8,128)(2,1)} %copy-done.28, ...), custom_call_target="tpu_custom_call" | custom-call | flops 1 | bytes 1 | tf_op jit(solution)/shard_map/project_qkv/pallas_call | solution.py:223
  131.8 12.6 %attend_blocks.2 = (bf16[256,256]{1,0:T(8,128)(2,1)}, bf16[256,256]{1,0:T(8,128)(2,1)}, f32[256,128]{1,0:T(8,128)}, f32[256,128]{1,0:T(8,128)}, bf16[256,2048]{1,0:T(8,128)(2,1)}, /*index=5*/bf16[256,2048]{1,0:T(8,128)(2,1)}) custom-call(s32[4]{0:T(128)} %pad_add_fusion.place_ref, bf16[1024,256]{1,0:T(8,128)(2,1)} %get-tuple-element.182.refs_0_.refs_1_, ...), custom_call_target="tpu_custom_call" | custom-call | flops 1 | bytes 1 | tf_op jit(solution)/shard_map/attend_blocks/pallas_call | solution.py:317
  147.6 12.4 %attend_blocks.3 = (bf16[256,256]{1,0:T(8,128)(2,1)}, bf16[256,256]{1,0:T(8,128)(2,1)}, f32[256,128]{1,0:T(8,128)}, f32[256,128]{1,0:T(8,128)}, bf16[256,2048]{1,0:T(8,128)(2,1)}, /*index=5*/bf16[256,2048]{1,0:T(8,128)(2,1)}) custom-call(s32[4]{0:T(128)} %pad_add_fusion.place_ref, bf16[1024,256]{1,0:T(8,128)(2,1)} %get-tuple-element.182.refs_0_.refs_1_, ...), custom_call_target="tpu_custom_call" | custom-call | flops 1 | bytes 1 | tf_op jit(solution)/shard_map/attend_blocks/pallas_call | solution.py:317
  160.1 8.7 %collective-permute-done.21 = bf16[128,2048]{1,0:T(8,128)(2,1)} collective-permute-done((bf16[128,2048]{1,0:T(8,128)(2,1)S(1)}, bf16[128,2048]{1,0:T(8,128)(2,1)}, u32[]{:S(2)}, u32[]{:S(2)}) %collective-permute-start.21) | collective-permute-done | bytes 524320 | tf_op jit(solution)/shard_map/ppermute | solution.py:23
  175.0 11.9 %collective-permute-done.23 = bf16[128,2048]{1,0:T(8,128)(2,1)S(1)} collective-permute-done((bf16[128,2048]{1,0:T(8,128)(2,1)S(1)}, bf16[128,2048]{1,0:T(8,128)(2,1)S(1)}, u32[]{:S(2)}, u32[]{:S(2)}) %collective-permute-start.23) | collective-permute-done | bytes 524320 | tf_op jit(solution)/shard_map/ppermute | solution.py:23
  189.1 15.0 %collective-permute-done.25 = bf16[128,2048]{1,0:T(8,128)(2,1)} collective-permute-done((bf16[128,2048]{1,0:T(8,128)(2,1)}, bf16[128,2048]{1,0:T(8,128)(2,1)}, u32[]{:S(2)}, u32[]{:S(2)}) %collective-permute-start.25) | collective-permute-done | bytes 524320 | tf_op jit(solution)/shard_map/ppermute | solution.py:23
  209.8 10.1 %collective-permute-done.28 = bf16[128,2048]{1,0:T(8,128)(2,1)S(1)} collective-permute-done((bf16[128,2048]{1,0:T(8,128)(2,1)S(1)}, bf16[128,2048]{1,0:T(8,128)(2,1)S(1)}, u32[]{:S(2)}, u32[]{:S(2)}) %collective-permute-start.28) | collective-permute-done | bytes 524320 | tf_op jit(solution)/shard_map/ppermute | solution.py:23
  221.5 11.0 %collective-permute-done.29.refs_10_ = bf16[512,1024]{1,0:T(8,128)(2,1)S(1)} collective-permute-done((bf16[512,1024]{1,0:T(8,128)(2,1)}, bf16[512,1024]{1,0:T(8,128)(2,1)S(1)}, u32[]{:S(2)}, u32[]{:S(2)}) %collective-permute-start.29) | collective-permute-done | bytes 1048608 | tf_op jit(solution)/shard_map/ppermute | solution.py:28
  234.3 18.0 %collective-permute-done.33.refs_7_ = bf16[512,1024]{1,0:T(8,128)(2,1)S(1)} collective-permute-done((bf16[512,1024]{1,0:T(8,128)(2,1)}, bf16[512,1024]{1,0:T(8,128)(2,1)S(1)}, u32[]{:S(2)}, u32[]{:S(2)}) %collective-permute-start.33) | collective-permute-done | bytes 1048608 | tf_op jit(solution)/shard_map/ppermute | solution.py:28
  254.2 4.0 collective-permute-done.34.refs_11_
  261.3 27.1 %mlp_blocks.2 = (bf16[1024,2048]{1,0:T(8,128)(2,1)}, bf16[1024,2048]{1,0:T(8,128)(2,1)}, bf16[1024,1024]{1,0:T(8,128)(2,1)}, bf16[1024,2048]{1,0:T(8,128)(2,1)},...) custom-call(s32[4]{0:T(128)} %pad_add_fusion.place_ref, ...), custom_call_target="tpu_custom_call" | custom-call | flops 1 | bytes 1 | tf_op jit(solution)/shard_map/mlp_blocks/pallas_call | solution.py:393
  295.4 21.1 %collective-permute-done.37.refs_2_ = bf16[128,4096]{1,0:T(8,128)(2,1)S(1)} collective-permute-done((bf16[128,4096]{1,0:T(8,128)(2,1)}, bf16[128,4096]{1,0:T(8,128)(2,1)S(1)}, u32[]{:S(2)}, u32[]{:S(2)}) %collective-permute-start.37) | collective-permute-done | bytes 1048608 | tf_op jit(solution)/shard_map/ppermute | solution.py:23
  319.3 27.3 %mlp_blocks.3 = (bf16[1024,2048]{1,0:T(8,128)(2,1)}, bf16[1024,2048]{1,0:T(8,128)(2,1)}, bf16[1024,1024]{1,0:T(8,128)(2,1)}, bf16[1024,2048]{1,0:T(8,128)(2,1)},...) custom-call(s32[4]{0:T(128)} %pad_add_fusion.place_ref, ...), custom_call_target="tpu_custom_call", output_to_operand_aliasing={{0}: (17, {}), {1}: (18, {}), {2}: (19, {}), {3}: (20, {})} | custom-call | flops 1 | bytes 1 | tf_op jit(solution)/shard_map/mlp_blocks/pallas_call | solution.py:393
  354.2 8.4 %weight_terms.2 = (bf16[512,1024]{1,0:T(8,128)(2,1)}, bf16[512,1024]{1,0:T(8,128)(2,1)}, bf16[512,1024]{1,0:T(8,128)(2,1)}, bf16[512,1024]{1,0:T(8,128)(2,1)}) custom-call(bf16[1024,2048]{1,0:T(8,128)(2,1)} %get-tuple-element.223.refs_0_, bf16[1024,1024]{1,0:T(8,128)(2,1)} %get-tuple-element.229.refs_1_), custom_call_target="tpu_custom_call" | custom-call | flops 1 | bytes 1 | tf_op jit(solution)/shard_map/weight_terms/pallas_call | solution.py:590
  362.7 13.7 %pair_term.1 = bf16[2048,2048]{1,0:T(8,128)(2,1)} custom-call(bf16[1024,2048]{1,0:T(8,128)(2,1)} %get-tuple-element.222.left_ref, bf16[1024,2048]{1,0:T(8,128)(2,1)} %get-tuple-element.231.right_ref), custom_call_target="tpu_custom_call" | custom-call | flops 1 | bytes 1 | tf_op jit(solution)/shard_map/pair_term/pallas_call | solution.py:609
  376.3 4.6 collective-permute-done.45
  386.0 24.8 %collective-permute-done.46 = bf16[128,4096]{1,0:T(8,128)(2,1)S(1)} collective-permute-done((bf16[128,4096]{1,0:T(8,128)(2,1)}, bf16[128,4096]{1,0:T(8,128)(2,1)S(1)}, u32[]{:S(2)}, u32[]{:S(2)}) %collective-permute-start.46) | collective-permute-done | bytes 1048608 | tf_op jit(solution)/shard_map/ppermute | solution.py:23
  412.6 17.1 %collective-permute-done.47 = bf16[512,1024]{1,0:T(8,128)(2,1)S(1)} collective-permute-done((bf16[512,1024]{1,0:T(8,128)(2,1)}, bf16[512,1024]{1,0:T(8,128)(2,1)S(1)}, u32[]{:S(2)}, u32[]{:S(2)}) %collective-permute-start.47) | collective-permute-done | bytes 1048608 | tf_op jit(solution)/shard_map/ppermute | solution.py:28
  432.8 2.5 collective-permute-start.55
  435.3 8.4 %collective-permute-done.48.refs_18_ = bf16[128,2048]{1,0:T(8,128)(2,1)S(1)} collective-permute-done((bf16[128,2048]{1,0:T(8,128)(2,1)S(1)}, bf16[128,2048]{1,0:T(8,128)(2,1)S(1)}, u32[]{:S(2)}, u32[]{:S(2)}) %collective-permute-start.48) | collective-permute-done | bytes 524320 | tf_op jit(solution)/shard_map/ppermute | solution.py:23
  446.4 14.8 %attend_back_blocks.2 = (bf16[1024,2048]{1,0:T(8,128)(2,1)}, f32[1024,256]{1,0:T(8,128)}, f32[1024,256]{1,0:T(8,128)}, bf16[256,256]{1,0:T(8,128)(2,1)}, bf16[256,256]{1,0:T(8,128)(2,1)}) custom-call(s32[4]{0:T(128)} %pad_add_fusion.place_ref, bf16[1024,256]{1,0:T(8,128)(2,1)} %get-tuple-element.182.refs_0_.refs_1_, ...), custom_call_target="tpu_custom_call" | custom-call | flops 1 | bytes 1 | tf_op jit(solution)/shard_map/attend_back_blocks/pallas_call | solution.py:481
  461.5 15.1 %collective-permute-done.55 = bf16[512,1024]{1,0:T(8,128)(2,1)} collective-permute-done((bf16[512,1024]{1,0:T(8,128)(2,1)}, bf16[512,1024]{1,0:T(8,128)(2,1)}, u32[]{:S(2)}, u32[]{:S(2)}) %collective-permute-start.55) | collective-permute-done | bytes 1048608 | tf_op jit(solution)/shard_map/ppermute | solution.py:28
  476.8 3.6 add_convert_fusion.18
  481.0 3.5 collective-permute-start.58
  485.8 15.4 %attend_back_blocks.3 = (bf16[1024,2048]{1,0:T(8,128)(2,1)}, f32[1024,256]{1,0:T(8,128)}, f32[1024,256]{1,0:T(8,128)}, bf16[256,256]{1,0:T(8,128)(2,1)}, bf16[256,256]{1,0:T(8,128)(2,1)}) custom-call(s32[4]{0:T(128)} %pad_add_fusion.place_ref, ...), custom_call_target="tpu_custom_call", output_to_operand_aliasing={{0}: (21, {}), {1}: (22, {}), {2}: (23, {})} | custom-call | flops 1 | bytes 1 | tf_op jit(solution)/shard_map/attend_back_blocks/pallas_call | solution.py:481
  501.1 7.1 %finish_blocks.2 = (bf16[256,768]{1,0:T(8,128)(2,1)}, bf16[256,768]{1,0:T(8,128)(2,1)}, f32[1,2048]{1,0:T(1,128)}, bf16[256,2048]{1,0:T(8,128)(2,1)}, bf16[256,2048]{1,0:T(8,128)(2,1)}) custom-call(bf16[256,256]{1,0:T(8,128)(2,1)} %get-tuple-element.245.refs_0_, bf16[256,256]{1,0:T(8,128)(2,1)} %get-tuple-element.259.refs_1_, ...), custom_call_target="tpu_custom_call" | custom-call | flops 1 | bytes 1 | tf_op jit(solution)/shard_map/finish_blocks/pallas_call | solution.py:551
  511.3 6.9 %finish_blocks.3 = (bf16[256,768]{1,0:T(8,128)(2,1)}, bf16[256,768]{1,0:T(8,128)(2,1)}, f32[1,2048]{1,0:T(1,128)}, bf16[256,2048]{1,0:T(8,128)(2,1)}, bf16[256,2048]{1,0:T(8,128)(2,1)}) custom-call(bf16[256,256]{1,0:T(8,128)(2,1)} %get-tuple-element.271.refs_0_, bf16[256,256]{1,0:T(8,128)(2,1)} %get-tuple-element.272.refs_1_, ...), custom_call_target="tpu_custom_call" | custom-call | flops 1 | bytes 1 | tf_op jit(solution)/shard_map/finish_blocks/pallas_call | solution.py:551
  522.3 9.6 %weight_terms.3 = (bf16[512,1024]{1,0:T(8,128)(2,1)}, bf16[512,1024]{1,0:T(8,128)(2,1)}, bf16[512,1024]{1,0:T(8,128)(2,1)}, bf16[512,1024]{1,0:T(8,128)(2,1)}) custom-call(bf16[1024,2048]{1,0:T(8,128)(2,1)} %get-tuple-element.278.refs_0_, bf16[256,768]{1,0:T(8,128)(2,1)} %get-tuple-element.279.refs_1_, bf16[256,768]{1,0:T(8,128)(2,1)} %get-tuple-element.280.refs_2_, ...), custom_call_target="tpu_custom_call" | custom-call | flops 1 | bytes 1 | tf_op jit(solution)/shard_map/weight_terms/pallas_call | solution.py:590
  531.9 4.1 collective-permute-done.60
  548.1 16.2 %collective-permute-done.64 = bf16[512,1024]{1,0:T(8,128)(2,1)S(1)} collective-permute-done((bf16[512,1024]{1,0:T(8,128)(2,1)S(1)}, bf16[512,1024]{1,0:T(8,128)(2,1)S(1)}, u32[]{:S(2)}, u32[]{:S(2)}) %collective-permute-start.64) | collective-permute-done | bytes 1048608 | tf_op jit(solution)/shard_map/ppermute | solution.py:28
  565.0 5.2 collective-permute-done.66
  575.0 3.8 collective-permute-start.72
  580.1 6.8 %collective-permute-done.67 = bf16[128,2048]{1,0:T(8,128)(2,1)S(1)} collective-permute-done((bf16[128,2048]{1,0:T(8,128)(2,1)S(1)}, bf16[128,2048]{1,0:T(8,128)(2,1)S(1)}, u32[]{:S(2)}, u32[]{:S(2)}) %collective-permute-start.67) | collective-permute-done | bytes 524320 | tf_op jit(solution)/shard_map/ppermute | solution.py:23
  589.0 8.4 %collective-permute-done.71 = bf16[512,1024]{1,0:T(8,128)(2,1)S(1)} collective-permute-done((bf16[512,1024]{1,0:T(8,128)(2,1)S(1)}, bf16[512,1024]{1,0:T(8,128)(2,1)S(1)}, u32[]{:S(2)}, u32[]{:S(2)}) %collective-permute-start.71) | collective-permute-done | bytes 1048608 | tf_op jit(solution)/shard_map/ppermute | solution.py:28
  603.1 3.9 collective-permute-start.75
  608.9 2.6 collective-permute-start.79
  612.3 14.0 %collective-permute-done.78 = bf16[128,1024]{1,0:T(8,128)(2,1)S(1)} collective-permute-done((bf16[128,1024]{1,0:T(8,128)(2,1)S(1)}, bf16[128,1024]{1,0:T(8,128)(2,1)S(1)}, u32[]{:S(2)}, u32[]{:S(2)}) %collective-permute-start.78) | collective-permute-done | bytes 262176 | tf_op jit(solution)/shard_map/ppermute | solution.py:23
  626.5 21.4 %collective-permute-done.80 = bf16[128,2048]{1,0:T(8,128)(2,1)S(1)} collective-permute-done((bf16[128,2048]{1,0:T(8,128)(2,1)S(1)}, bf16[128,2048]{1,0:T(8,128)(2,1)S(1)}, u32[]{:S(2)}, u32[]{:S(2)}) %collective-permute-start.80) | collective-permute-done | bytes 524320 | tf_op jit(solution)/shard_map/ppermute | solution.py:23
  (392 shorter events, 133.0 us)
Async XLA Ops:
  7.2 531.2 %reduce-scatter.2.cloned.1.call-start = ((), (), s32[]{:S(2)}) async-start(), calls=%async_computation.1 | async-start | bytes 10485760 | tf_op jit(solution)/shard_map/reduce_scatter | solution.py:798
  8.7 36.8 %collective-permute-start = (bf16[128,2048]{1,0:T(8,128)(2,1)S(1)}, bf16[128,2048]{1,0:T(8,128)(2,1)S(1)}, u32[]{:S(2)}, u32[]{:S(2)}) collective-permute-start(bf16[128,2048]{1,0:T(8,128)(2,1)S(1)} %get-tuple-element.314.refs_0_.refs_16_), channel_id=1, source_target_pairs={{0,4},{4,0},{1,5},{5,1},{2,6},{6,2},{3,7},{7,3},{8,12},{12,8},{9,1... | collective-permute-start | bytes 1572872 | tf_op jit(solution)/shard_map/ppermute | solution.py:28
  9.2 36.3 %collective-permute-start.1 = (bf16[128,2048]{1,0:T(8,128)(2,1)S(1)}, bf16[128,2048]{1,0:T(8,128)(2,1)S(1)}, u32[]{:S(2)}, u32[]{:S(2)}) collective-permute-start(bf16[128,2048]{1,0:T(8,128)(2,1)S(1)} %get-tuple-element.314.refs_0_.refs_16_), channel_id=1, source_target_pairs={{0,1},{1,2},{2,3},{3,0},{4,5},{5,6},{6,7},{7,4},{8,9},{9,10},{10,1... | collective-permute-start | bytes 1572872 | tf_op jit(solution)/shard_map/ppermute | solution.py:23
  15.5 28.0 %collective-permute-start.3 = (bf16[128,1024]{1,0:T(8,128)(2,1)}, bf16[128,1024]{1,0:T(8,128)(2,1)}, u32[]{:S(2)}, u32[]{:S(2)}) collective-permute-start(bf16[128,1024]{1,0:T(8,128)(2,1)} %pad_maximum_fusion.11), channel_id=1, source_target_pairs={{0,2},{1,3},{2,0},{3,1},{4,6},{5,7},{6,4},{7,5},{8,10},{9,11},{10,... | collective-permute-start | bytes 786440 | tf_op jit(solution)/shard_map/ppermute | solution.py:23
  17.3 27.1 %collective-permute-start.4 = (bf16[128,1024]{1,0:T(8,128)(2,1)}, bf16[128,1024]{1,0:T(8,128)(2,1)}, u32[]{:S(2)}, u32[]{:S(2)}) collective-permute-start(bf16[128,1024]{1,0:T(8,128)(2,1)} %pad_maximum_fusion.12), channel_id=1, source_target_pairs={{0,3},{1,0},{2,1},{3,2},{4,7},{5,4},{6,5},{7,6},{8,11},{9,8},{10,9... | collective-permute-start | bytes 786440 | tf_op jit(solution)/shard_map/ppermute | solution.py:23
  47.3 32.8 %collective-permute-start.6 = (bf16[512,1024]{1,0:T(8,128)(2,1)S(1)}, bf16[512,1024]{1,0:T(8,128)(2,1)S(1)}, u32[]{:S(2)}, u32[]{:S(2)}) collective-permute-start(bf16[512,1024]{1,0:T(8,128)(2,1)S(1)} %constant_dynamic-update-slice_fusion.8.refs_8_.refs_4_.refs_12_.refs_10_), channel_id=1, source_target_pairs={{0,8},{8,0},{16,24},{24,16},{1,9},{9,1},{17,25},{25,17},{2,10},{10... | collective-permute-start | bytes 3145736 | tf_op jit(solution)/shard_map/ppermute | solution.py:28
  48.8 31.3 %collective-permute-start.7 = (bf16[512,1024]{1,0:T(8,128)(2,1)S(1)}, bf16[512,1024]{1,0:T(8,128)(2,1)S(1)}, u32[]{:S(2)}, u32[]{:S(2)}) collective-permute-start(bf16[512,1024]{1,0:T(8,128)(2,1)S(1)} %constant_dynamic-update-slice_fusion.8.refs_8_.refs_4_.refs_12_.refs_10_), channel_id=1, source_target_pairs={{0,16},{8,24},{16,0},{24,8},{1,17},{9,25},{17,1},{25,9},{2,18},{10... | collective-permute-start | bytes 3145736 | tf_op jit(solution)/shard_map/ppermute | solution.py:28
  50.3 29.7 %collective-permute-start.5 = (bf16[128,2048]{1,0:T(8,128)(2,1)}, bf16[128,2048]{1,0:T(8,128)(2,1)}, u32[]{:S(2)}, u32[]{:S(2)}) collective-permute-start(bf16[128,2048]{1,0:T(8,128)(2,1)} %copy-done.25), channel_id=1, source_target_pairs={{0,1},{1,2},{2,3},{3,0},{4,5},{5,6},{6,7},{7,4},{8,9},{9,10},{10,1... | collective-permute-start | bytes 1572872 | tf_op jit(solution)/shard_map/ppermute | solution.py:23
  57.3 22.8 %collective-permute-start.9 = (bf16[128,1024]{1,0:T(8,128)(2,1)S(1)}, bf16[128,1024]{1,0:T(8,128)(2,1)S(1)}, u32[]{:S(2)}, u32[]{:S(2)}) collective-permute-start(bf16[128,1024]{1,0:T(8,128)(2,1)S(1)} %copy-done.69), channel_id=1, source_target_pairs={{0,3},{1,0},{2,1},{3,2},{4,7},{5,4},{6,5},{7,6},{8,11},{9,8},{10,9... | collective-permute-start | bytes 786440 | tf_op jit(solution)/shard_map/ppermute | solution.py:23
  80.1 30.5 %collective-permute-start.14 = (bf16[512,1024]{1,0:T(8,128)(2,1)S(1)}, bf16[512,1024]{1,0:T(8,128)(2,1)S(1)}, u32[]{:S(2)}, u32[]{:S(2)}) collective-permute-start(bf16[512,1024]{1,0:T(8,128)(2,1)S(1)} %collective-permute-done.6.refs_9_.refs_5_.refs_13_.refs_11_), channel_id=1, source_target_pairs={{0,16},{8,24},{16,0},{24,8},{1,17},{9,25},{17,1},{25,9},{2,18},{10... | collective-permute-start | bytes 3145736 | tf_op jit(solution)/shard_map/ppermute | solution.py:28
  81.9 28.7 %collective-permute-start.11 = (bf16[128,2048]{1,0:T(8,128)(2,1)}, bf16[128,2048]{1,0:T(8,128)(2,1)S(1)}, u32[]{:S(2)}, u32[]{:S(2)}) collective-permute-start(bf16[128,2048]{1,0:T(8,128)(2,1)} %collective-permute-done.5.refs_4_.refs_16_), channel_id=1, source_target_pairs={{0,4},{4,0},{1,5},{5,1},{2,6},{6,2},{3,7},{7,3},{8,12},{12,8},{9,1... | collective-permute-start | bytes 1572872 | tf_op jit(solution)/shard_map/ppermute | solution.py:28
  82.0 28.6 %collective-permute-start.12 = (bf16[128,2048]{1,0:T(8,128)(2,1)}, bf16[128,2048]{1,0:T(8,128)(2,1)}, u32[]{:S(2)}, u32[]{:S(2)}) collective-permute-start(bf16[128,2048]{1,0:T(8,128)(2,1)} %collective-permute-done.5.refs_4_.refs_16_), channel_id=1, source_target_pairs={{0,1},{1,2},{2,3},{3,0},{4,5},{5,6},{6,7},{7,4},{8,9},{9,10},{10,1... | collective-permute-start | bytes 1572872 | tf_op jit(solution)/shard_map/ppermute | solution.py:23
  82.6 27.9 %collective-permute-start.10 = (bf16[128,2048]{1,0:T(8,128)(2,1)S(1)}, bf16[128,2048]{1,0:T(8,128)(2,1)S(1)}, u32[]{:S(2)}, u32[]{:S(2)}) collective-permute-start(bf16[128,2048]{1,0:T(8,128)(2,1)S(1)} %copy-done.26), channel_id=1, source_target_pairs={{0,4},{4,0},{1,5},{5,1},{2,6},{6,2},{3,7},{7,3},{8,12},{12,8},{9,1... | collective-permute-start | bytes 1572872 | tf_op jit(solution)/shard_map/ppermute | solution.py:28
  82.8 26.3 %collective-permute-start.13 = (bf16[128,1024]{1,0:T(8,128)(2,1)S(1)}, bf16[128,1024]{1,0:T(8,128)(2,1)S(1)}, u32[]{:S(2)}, u32[]{:S(2)}) collective-permute-start(bf16[128,1024]{1,0:T(8,128)(2,1)S(1)} %copy-done.68), channel_id=1, source_target_pairs={{0,2},{1,3},{2,0},{3,1},{4,6},{5,7},{6,4},{7,5},{8,10},{9,11},{10,... | collective-permute-start | bytes 786440 | tf_op jit(solution)/shard_map/ppermute | solution.py:23
  110.6 33.8 %collective-permute-start.16 = (bf16[512,1024]{1,0:T(8,128)(2,1)}, bf16[512,1024]{1,0:T(8,128)(2,1)S(1)}, u32[]{:S(2)}, u32[]{:S(2)}) collective-permute-start(bf16[512,1024]{1,0:T(8,128)(2,1)} %constant_dynamic-update-slice_fusion.4.refs_12_), channel_id=1, source_target_pairs={{0,16},{8,24},{16,0},{24,8},{1,17},{9,25},{17,1},{25,9},{2,18},{10... | collective-permute-start | bytes 3145736 | tf_op jit(solution)/shard_map/ppermute | solution.py:28
  112.2 32.2 %collective-permute-start.17 = (bf16[512,1024]{1,0:T(8,128)(2,1)}, bf16[512,1024]{1,0:T(8,128)(2,1)S(1)}, u32[]{:S(2)}, u32[]{:S(2)}) collective-permute-start(bf16[512,1024]{1,0:T(8,128)(2,1)} %constant_dynamic-update-slice_fusion.4.refs_12_), channel_id=1, source_target_pairs={{0,8},{8,0},{16,24},{24,16},{1,9},{9,1},{17,25},{25,17},{2,10},{10... | collective-permute-start | bytes 3145736 | tf_op jit(solution)/shard_map/ppermute | solution.py:28
  112.7 31.6 %collective-permute-start.18 = (bf16[128,2048]{1,0:T(8,128)(2,1)}, bf16[128,2048]{1,0:T(8,128)(2,1)}, u32[]{:S(2)}, u32[]{:S(2)}) collective-permute-start(bf16[128,2048]{1,0:T(8,128)(2,1)} %pad_maximum_fusion.6), channel_id=1, source_target_pairs={{0,1},{1,2},{2,3},{3,0},{4,5},{5,6},{6,7},{7,4},{8,9},{9,10},{10,1... | collective-permute-start | bytes 1572872 | tf_op jit(solution)/shard_map/ppermute | solution.py:23
  112.7 31.6 %collective-permute-start.19 = (bf16[128,2048]{1,0:T(8,128)(2,1)}, bf16[128,2048]{1,0:T(8,128)(2,1)}, u32[]{:S(2)}, u32[]{:S(2)}) collective-permute-start(bf16[128,2048]{1,0:T(8,128)(2,1)} %pad_maximum_fusion.8), channel_id=1, source_target_pairs={{0,3},{1,0},{2,1},{3,2},{4,7},{5,4},{6,5},{7,6},{8,11},{9,8},{10,9... | collective-permute-start | bytes 1572872 | tf_op jit(solution)/shard_map/ppermute | solution.py:23
  144.4 26.6 %collective-permute-start.20 = (bf16[256,2048]{1,0:T(8,128)(2,1)}, bf16[256,2048]{1,0:T(8,128)(2,1)S(1)}, u32[]{:S(2)}, u32[]{:S(2)}) collective-permute-start(bf16[256,2048]{1,0:T(8,128)(2,1)} %get-tuple-element.180), channel_id=1, source_target_pairs={{0,4},{4,0},{1,5},{5,1},{2,6},{6,2},{3,7},{7,3},{8,12},{12,8},{9,1... | collective-permute-start | bytes 3145736 | tf_op jit(solution)/shard_map/ppermute | solution.py:28
  144.5 24.3 %collective-permute-start.21 = (bf16[128,2048]{1,0:T(8,128)(2,1)S(1)}, bf16[128,2048]{1,0:T(8,128)(2,1)}, u32[]{:S(2)}, u32[]{:S(2)}) collective-permute-start(bf16[128,2048]{1,0:T(8,128)(2,1)S(1)} %copy-done.62), channel_id=1, source_target_pairs={{0,2},{1,3},{2,0},{3,1},{4,6},{5,7},{6,4},{7,5},{8,10},{9,11},{10,... | collective-permute-start | bytes 1572872 | tf_op jit(solution)/shard_map/ppermute | solution.py:23
  146.1 25.2 %collective-permute-start.22 = (bf16[512,1024]{1,0:T(8,128)(2,1)S(1)}, bf16[512,1024]{1,0:T(8,128)(2,1)S(1)}, u32[]{:S(2)}, u32[]{:S(2)}) collective-permute-start(bf16[512,1024]{1,0:T(8,128)(2,1)S(1)} %collective-permute-done.16.refs_14_), channel_id=1, source_target_pairs={{0,8},{8,0},{16,24},{24,16},{1,9},{9,1},{17,25},{25,17},{2,10},{10... | collective-permute-start | bytes 3145736 | tf_op jit(solution)/shard_map/ppermute | solution.py:28
  171.5 32.6 %collective-permute-start.24 = (bf16[256,2048]{1,0:T(8,128)(2,1)}, bf16[256,2048]{1,0:T(8,128)(2,1)}, u32[]{:S(2)}, u32[]{:S(2)}) collective-permute-start(bf16[256,2048]{1,0:T(8,128)(2,1)} %get-tuple-element.189), channel_id=1, source_target_pairs={{0,4},{4,0},{1,5},{5,1},{2,6},{6,2},{3,7},{7,3},{8,12},{12,8},{9,1... | collective-permute-start | bytes 3145736 | tf_op jit(solution)/shard_map/ppermute | solution.py:28
  172.7 33.0 %collective-permute-start.26 = (bf16[512,1024]{1,0:T(8,128)(2,1)S(1)}, bf16[512,1024]{1,0:T(8,128)(2,1)}, u32[]{:S(2)}, u32[]{:S(2)}) collective-permute-start(bf16[512,1024]{1,0:T(8,128)(2,1)S(1)} %get-tuple-element.336.refs_4_), channel_id=1, source_target_pairs={{0,8},{8,0},{16,24},{24,16},{1,9},{9,1},{17,25},{25,17},{2,10},{10... | collective-permute-start | bytes 3145736 | tf_op jit(solution)/shard_map/ppermute | solution.py:28
  174.3 31.4 %collective-permute-start.27 = (bf16[512,1024]{1,0:T(8,128)(2,1)S(1)}, bf16[512,1024]{1,0:T(8,128)(2,1)S(1)}, u32[]{:S(2)}, u32[]{:S(2)}) collective-permute-start(bf16[512,1024]{1,0:T(8,128)(2,1)S(1)} %get-tuple-element.336.refs_4_), channel_id=1, source_target_pairs={{0,16},{8,24},{16,0},{24,8},{1,17},{9,25},{17,1},{25,9},{2,18},{10... | collective-permute-start | bytes 3145736 | tf_op jit(solution)/shard_map/ppermute | solution.py:28
  206.2 26.4 %collective-permute-start.29 = (bf16[512,1024]{1,0:T(8,128)(2,1)}, bf16[512,1024]{1,0:T(8,128)(2,1)S(1)}, u32[]{:S(2)}, u32[]{:S(2)}) collective-permute-start(bf16[512,1024]{1,0:T(8,128)(2,1)} %get-tuple-element.192.refs_8_), channel_id=1, source_target_pairs={{0,16},{8,24},{16,0},{24,8},{1,17},{9,25},{17,1},{25,9},{2,18},{10... | collective-permute-start | bytes 3145736 | tf_op jit(solution)/shard_map/ppermute | solution.py:28
  207.0 25.6 %collective-permute-start.30 = (bf16[512,1024]{1,0:T(8,128)(2,1)}, bf16[512,1024]{1,0:T(8,128)(2,1)S(1)}, u32[]{:S(2)}, u32[]{:S(2)}) collective-permute-start(bf16[512,1024]{1,0:T(8,128)(2,1)} %get-tuple-element.192.refs_8_), channel_id=1, source_target_pairs={{0,8},{8,0},{16,24},{24,16},{1,9},{9,1},{17,25},{25,17},{2,10},{10... | collective-permute-start | bytes 3145736 | tf_op jit(solution)/shard_map/ppermute | solution.py:28
  208.5 43.7 %collective-permute-start.33 = (bf16[512,1024]{1,0:T(8,128)(2,1)}, bf16[512,1024]{1,0:T(8,128)(2,1)S(1)}, u32[]{:S(2)}, u32[]{:S(2)}) collective-permute-start(bf16[512,1024]{1,0:T(8,128)(2,1)} %collective-permute-done.26.refs_5_), channel_id=1, source_target_pairs={{0,16},{8,24},{16,0},{24,8},{1,17},{9,25},{17,1},{25,9},{2,18},{10... | collective-permute-start | bytes 3145736 | tf_op jit(solution)/shard_map/ppermute | solution.py:28
  232.7 25.6 %collective-permute-start.34 = (bf16[512,1024]{1,0:T(8,128)(2,1)S(1)}, bf16[512,1024]{1,0:T(8,128)(2,1)S(1)}, u32[]{:S(2)}, u32[]{:S(2)}) collective-permute-start(bf16[512,1024]{1,0:T(8,128)(2,1)S(1)} %collective-permute-done.29.refs_10_), channel_id=1, source_target_pairs={{0,8},{8,0},{16,24},{24,16},{1,9},{9,1},{17,25},{25,17},{2,10},{10... | collective-permute-start | bytes 3145736 | tf_op jit(solution)/shard_map/ppermute | solution.py:28
  258.3 30.1 %collective-permute-start.35 = (bf16[128,4096]{1,0:T(8,128)(2,1)}, bf16[128,4096]{1,0:T(8,128)(2,1)}, u32[]{:S(2)}, u32[]{:S(2)}) collective-permute-start(bf16[128,4096]{1,0:T(8,128)(2,1)} %collective-permute-done.31.refs_2_), channel_id=1, source_target_pairs={{0,1},{1,2},{2,3},{3,0},{4,5},{5,6},{6,7},{7,4},{8,9},{9,10},{10,1... | collective-permute-start | bytes 3145736 | tf_op jit(solution)/shard_map/ppermute | solution.py:23
  289.0 27.5 %collective-permute-start.37 = (bf16[128,4096]{1,0:T(8,128)(2,1)}, bf16[128,4096]{1,0:T(8,128)(2,1)S(1)}, u32[]{:S(2)}, u32[]{:S(2)}) collective-permute-start(bf16[128,4096]{1,0:T(8,128)(2,1)} %collective-permute-done.35.refs_0_), channel_id=1, source_target_pairs={{0,1},{1,2},{2,3},{3,0},{4,5},{5,6},{6,7},{7,4},{8,9},{9,10},{10,1... | collective-permute-start | bytes 3145736 | tf_op jit(solution)/shard_map/ppermute | solution.py:23
  290.9 25.5 %collective-permute-start.40 = (bf16[128,4096]{1,0:T(8,128)(2,1)}, bf16[128,4096]{1,0:T(8,128)(2,1)}, u32[]{:S(2)}, u32[]{:S(2)}) collective-permute-start(bf16[128,4096]{1,0:T(8,128)(2,1)} %collective-permute-done.35.refs_0_), channel_id=1, source_target_pairs={{0,4},{4,0},{1,5},{5,1},{2,6},{6,2},{3,7},{7,3},{8,12},{12,8},{9,1... | collective-permute-start | bytes 3145736 | tf_op jit(solution)/shard_map/ppermute | solution.py:28
  316.5 30.1 %collective-permute-start.41 = (bf16[128,4096]{1,0:T(8,128)(2,1)}, bf16[128,4096]{1,0:T(8,128)(2,1)}, u32[]{:S(2)}, u32[]{:S(2)}) collective-permute-start(bf16[128,4096]{1,0:T(8,128)(2,1)} %pad_maximum_fusion.1), channel_id=1, source_target_pairs={{0,1},{1,2},{2,3},{3,0},{4,5},{5,6},{6,7},{7,4},{8,9},{9,10},{10,1... | collective-permute-start | bytes 3145736 | tf_op jit(solution)/shard_map/ppermute | solution.py:23
  353.6 27.3 %collective-permute-start.45 = (bf16[128,4096]{1,0:T(8,128)(2,1)S(1)}, bf16[128,4096]{1,0:T(8,128)(2,1)}, u32[]{:S(2)}, u32[]{:S(2)}) collective-permute-start(bf16[128,4096]{1,0:T(8,128)(2,1)S(1)} %pad_maximum_fusion.2), channel_id=1, source_target_pairs={{0,1},{1,2},{2,3},{3,0},{4,5},{5,6},{6,7},{7,4},{8,9},{9,10},{10,1... | collective-permute-start | bytes 3145736 | tf_op jit(solution)/shard_map/ppermute | solution.py:23
  384.3 26.4 %collective-permute-start.46 = (bf16[128,4096]{1,0:T(8,128)(2,1)}, bf16[128,4096]{1,0:T(8,128)(2,1)S(1)}, u32[]{:S(2)}, u32[]{:S(2)}) collective-permute-start(bf16[128,4096]{1,0:T(8,128)(2,1)} %pad_maximum_fusion.3), channel_id=1, source_target_pairs={{0,1},{1,2},{2,3},{3,0},{4,5},{5,6},{6,7},{7,4},{8,9},{9,10},{10,1... | collective-permute-start | bytes 3145736 | tf_op jit(solution)/shard_map/ppermute | solution.py:23
  384.4 45.3 %collective-permute-start.47 = (bf16[512,1024]{1,0:T(8,128)(2,1)}, bf16[512,1024]{1,0:T(8,128)(2,1)S(1)}, u32[]{:S(2)}, u32[]{:S(2)}) collective-permute-start(bf16[512,1024]{1,0:T(8,128)(2,1)} %get-tuple-element.240), channel_id=1, source_target_pairs={{0,8},{8,0},{16,24},{24,16},{1,9},{9,1},{17,25},{25,17},{2,10},{10... | collective-permute-start | bytes 3145736 | tf_op jit(solution)/shard_map/ppermute | solution.py:28
  432.8 43.8 %collective-permute-start.55 = (bf16[512,1024]{1,0:T(8,128)(2,1)}, bf16[512,1024]{1,0:T(8,128)(2,1)}, u32[]{:S(2)}, u32[]{:S(2)}) collective-permute-start(bf16[512,1024]{1,0:T(8,128)(2,1)} %get-tuple-element.255), channel_id=1, source_target_pairs={{0,8},{8,0},{16,24},{24,16},{1,9},{9,1},{17,25},{25,17},{2,10},{10... | collective-permute-start | bytes 3145736 | tf_op jit(solution)/shard_map/ppermute | solution.py:28
  435.3 41.3 %collective-permute-start.54 = (bf16[512,1024]{1,0:T(8,128)(2,1)}, bf16[512,1024]{1,0:T(8,128)(2,1)}, u32[]{:S(2)}, u32[]{:S(2)}) collective-permute-start(bf16[512,1024]{1,0:T(8,128)(2,1)} %add_convert_fusion.1), channel_id=1, source_target_pairs={{0,16},{8,24},{16,0},{24,8},{1,17},{9,25},{17,1},{25,9},{2,18},{10... | collective-permute-start | bytes 3145736 | tf_op jit(solution)/shard_map/ppermute | solution.py:28
  480.5 27.8 %collective-permute-start.57 = (bf16[128,1024]{1,0:T(8,128)(2,1)}, bf16[128,1024]{1,0:T(8,128)(2,1)}, u32[]{:S(2)}, u32[]{:S(2)}) collective-permute-start(bf16[128,1024]{1,0:T(8,128)(2,1)} %get-tuple-element.266), channel_id=1, source_target_pairs={{0,1},{1,2},{2,3},{3,0},{4,5},{5,6},{6,7},{7,4},{8,9},{9,10},{10,1... | collective-permute-start | bytes 786440 | tf_op jit(solution)/shard_map/ppermute | solution.py:23
  481.0 27.2 %collective-permute-start.58 = (bf16[128,1024]{1,0:T(8,128)(2,1)}, bf16[128,1024]{1,0:T(8,128)(2,1)}, u32[]{:S(2)}, u32[]{:S(2)}) collective-permute-start(bf16[128,1024]{1,0:T(8,128)(2,1)} %get-tuple-element.268), channel_id=1, source_target_pairs={{0,3},{1,0},{2,1},{3,2},{4,7},{5,4},{6,5},{7,6},{8,11},{9,8},{10,9... | collective-permute-start | bytes 786440 | tf_op jit(solution)/shard_map/ppermute | solution.py:23
  511.0 29.0 %collective-permute-start.61 = (bf16[128,1024]{1,0:T(8,128)(2,1)S(1)}, bf16[128,1024]{1,0:T(8,128)(2,1)}, u32[]{:S(2)}, u32[]{:S(2)}) collective-permute-start(bf16[128,1024]{1,0:T(8,128)(2,1)S(1)} %get-tuple-element.288), channel_id=1, source_target_pairs={{0,2},{1,3},{2,0},{3,1},{4,6},{5,7},{6,4},{7,5},{8,10},{9,11},{10,... | collective-permute-start | bytes 786440 | tf_op jit(solution)/shard_map/ppermute | solution.py:23
  540.1 24.2 %collective-permute-start.64 = (bf16[512,1024]{1,0:T(8,128)(2,1)S(1)}, bf16[512,1024]{1,0:T(8,128)(2,1)S(1)}, u32[]{:S(2)}, u32[]{:S(2)}) collective-permute-start(bf16[512,1024]{1,0:T(8,128)(2,1)S(1)} %copy-done.75), channel_id=1, source_target_pairs={{0,16},{8,24},{16,0},{24,8},{1,17},{9,25},{17,1},{25,9},{2,18},{10... | collective-permute-start | bytes 3145736 | tf_op jit(solution)/shard_map/ppermute | solution.py:28
  541.7 23.0 %collective-permute-start.63 = (bf16[256,2048]{1,0:T(8,128)(2,1)S(1)}, bf16[256,2048]{1,0:T(8,128)(2,1)S(1)}, u32[]{:S(2)}, u32[]{:S(2)}) collective-permute-start(bf16[256,2048]{1,0:T(8,128)(2,1)S(1)} %copy-done.74), channel_id=1, source_target_pairs={{0,4},{4,0},{1,5},{5,1},{2,6},{6,2},{3,7},{7,3},{8,12},{12,8},{9,1... | collective-permute-start | bytes 3145736 | tf_op jit(solution)/shard_map/ppermute | solution.py:28
  542.8 21.9 %collective-permute-start.62 = (bf16[128,2048]{1,0:T(8,128)(2,1)S(1)}, bf16[128,2048]{1,0:T(8,128)(2,1)S(1)}, u32[]{:S(2)}, u32[]{:S(2)}) collective-permute-start(bf16[128,2048]{1,0:T(8,128)(2,1)S(1)} %copy-done.63), channel_id=1, source_target_pairs={{0,1},{1,2},{2,3},{3,0},{4,5},{5,6},{6,7},{7,4},{8,9},{9,10},{10,1... | collective-permute-start | bytes 1572872 | tf_op jit(solution)/shard_map/ppermute | solution.py:23
  543.4 26.8 %collective-permute-start.66 = (bf16[128,2048]{1,0:T(8,128)(2,1)S(1)}, bf16[128,2048]{1,0:T(8,128)(2,1)S(1)}, u32[]{:S(2)}, u32[]{:S(2)}) collective-permute-start(bf16[128,2048]{1,0:T(8,128)(2,1)S(1)} %get-tuple-element.294), channel_id=1, source_target_pairs={{0,1},{1,2},{2,3},{3,0},{4,5},{5,6},{6,7},{7,4},{8,9},{9,10},{10,1... | collective-permute-start | bytes 1572872 | tf_op jit(solution)/shard_map/ppermute | solution.py:23
  572.8 24.6 %collective-permute-start.71 = (bf16[512,1024]{1,0:T(8,128)(2,1)S(1)}, bf16[512,1024]{1,0:T(8,128)(2,1)S(1)}, u32[]{:S(2)}, u32[]{:S(2)}) collective-permute-start(bf16[512,1024]{1,0:T(8,128)(2,1)S(1)} %copy-done.73), channel_id=1, source_target_pairs={{0,16},{8,24},{16,0},{24,8},{1,17},{9,25},{17,1},{25,9},{2,18},{10... | collective-permute-start | bytes 3145736 | tf_op jit(solution)/shard_map/ppermute | solution.py:28
  574.2 24.3 %collective-permute-start.70 = (bf16[512,1024]{1,0:T(8,128)(2,1)S(1)}, bf16[512,1024]{1,0:T(8,128)(2,1)S(1)}, u32[]{:S(2)}, u32[]{:S(2)}) collective-permute-start(bf16[512,1024]{1,0:T(8,128)(2,1)S(1)} %add_convert_fusion), channel_id=1, source_target_pairs={{0,8},{8,0},{16,24},{24,16},{1,9},{9,1},{17,25},{25,17},{2,10},{10... | collective-permute-start | bytes 3145736 | tf_op jit(solution)/shard_map/ppermute | solution.py:28
  575.0 24.2 %collective-permute-start.72 = (bf16[128,2048]{1,0:T(8,128)(2,1)S(1)}, bf16[128,2048]{1,0:T(8,128)(2,1)S(1)}, u32[]{:S(2)}, u32[]{:S(2)}) collective-permute-start(bf16[128,2048]{1,0:T(8,128)(2,1)S(1)} %get-tuple-element.303), channel_id=1, source_target_pairs={{0,3},{1,0},{2,1},{3,2},{4,7},{5,4},{6,5},{7,6},{8,11},{9,8},{10,9... | collective-permute-start | bytes 1572872 | tf_op jit(solution)/shard_map/ppermute | solution.py:23
  611.5 36.4 %collective-permute-start.80 = (bf16[128,2048]{1,0:T(8,128)(2,1)S(1)}, bf16[128,2048]{1,0:T(8,128)(2,1)S(1)}, u32[]{:S(2)}, u32[]{:S(2)}) collective-permute-start(bf16[128,2048]{1,0:T(8,128)(2,1)S(1)} %get-tuple-element.308), channel_id=1, source_target_pairs={{0,2},{1,3},{2,0},{3,1},{4,6},{5,7},{6,4},{7,5},{8,10},{9,11},{10,... | collective-permute-start | bytes 1572872 | tf_op jit(solution)/shard_map/ppermute | solution.py:23
  (110 other events, 1233.0 us)
Sparse Core Ops, SparseCore 0:
  384.4 120.2 reduce-scatter.1

commit v3 on v2

--- a/solution.py
+++ b/solution.py
@@ -1,3 +1,4 @@
+import math
 from functools import partial
 
 import jax
@@ -139,16 +140,17 @@
     return [cut((rank + k) % blks) for k in range(blks)]
 
 
-def join_owners(exchanged, cuts, scale):
+def join_owners(exchanges, cuts, scale):
     blks, rank = lax.axis_size("blk"), lax.axis_index("blk")
     wide = sum(width for _, width in cuts)
-    out = jnp.zeros((exchanged.got[0].shape[0], blks * wide), WIDE)
-    for k in range(blks):
-        first = (rank - k) % blks * wide
-        for at, width in cuts:
-            part = exchanged.got[k][:, at : at + width].astype(WIDE) * scale
-            out = lax.dynamic_update_slice(out, part, (0, first))
-            first = first + width
+    out = jnp.zeros((exchanges[0].got[0].shape[0], blks * wide * len(exchanges)), WIDE)
+    for n, exchanged in enumerate(exchanges):
+        for k in range(blks):
+            first = ((rank - k) % blks * len(exchanges) + n) * wide
+            for at, width in cuts:
+                part = exchanged.got[k][:, at : at + width].astype(WIDE) * scale
+                out = lax.dynamic_update_slice(out, part, (0, first))
+                first = first + width
     return out
 
 
@@ -185,6 +187,32 @@
     for first in range(0, width, HEAD_DIM):
         parts += [vectors[:, first + HALF : first + HEAD_DIM], vectors[:, first : first + HALF]]
     return jnp.concatenate(parts, axis=1)
+
+
+def table_kernel(dims, place_ref, cos_ref, sin_ref):
+    total, blks, seqs, size = dims
+    wide = cos_ref.shape[1]
+    index = lax.broadcasted_iota(jnp.int32, (total, 1), 0)
+    position = row_positions(index, place_ref[0], place_ref[1], blks, seqs, size).astype(WIDE)
+    lane = lax.broadcasted_iota(jnp.int32, (1, wide), 1)
+    power = (lane % HALF).astype(WIDE) * (-2.0 / HEAD_DIM)
+    angle = position * jnp.exp(power * math.log(ROPE_BASE))
+    cos_ref[...] = jnp.cos(angle)
+    sin_ref[...] = jnp.where(lane % HEAD_DIM < HALF, -jnp.sin(angle), jnp.sin(angle))
+
+
+def rotary_tables(place, total, size, wide):
+    dims = (total, lax.axis_size("blk"), lax.axis_size("seq"), size)
+    return pl.pallas_call(
+        partial(table_kernel, dims),
+        grid_spec=pltpu.PrefetchScalarGridSpec(
+            num_scalar_prefetch=1, grid=(1,), in_specs=[], out_specs=[vmem((total, wide))] * 2
+        ),
+        out_shape=[jax.ShapeDtypeStruct((total, wide), WIDE)] * 2,
+        compiler_params=params(32),
+        cost_estimate=cost(),
+        name="rotary_tables",
+    )(place)
 
 
 def widen(table, width):
@@ -268,10 +296,13 @@
 
 
 def put_parts(terms, size, column, value):
-    seqs = len(terms)
-    for n in range(value.shape[0] // size):
-        g, m = n // seqs, n % seqs
-        terms[m][g * size : (g + 1) * size, column : column + value.shape[1]] = value[n * size : (n + 1) * size]
+    for n, term in enumerate(terms):
+        term[:, column : column + value.shape[1]] = value[n * size : (n + 1) * size]
+
+
+def by_block(terms, count):
+    some = len(terms) // count
+    return [terms[g * some : (g + 1) * some] for g in range(count)]
 
 
 def attend_kernel(dims, ks, width, place_ref, *refs):
@@ -320,98 +351,74 @@
             num_scalar_prefetch=1,
             grid=(1,),
             in_specs=[rows_at(k, width) for k in ks] + [vmem((total, width))] * 2 + [vmem(w.shape) for w in weights],
-            out_specs=[vmem((block, width))] * count + [vmem((block, 128))] * count + [vmem((count * size, model))] * seqs,
+            out_specs=[vmem((block, width))] * count + [vmem((block, 128))] * count + [vmem((size, model))] * (count * seqs),
         ),
         out_shape=[jax.ShapeDtypeStruct((block, width), LOW)] * count
         + [jax.ShapeDtypeStruct((block, 128), WIDE)] * count
-        + [jax.ShapeDtypeStruct((count * size, model), LOW)] * seqs,
+        + [jax.ShapeDtypeStruct((size, model), LOW)] * (count * seqs),
         compiler_params=params(56),
         cost_estimate=cost(),
         name="attend_blocks",
     )(place, *[queries] * count, key_rows, val_rows, *weights)
-    return got[:count], got[count : 2 * count], got[2 * count :]
-
-
-def mlp_kernel(count, seqs, place_ref, *refs):
-    parts, pairs, down = refs[:count], (refs[count : count + 4], refs[count + 4 : count + 8]), refs[count + 8 : count + 12]
-    grad_acc, out_acc, h_rel = refs[-3:]
-    outs = refs[-3 - 4 - 2 * seqs : -3]
-    h_ref, c_ref, act_ref, pair_ref = outs[:4]
-    grad_terms, out_terms = outs[4 : 4 + seqs], outs[4 + seqs :]
+    return got[:count], got[count : 2 * count], by_block(got[2 * count :], count)
+
+
+def mlp_kernel(count, *refs):
+    parts, pairs, down = refs[:count], (refs[count : count + 4], refs[count + 4 : count + 8]), refs[count + 8 : count + 13]
+    outs = refs[-5 - 2 * count :]
+    h_ref, c_ref, act_ref, pair_refs = outs[0], outs[1], outs[2], outs[3:5]
+    grad_terms, out_terms = outs[5 : 5 + count], outs[5 + count :]
     size, model = parts[0].shape[0], h_ref.shape[1]
-    step, hidden = model // GROUPS, down[0].shape[1]
-    j = pl.program_id(0)
+    step, hidden = model // GROUPS, down[0].shape[1] // 2
     groups = [slice(i * step, (i + 1) * step) for i in range(GROUPS)]
-
-    @pl.when(j == 0)
-    def _():
-        for m in range(count):
-            rows = slice(m * size, (m + 1) * size)
-            h_rel[rows, :] = parts[m][:, :model]
-            c_ref[rows, :] = parts[m][:, model:]
-            for i in range(GROUPS):
-                there = pl.multiple_of((place_ref[3] ^ i) * step, step)
-                h_ref[rows, pl.ds(there, step)] = parts[m][:, groups[i]]
-
-    def pair_weight(i):
-        return jnp.where(j == 0, pairs[0][i][...], pairs[1][i][...])
-
-    both = matmul(h_rel[:, groups[0]], pair_weight(0))
-    grad_act = matmul(c_ref[:, groups[0]], down[0][...])
-    for i in range(1, GROUPS):
-        both += matmul(h_rel[:, groups[i]], pair_weight(i))
-        grad_act += matmul(c_ref[:, groups[i]], down[i][...])
-    gate, up = both[:, :hidden], both[:, hidden:]
-    sig = jax.nn.sigmoid(gate)
-    act_ref[...] = (gate * sig * up).astype(LOW)
-    pair_ref[:, :hidden] = (grad_act * up * sig * (1.0 + gate * (1.0 - sig))).astype(LOW)
-    pair_ref[:, hidden:] = (grad_act * gate * sig).astype(LOW)
-    for i, here in enumerate(groups):
-        grad = over_cols(pair_ref[...], pair_weight(i))
-        out = over_cols(act_ref[...], down[i][...])
-
-        @pl.when(j == 0)
-        def _():
-            grad_acc[:, here] = grad
-            out_acc[:, here] = out
-
-        @pl.when(j == 1)
-        def _():
-            grad_sum, out_sum = grad_acc[:, here] + grad, out_acc[:, here] + out
-            put_parts(grad_terms, size, i * step, grad_sum.astype(LOW))
-            put_parts(out_terms, size, i * step, out_sum.astype(LOW))
-
-
-def mlp_blocks(at, seqs, place, parts, pairs, down, held, total):
+    for m in range(count):
+        rows = slice(m * size, (m + 1) * size)
+        h_ref[rows, :] = parts[m][:, :model]
+        c_ref[rows, :] = parts[m][:, model:]
+    down_half = lambda i, j: down[i][:, j * hidden : (j + 1) * hidden] if i < 3 else down[3 + j][...]
+    for j, pair_ref in enumerate(pair_refs):
+        half = slice(j * hidden, (j + 1) * hidden)
+        both = matmul(h_ref[:, groups[0]], pairs[j][0][...])
+        grad_act = matmul(c_ref[:, groups[0]], down_half(0, j))
+        for i in range(1, GROUPS):
+            both += matmul(h_ref[:, groups[i]], pairs[j][i][...])
+            grad_act += matmul(c_ref[:, groups[i]], down_half(i, j))
+        gate, up = both[:, :hidden], both[:, hidden:]
+        sig = jax.nn.sigmoid(gate)
+        act_ref[:, half] = (gate * sig * up).astype(LOW)
+        pair_ref[:, :hidden] = (grad_act * up * sig * (1.0 + gate * (1.0 - sig))).astype(LOW)
+        pair_ref[:, hidden:] = (grad_act * gate * sig).astype(LOW)
+    for i in range(GROUPS):
+        grad = over_cols(pair_refs[0][...], pairs[0][i][...]) + over_cols(pair_refs[1][...], pairs[1][i][...])
+        put_parts(grad_terms, size, i * step, grad.astype(LOW))
+        if i < 3:
+            out = over_cols(act_ref[...], down[i][...])
+        else:
+            out = over_cols(act_ref[:, :hidden], down[3][...]) + over_cols(act_ref[:, hidden:], down[4][...])
+        put_parts(out_terms, size, i * step, out.astype(LOW))
+
+
+def mlp_blocks(at, seqs, parts, pairs, down, held, total):
     count, (size, model) = len(parts), (parts[0].shape[0], parts[0].shape[1] // 2)
-    step, hidden = model // GROUPS, down[0].shape[1] // 2
+    hidden = down[0].shape[1]
     rows = count * size
     old = [] if held is None else list(held)
-    mine = lambda wide: pl.BlockSpec((rows, wide), lambda j, place: (at, 0))
-    mine_half = lambda wide: pl.BlockSpec((rows, wide), lambda j, place: (at, j))
-    half = lambda wide: pl.BlockSpec((step, wide), lambda j, place: (0, j))
+    widths = [model, model, hidden, hidden, hidden]
     got = pl.pallas_call(
-        partial(mlp_kernel, count, seqs),
-        grid_spec=pltpu.PrefetchScalarGridSpec(
-            num_scalar_prefetch=1,
-            grid=(2,),
-            in_specs=[vmem((size, 2 * model))] * count
-            + [vmem((step, 2 * hidden))] * 8
-            + [half(hidden)] * 4
-            + [ANY] * len(old),
-            out_specs=[mine(model), mine(model), mine_half(hidden), mine_half(2 * hidden)]
-            + [vmem((rows // seqs, model))] * (2 * seqs),
-            scratch_shapes=[pltpu.VMEM((rows, model), WIDE)] * 2 + [pltpu.VMEM((rows, model), LOW)],
-        ),
-        out_shape=[jax.ShapeDtypeStruct((total, model), LOW)] * 2
-        + [jax.ShapeDtypeStruct((total, 2 * hidden), LOW), jax.ShapeDtypeStruct((total, 4 * hidden), LOW)]
-        + [jax.ShapeDtypeStruct((rows // seqs, model), LOW)] * (2 * seqs),
-        input_output_aliases={count + 13 + i: i for i in range(4)} if old else {},
+        partial(mlp_kernel, count),
+        grid=(1,),
+        in_specs=[vmem((size, 2 * model))] * count
+        + [vmem(w.shape) for w in (*pairs[0], *pairs[1], *down)]
+        + [ANY] * len(old),
+        out_specs=[pl.BlockSpec((rows, wide), lambda _: (at, 0)) for wide in widths] + [vmem((size, model))] * (2 * count),
+        out_shape=[jax.ShapeDtypeStruct((total, wide), LOW) for wide in widths]
+        + [jax.ShapeDtypeStruct((size, model), LOW)] * (2 * count),
+        input_output_aliases={count + 13 + i: i for i in range(5)} if old else {},
         compiler_params=params(60),
         cost_estimate=cost(),
         name="mlp_blocks",
-    )(place, *parts, *pairs[0], *pairs[1], *down, *old)
-    return got[:4], got[4 : 4 + seqs], got[4 + seqs :]
+    )(*parts, *pairs[0], *pairs[1], *down, *old)
+    return got[:5], by_block(got[5 : 5 + count], count // seqs), by_block(got[5 + count :], count // seqs)
 
 
 def attend_back_kernel(dims, ks, width, fresh, place_ref, *refs):
@@ -516,7 +523,7 @@
 
     gq_refs, gk_refs, gv_refs, cos_refs, sin_refs = (some(count) for _ in range(5))
     weights, parts = some(4), some(count * seqs)
-    outs, (gain_ref,), terms = some(count), some(1), some(seqs)
+    outs, (gain_ref,), terms = some(count), some(1), some(count * seqs)
     size = parts[0].shape[0]
     step = weights[0].shape[0]
     for g, out_ref in enumerate(outs):
@@ -556,15 +563,15 @@
         + tables * 2
         + [vmem(w.shape) for w in weights]
         + [vmem((size, model))] * (count * seqs),
-        out_specs=[vmem((block, 3 * width))] * count + [vmem((1, model))] + [vmem((count * size, model))] * seqs,
+        out_specs=[vmem((block, 3 * width))] * count + [vmem((1, model))] + [vmem((size, model))] * (count * seqs),
         out_shape=[jax.ShapeDtypeStruct((block, 3 * width), LOW)] * count
         + [jax.ShapeDtypeStruct((1, model), WIDE)]
-        + [jax.ShapeDtypeStruct((count * size, model), LOW)] * seqs,
+        + [jax.ShapeDtypeStruct((size, model), LOW)] * (count * seqs),
         compiler_params=params(56),
         cost_estimate=cost(),
         name="finish_blocks",
     )(*[grad_q[k] for k in ks], *[grad_k] * count, *[grad_v] * count, *[cos] * count, *[sin] * count, *weights, *parts)
-    return got[:count], got[count], got[count + 1 :]
+    return got[:count], got[count], by_block(got[count + 1 :], count)
 
 
 def weight_kernel(counts, *refs):
@@ -599,25 +606,6 @@
     )(*arrays)
 
 
-def pair_kernel(left_ref, right_ref, out_ref):
-    out_ref[...] = over_rows(left_ref[...], right_ref[...]).astype(LOW)
-
-
-def pair_term(left, right):
-    (total, model), cols = left.shape, right.shape[1]
-    tall, wide = min(model, 1024), min(cols, 1024)
-    return pl.pallas_call(
-        pair_kernel,
-        grid=(model // tall, cols // wide),
-        in_specs=[pl.BlockSpec((total, tall), lambda i, j: (0, i)), pl.BlockSpec((total, wide), lambda i, j: (0, j))],
-        out_specs=pl.BlockSpec((tall, wide), lambda i, j: (i, j)),
-        out_shape=jax.ShapeDtypeStruct((model, cols), LOW),
-        compiler_params=params(60),
-        cost_estimate=cost(),
-        name="pair_term",
-    )(left, right)
-
-
 def shards(
     tokens, out_grad, lengths, attn_gain, w_query, w_key, w_value, output_weight, mlp_gain, gate_weight, up_weight, down_weight
 ):
@@ -633,14 +621,7 @@
     live_rows = (positions < length)[:, None]
     place = jnp.stack([blk_rank, seq_rank, length, lax.axis_index("slot")]).astype(jnp.int32)
 
-    all_pos = row_positions(jnp.arange(total, dtype=jnp.int32), blk_rank, seq_rank, blks, seqs, size)
-    frequency = ROPE_BASE ** (-jnp.arange(HALF, dtype=WIDE) * 2.0 / HEAD_DIM)
-    angles = all_pos.astype(WIDE)[:, None] * frequency[None, :]
-    cos_tab, sin_tab = jnp.cos(angles), jnp.sin(angles)
-    table = min(width, 128)
-    cos_wide = jnp.tile(cos_tab, (1, table // HALF))
-    sin_wide = jnp.tile(jnp.concatenate([-sin_tab, sin_tab], axis=1), (1, table // HEAD_DIM))
-
+    cos_wide, sin_wide = rotary_tables(place, total, size, min(width, 128))
     own_tokens = slot_order(tokens[0])
     own_cot = jnp.where(live_rows, slot_order(out_grad[0]), 0)
     gain_attn, gain_mlp = attn_gain.astype(WIDE)[:, None], mlp_gain.astype(WIDE)[:, None]
@@ -661,41 +642,29 @@
     def calls(ks):
         return [ks] if block * len(ks) <= 512 else [[k] for k in ks]
 
-    def reduced(ks, parts):
-        summands = seq_reduce(parts)
-        return [[s[g * size : (g + 1) * size] for s in summands] for g in range(len(ks))]
-
-    def reduce_calls(got):
-        for ks, parts in got:
-            for k, summands in zip(ks, reduced(ks, parts)):
-                terms[k] = summands
-
     token_blocks = [None] * blks
     ahead = turn(own_tokens, "blk", 1)
     attn_out.send(1, 2, 3)
     token_blocks[0] = seq_gather(own_tokens)
-    part_attn = attn_out.by_rank()
-    phase.end(ahead, part_attn, token_blocks[0], cos_wide, sin_wide, place)
-
-    moving, part_attn, down_out.pieces = phase.take(ahead, part_attn, down_out.pieces)
+    phase.end(ahead, attn_out.got, token_blocks[0])
+
+    moving, part_attn, pair_out.pieces = phase.take(ahead, attn_out.by_rank(), pair_out.pieces)
     ahead = turn(moving, "blk", 1)
     near_x, near_y = swap(part_attn, "slot", 1), swap(part_attn, "slot", 2)
-    down_out.send(1, 3)
-    phase.end(ahead, near_x, near_y, down_out.got)
-
-    second, moving, near_x, down_out.pieces = phase.take(moving, ahead, near_x, down_out.pieces)
+    pair_out.send(1)
+    phase.end(ahead, near_x, near_y, pair_out.got, cos_wide, sin_wide)
+
+    second, moving, near_x, pair_out.pieces = phase.take(moving, ahead, near_x, pair_out.pieces)
     ahead = turn(moving, "blk", 1)
     far = swap(near_x, "slot", 2)
-    down_out.send(2)
+    pair_out.send(3)
     token_blocks[1], token_blocks[2] = seq_gather(second), seq_gather(moving)
     full_attn = [part_attn, near_x, near_y, far]
-    part_down = down_out.by_rank()
-    phase.end(ahead, far, token_blocks[1:3], part_down)
-
-    moving, part_down, pair_out.pieces = phase.take(ahead, part_down, pair_out.pieces)
+    phase.end(ahead, far, token_blocks[1:3], pair_out.got)
+
+    moving, pair_out.pieces = phase.take(ahead, pair_out.pieces)
     token_blocks[3] = seq_gather(moving)
-    near_x, near_y = swap(part_down, "slot", 1), swap(part_down, "slot", 2)
-    pair_out.send(1, 3)
+    pair_out.send(2)
     got = []
     for ks in [list(range(blks))] if total <= 1024 else [[k] for k in range(blks)]:
         here = slice(ks[0] * block, (ks[-1] + 1) * block)
@@ -706,111 +675,112 @@
     attended, lse, terms = [None] * blks, [None] * blks, [None] * blks
 
     def attend(ks, queries):
-        got = []
         for some in calls(ks):
-            outs, lses, parts = attend_blocks(some, place, queries, key_rows, val_rows, full_attn, size, model)
-            got.append((some, parts))
-            for k, out, log in zip(some, outs, lses):
-                attended[k], lse[k] = out, log
-        return [ks for ks, _ in got], [parts for _, parts in got]
-
-    takers, parts = attend(in_turn[0], queries)
-    phase.end(near_x, near_y, pair_out.got, parts)
-
-    queries, near_y, pair_out.pieces, parts = phase.take(queries, near_y, pair_out.pieces, parts)
-    pair_out.send(2)
-    full_down = [part_down, near_x, near_y, swap(near_y, "slot", 1)]
-    reduce_calls(zip(takers, parts))
-    takers, parts = attend(in_turn[1], queries)
+            for k, *got in zip(some, *attend_blocks(some, place, queries, key_rows, val_rows, full_attn, size, model)):
+                attended[k], lse[k], terms[k] = got
+
+    attend(in_turn[0], queries)
+    phase.end(pair_out.got, terms[1], terms[2])
+
+    queries, pair_out.got, down_out.pieces, terms[1], terms[2] = phase.take(
+        queries, pair_out.got, down_out.pieces, terms[1], terms[2]
+    )
     part_pair = pair_out.by_rank()
-    phase.end(part_pair, full_down, parts, terms[1], terms[2])
-
-    moving, part_pair, parts = phase.take(add_up(terms[1]).astype(LOW), part_pair, parts)
-    halves = [part_pair[:, :hidden], part_pair[:, hidden:]]
-    near_x, near_y = [swap(halves[0], "slot", 1)], [swap(halves[0], "slot", 2)]
-    reduce_calls(zip(takers, parts))
-    moving = turn(moving, "blk", 1)
-    phase.end(moving, terms)
-    moving, half_b = phase.take(add_up([moving, *terms[2]]).astype(LOW), halves[1])
+    half_a, half_b = part_pair[:, :hidden], part_pair[:, hidden:]
+    near_x, near_y = [swap(half_a, "slot", 1)], [swap(half_a, "slot", 2)]
+    terms[1] = seq_reduce(terms[1])
+    moving = turn(add_up(terms[1]).astype(LOW), "blk", 1)
+    down_out.send(2)
+    terms[2] = seq_reduce(terms[2])
+    attend(in_turn[1], queries)
+    phase.end(moving, terms, near_x, near_y, down_out.got)
+
+    moving, half_b, down_out.pieces, terms[3], terms[0] = phase.take(
+        add_up([moving, *terms[2]]).astype(LOW), half_b, down_out.pieces, terms[3], terms[0]
+    )
     near_x, near_y = near_x + [swap(half_b, "slot", 1)], near_y + [swap(half_b, "slot", 2)]
     moving = turn(moving, "blk", 1)
-    phase.end(moving, near_x[0], near_y[0])
-    moving, far = phase.take(add_up([moving, *terms[3]]).astype(LOW), near_x[0])
-    far_a = swap(far, "slot", 2)
+    down_out.send(1)
+    terms[3] = seq_reduce(terms[3])
+    phase.end(moving, terms[3], near_x, near_y, down_out.got)
+
+    moving, far_x, far_y, down_out.pieces, terms[0] = phase.take(
+        add_up([moving, *terms[3]]).astype(LOW), near_x[0], near_y[1], down_out.pieces, terms[0]
+    )
     moving = turn(moving, "blk", 1)
-    phase.end(moving, near_x, near_y)
+    down_out.send(3)
+    far_a, far_b = swap(far_x, "slot", 2), swap(far_y, "slot", 1)
+    terms[0] = seq_reduce(terms[0])
+    full_pair = [[half_a, near_x[0], near_y[0], far_a], [half_b, near_x[1], near_y[1], far_b]]
+    phase.end(moving, terms[0], down_out.got)
     resid = rows_f + add_up([moving, *terms[0]])
     normed_mlp, inverse_mlp = norm_rows(resid)
 
+    grads_of, outs_of = [None] * blks, [None] * blks
+
     def feed(ks, held):
-        got = []
         for some in calls(ks):
             held, grads, outs = mlp_blocks(
-                some[0] // len(some), seqs, place, flat([blocks[k] for k in some]), full_pair, full_down, held, total
+                some[0] // len(some), seqs, flat([blocks[k] for k in some]), full_pair, full_down, held, total
             )
-            got.append([grads, outs])
-        return held, calls(ks), got
-
-    def reduce_pairs(takers, got):
-        for ks, (grads, outs) in zip(takers, got):
-            for k, grad, out in zip(ks, reduced(ks, grads), reduced(ks, outs)):
-                terms[k] = [grad, out]
-
-    def join_pair(moving, pair):
-        sums = pair if moving is None else [[moving[:, i * model : (i + 1) * model], *part] for i, part in enumerate(pair)]
-        return jnp.concatenate([add_up(part).astype(LOW) for part in sums], axis=1)
-
-    blocks, terms = [None] * blks, [None] * blks
-    moving, far = phase.take(jnp.concatenate([normed_mlp.astype(LOW), own_cot], axis=1), near_y[1])
-    far_b = swap(far, "slot", 1)
-    full_pair = [[halves[0], near_x[0], near_y[0], far_a], [halves[1], near_x[1], near_y[1], far_b]]
+            for k, grad, out in zip(some, grads, outs):
+                grads_of[k], outs_of[k] = grad, out
+        return held
+
+    blocks = [None] * blks
+    moving, part_down = phase.take(
+        jnp.concatenate([normed_mlp.astype(LOW), own_cot], axis=1), down_out.by_rank()
+    )
     ahead = turn(moving, "blk", 1)
+    near_x, near_y = swap(part_down, "slot", 1), swap(part_down, "slot", 2)
     blocks[0] = seq_gather(moving)
     phase.end(ahead, far_a, far_b, blocks[0])
 
-    moving, blocks[0] = phase.take(ahead, blocks[0])
+    moving = phase.take(ahead)
     ahead = turn(moving, "blk", 1)
+    cut = hidden // 2
+    full_down = [part_down, near_x, near_y, swap(near_x[:, :cut], "slot", 2), swap(near_y[:, cut:], "slot", 1)]
     blocks[1] = seq_gather(moving)
-    held, takers, got = feed(in_order[0], None)
-    phase.end(ahead, blocks[1], held)
-
-    moving, got = phase.take(ahead, got)
+    phase.end(ahead, blocks[1], full_down)
+
+    moving, blocks[0], blocks[1] = phase.take(ahead, blocks[0], blocks[1])
     ahead = turn(moving, "blk", 1)
     blocks[2] = seq_gather(moving)
-    reduce_pairs(takers, got)
-    phase.end(ahead, blocks[2], terms[1])
-
-    moving, summed, blocks[2] = phase.take(ahead, join_pair(None, terms[1]), blocks[2])
+    held = feed(in_order[0], None)
+    phase.end(ahead, blocks[2], held)
+
+    moving, blocks[2], grads_of[:2], outs_of[:2] = phase.take(ahead, blocks[2], grads_of[:2], outs_of[:2])
+    grads_of[1] = seq_reduce(grads_of[1])
     blocks[3] = seq_gather(moving)
-    moving = turn(summed, "blk", 1)
-    held, takers, got = feed(in_order[1], held)
-    phase.end(moving, held)
-    hidden_mlp, all_cot, activation, grad_pair = held
-
-    moving, got, grad_pair, activation = phase.take(moving, got, grad_pair, activation)
-    reduce_pairs(takers, got)
-    moving = turn(join_pair(moving, terms[2]), "blk", 1)
-    term = pair_term(hidden_mlp, grad_pair)
+    grad = turn(add_up(grads_of[1]).astype(LOW), "blk", 1)
+    outs_of[1] = seq_reduce(outs_of[1])
+    out = turn(add_up(outs_of[1]).astype(LOW), "blk", 1)
+    held = feed(in_order[1], held)
+    phase.end(grad, out, held)
+    hidden_mlp, all_cot, activation, *grad_pair = held
+
+    grad, grads_of[2], outs_of[2], out, activation, grad_pair[1] = phase.take(
+        grad, grads_of[2], outs_of[2], out, activation, grad_pair[1]
+    )
+    grads_of[2], outs_of[2] = seq_reduce(grads_of[2]), seq_reduce(outs_of[2])
+    grad = turn(add_up([grad, *grads_of[2]]).astype(LOW), "blk", 1)
+    out = turn(add_up([out, *outs_of[2]]).astype(LOW), "blk", 1)
     down_terms = weight_terms((all_cot, [activation]))
-    phase.end(moving, terms, term, down_terms)
-
-    moving, far, term = phase.take(join_pair(moving, terms[3]), down_terms[3], term)
-    sum_pair = lax.psum_scatter(term, "slot", scatter_dimension=0, tiled=True)
-    moving = turn(moving, "blk", 1)
-    far = swap(far, "slot", 1)
-    phase.end(moving, far)
-    grad_part, out_part = (add_up([moving[:, i * model : (i + 1) * model], *terms[0][i]]) for i in range(2))
-    layer_out = jnp.where(live_rows, resid + out_part, 0.0)
+    pair_b = weight_terms((hidden_mlp, [grad_pair[1]]))
+    phase.end(grad, out, down_terms, pair_b)
+
+    grad, grads_of[3], grads_of[0], far_down, far_b, half = phase.take(
+        grad, grads_of[3], grads_of[0], down_terms[3], pair_b[3], grad_pair[0]
+    )
+    grads_of[3] = seq_reduce(grads_of[3])
+    grad = turn(add_up([grad, *grads_of[3]]).astype(LOW), "blk", 1)
+    far_down, far_b = swap(far_down, "slot", 1), swap(far_b, "slot", 2)
+    grads_of[0] = seq_reduce(grads_of[0])
+    pair_a = weight_terms((hidden_mlp, [half]))
+    phase.end(grad, grads_of[0], pair_a)
+    grad_part = add_up([grad, *grads_of[0]])
     grad_resid_part, gain_mlp_term = norm_back(normed_mlp, inverse_mlp, grad_part)
     grad_resid = own_cot.astype(WIDE) + grad_resid_part
-
-    moving, relay, near_term = phase.take(
-        grad_resid.astype(LOW), add_up([down_terms[2], far]).astype(LOW), down_terms[1]
-    )
-    ahead = turn(moving, "blk", 1)
-    one, two = swap(relay, "slot", 2), swap(near_term, "slot", 1)
-    blocks = [seq_gather(moving), None, None, None]
-    phase.end(ahead, blocks[0])
 
     grad_q = [None] * blks
 
@@ -824,87 +794,109 @@
                 grad_q[k] = grad
         return held
 
-    moving, blocks[0] = phase.take(ahead, blocks[0])
+    moving, out, outs_of[3], outs_of[0] = phase.take(grad_resid.astype(LOW), out, outs_of[3], outs_of[0])
     ahead = turn(moving, "blk", 1)
+    blocks = [seq_gather(moving), None, None, None]
+    outs_of[3] = seq_reduce(outs_of[3])
+    phase.end(ahead, blocks[0], outs_of[3], far_down, far_b)
+
+    moving, blocks[0], far_down, down_terms, out = phase.take(
+        ahead, blocks[0], far_down, down_terms, add_up([out, *outs_of[3]]).astype(LOW)
+    )
+    ahead = turn(moving, "blk", 1)
+    one = swap(add_up([down_terms[2], far_down]).astype(LOW), "slot", 2)
+    two = swap(down_terms[1], "slot", 1)
+    out = turn(out, "blk", 1)
     blocks[1] = seq_gather(moving)
     held = attend_back(in_order[0], None)
     phase.end(ahead, blocks[1], held)
 
-    moving = phase.take(ahead)
+    moving, far_a = phase.take(ahead, pair_a[3])
     ahead = turn(moving, "blk", 1)
+    far_a = swap(far_a, "slot", 1)
     blocks[2] = seq_gather(moving)
-    phase.end(ahead, blocks[2], one, two)
-
-    down_back = Exchange(row_pieces([down_terms[0], one, two]))
-    moving, blocks[2], down_back.pieces = phase.take(ahead, blocks[2], down_back.pieces)
+    phase.end(ahead, blocks[2], one, two, out)
+
+    moving, blocks[2], two_b, one_b, one, two = phase.take(
+        ahead, blocks[2], pair_b[2], add_up([pair_b[1], far_b]).astype(LOW), one, two
+    )
     blocks[3] = seq_gather(moving)
-    down_back.send(1, 3)
+    two_b, one_b = swap(two_b, "slot", 2), swap(one_b, "slot", 1)
     held = attend_back(in_order[1], held)
     all_resid, grad_k, grad_v = held
-    phase.end(held)
+    down_back = Exchange(row_pieces([down_terms[0], one, two]))
+    phase.end(held, far_a, down_back.pieces)
 
     grad_qkv, terms, gain_terms = [None] * blks, [None] * blks, []
 
     def finish(ks, grad_k):
-        got = []
         for some in calls(ks):
             outs, gain_term, parts = finish_blocks(
                 some, grad_q, grad_k, grad_v, cos_wide, sin_wide, full_attn, flat([token_blocks[k] for k in some])
             )
             gain_terms.append(gain_term)
-            got.append(parts)
-            for k, out in zip(some, outs):
-                grad_qkv[k] = out
-        return calls(ks), got
-
-    grad_k = phase.take(grad_k)
-    takers, parts = finish(in_turn[0], grad_k)
-    phase.end(parts, down_back.got)
-
-    parts, grad_k, down_back.pieces = phase.take(parts, grad_k, down_back.pieces)
-    reduce_calls(zip(takers, parts))
-    moving = turn(add_up(terms[1]).astype(LOW), "blk", 1)
-    down_back.send(2)
-    takers, parts = finish(in_turn[1], grad_k)
+            for k, out, part in zip(some, outs, parts):
+                grad_qkv[k], terms[k] = out, part
+
+    grad_k, down_back.pieces, outs_of[0] = phase.take(grad_k, down_back.pieces, outs_of[0])
+    down_back.send(1, 2, 3)
+    outs_of[0] = seq_reduce(outs_of[0])
+    finish(in_turn[0], grad_k)
+    finish(in_turn[1], grad_k)
+    phase.end(terms, one_b, two_b)
+
+    terms[1] = phase.take(terms[1])
+    terms[1] = seq_reduce(terms[1])
+    phase.end(terms[1])
+
+    moving, terms[2], grad_qkv, one_a, two_a, one_b, two_b = phase.take(
+        add_up(terms[1]).astype(LOW), terms[2], grad_qkv, add_up([pair_a[2], far_a]).astype(LOW), pair_a[1], one_b, two_b
+    )
+    moving = turn(moving, "blk", 1)
+    one_a, two_a = swap(one_a, "slot", 2), swap(two_a, "slot", 1)
+    terms[2] = seq_reduce(terms[2])
     last_terms = weight_terms((hidden_attn, grad_qkv), (all_resid, attended))
     gain_terms = jnp.concatenate([add_up(gain_terms), jnp.sum(gain_mlp_term, axis=0, keepdims=True)], axis=0)
-    phase.end(moving, terms[1], terms[2], parts, gain_terms, last_terms, down_back.got, sum_pair)
-
-    pair_back = Exchange(row_pieces([sum_pair]))
-    moving, parts, gain_terms, far, pair_back.pieces = phase.take(
-        add_up([moving, *terms[2]]).astype(LOW), parts, gain_terms, last_terms[3], pair_back.pieces
+    back_b = Exchange(row_pieces([pair_b[0], one_b, two_b]))
+    phase.end(moving, terms[2], last_terms, down_back.got, gain_terms, back_b.pieces)
+
+    moving, gain_terms, far, back_b.pieces, terms[3], one_a, two_a = phase.take(
+        add_up([moving, *terms[2]]).astype(LOW), gain_terms, last_terms[3], back_b.pieces, terms[3], one_a, two_a
     )
     moving = turn(moving, "blk", 1)
     far = swap(far, "slot", 2)
-    pair_back.send(1)
+    back_b.send(1, 3)
     bit = 1
     while bit < seqs:
         gain_terms = gain_terms + swap(gain_terms, "seq", bit)
         bit *= 2
-    reduce_calls(zip(takers, parts))
-    phase.end(moving, far, terms, gain_terms, pair_back.got)
+    terms[3] = seq_reduce(terms[3])
+    back_a = Exchange(row_pieces([pair_a[0], one_a, two_a]))
+    phase.end(moving, far, terms[3], back_b.got, back_a.pieces, gain_terms)
 
     gain_parts = jnp.split(gain_terms, GROUPS, axis=1)
-    moving, relay, near_term, gain_far, gain_two, pair_back.pieces = phase.take(
+    moving, relay, near_term, back_a.pieces, back_b.pieces, terms[0], gain_far, gain_two = phase.take(
         add_up([moving, *terms[3]]).astype(LOW), add_up([last_terms[1], far]).astype(LOW), last_terms[2],
-        gain_parts[3], gain_parts[1], pair_back.pieces,
+        back_a.pieces, back_b.pieces, terms[0], gain_parts[3], gain_parts[1],
     )
     gain_far, gain_two = swap(gain_far, "slot", 1), swap(gain_two, "slot", 1)
     moving = turn(moving, "blk", 1)
     one, two = swap(relay, "slot", 1), swap(near_term, "slot", 2)
-    pair_back.send(3)
-    phase.end(moving, one, two, pair_back.got, gain_far, gain_two)
+    back_b.send(2)
+    phase.end(moving, one, two, back_b.got, gain_far, gain_two)
 
     last_back = Exchange(row_pieces([last_terms[0], one, two]))
-    gain_relay, last_back.pieces, pair_back.pieces = phase.take(
-        gain_parts[2] + gain_far, last_back.pieces, pair_back.pieces
-    )
+    gain_relay, last_back.pieces, back_a.pieces, terms[0] = phase.take(
+        gain_parts[2] + gain_far, last_back.pieces, back_a.pieces, terms[0]
+    )
+    back_a.send(1, 2, 3)
+    terms[0] = seq_reduce(terms[0])
+    last_back.send(1, 2, 3)
     gain_one = swap(gain_relay, "slot", 2)
-    gain_sum = gain_parts[0] + gain_two + gain_one
-    pair_back.send(2)
-    last_back.send(1, 2, 3)
+    gain_sum = after(gain_parts[0] + gain_two + gain_one, back_a.got[1])
     gain_sums = [gain_sum] + [turn(gain_sum, "blk", k) for k in range(1, blks)]
 
+    layer_out = jnp.where(live_rows, resid + add_up([out, *outs_of[0]]), 0.0)
     grad_hidden_attn = add_up([moving, *terms[0]])
     normed_attn, inverse_attn = norm_rows(rows_f)
     grad_in_part, _ = norm_back(normed_attn, inverse_attn, grad_hidden_attn)
@@ -915,14 +907,14 @@
         slot_order(layer_out).astype(LOW)[None],
         slot_order(grad_resid + grad_in_part)[None],
         gain_grads[0] / gain_attn[:, 0],
-        join_owners(last_back, [(0, width)], gain_attn),
-        join_owners(last_back, [(width, width)], gain_attn),
-        join_owners(last_back, [(2 * width, width)], gain_attn),
-        join_owners(last_back, [(3 * width, width)], 1.0),
+        join_owners([last_back], [(0, width)], gain_attn),
+        join_owners([last_back], [(width, width)], gain_attn),
+        join_owners([last_back], [(2 * width, width)], gain_attn),
+        join_owners([last_back], [(3 * width, width)], 1.0),
         gain_grads[1] / gain_mlp[:, 0],
-        join_owners(pair_back, [(0, half), (hidden, half)], gain_mlp),
-        join_owners(pair_back, [(half, half), (hidden + half, half)], gain_mlp),
-        join_owners(down_back, [(0, hidden)], 1.0),
+        join_owners([back_a, back_b], [(0, half)], gain_mlp),
+        join_owners([back_a, back_b], [(half, half)], gain_mlp),
+        join_owners([down_back], [(0, hidden)], 1.0),
     )
 
 

time: 663 us -> 608 us (0.917)
  waiting for transfers between devices: 319 us -> 264 us
  starting transfers between devices: 78.2 us -> 104 us
  between operations: 16.5 us -> 3.1 us
    ppermute x39 -> x45, waiting for transfers between devices: 216 us -> 180 us  [turn(): lax.ppermute(value, axis, [(i, (i + by) % count) for i in range(count)])]
    pallas_call x3, Pallas kernels: 68.1 us -> 45.8 us  [the longest x2 42.9 us: mlp_blocks(): pl.pallas_call(partial(mlp_kernel, count), grid=(1,), in_specs=[vmem((siz...]
    ppermute x39 -> x45, starting transfers between devices: 49.9 us -> 69.1 us  [turn(): lax.ppermute(value, axis, [(i, (i + by) % count) for i in range(count)])]
    ppermute x42 -> x57, waiting for transfers between devices: 104 us -> 84.5 us  [swap(): return lax.ppermute(value, axis, [(i, i ^ mask) for i in range(count)])]
    pallas_call x2 -> x4, Pallas kernels: 18 us -> 34.8 us  [weight_terms(): pl.pallas_call(partial(weight_kernel, [len(rights) for _, rights in pairs...]
    ppermute x42 -> x57, starting transfers between devices: 28.3 us -> 34.5 us  [swap(): return lax.ppermute(value, axis, [(i, i ^ mask) for i in range(count)])]
  transfers between devices with their start and end apart: 82 -> 102, of which waited for: 35 -> 45; matrix products, arithmetic and copies ran while one was open for 9% -> 10% of each run, Pallas kernels for 25% -> 26%
where the time goes in v3:
time: 608 us; the launch traced here: 603 us
  waiting for transfers between devices  264 us (43%)
  Pallas kernels  160 us (26%)
  starting transfers between devices  104 us (17%)
  other arithmetic  47.6 us (8%)
  local copies, waits for them, and re-layouts  25.1 us (4%)
    ppermute x45, waiting for transfers between devices, turn(): lax.ppermute(value, axis, [(i, (i + by) % count) for i in range(count)])  180 us
    ppermute x57, waiting for transfers between devices, swap(): return lax.ppermute(value, axis, [(i, i ^ mask) for i in range(count)])  84.5 us
    ppermute x45, starting transfers between devices, turn(): lax.ppermute(value, axis, [(i, (i + by) % count) for i in range(count)])  69.1 us
    pallas_call x2, Pallas kernels, mlp_blocks(): pl.pallas_call(partial(mlp_kernel, count), grid=(1,), in_specs=[vmem((siz...  42.9 us
    pallas_call x4, Pallas kernels, weight_terms(): pl.pallas_call(partial(weight_kernel, [len(rights) for _, rights in pairs...  34.8 us
    ppermute x57, starting transfers between devices, swap(): return lax.ppermute(value, axis, [(i, i ^ mask) for i in range(count)])  34.5 us
    pallas_call x2, Pallas kernels, attend_back_blocks(): pl.pallas_call(partial(attend_back_kernel, (total, blks, seqs, size), ks,...  29.7 us
    pallas_call x2, Pallas kernels, attend_blocks(): pl.pallas_call(partial(attend_kernel, (total, blks, seqs, size), ks, widt...  24.7 us
  transfers between devices with their start and end apart: 102, of which 45 were waited for; matrix products, arithmetic and copies ran while one was open for 10% of the time, Pallas kernels for 26%

profile of v3, /device:TPU:0, one launch (start us, length us, event | category | flops | bytes accessed | tf_op | source)
XLA Modules:
  0.0 603.1 jit_solution(3839830973035633685)
XLA Ops:
  18.2 18.7 %collective-permute-done.2 = bf16[128,1024]{1,0:T(8,128)(2,1)} collective-permute-done((bf16[128,1024]{1,0:T(8,128)(2,1)}, bf16[128,1024]{1,0:T(8,128)(2,1)}, u32[]{:S(2)}, u32[]{:S(2)}) %collective-permute-start.2) | collective-permute-done | bytes 262176 | tf_op jit(solution)/shard_map/ppermute | solution.py:24
  37.9 4.5 collective-permute-done.3
  55.8 9.4 %collective-permute-done.5.refs_4_.refs_16_ = bf16[128,2048]{1,0:T(8,128)(2,1)} collective-permute-done((bf16[128,2048]{1,0:T(8,128)(2,1)}, bf16[128,2048]{1,0:T(8,128)(2,1)}, u32[]{:S(2)}, u32[]{:S(2)}) %collective-permute-start.5) | collective-permute-done | bytes 524320 | tf_op jit(solution)/shard_map/ppermute | solution.py:24
  65.2 9.7 %collective-permute-done.8 = bf16[128,2048]{1,0:T(8,128)(2,1)} collective-permute-done((bf16[128,2048]{1,0:T(8,128)(2,1)}, bf16[128,2048]{1,0:T(8,128)(2,1)}, u32[]{:S(2)}, u32[]{:S(2)}) %collective-permute-start.8) | collective-permute-done | bytes 524320 | tf_op jit(solution)/shard_map/ppermute | solution.py:24
  75.5 4.0 collective-permute-start.13
  79.5 12.8 %collective-permute-done.11.refs_6_.refs_14_ = bf16[128,2048]{1,0:T(8,128)(2,1)S(1)} collective-permute-done((bf16[128,2048]{1,0:T(8,128)(2,1)}, bf16[128,2048]{1,0:T(8,128)(2,1)S(1)}, u32[]{:S(2)}, u32[]{:S(2)}) %collective-permute-start.11) | collective-permute-done | bytes 524320 | tf_op jit(solution)/shard_map/ppermute | solution.py:24
  92.3 9.2 %collective-permute-done.13 = bf16[128,2048]{1,0:T(8,128)(2,1)S(1)} collective-permute-done((bf16[128,2048]{1,0:T(8,128)(2,1)}, bf16[128,2048]{1,0:T(8,128)(2,1)S(1)}, u32[]{:S(2)}, u32[]{:S(2)}) %collective-permute-start.13) | collective-permute-done | bytes 524320 | tf_op jit(solution)/shard_map/ppermute | solution.py:24
  108.4 10.9 %project_qkv.1 = (bf16[1024,2048]{1,0:T(8,128)(2,1)}, bf16[1024,256]{1,0:T(8,128)(2,1)}, bf16[1024,256]{1,0:T(8,128)(2,1)}, bf16[1024,256]{1,0:T(8,128)(2,1)}) custom-call(bf16[128,2048]{1,0:T(8,128)(2,1)} %copy-done.7, bf16[128,2048]{1,0:T(8,128)(2,1)} %copy-done.23, bf16[128,2048]{1,0:T(8,128)(2,1)} %collective-permute-done.1.refs_2_.refs_14_, ...), custom_call_target="tpu_custom_call" | custom-call | flops 1 | bytes 1 | tf_op jit(solution)/shard_map/project_qkv/pallas_call | solution.py:251
  119.3 12.4 %attend_blocks.2 = (bf16[256,256]{1,0:T(8,128)(2,1)}, bf16[256,256]{1,0:T(8,128)(2,1)}, f32[256,128]{1,0:T(8,128)}, f32[256,128]{1,0:T(8,128)}, bf16[128,2048]{1...) custom-call(s32[4]{0:T(128)} %copy-done.2, ...), custom_call_target="tpu_custom_call" | custom-call | flops 1 | bytes 1 | tf_op jit(solution)/shard_map/attend_blocks/pallas_call | solution.py:348
  138.4 12.4 %attend_blocks.3 = (bf16[256,256]{1,0:T(8,128)(2,1)}, bf16[256,256]{1,0:T(8,128)(2,1)}, f32[256,128]{1,0:T(8,128)}, f32[256,128]{1,0:T(8,128)}, bf16[128,2048]{1...) custom-call(s32[4]{0:T(128)} %copy-done.2, ...), custom_call_target="tpu_custom_call" | custom-call | flops 1 | bytes 1 | tf_op jit(solution)/shard_map/attend_blocks/pallas_call | solution.py:348
  150.8 3.5 collective-permute-done.17
  155.3 8.9 %collective-permute-done.21 = bf16[128,1024]{1,0:T(8,128)(2,1)S(1)} collective-permute-done((bf16[128,1024]{1,0:T(8,128)(2,1)S(1)}, bf16[128,1024]{1,0:T(8,128)(2,1)S(1)}, u32[]{:S(2)}, u32[]{:S(2)}) %collective-permute-start.21) | collective-permute-done | bytes 262176 | tf_op jit(solution)/shard_map/ppermute | solution.py:24
  166.8 16.7 %collective-permute-done.22 = bf16[128,2048]{1,0:T(8,128)(2,1)} collective-permute-done((bf16[128,2048]{1,0:T(8,128)(2,1)}, bf16[128,2048]{1,0:T(8,128)(2,1)}, u32[]{:S(2)}, u32[]{:S(2)}) %collective-permute-start.22) | collective-permute-done | bytes 524320 | tf_op jit(solution)/shard_map/ppermute | solution.py:24
  195.8 11.3 %collective-permute-done.29 = bf16[128,1024]{1,0:T(8,128)(2,1)S(1)} collective-permute-done((bf16[128,1024]{1,0:T(8,128)(2,1)S(1)}, bf16[128,1024]{1,0:T(8,128)(2,1)S(1)}, u32[]{:S(2)}, u32[]{:S(2)}) %collective-permute-start.29) | collective-permute-done | bytes 262176 | tf_op jit(solution)/shard_map/ppermute | solution.py:24
  210.4 8.0 %collective-permute-done.31.refs_7_ = bf16[512,1024]{1,0:T(8,128)(2,1)S(1)} collective-permute-done((bf16[512,1024]{1,0:T(8,128)(2,1)S(1)}, bf16[512,1024]{1,0:T(8,128)(2,1)S(1)}, u32[]{:S(2)}, u32[]{:S(2)}) %collective-permute-start.31) | collective-permute-done | bytes 1048608 | tf_op jit(solution)/shard_map/ppermute | solution.py:29
  220.5 11.3 %collective-permute-done.30.refs_2_ = bf16[128,4096]{1,0:T(8,128)(2,1)S(1)} collective-permute-done((bf16[128,4096]{1,0:T(8,128)(2,1)S(1)}, bf16[128,4096]{1,0:T(8,128)(2,1)S(1)}, u32[]{:S(2)}, u32[]{:S(2)}) %collective-permute-start.30) | collective-permute-done | bytes 1048608 | tf_op jit(solution)/shard_map/ppermute | solution.py:24
  232.1 10.1 %collective-permute-done.36.refs_13_ = bf16[512,1024]{1,0:T(8,128)(2,1)S(1)} collective-permute-done((bf16[512,1024]{1,0:T(8,128)(2,1)}, bf16[512,1024]{1,0:T(8,128)(2,1)S(1)}, u32[]{:S(2)}, u32[]{:S(2)}) %collective-permute-start.36) | collective-permute-done | bytes 1048608 | tf_op jit(solution)/shard_map/ppermute | solution.py:29
  245.0 10.7 %collective-permute-done.38.refs_15_ = bf16[512,512]{1,0:T(8,128)(2,1)S(1)} collective-permute-done((bf16[512,512]{1,0:T(8,128)(2,1)S(1)}, bf16[512,512]{1,0:T(8,128)(2,1)S(1)}, u32[]{:S(2)}, u32[]{:S(2)}) %collective-permute-start.38) | collective-permute-done | bytes 524320 | tf_op jit(solution)/shard_map/ppermute | solution.py:29
  258.3 21.5 %mlp_blocks.2 = (bf16[1024,2048]{1,0:T(8,128)(2,1)}, bf16[1024,2048]{1,0:T(8,128)(2,1)}, bf16[1024,1024]{1,0:T(8,128)(2,1)}, bf16[1024,1024]{1,0:T(8,128)(2,1)},...) custom-call(bf16[128,4096]{1,0:T(8,128)(2,1)} %copy-done.20, ...), custom_call_target="tpu_custom_call" | custom-call | flops 1 | bytes 1 | tf_op jit(solution)/shard_map/mlp_blocks/pallas_call | solution.py:407
  279.8 3.4 collective-permute-done.40.refs_2_
  289.3 21.4 %mlp_blocks.3 = (bf16[1024,2048]{1,0:T(8,128)(2,1)}, bf16[1024,2048]{1,0:T(8,128)(2,1)}, bf16[1024,1024]{1,0:T(8,128)(2,1)}, bf16[1024,1024]{1,0:T(8,128)(2,1)},...) custom-call(bf16[128,4096]{1,0:T(8,128)(2,1)} %collective-permute-do, ...), custom_call_target="tpu_custom_call", output_to_operand_aliasing={{0}: (17, {}), {1}: (18, {}), {2}: (19, {}), {3}: (20, {}),... | custom-call | flops 1 | bytes 1 | tf_op jit(solution)/shard_map/mlp_blocks/pallas_call | solution.py:407
  310.7 3.0 collective-permute-done.43
  321.6 8.4 %weight_terms.5 = (bf16[512,1024]{1,0:T(8,128)(2,1)}, bf16[512,1024]{1,0:T(8,128)(2,1)}, bf16[512,1024]{1,0:T(8,128)(2,1)}, bf16[512,1024]{1,0:T(8,128)(2,1)}) custom-call(bf16[1024,2048]{1,0:T(8,128)(2,1)} %get-tuple-element.330.refs_0_, bf16[1024,1024]{1,0:T(8,128)(2,1)} %get-tuple-element.342.refs_1_), custom_call_target="tpu_custom_call" | custom-call | flops 1 | bytes 1 | tf_op jit(solution)/shard_map/weight_terms/pallas_call | solution.py:597
  329.9 8.5 %weight_terms.4 = (bf16[512,1024]{1,0:T(8,128)(2,1)}, bf16[512,1024]{1,0:T(8,128)(2,1)}, bf16[512,1024]{1,0:T(8,128)(2,1)}, bf16[512,1024]{1,0:T(8,128)(2,1)}) custom-call(bf16[1024,2048]{1,0:T(8,128)(2,1)} %get-tuple-element.331.refs_0_, bf16[1024,1024]{1,0:T(8,128)(2,1)} %get-tuple-element.340.refs_1_), custom_call_target="tpu_custom_call" | custom-call | flops 1 | bytes 1 | tf_op jit(solution)/shard_map/weight_terms/pallas_call | solution.py:597
  338.4 5.9 collective-permute-done.48
  346.8 8.5 %weight_terms.6 = (bf16[512,1024]{1,0:T(8,128)(2,1)}, bf16[512,1024]{1,0:T(8,128)(2,1)}, bf16[512,1024]{1,0:T(8,128)(2,1)}, bf16[512,1024]{1,0:T(8,128)(2,1)}) custom-call(bf16[1024,2048]{1,0:T(8,128)(2,1)} %get-tuple-element.330.refs_0_, bf16[1024,1024]{1,0:T(8,128)(2,1)} %get-tuple-element.362.refs_1_), custom_call_target="tpu_custom_call" | custom-call | flops 1 | bytes 1 | tf_op jit(solution)/shard_map/weight_terms/pallas_call | solution.py:597
  357.4 5.1 collective-permute-done.52
  368.2 12.5 %collective-permute-done.56 = bf16[512,1024]{1,0:T(8,128)(2,1)S(1)} collective-permute-done((bf16[512,1024]{1,0:T(8,128)(2,1)}, bf16[512,1024]{1,0:T(8,128)(2,1)S(1)}, u32[]{:S(2)}, u32[]{:S(2)}) %collective-permute-start.56) | collective-permute-done | bytes 1048608 | tf_op jit(solution)/shard_map/ppermute | solution.py:29
  386.2 14.5 %attend_back_blocks.2 = (bf16[1024,2048]{1,0:T(8,128)(2,1)}, f32[1024,256]{1,0:T(8,128)}, f32[1024,256]{1,0:T(8,128)}, bf16[256,256]{1,0:T(8,128)(2,1)}, bf16[256,256]{1,0:T(8,128)(2,1)}) custom-call(s32[4]{0:T(128)} %copy-done.2, bf16[1024,256]{1,0:T(8,128)(2,1)} %get-tuple-element.277.refs_0_.refs_1_, ...), custom_call_target="tpu_custom_call" | custom-call | flops 1 | bytes 1 | tf_op jit(solution)/shard_map/attend_back_blocks/pallas_call | solution.py:488
  400.7 4.2 collective-permute-start.62
  404.9 5.2 collective-permute-done.59
  414.0 6.9 %collective-permute-done.62.refs_18_ = bf16[128,2048]{1,0:T(8,128)(2,1)} collective-permute-done((bf16[128,2048]{1,0:T(8,128)(2,1)S(1)}, bf16[128,2048]{1,0:T(8,128)(2,1)}, u32[]{:S(2)}, u32[]{:S(2)}) %collective-permute-start.62) | collective-permute-done | bytes 524320 | tf_op jit(solution)/shard_map/ppermute | solution.py:24
  427.9 15.2 %attend_back_blocks.3 = (bf16[1024,2048]{1,0:T(8,128)(2,1)}, f32[1024,256]{1,0:T(8,128)}, f32[1024,256]{1,0:T(8,128)}, bf16[256,256]{1,0:T(8,128)(2,1)}, bf16[256,256]{1,0:T(8,128)(2,1)}) custom-call(s32[4]{0:T(128)} %copy-done.2, ...), custom_call_target="tpu_custom_call", output_to_operand_aliasing={{0}: (21, {}), {1}: (22, {}), {2}: (23, {})} | custom-call | flops 1 | bytes 1 | tf_op jit(solution)/shard_map/attend_back_blocks/pallas_call | solution.py:488
  447.3 6.8 %finish_blocks.3 = (bf16[256,768]{1,0:T(8,128)(2,1)}, bf16[256,768]{1,0:T(8,128)(2,1)}, f32[1,2048]{1,0:T(1,128)}, bf16[128,2048]{1,0:T(8,128)(2,1)}, bf16[128,2...) custom-call(bf16[256,256]{1,0:T(8,128)(2,1)} %get-tuple-element.411.refs_0_, ...), custom_call_target="tpu_custom_call" | custom-call | flops 1 | bytes 1 | tf_op jit(solution)/shard_map/finish_blocks/pallas_call | solution.py:558
  454.1 6.9 %finish_blocks.2 = (bf16[256,768]{1,0:T(8,128)(2,1)}, bf16[256,768]{1,0:T(8,128)(2,1)}, f32[1,2048]{1,0:T(1,128)}, bf16[128,2048]{1,0:T(8,128)(2,1)}, bf16[128,2...) custom-call(bf16[256,256]{1,0:T(8,128)(2,1)} %get-tuple-element.406.refs_0_, ...), custom_call_target="tpu_custom_call" | custom-call | flops 1 | bytes 1 | tf_op jit(solution)/shard_map/finish_blocks/pallas_call | solution.py:558
  469.3 2.9 add_convert_fusion.24
  472.2 9.5 %weight_terms.7 = (bf16[512,1024]{1,0:T(8,128)(2,1)}, bf16[512,1024]{1,0:T(8,128)(2,1)}, bf16[512,1024]{1,0:T(8,128)(2,1)}, bf16[512,1024]{1,0:T(8,128)(2,1)}) custom-call(bf16[1024,2048]{1,0:T(8,128)(2,1)} %get-tuple-element.432.refs_0_, bf16[256,768]{1,0:T(8,128)(2,1)} %get-tuple-element.433.refs_1_, bf16[256,768]{1,0:T(8,128)(2,1)} %get-tuple-element.434.refs_2_, ...), custom_call_target="tpu_custom_call" | custom-call | flops 1 | bytes 1 | tf_op jit(solution)/shard_map/weight_terms/pallas_call | solution.py:597
  483.5 7.3 %collective-permute-done.74 = bf16[512,1024]{1,0:T(8,128)(2,1)S(1)} collective-permute-done((bf16[512,1024]{1,0:T(8,128)(2,1)}, bf16[512,1024]{1,0:T(8,128)(2,1)S(1)}, u32[]{:S(2)}, u32[]{:S(2)}) %collective-permute-start.74) | collective-permute-done | bytes 1048608 | tf_op jit(solution)/shard_map/ppermute | solution.py:29
  492.6 5.4 collective-permute-start.79
  502.0 4.0 collective-permute-start.84
  506.1 4.2 collective-permute-done.79
  510.5 5.6 collective-permute-done.81
  516.6 4.2 collective-permute-done.84
  530.0 15.4 %collective-permute-done.86 = f32[2,512]{1,0:T(2,128)S(1)} collective-permute-done((f32[2,512]{1,0:T(2,128)S(1)}, f32[2,512]{1,0:T(2,128)S(1)}, u32[]{:S(2)}, u32[]{:S(2)}) %collective-permute-start.86) | collective-permute-done | bytes 4128 | tf_op jit(solution)/shard_map/ppermute | solution.py:29
  562.6 19.5 %collective-permute-done.100 = bf16[128,1024]{1,0:T(8,128)(2,1)S(1)} collective-permute-done((bf16[128,1024]{1,0:T(8,128)(2,1)S(1)}, bf16[128,1024]{1,0:T(8,128)(2,1)S(1)}, u32[]{:S(2)}, u32[]{:S(2)}) %collective-permute-start.100) | collective-permute-done | bytes 262176 | tf_op jit(solution)/shard_map/ppermute | solution.py:24
  582.3 7.0 %collective-permute-start.94 = (f32[2,512]{1,0:T(2,128)S(1)}, f32[2,512]{1,0:T(2,128)S(1)}, u32[]{:S(2)}, u32[]{:S(2)}) collective-permute-start(f32[2,512]{1,0:T(2,128)S(1)} %fusion.11), channel_id=1, source_target_pairs={{0,1},{1,2},{2,3},{3,0},{4,5},{5,6},{6,7},{7,4},{8,9},{9,10},{10,1... | collective-permute-start | bytes 12296 | tf_op jit(solution)/shard_map/ppermute | solution.py:24
  589.6 3.7 collective-permute-start.95
  594.3 4.1 collective-permute-start.96
  (458 shorter events, 164.9 us)
Async XLA Ops:
  2.1 42.3 %collective-permute-start = (bf16[128,2048]{1,0:T(8,128)(2,1)S(1)}, bf16[128,2048]{1,0:T(8,128)(2,1)S(1)}, u32[]{:S(2)}, u32[]{:S(2)}) collective-permute-start(bf16[128,2048]{1,0:T(8,128)(2,1)S(1)} %get-tuple-element.484.refs_0_.refs_16_), channel_id=1, source_target_pairs={{0,4},{4,0},{1,5},{5,1},{2,6},{6,2},{3,7},{7,3},{8,12},{12,8},{9,1... | collective-permute-start | bytes 1572872 | tf_op jit(solution)/shard_map/ppermute | solution.py:29
  2.6 42.6 %collective-permute-start.1 = (bf16[128,2048]{1,0:T(8,128)(2,1)S(1)}, bf16[128,2048]{1,0:T(8,128)(2,1)}, u32[]{:S(2)}, u32[]{:S(2)}) collective-permute-start(bf16[128,2048]{1,0:T(8,128)(2,1)S(1)} %get-tuple-element.484.refs_0_.refs_16_), channel_id=1, source_target_pairs={{0,1},{1,2},{2,3},{3,0},{4,5},{5,6},{6,7},{7,4},{8,9},{9,10},{10,1... | collective-permute-start | bytes 1572872 | tf_op jit(solution)/shard_map/ppermute | solution.py:24
  7.6 35.8 %collective-permute-start.4 = (bf16[128,1024]{1,0:T(8,128)(2,1)}, bf16[128,1024]{1,0:T(8,128)(2,1)}, u32[]{:S(2)}, u32[]{:S(2)}) collective-permute-start(bf16[128,1024]{1,0:T(8,128)(2,1)} %pad_maximum_fusion.10), channel_id=1, source_target_pairs={{0,3},{1,0},{2,1},{3,2},{4,7},{5,4},{6,5},{7,6},{8,11},{9,8},{10,9... | collective-permute-start | bytes 786440 | tf_op jit(solution)/shard_map/ppermute | solution.py:24
  10.5 31.9 %collective-permute-start.3 = (bf16[128,1024]{1,0:T(8,128)(2,1)}, bf16[128,1024]{1,0:T(8,128)(2,1)}, u32[]{:S(2)}, u32[]{:S(2)}) collective-permute-start(bf16[128,1024]{1,0:T(8,128)(2,1)} %pad_maximum_fusion.9), channel_id=1, source_target_pairs={{0,2},{1,3},{2,0},{3,1},{4,6},{5,7},{6,4},{7,5},{8,10},{9,11},{10,... | collective-permute-start | bytes 786440 | tf_op jit(solution)/shard_map/ppermute | solution.py:24
  12.1 24.8 %collective-permute-start.2 = (bf16[128,1024]{1,0:T(8,128)(2,1)}, bf16[128,1024]{1,0:T(8,128)(2,1)}, u32[]{:S(2)}, u32[]{:S(2)}) collective-permute-start(bf16[128,1024]{1,0:T(8,128)(2,1)} %pad_maximum_fusion.8), channel_id=1, source_target_pairs={{0,1},{1,2},{2,3},{3,0},{4,5},{5,6},{6,7},{7,4},{8,9},{9,10},{10,1... | collective-permute-start | bytes 786440 | tf_op jit(solution)/shard_map/ppermute | solution.py:24
  45.2 29.7 %collective-permute-start.6 = (bf16[512,1024]{1,0:T(8,128)(2,1)S(1)}, bf16[512,1024]{1,0:T(8,128)(2,1)S(1)}, u32[]{:S(2)}, u32[]{:S(2)}) collective-permute-start(bf16[512,1024]{1,0:T(8,128)(2,1)S(1)} %constant_dynamic-update-slice_fusion.8.refs_8_.refs_4_.refs_12_.refs_10_), channel_id=1, source_target_pairs={{0,8},{8,0},{16,24},{24,16},{1,9},{9,1},{17,25},{25,17},{2,10},{10... | collective-permute-start | bytes 3145736 | tf_op jit(solution)/shard_map/ppermute | solution.py:29
  46.7 28.2 %collective-permute-start.7 = (bf16[512,1024]{1,0:T(8,128)(2,1)S(1)}, bf16[512,1024]{1,0:T(8,128)(2,1)S(1)}, u32[]{:S(2)}, u32[]{:S(2)}) collective-permute-start(bf16[512,1024]{1,0:T(8,128)(2,1)S(1)} %constant_dynamic-update-slice_fusion.8.refs_8_.refs_4_.refs_12_.refs_10_), channel_id=1, source_target_pairs={{0,16},{8,24},{16,0},{24,8},{1,17},{9,25},{17,1},{25,9},{2,18},{10... | collective-permute-start | bytes 3145736 | tf_op jit(solution)/shard_map/ppermute | solution.py:29
  48.3 26.7 %collective-permute-start.8 = (bf16[128,2048]{1,0:T(8,128)(2,1)}, bf16[128,2048]{1,0:T(8,128)(2,1)}, u32[]{:S(2)}, u32[]{:S(2)}) collective-permute-start(bf16[128,2048]{1,0:T(8,128)(2,1)} %pad_maximum_fusion.3), channel_id=1, source_target_pairs={{0,1},{1,2},{2,3},{3,0},{4,5},{5,6},{6,7},{7,4},{8,9},{9,10},{10,1... | collective-permute-start | bytes 1572872 | tf_op jit(solution)/shard_map/ppermute | solution.py:24
  74.9 26.5 %collective-permute-start.12 = (bf16[512,1024]{1,0:T(8,128)(2,1)S(1)}, bf16[512,1024]{1,0:T(8,128)(2,1)S(1)}, u32[]{:S(2)}, u32[]{:S(2)}) collective-permute-start(bf16[512,1024]{1,0:T(8,128)(2,1)S(1)} %collective-permute-done.6.refs_9_.refs_5_.refs_13_.refs_11_), channel_id=1, source_target_pairs={{0,16},{8,24},{16,0},{24,8},{1,17},{9,25},{17,1},{25,9},{2,18},{10... | collective-permute-start | bytes 3145736 | tf_op jit(solution)/shard_map/ppermute | solution.py:29
  75.5 25.9 %collective-permute-start.13 = (bf16[128,2048]{1,0:T(8,128)(2,1)}, bf16[128,2048]{1,0:T(8,128)(2,1)S(1)}, u32[]{:S(2)}, u32[]{:S(2)}) collective-permute-start(bf16[128,2048]{1,0:T(8,128)(2,1)} %pad_maximum_fusion.5), channel_id=1, source_target_pairs={{0,3},{1,0},{2,1},{3,2},{4,7},{5,4},{6,5},{7,6},{8,11},{9,8},{10,9... | collective-permute-start | bytes 1572872 | tf_op jit(solution)/shard_map/ppermute | solution.py:24
  102.8 29.0 %collective-permute-start.15 = (bf16[128,2048]{1,0:T(8,128)(2,1)}, bf16[128,2048]{1,0:T(8,128)(2,1)}, u32[]{:S(2)}, u32[]{:S(2)}) collective-permute-start(bf16[128,2048]{1,0:T(8,128)(2,1)} %pad_maximum_fusion.4), channel_id=1, source_target_pairs={{0,2},{1,3},{2,0},{3,1},{4,6},{5,7},{6,4},{7,5},{8,10},{9,11},{10,... | collective-permute-start | bytes 1572872 | tf_op jit(solution)/shard_map/ppermute | solution.py:24
  135.3 28.9 %collective-permute-start.19 = (bf16[512,1024]{1,0:T(8,128)(2,1)S(1)}, bf16[512,1024]{1,0:T(8,128)(2,1)S(1)}, u32[]{:S(2)}, u32[]{:S(2)}) collective-permute-start(bf16[512,1024]{1,0:T(8,128)(2,1)S(1)} %get-tuple-element.508.refs_4_), channel_id=1, source_target_pairs={{0,8},{8,0},{16,24},{24,16},{1,9},{9,1},{17,25},{25,17},{2,10},{10... | collective-permute-start | bytes 3145736 | tf_op jit(solution)/shard_map/ppermute | solution.py:29
  135.9 28.3 %collective-permute-start.20 = (bf16[512,1024]{1,0:T(8,128)(2,1)S(1)}, bf16[512,1024]{1,0:T(8,128)(2,1)S(1)}, u32[]{:S(2)}, u32[]{:S(2)}) collective-permute-start(bf16[512,1024]{1,0:T(8,128)(2,1)S(1)} %get-tuple-element.508.refs_4_), channel_id=1, source_target_pairs={{0,16},{8,24},{16,0},{24,8},{1,17},{9,25},{17,1},{25,9},{2,18},{10... | collective-permute-start | bytes 3145736 | tf_op jit(solution)/shard_map/ppermute | solution.py:29
  137.9 26.3 %collective-permute-start.21 = (bf16[128,1024]{1,0:T(8,128)(2,1)S(1)}, bf16[128,1024]{1,0:T(8,128)(2,1)S(1)}, u32[]{:S(2)}, u32[]{:S(2)}) collective-permute-start(bf16[128,1024]{1,0:T(8,128)(2,1)S(1)} %copy-done.77), channel_id=1, source_target_pairs={{0,2},{1,3},{2,0},{3,1},{4,6},{5,7},{6,4},{7,5},{8,10},{9,11},{10,... | collective-permute-start | bytes 786440 | tf_op jit(solution)/shard_map/ppermute | solution.py:24
  164.2 24.8 %collective-permute-start.24 = (bf16[512,1024]{1,0:T(8,128)(2,1)S(1)}, bf16[512,1024]{1,0:T(8,128)(2,1)}, u32[]{:S(2)}, u32[]{:S(2)}) collective-permute-start(bf16[512,1024]{1,0:T(8,128)(2,1)S(1)} %get-tuple-element.285.refs_8_), channel_id=1, source_target_pairs={{0,16},{8,24},{16,0},{24,8},{1,17},{9,25},{17,1},{25,9},{2,18},{10... | collective-permute-start | bytes 3145736 | tf_op jit(solution)/shard_map/ppermute | solution.py:29
  164.8 24.3 %collective-permute-start.25 = (bf16[512,1024]{1,0:T(8,128)(2,1)S(1)}, bf16[512,1024]{1,0:T(8,128)(2,1)S(1)}, u32[]{:S(2)}, u32[]{:S(2)}) collective-permute-start(bf16[512,1024]{1,0:T(8,128)(2,1)S(1)} %get-tuple-element.285.refs_8_), channel_id=1, source_target_pairs={{0,8},{8,0},{16,24},{24,16},{1,9},{9,1},{17,25},{25,17},{2,10},{10... | collective-permute-start | bytes 3145736 | tf_op jit(solution)/shard_map/ppermute | solution.py:29
  192.8 25.6 %collective-permute-start.31 = (bf16[512,1024]{1,0:T(8,128)(2,1)S(1)}, bf16[512,1024]{1,0:T(8,128)(2,1)S(1)}, u32[]{:S(2)}, u32[]{:S(2)}) collective-permute-start(bf16[512,1024]{1,0:T(8,128)(2,1)S(1)} %copy-done.15), channel_id=1, source_target_pairs={{0,16},{8,24},{16,0},{24,8},{1,17},{9,25},{17,1},{25,9},{2,18},{10... | collective-permute-start | bytes 3145736 | tf_op jit(solution)/shard_map/ppermute | solution.py:29
  194.3 26.2 %collective-permute-start.32 = (bf16[512,1024]{1,0:T(8,128)(2,1)}, bf16[512,1024]{1,0:T(8,128)(2,1)S(1)}, u32[]{:S(2)}, u32[]{:S(2)}) collective-permute-start(bf16[512,1024]{1,0:T(8,128)(2,1)} %collective-permute-done.24.refs_10_), channel_id=1, source_target_pairs={{0,8},{8,0},{16,24},{24,16},{1,9},{9,1},{17,25},{25,17},{2,10},{10... | collective-permute-start | bytes 3145736 | tf_op jit(solution)/shard_map/ppermute | solution.py:29
  208.9 33.4 %collective-permute-start.36 = (bf16[512,1024]{1,0:T(8,128)(2,1)}, bf16[512,1024]{1,0:T(8,128)(2,1)S(1)}, u32[]{:S(2)}, u32[]{:S(2)}) collective-permute-start(bf16[512,1024]{1,0:T(8,128)(2,1)} %constant_dynamic-update-slice_fusion.refs_12_), channel_id=1, source_target_pairs={{0,8},{8,0},{16,24},{24,16},{1,9},{9,1},{17,25},{25,17},{2,10},{10... | collective-permute-start | bytes 3145736 | tf_op jit(solution)/shard_map/ppermute | solution.py:29
  218.4 25.0 %collective-permute-start.37 = (bf16[512,1024]{1,0:T(8,128)(2,1)}, bf16[512,1024]{1,0:T(8,128)(2,1)S(1)}, u32[]{:S(2)}, u32[]{:S(2)}) collective-permute-start(bf16[512,1024]{1,0:T(8,128)(2,1)} %constant_dynamic-update-slice_fusion.refs_12_), channel_id=1, source_target_pairs={{0,16},{8,24},{16,0},{24,8},{1,17},{9,25},{17,1},{25,9},{2,18},{10... | collective-permute-start | bytes 3145736 | tf_op jit(solution)/shard_map/ppermute | solution.py:29
  231.9 25.4 %collective-permute-start.34 = (bf16[128,4096]{1,0:T(8,128)(2,1)S(1)}, bf16[128,4096]{1,0:T(8,128)(2,1)}, u32[]{:S(2)}, u32[]{:S(2)}) collective-permute-start(bf16[128,4096]{1,0:T(8,128)(2,1)S(1)} %collective-permute-done.30.refs_2_), channel_id=1, source_target_pairs={{0,1},{1,2},{2,3},{3,0},{4,5},{5,6},{6,7},{7,4},{8,9},{9,10},{10,1... | collective-permute-start | bytes 3145736 | tf_op jit(solution)/shard_map/ppermute | solution.py:24
  232.1 25.2 %collective-permute-start.35 = (bf16[128,4096]{1,0:T(8,128)(2,1)S(1)}, bf16[128,4096]{1,0:T(8,128)(2,1)S(1)}, u32[]{:S(2)}, u32[]{:S(2)}) collective-permute-start(bf16[128,4096]{1,0:T(8,128)(2,1)S(1)} %collective-permute-done.30.refs_2_), channel_id=1, source_target_pairs={{0,4},{4,0},{1,5},{5,1},{2,6},{6,2},{3,7},{7,3},{8,12},{12,8},{9,1... | collective-permute-start | bytes 3145736 | tf_op jit(solution)/shard_map/ppermute | solution.py:29
  257.3 25.9 %collective-permute-start.40 = (bf16[128,4096]{1,0:T(8,128)(2,1)}, bf16[128,4096]{1,0:T(8,128)(2,1)}, u32[]{:S(2)}, u32[]{:S(2)}) collective-permute-start(bf16[128,4096]{1,0:T(8,128)(2,1)} %collective-permute-done.34.refs_0_), channel_id=1, source_target_pairs={{0,1},{1,2},{2,3},{3,0},{4,5},{5,6},{6,7},{7,4},{8,9},{9,10},{10,1... | collective-permute-start | bytes 3145736 | tf_op jit(solution)/shard_map/ppermute | solution.py:24
  258.3 25.0 %collective-permute-start.41 = (bf16[128,4096]{1,0:T(8,128)(2,1)}, bf16[128,4096]{1,0:T(8,128)(2,1)}, u32[]{:S(2)}, u32[]{:S(2)}) collective-permute-start(bf16[128,4096]{1,0:T(8,128)(2,1)} %collective-permute-done.34.refs_0_), channel_id=1, source_target_pairs={{0,4},{4,0},{1,5},{5,1},{2,6},{6,2},{3,7},{7,3},{8,12},{12,8},{9,1... | collective-permute-start | bytes 3145736 | tf_op jit(solution)/shard_map/ppermute | solution.py:29
  286.6 24.1 %collective-permute-start.46 = (bf16[128,2048]{1,0:T(8,128)(2,1)S(1)}, bf16[128,2048]{1,0:T(8,128)(2,1)}, u32[]{:S(2)}, u32[]{:S(2)}) collective-permute-start(bf16[128,2048]{1,0:T(8,128)(2,1)S(1)} %add_convert_fusion.11), channel_id=1, source_target_pairs={{0,1},{1,2},{2,3},{3,0},{4,5},{5,6},{6,7},{7,4},{8,9},{9,10},{10,1... | collective-permute-start | bytes 1572872 | tf_op jit(solution)/shard_map/ppermute | solution.py:24
  287.8 25.9 %collective-permute-start.43 = (bf16[128,2048]{1,0:T(8,128)(2,1)S(1)}, bf16[128,2048]{1,0:T(8,128)(2,1)}, u32[]{:S(2)}, u32[]{:S(2)}) collective-permute-start(bf16[128,2048]{1,0:T(8,128)(2,1)S(1)} %add_convert_fusion.12), channel_id=1, source_target_pairs={{0,1},{1,2},{2,3},{3,0},{4,5},{5,6},{6,7},{7,4},{8,9},{9,10},{10,1... | collective-permute-start | bytes 1572872 | tf_op jit(solution)/shard_map/ppermute | solution.py:24
  319.4 24.9 %collective-permute-start.48 = (bf16[128,2048]{1,0:T(8,128)(2,1)}, bf16[128,2048]{1,0:T(8,128)(2,1)S(1)}, u32[]{:S(2)}, u32[]{:S(2)}) collective-permute-start(bf16[128,2048]{1,0:T(8,128)(2,1)} %add_convert_fusion.10), channel_id=1, source_target_pairs={{0,1},{1,2},{2,3},{3,0},{4,5},{5,6},{6,7},{7,4},{8,9},{9,10},{10,1... | collective-permute-start | bytes 1572872 | tf_op jit(solution)/shard_map/ppermute | solution.py:24
  355.2 25.4 %collective-permute-start.56 = (bf16[512,1024]{1,0:T(8,128)(2,1)}, bf16[512,1024]{1,0:T(8,128)(2,1)S(1)}, u32[]{:S(2)}, u32[]{:S(2)}) collective-permute-start(bf16[512,1024]{1,0:T(8,128)(2,1)} %get-tuple-element.368), channel_id=1, source_target_pairs={{0,8},{8,0},{16,24},{24,16},{1,9},{9,1},{17,25},{25,17},{2,10},{10... | collective-permute-start | bytes 3145736 | tf_op jit(solution)/shard_map/ppermute | solution.py:29
  356.7 25.1 %collective-permute-start.58 = (bf16[512,1024]{1,0:T(8,128)(2,1)}, bf16[512,1024]{1,0:T(8,128)(2,1)S(1)}, u32[]{:S(2)}, u32[]{:S(2)}) collective-permute-start(bf16[512,1024]{1,0:T(8,128)(2,1)} %get-tuple-element.372), channel_id=1, source_target_pairs={{0,16},{8,24},{16,0},{24,8},{1,17},{9,25},{17,1},{25,9},{2,18},{10... | collective-permute-start | bytes 3145736 | tf_op jit(solution)/shard_map/ppermute | solution.py:29
  383.7 30.3 %collective-permute-start.64 = (bf16[512,1024]{1,0:T(8,128)(2,1)}, bf16[512,1024]{1,0:T(8,128)(2,1)}, u32[]{:S(2)}, u32[]{:S(2)}) collective-permute-start(bf16[512,1024]{1,0:T(8,128)(2,1)} %add_convert_fusion.2), channel_id=1, source_target_pairs={{0,16},{8,24},{16,0},{24,8},{1,17},{9,25},{17,1},{25,9},{2,18},{10... | collective-permute-start | bytes 3145736 | tf_op jit(solution)/shard_map/ppermute | solution.py:29
  384.3 37.4 %collective-permute-start.65 = (bf16[512,1024]{1,0:T(8,128)(2,1)}, bf16[512,1024]{1,0:T(8,128)(2,1)}, u32[]{:S(2)}, u32[]{:S(2)}) collective-permute-start(bf16[512,1024]{1,0:T(8,128)(2,1)} %get-tuple-element.391), channel_id=1, source_target_pairs={{0,8},{8,0},{16,24},{24,16},{1,9},{9,1},{17,25},{25,17},{2,10},{10... | collective-permute-start | bytes 3145736 | tf_op jit(solution)/shard_map/ppermute | solution.py:29
  385.3 24.8 %collective-permute-start.59 = (bf16[128,2048]{1,0:T(8,128)(2,1)}, bf16[128,2048]{1,0:T(8,128)(2,1)}, u32[]{:S(2)}, u32[]{:S(2)}) collective-permute-start(bf16[128,2048]{1,0:T(8,128)(2,1)} %add_convert_fusion.7), channel_id=1, source_target_pairs={{0,1},{1,2},{2,3},{3,0},{4,5},{5,6},{6,7},{7,4},{8,9},{9,10},{10,1... | collective-permute-start | bytes 1572872 | tf_op jit(solution)/shard_map/ppermute | solution.py:24
  410.1 32.9 %collective-permute-start.67 = (bf16[512,1024]{1,0:T(8,128)(2,1)}, bf16[512,1024]{1,0:T(8,128)(2,1)S(1)}, u32[]{:S(2)}, u32[]{:S(2)}) collective-permute-start(bf16[512,1024]{1,0:T(8,128)(2,1)} %get-tuple-element.403), channel_id=1, source_target_pairs={{0,8},{8,0},{16,24},{24,16},{1,9},{9,1},{17,25},{25,17},{2,10},{10... | collective-permute-start | bytes 3145736 | tf_op jit(solution)/shard_map/ppermute | solution.py:29
  421.7 39.3 %collective-permute-start.69 = (bf16[512,1024]{1,0:T(8,128)(2,1)}, bf16[512,1024]{1,0:T(8,128)(2,1)}, u32[]{:S(2)}, u32[]{:S(2)}) collective-permute-start(bf16[512,1024]{1,0:T(8,128)(2,1)} %add_convert_fusion.3), channel_id=1, source_target_pairs={{0,8},{8,0},{16,24},{24,16},{1,9},{9,1},{17,25},{25,17},{2,10},{10... | collective-permute-start | bytes 3145736 | tf_op jit(solution)/shard_map/ppermute | solution.py:29
  422.7 38.3 %collective-permute-start.70 = (bf16[512,1024]{1,0:T(8,128)(2,1)}, bf16[512,1024]{1,0:T(8,128)(2,1)}, u32[]{:S(2)}, u32[]{:S(2)}) collective-permute-start(bf16[512,1024]{1,0:T(8,128)(2,1)} %get-tuple-element.420), channel_id=1, source_target_pairs={{0,16},{8,24},{16,0},{24,8},{1,17},{9,25},{17,1},{25,9},{2,18},{10... | collective-permute-start | bytes 3145736 | tf_op jit(solution)/shard_map/ppermute | solution.py:29
  444.9 23.5 %collective-permute-start.78 = (bf16[128,1024]{1,0:T(8,128)(2,1)S(1)}, bf16[128,1024]{1,0:T(8,128)(2,1)S(1)}, u32[]{:S(2)}, u32[]{:S(2)}) collective-permute-start(bf16[128,1024]{1,0:T(8,128)(2,1)S(1)} %get-tuple-element.447), channel_id=1, source_target_pairs={{0,3},{1,0},{2,1},{3,2},{4,7},{5,4},{6,5},{7,6},{8,11},{9,8},{10,9... | collective-permute-start | bytes 786440 | tf_op jit(solution)/shard_map/ppermute | solution.py:24
  465.2 25.6 %collective-permute-start.74 = (bf16[512,1024]{1,0:T(8,128)(2,1)}, bf16[512,1024]{1,0:T(8,128)(2,1)S(1)}, u32[]{:S(2)}, u32[]{:S(2)}) collective-permute-start(bf16[512,1024]{1,0:T(8,128)(2,1)} %add_convert_fusion.1), channel_id=1, source_target_pairs={{0,16},{8,24},{16,0},{24,8},{1,17},{9,25},{17,1},{25,9},{2,18},{10... | collective-permute-start | bytes 3145736 | tf_op jit(solution)/shard_map/ppermute | solution.py:29
  466.5 25.4 %collective-permute-start.75 = (bf16[512,1024]{1,0:T(8,128)(2,1)}, bf16[512,1024]{1,0:T(8,128)(2,1)}, u32[]{:S(2)}, u32[]{:S(2)}) collective-permute-start(bf16[512,1024]{1,0:T(8,128)(2,1)} %get-tuple-element.441), channel_id=1, source_target_pairs={{0,8},{8,0},{16,24},{24,16},{1,9},{9,1},{17,25},{25,17},{2,10},{10... | collective-permute-start | bytes 3145736 | tf_op jit(solution)/shard_map/ppermute | solution.py:29
  468.4 29.6 %collective-permute-start.68 = (bf16[128,2048]{1,0:T(8,128)(2,1)}, bf16[128,2048]{1,0:T(8,128)(2,1)}, u32[]{:S(2)}, u32[]{:S(2)}) collective-permute-start(bf16[128,2048]{1,0:T(8,128)(2,1)} %get-tuple-element.405), channel_id=1, source_target_pairs={{0,4},{4,0},{1,5},{5,1},{2,6},{6,2},{3,7},{7,3},{8,12},{12,8},{9,1... | collective-permute-start | bytes 1572872 | tf_op jit(solution)/shard_map/ppermute | solution.py:29
  491.9 24.2 %collective-permute-start.81 = (bf16[512,1024]{1,0:T(8,128)(2,1)S(1)}, bf16[512,1024]{1,0:T(8,128)(2,1)S(1)}, u32[]{:S(2)}, u32[]{:S(2)}) collective-permute-start(bf16[512,1024]{1,0:T(8,128)(2,1)S(1)} %copy-done.85), channel_id=1, source_target_pairs={{0,16},{8,24},{16,0},{24,8},{1,17},{9,25},{17,1},{25,9},{2,18},{10... | collective-permute-start | bytes 3145736 | tf_op jit(solution)/shard_map/ppermute | solution.py:29
  520.8 25.6 %collective-permute-start.87 = (bf16[512,1024]{1,0:T(8,128)(2,1)S(1)}, bf16[512,1024]{1,0:T(8,128)(2,1)S(1)}, u32[]{:S(2)}, u32[]{:S(2)}) collective-permute-start(bf16[512,1024]{1,0:T(8,128)(2,1)S(1)} %add_convert_fusion), channel_id=1, source_target_pairs={{0,8},{8,0},{16,24},{24,16},{1,9},{9,1},{17,25},{25,17},{2,10},{10... | collective-permute-start | bytes 3145736 | tf_op jit(solution)/shard_map/ppermute | solution.py:29
  521.8 24.6 %collective-permute-start.88 = (bf16[512,1024]{1,0:T(8,128)(2,1)S(1)}, bf16[512,1024]{1,0:T(8,128)(2,1)S(1)}, u32[]{:S(2)}, u32[]{:S(2)}) collective-permute-start(bf16[512,1024]{1,0:T(8,128)(2,1)S(1)} %copy-done.84), channel_id=1, source_target_pairs={{0,16},{8,24},{16,0},{24,8},{1,17},{9,25},{17,1},{25,9},{2,18},{10... | collective-permute-start | bytes 3145736 | tf_op jit(solution)/shard_map/ppermute | solution.py:29
  523.7 26.5 %collective-permute-start.85 = (bf16[128,2048]{1,0:T(8,128)(2,1)S(1)}, bf16[128,2048]{1,0:T(8,128)(2,1)S(1)}, u32[]{:S(2)}, u32[]{:S(2)}) collective-permute-start(bf16[128,2048]{1,0:T(8,128)(2,1)S(1)} %add_convert_fusion.4), channel_id=1, source_target_pairs={{0,1},{1,2},{2,3},{3,0},{4,5},{5,6},{6,7},{7,4},{8,9},{9,10},{10,1... | collective-permute-start | bytes 1572872 | tf_op jit(solution)/shard_map/ppermute | solution.py:24
  551.2 30.9 %collective-permute-start.100 = (bf16[128,1024]{1,0:T(8,128)(2,1)S(1)}, bf16[128,1024]{1,0:T(8,128)(2,1)S(1)}, u32[]{:S(2)}, u32[]{:S(2)}) collective-permute-start(bf16[128,1024]{1,0:T(8,128)(2,1)S(1)} %get-tuple-element.477), channel_id=1, source_target_pairs={{0,2},{1,3},{2,0},{3,1},{4,6},{5,7},{6,4},{7,5},{8,10},{9,11},{10,... | collective-permute-start | bytes 786440 | tf_op jit(solution)/shard_map/ppermute | solution.py:24
  553.8 28.4 %collective-permute-start.101 = (bf16[128,1024]{1,0:T(8,128)(2,1)S(1)}, bf16[128,1024]{1,0:T(8,128)(2,1)S(1)}, u32[]{:S(2)}, u32[]{:S(2)}) collective-permute-start(bf16[128,1024]{1,0:T(8,128)(2,1)S(1)} %get-tuple-element.478), channel_id=1, source_target_pairs={{0,3},{1,0},{2,1},{3,2},{4,7},{5,4},{6,5},{7,6},{8,11},{9,8},{10,9... | collective-permute-start | bytes 786440 | tf_op jit(solution)/shard_map/ppermute | solution.py:24
  556.0 33.6 %collective-permute-start.97 = (bf16[128,1024]{1,0:T(8,128)(2,1)S(1)}, bf16[128,1024]{1,0:T(8,128)(2,1)S(1)}, u32[]{:S(2)}, u32[]{:S(2)}) collective-permute-start(bf16[128,1024]{1,0:T(8,128)(2,1)S(1)} %get-tuple-element.474), channel_id=1, source_target_pairs={{0,1},{1,2},{2,3},{3,0},{4,5},{5,6},{6,7},{7,4},{8,9},{9,10},{10,1... | collective-permute-start | bytes 786440 | tf_op jit(solution)/shard_map/ppermute | solution.py:24
  558.2 36.2 %collective-permute-start.98 = (bf16[128,1024]{1,0:T(8,128)(2,1)S(1)}, bf16[128,1024]{1,0:T(8,128)(2,1)S(1)}, u32[]{:S(2)}, u32[]{:S(2)}) collective-permute-start(bf16[128,1024]{1,0:T(8,128)(2,1)S(1)} %get-tuple-element.475), channel_id=1, source_target_pairs={{0,2},{1,3},{2,0},{3,1},{4,6},{5,7},{6,4},{7,5},{8,10},{9,11},{10,... | collective-permute-start | bytes 786440 | tf_op jit(solution)/shard_map/ppermute | solution.py:24
  561.3 37.3 %collective-permute-start.99 = (bf16[128,1024]{1,0:T(8,128)(2,1)S(1)}, bf16[128,1024]{1,0:T(8,128)(2,1)S(1)}, u32[]{:S(2)}, u32[]{:S(2)}) collective-permute-start(bf16[128,1024]{1,0:T(8,128)(2,1)S(1)} %get-tuple-element.476), channel_id=1, source_target_pairs={{0,3},{1,0},{2,1},{3,2},{4,7},{5,4},{6,5},{7,6},{8,11},{9,8},{10,9... | collective-permute-start | bytes 786440 | tf_op jit(solution)/shard_map/ppermute | solution.py:24
  (144 other events, 1812.3 us)

commit v4 on v3

--- a/solution.py
+++ b/solution.py
@@ -107,12 +107,13 @@
             self.got[k] = turn(self.pieces[k], "blk", k)
         return [self.got[k] for k in steps]
 
-    def by_rank(self):
+    def by_rank(self, columns=slice(None)):
         blks, rank = lax.axis_size("blk"), lax.axis_index("blk")
-        rows, cols = self.got[0].shape
-        full = jnp.zeros((blks * rows, cols), self.got[0].dtype)
+        parts = [self.got[k][:, columns] for k in range(blks)]
+        rows, cols = parts[0].shape
+        full = jnp.zeros((blks * rows, cols), parts[0].dtype)
         for k in range(blks):
-            full = lax.dynamic_update_slice(full, self.got[k], ((rank - k) % blks * rows, 0))
+            full = lax.dynamic_update_slice(full, parts[k], ((rank - k) % blks * rows, 0))
         return full
 
 
@@ -522,9 +523,9 @@
         return taken
 
     gq_refs, gk_refs, gv_refs, cos_refs, sin_refs = (some(count) for _ in range(5))
-    weights, parts = some(4), some(count * seqs)
+    weights, normed = some(4), some(count)
     outs, (gain_ref,), terms = some(count), some(1), some(count * seqs)
-    size = parts[0].shape[0]
+    size = terms[0].shape[0]
     step = weights[0].shape[0]
     for g, out_ref in enumerate(outs):
         low_k = gk_refs[g][...].astype(LOW).astype(WIDE)
@@ -533,26 +534,20 @@
         out_ref[:, width : 2 * width] = (low_k * cos - partner(low_k) * sin).astype(LOW)
         out_ref[:, 2 * width :] = gv_refs[g][...].astype(LOW)
     grads = jnp.concatenate([ref[...] for ref in outs], axis=0)
-    inverses = []
-    for part in parts:
-        rows = part[...].astype(WIDE)
-        inverses.append(lax.rsqrt(jnp.mean(rows * rows, axis=-1, keepdims=True) + EPSILON))
     for i in range(GROUPS):
         here = slice(i * step, (i + 1) * step)
         grad = over_cols(grads, weights[i][:, : 3 * width])
         put_parts(terms, size, i * step, grad.astype(LOW))
-        gain = 0.0
-        for n, part in enumerate(parts):
-            mine = grad[n * size : (n + 1) * size]
-            gain += jnp.sum(mine * (part[:, here].astype(WIDE) * inverses[n]), axis=0, keepdims=True)
-        gain_ref[:, here] = gain
-
-
-def finish_blocks(ks, grad_q, grad_k, grad_v, cos, sin, weights, parts):
+        rows = jnp.concatenate([ref[:, here] for ref in normed], axis=0).astype(WIDE)
+        gain_ref[:, here] = jnp.sum(grad * rows, axis=0, keepdims=True)
+
+
+def finish_blocks(ks, seqs, grad_q, grad_k, grad_v, cos, sin, weights, normed):
     count = len(ks)
     total, width = grad_k.shape
-    seqs, (size, model) = len(parts) // count, parts[0].shape
-    block = size * seqs
+    model = normed.shape[1]
+    block = total // lax.axis_size("blk")
+    size = block // seqs
     rows_at = lambda k, wide: pl.BlockSpec((block, wide), lambda _: (k, 0))
     tables = [rows_at(k, cos.shape[1]) for k in ks]
     got = pl.pallas_call(
@@ -562,7 +557,7 @@
         + [rows_at(k, width) for k in ks] * 2
         + tables * 2
         + [vmem(w.shape) for w in weights]
-        + [vmem((size, model))] * (count * seqs),
+        + [rows_at(k, model) for k in ks],
         out_specs=[vmem((block, 3 * width))] * count + [vmem((1, model))] + [vmem((size, model))] * (count * seqs),
         out_shape=[jax.ShapeDtypeStruct((block, 3 * width), LOW)] * count
         + [jax.ShapeDtypeStruct((1, model), WIDE)]
@@ -570,7 +565,7 @@
         compiler_params=params(56),
         cost_estimate=cost(),
         name="finish_blocks",
-    )(*[grad_q[k] for k in ks], *[grad_k] * count, *[grad_v] * count, *[cos] * count, *[sin] * count, *weights, *parts)
+    )(*[grad_q[k] for k in ks], *[grad_k] * count, *[grad_v] * count, *[cos] * count, *[sin] * count, *weights, *[normed] * count)
     return got[:count], got[count], by_block(got[count + 1 :], count)
 
 
@@ -639,8 +634,8 @@
     flat = lambda lists: [item for items in lists for item in items]
     in_order, in_turn = [[0, 1], [2, 3]], [[1, 2], [3, 0]]
 
-    def calls(ks):
-        return [ks] if block * len(ks) <= 512 else [[k] for k in ks]
+    def calls(ks, most=512):
+        return [ks] if block * len(ks) <= most else [[k] for k in ks]
 
     token_blocks = [None] * blks
     ahead = turn(own_tokens, "blk", 1)
@@ -652,7 +647,7 @@
     ahead = turn(moving, "blk", 1)
     near_x, near_y = swap(part_attn, "slot", 1), swap(part_attn, "slot", 2)
     pair_out.send(1)
-    phase.end(ahead, near_x, near_y, pair_out.got, cos_wide, sin_wide)
+    phase.end(ahead, near_x, near_y, pair_out.got, pair_out.pieces, down_out.pieces, cos_wide, sin_wide)
 
     second, moving, near_x, pair_out.pieces = phase.take(moving, ahead, near_x, pair_out.pieces)
     ahead = turn(moving, "blk", 1)
@@ -685,8 +680,7 @@
     queries, pair_out.got, down_out.pieces, terms[1], terms[2] = phase.take(
         queries, pair_out.got, down_out.pieces, terms[1], terms[2]
     )
-    part_pair = pair_out.by_rank()
-    half_a, half_b = part_pair[:, :hidden], part_pair[:, hidden:]
+    half_a = pair_out.by_rank(slice(0, hidden))
     near_x, near_y = [swap(half_a, "slot", 1)], [swap(half_a, "slot", 2)]
     terms[1] = seq_reduce(terms[1])
     moving = turn(add_up(terms[1]).astype(LOW), "blk", 1)
@@ -695,6 +689,7 @@
     attend(in_turn[1], queries)
     phase.end(moving, terms, near_x, near_y, down_out.got)
 
+    half_b = pair_out.by_rank(slice(hidden, None))
     moving, half_b, down_out.pieces, terms[3], terms[0] = phase.take(
         add_up([moving, *terms[2]]).astype(LOW), half_b, down_out.pieces, terms[3], terms[0]
     )
@@ -769,15 +764,14 @@
     pair_b = weight_terms((hidden_mlp, [grad_pair[1]]))
     phase.end(grad, out, down_terms, pair_b)
 
-    grad, grads_of[3], grads_of[0], far_down, far_b, half = phase.take(
-        grad, grads_of[3], grads_of[0], down_terms[3], pair_b[3], grad_pair[0]
+    grad, grads_of[3], grads_of[0], far_down, far_b = phase.take(
+        grad, grads_of[3], grads_of[0], down_terms[3], pair_b[3]
     )
     grads_of[3] = seq_reduce(grads_of[3])
     grad = turn(add_up([grad, *grads_of[3]]).astype(LOW), "blk", 1)
     far_down, far_b = swap(far_down, "slot", 1), swap(far_b, "slot", 2)
     grads_of[0] = seq_reduce(grads_of[0])
-    pair_a = weight_terms((hidden_mlp, [half]))
-    phase.end(grad, grads_of[0], pair_a)
+    phase.end(grad, grads_of[0])
     grad_part = add_up([grad, *grads_of[0]])
     grad_resid_part, gain_mlp_term = norm_back(normed_mlp, inverse_mlp, grad_part)
     grad_resid = own_cot.astype(WIDE) + grad_resid_part
@@ -794,11 +788,14 @@
                 grad_q[k] = grad
         return held
 
-    moving, out, outs_of[3], outs_of[0] = phase.take(grad_resid.astype(LOW), out, outs_of[3], outs_of[0])
+    moving, out, outs_of[3], outs_of[0], half = phase.take(
+        grad_resid.astype(LOW), out, outs_of[3], outs_of[0], grad_pair[0]
+    )
     ahead = turn(moving, "blk", 1)
+    pair_a = weight_terms((hidden_mlp, [half]))
     blocks = [seq_gather(moving), None, None, None]
     outs_of[3] = seq_reduce(outs_of[3])
-    phase.end(ahead, blocks[0], outs_of[3], far_down, far_b)
+    phase.end(ahead, blocks[0], outs_of[3], far_down, far_b, pair_a)
 
     moving, blocks[0], far_down, down_terms, out = phase.take(
         ahead, blocks[0], far_down, down_terms, add_up([out, *outs_of[3]]).astype(LOW)
@@ -809,81 +806,78 @@
     out = turn(out, "blk", 1)
     blocks[1] = seq_gather(moving)
     held = attend_back(in_order[0], None)
-    phase.end(ahead, blocks[1], held)
-
-    moving, far_a = phase.take(ahead, pair_a[3])
+    phase.end(ahead, blocks[1], held, one, two)
+
+    moving, far_a, down_terms, one, two = phase.take(ahead, pair_a[3], down_terms, one, two)
     ahead = turn(moving, "blk", 1)
     far_a = swap(far_a, "slot", 1)
     blocks[2] = seq_gather(moving)
-    phase.end(ahead, blocks[2], one, two, out)
-
-    moving, blocks[2], two_b, one_b, one, two = phase.take(
-        ahead, blocks[2], pair_b[2], add_up([pair_b[1], far_b]).astype(LOW), one, two
-    )
+    down_back = Exchange(row_pieces([down_terms[0], one, two]))
+    relay_b = add_up([pair_b[1], far_b]).astype(LOW)
+    phase.end(ahead, blocks[2], down_back.pieces, relay_b, out)
+
+    moving, blocks[2], two_b, one_b, down_back.pieces = phase.take(ahead, blocks[2], pair_b[2], relay_b, down_back.pieces)
     blocks[3] = seq_gather(moving)
     two_b, one_b = swap(two_b, "slot", 2), swap(one_b, "slot", 1)
+    down_back.send(1, 2)
     held = attend_back(in_order[1], held)
     all_resid, grad_k, grad_v = held
-    down_back = Exchange(row_pieces([down_terms[0], one, two]))
-    phase.end(held, far_a, down_back.pieces)
+    phase.end(held, far_a, down_back.got)
 
     grad_qkv, terms, gain_terms = [None] * blks, [None] * blks, []
 
     def finish(ks, grad_k):
-        for some in calls(ks):
+        for some in calls(ks, 1024):
             outs, gain_term, parts = finish_blocks(
-                some, grad_q, grad_k, grad_v, cos_wide, sin_wide, full_attn, flat([token_blocks[k] for k in some])
+                some, seqs, grad_q, grad_k, grad_v, cos_wide, sin_wide, full_attn, hidden_attn
             )
             gain_terms.append(gain_term)
             for k, out, part in zip(some, outs, parts):
                 grad_qkv[k], terms[k] = out, part
 
     grad_k, down_back.pieces, outs_of[0] = phase.take(grad_k, down_back.pieces, outs_of[0])
-    down_back.send(1, 2, 3)
+    down_back.send(3)
     outs_of[0] = seq_reduce(outs_of[0])
-    finish(in_turn[0], grad_k)
-    finish(in_turn[1], grad_k)
-    phase.end(terms, one_b, two_b)
-
-    terms[1] = phase.take(terms[1])
-    terms[1] = seq_reduce(terms[1])
+    finish([*in_turn[0], *in_turn[1]], grad_k)
+    phase.end(terms, one_b, two_b, gain_terms, down_back.got)
+
+    terms[1] = seq_reduce(phase.take(terms[1]))
     phase.end(terms[1])
 
-    moving, terms[2], grad_qkv, one_a, two_a, one_b, two_b = phase.take(
-        add_up(terms[1]).astype(LOW), terms[2], grad_qkv, add_up([pair_a[2], far_a]).astype(LOW), pair_a[1], one_b, two_b
+    moving, terms[2], terms[3], grad_qkv, gain_terms, far_a, near_a, middle_a, one_b, two_b = phase.take(
+        add_up(terms[1]).astype(LOW), terms[2], terms[3], grad_qkv, gain_terms, far_a, pair_a[1], pair_a[2], one_b, two_b
     )
     moving = turn(moving, "blk", 1)
-    one_a, two_a = swap(one_a, "slot", 2), swap(two_a, "slot", 1)
-    terms[2] = seq_reduce(terms[2])
-    last_terms = weight_terms((hidden_attn, grad_qkv), (all_resid, attended))
+    one_a, two_a = swap(add_up([middle_a, far_a]).astype(LOW), "slot", 2), swap(near_a, "slot", 1)
+    terms[2], terms[3] = seq_reduce(terms[2]), seq_reduce(terms[3])
     gain_terms = jnp.concatenate([add_up(gain_terms), jnp.sum(gain_mlp_term, axis=0, keepdims=True)], axis=0)
-    back_b = Exchange(row_pieces([pair_b[0], one_b, two_b]))
-    phase.end(moving, terms[2], last_terms, down_back.got, gain_terms, back_b.pieces)
-
-    moving, gain_terms, far, back_b.pieces, terms[3], one_a, two_a = phase.take(
-        add_up([moving, *terms[2]]).astype(LOW), gain_terms, last_terms[3], back_b.pieces, terms[3], one_a, two_a
-    )
-    moving = turn(moving, "blk", 1)
-    far = swap(far, "slot", 2)
-    back_b.send(1, 3)
     bit = 1
     while bit < seqs:
         gain_terms = gain_terms + swap(gain_terms, "seq", bit)
         bit *= 2
-    terms[3] = seq_reduce(terms[3])
-    back_a = Exchange(row_pieces([pair_a[0], one_a, two_a]))
-    phase.end(moving, far, terms[3], back_b.got, back_a.pieces, gain_terms)
+    last_terms = weight_terms((hidden_attn, grad_qkv), (all_resid, attended))
+    back_b = Exchange(row_pieces([pair_b[0], one_b, two_b]))
+    phase.end(moving, terms[2], terms[3], last_terms, back_b.pieces, gain_terms)
 
     gain_parts = jnp.split(gain_terms, GROUPS, axis=1)
-    moving, relay, near_term, back_a.pieces, back_b.pieces, terms[0], gain_far, gain_two = phase.take(
+    moving, far, back_b.pieces, gain_far, gain_two = phase.take(
+        add_up([moving, *terms[2]]).astype(LOW), last_terms[3], back_b.pieces, gain_parts[3], gain_parts[1]
+    )
+    moving = turn(moving, "blk", 1)
+    far = swap(far, "slot", 2)
+    back_b.send(1, 3)
+    gain_far, gain_two = swap(gain_far, "slot", 1), swap(gain_two, "slot", 1)
+    phase.end(moving, far, back_b.got, gain_far, gain_two, one_a, two_a)
+
+    moving, relay, near_term, back_b.pieces, terms[0], one_a, two_a = phase.take(
         add_up([moving, *terms[3]]).astype(LOW), add_up([last_terms[1], far]).astype(LOW), last_terms[2],
-        back_a.pieces, back_b.pieces, terms[0], gain_parts[3], gain_parts[1],
-    )
-    gain_far, gain_two = swap(gain_far, "slot", 1), swap(gain_two, "slot", 1)
+        back_b.pieces, terms[0], one_a, two_a,
+    )
     moving = turn(moving, "blk", 1)
     one, two = swap(relay, "slot", 1), swap(near_term, "slot", 2)
     back_b.send(2)
-    phase.end(moving, one, two, back_b.got, gain_far, gain_two)
+    back_a = Exchange(row_pieces([pair_a[0], one_a, two_a]))
+    phase.end(moving, one, two, back_b.got, back_a.pieces)
 
     last_back = Exchange(row_pieces([last_terms[0], one, two]))
     gain_relay, last_back.pieces, back_a.pieces, terms[0] = phase.take(

time: 608 us -> 599 us (0.985)
  waiting for transfers between devices: 264 us -> 256 us
    ppermute x57, waiting for transfers between devices: 84.5 us -> 66.5 us  [swap(): return lax.ppermute(value, axis, [(i, i ^ mask) for i in range(count)])]
    ppermute x45, waiting for transfers between devices: 180 us -> 190 us  [turn(): lax.ppermute(value, axis, [(i, (i + by) % count) for i in range(count)])]
    pallas_call x2 -> x1, Pallas kernels: 13.7 us -> 10 us  [finish_blocks(): pl.pallas_call(partial(finish_kernel, width, count, seqs), grid=(1,), in_...]
  transfers between devices with their start and end apart: 102 -> 102, of which waited for: 45 -> 49; matrix products, arithmetic and copies ran while one was open for 10% -> 10% of each run, Pallas kernels for 26% -> 26%
where the time goes in v4:
time: 599 us; the launch traced here: 594 us
  waiting for transfers between devices  256 us (43%)
  Pallas kernels  156 us (26%)
  starting transfers between devices  106 us (18%)
  other arithmetic  52.2 us (9%)
  local copies, waits for them, and re-layouts  20.5 us (3%)
    ppermute x45, waiting for transfers between devices, turn(): lax.ppermute(value, axis, [(i, (i + by) % count) for i in range(count)])  190 us
    ppermute x45, starting transfers between devices, turn(): lax.ppermute(value, axis, [(i, (i + by) % count) for i in range(count)])  69 us
    ppermute x57, waiting for transfers between devices, swap(): return lax.ppermute(value, axis, [(i, i ^ mask) for i in range(count)])  66.5 us
    pallas_call x2, Pallas kernels, mlp_blocks(): pl.pallas_call(partial(mlp_kernel, count), grid=(1,), in_specs=[vmem((siz...  42.9 us
    ppermute x57, starting transfers between devices, swap(): return lax.ppermute(value, axis, [(i, i ^ mask) for i in range(count)])  36.7 us
    pallas_call x4, Pallas kernels, weight_terms(): pl.pallas_call(partial(weight_kernel, [len(rights) for _, rights in pairs...  34.8 us
    pallas_call x2, Pallas kernels, attend_back_blocks(): pl.pallas_call(partial(attend_back_kernel, (total, blks, seqs, size), ks,...  29.7 us
    pallas_call x2, Pallas kernels, attend_blocks(): pl.pallas_call(partial(attend_kernel, (total, blks, seqs, size), ks, widt...  24.9 us
  transfers between devices with their start and end apart: 102, of which 49 were waited for; matrix products, arithmetic and copies ran while one was open for 10% of the time, Pallas kernels for 26%

profile of v4, /device:TPU:0, one launch (start us, length us, event | category | flops | bytes accessed | tf_op | source)
XLA Modules:
  0.0 593.6 jit_solution(10801335164570220537)
XLA Ops:
  18.2 18.7 %collective-permute-done.2 = bf16[128,1024]{1,0:T(8,128)(2,1)} collective-permute-done((bf16[128,1024]{1,0:T(8,128)(2,1)}, bf16[128,1024]{1,0:T(8,128)(2,1)}, u32[]{:S(2)}, u32[]{:S(2)}) %collective-permute-start.2) | collective-permute-done | bytes 262176 | tf_op jit(solution)/shard_map/ppermute | solution.py:24
  37.9 4.5 collective-permute-done.3
  51.3 2.8 rotary_tables.1
  58.0 7.2 %collective-permute-done.5.refs_4_ = bf16[128,2048]{1,0:T(8,128)(2,1)} collective-permute-done((bf16[128,2048]{1,0:T(8,128)(2,1)}, bf16[128,2048]{1,0:T(8,128)(2,1)}, u32[]{:S(2)}, u32[]{:S(2)}) %collective-permute-start.5) | collective-permute-done | bytes 524320 | tf_op jit(solution)/shard_map/ppermute | solution.py:24
  65.2 9.7 %collective-permute-done.8 = bf16[128,2048]{1,0:T(8,128)(2,1)} collective-permute-done((bf16[128,2048]{1,0:T(8,128)(2,1)}, bf16[128,2048]{1,0:T(8,128)(2,1)}, u32[]{:S(2)}, u32[]{:S(2)}) %collective-permute-start.8) | collective-permute-done | bytes 524320 | tf_op jit(solution)/shard_map/ppermute | solution.py:24
  75.5 4.0 collective-permute-start.13
  79.5 12.8 %collective-permute-done.11.refs_6_ = bf16[128,2048]{1,0:T(8,128)(2,1)S(1)} collective-permute-done((bf16[128,2048]{1,0:T(8,128)(2,1)}, bf16[128,2048]{1,0:T(8,128)(2,1)S(1)}, u32[]{:S(2)}, u32[]{:S(2)}) %collective-permute-start.11) | collective-permute-done | bytes 524320 | tf_op jit(solution)/shard_map/ppermute | solution.py:24
  92.2 9.0 %collective-permute-done.13 = bf16[128,2048]{1,0:T(8,128)(2,1)S(1)} collective-permute-done((bf16[128,2048]{1,0:T(8,128)(2,1)S(1)}, bf16[128,2048]{1,0:T(8,128)(2,1)S(1)}, u32[]{:S(2)}, u32[]{:S(2)}) %collective-permute-start.13) | collective-permute-done | bytes 524320 | tf_op jit(solution)/shard_map/ppermute | solution.py:24
  105.0 10.9 %project_qkv.1 = (bf16[1024,2048]{1,0:T(8,128)(2,1)}, bf16[1024,256]{1,0:T(8,128)(2,1)}, bf16[1024,256]{1,0:T(8,128)(2,1)}, bf16[1024,256]{1,0:T(8,128)(2,1)}) custom-call(bf16[128,2048]{1,0:T(8,128)(2,1)} %copy-done.7, bf16[128,2048]{1,0:T(8,128)(2,1)} %copy-done.43, bf16[128,2048]{1,0:T(8,128)(2,1)} %collective-permute-done.1.refs_2_, ...), custom_call_target="tpu_custom_call" | custom-call | flops 1 | bytes 1 | tf_op jit(solution)/shard_map/project_qkv/pallas_call | solution.py:252
  115.9 12.5 %attend_blocks.2 = (bf16[256,256]{1,0:T(8,128)(2,1)}, bf16[256,256]{1,0:T(8,128)(2,1)}, f32[256,128]{1,0:T(8,128)}, f32[256,128]{1,0:T(8,128)}, bf16[128,2048]{1...) custom-call(s32[4]{0:T(128)} %copy-done.2, ...), custom_call_target="tpu_custom_call" | custom-call | flops 1 | bytes 1 | tf_op jit(solution)/shard_map/attend_blocks/pallas_call | solution.py:349
  137.1 12.4 %attend_blocks.3 = (bf16[256,256]{1,0:T(8,128)(2,1)}, bf16[256,256]{1,0:T(8,128)(2,1)}, f32[256,128]{1,0:T(8,128)}, f32[256,128]{1,0:T(8,128)}, bf16[128,2048]{1...) custom-call(s32[4]{0:T(128)} %copy-done.2, ...), custom_call_target="tpu_custom_call" | custom-call | flops 1 | bytes 1 | tf_op jit(solution)/shard_map/attend_blocks/pallas_call | solution.py:349
  152.0 8.9 %collective-permute-done.21 = bf16[128,1024]{1,0:T(8,128)(2,1)S(1)} collective-permute-done((bf16[128,1024]{1,0:T(8,128)(2,1)S(1)}, bf16[128,1024]{1,0:T(8,128)(2,1)S(1)}, u32[]{:S(2)}, u32[]{:S(2)}) %collective-permute-start.21) | collective-permute-done | bytes 262176 | tf_op jit(solution)/shard_map/ppermute | solution.py:24
  163.6 16.3 %collective-permute-done.22 = bf16[128,2048]{1,0:T(8,128)(2,1)} collective-permute-done((bf16[128,2048]{1,0:T(8,128)(2,1)}, bf16[128,2048]{1,0:T(8,128)(2,1)}, u32[]{:S(2)}, u32[]{:S(2)}) %collective-permute-start.22) | collective-permute-done | bytes 524320 | tf_op jit(solution)/shard_map/ppermute | solution.py:24
  191.3 3.7 collective-permute-done.29
  195.0 9.4 %collective-permute-done.27 = bf16[128,2048]{1,0:T(8,128)(2,1)S(1)} collective-permute-done((bf16[128,2048]{1,0:T(8,128)(2,1)S(1)}, bf16[128,2048]{1,0:T(8,128)(2,1)S(1)}, u32[]{:S(2)}, u32[]{:S(2)}) %collective-permute-start.27) | collective-permute-done | bytes 524320 | tf_op jit(solution)/shard_map/ppermute | solution.py:24
  208.5 5.3 collective-permute-done.31.refs_7_
  216.0 14.1 %collective-permute-done.30.refs_2_ = bf16[128,4096]{1,0:T(8,128)(2,1)S(1)} collective-permute-done((bf16[128,4096]{1,0:T(8,128)(2,1)S(1)}, bf16[128,4096]{1,0:T(8,128)(2,1)S(1)}, u32[]{:S(2)}, u32[]{:S(2)}) %collective-permute-start.30) | collective-permute-done | bytes 1048608 | tf_op jit(solution)/shard_map/ppermute | solution.py:24
  230.2 7.6 %collective-permute-done.36.refs_13_ = bf16[512,1024]{1,0:T(8,128)(2,1)S(1)} collective-permute-done((bf16[512,1024]{1,0:T(8,128)(2,1)S(1)}, bf16[512,1024]{1,0:T(8,128)(2,1)S(1)}, u32[]{:S(2)}, u32[]{:S(2)}) %collective-permute-start.36) | collective-permute-done | bytes 1048608 | tf_op jit(solution)/shard_map/ppermute | solution.py:29
  241.3 9.9 %collective-permute-done.38.refs_15_ = bf16[512,512]{1,0:T(8,128)(2,1)S(1)} collective-permute-done((bf16[512,512]{1,0:T(8,128)(2,1)S(1)}, bf16[512,512]{1,0:T(8,128)(2,1)S(1)}, u32[]{:S(2)}, u32[]{:S(2)}) %collective-permute-start.38) | collective-permute-done | bytes 524320 | tf_op jit(solution)/shard_map/ppermute | solution.py:29
  255.1 21.5 %mlp_blocks.2 = (bf16[1024,2048]{1,0:T(8,128)(2,1)}, bf16[1024,2048]{1,0:T(8,128)(2,1)}, bf16[1024,1024]{1,0:T(8,128)(2,1)}, bf16[1024,1024]{1,0:T(8,128)(2,1)},...) custom-call(bf16[128,4096]{1,0:T(8,128)(2,1)} %copy-done.21, ...), custom_call_target="tpu_custom_call" | custom-call | flops 1 | bytes 1 | tf_op jit(solution)/shard_map/mlp_blocks/pallas_call | solution.py:408
  276.6 3.4 collective-permute-done.40.refs_2_
  287.3 21.4 %mlp_blocks.3 = (bf16[1024,2048]{1,0:T(8,128)(2,1)}, bf16[1024,2048]{1,0:T(8,128)(2,1)}, bf16[1024,1024]{1,0:T(8,128)(2,1)}, bf16[1024,1024]{1,0:T(8,128)(2,1)},...) custom-call(bf16[128,4096]{1,0:T(8,128)(2,1)} %collective-permute-do, ...), custom_call_target="tpu_custom_call", output_to_operand_aliasing={{0}: (17, {}), {1}: (18, {}), {2}: (19, {}), {3}: (20, {}),... | custom-call | flops 1 | bytes 1 | tf_op jit(solution)/shard_map/mlp_blocks/pallas_call | solution.py:408
  319.8 8.4 %weight_terms.5 = (bf16[512,1024]{1,0:T(8,128)(2,1)}, bf16[512,1024]{1,0:T(8,128)(2,1)}, bf16[512,1024]{1,0:T(8,128)(2,1)}, bf16[512,1024]{1,0:T(8,128)(2,1)}) custom-call(bf16[1024,2048]{1,0:T(8,128)(2,1)} %get-tuple-element.329.refs_0_, bf16[1024,1024]{1,0:T(8,128)(2,1)} %get-tuple-element.341.refs_1_), custom_call_target="tpu_custom_call" | custom-call | flops 1 | bytes 1 | tf_op jit(solution)/shard_map/weight_terms/pallas_call | solution.py:592
  328.2 8.4 %weight_terms.4 = (bf16[512,1024]{1,0:T(8,128)(2,1)}, bf16[512,1024]{1,0:T(8,128)(2,1)}, bf16[512,1024]{1,0:T(8,128)(2,1)}, bf16[512,1024]{1,0:T(8,128)(2,1)}) custom-call(bf16[1024,2048]{1,0:T(8,128)(2,1)} %get-tuple-element.330.refs_0_, bf16[1024,1024]{1,0:T(8,128)(2,1)} %get-tuple-element.339.refs_1_), custom_call_target="tpu_custom_call" | custom-call | flops 1 | bytes 1 | tf_op jit(solution)/shard_map/weight_terms/pallas_call | solution.py:592
  336.7 5.4 collective-permute-done.48
  346.4 13.9 %collective-permute-done.52 = bf16[128,2048]{1,0:T(8,128)(2,1)S(1)} collective-permute-done((bf16[128,2048]{1,0:T(8,128)(2,1)S(1)}, bf16[128,2048]{1,0:T(8,128)(2,1)S(1)}, u32[]{:S(2)}, u32[]{:S(2)}) %collective-permute-start.52) | collective-permute-done | bytes 524320 | tf_op jit(solution)/shard_map/ppermute | solution.py:24
  362.0 8.4 %weight_terms.6 = (bf16[512,1024]{1,0:T(8,128)(2,1)}, bf16[512,1024]{1,0:T(8,128)(2,1)}, bf16[512,1024]{1,0:T(8,128)(2,1)}, bf16[512,1024]{1,0:T(8,128)(2,1)}) custom-call(bf16[1024,2048]{1,0:T(8,128)(2,1)} %get-tuple-element.329.refs_0_, bf16[1024,1024]{1,0:T(8,128)(2,1)} %get-tuple-element.367.refs_1_), custom_call_target="tpu_custom_call" | custom-call | flops 1 | bytes 1 | tf_op jit(solution)/shard_map/weight_terms/pallas_call | solution.py:592
  372.9 4.7 collective-permute-done.54.refs_18_
  384.9 14.5 %attend_back_blocks.2 = (bf16[1024,2048]{1,0:T(8,128)(2,1)}, f32[1024,256]{1,0:T(8,128)}, f32[1024,256]{1,0:T(8,128)}, bf16[256,256]{1,0:T(8,128)(2,1)}, bf16[256,256]{1,0:T(8,128)(2,1)}) custom-call(s32[4]{0:T(128)} %copy-done.2, bf16[1024,256]{1,0:T(8,128)(2,1)} %get-tuple-element.276.refs_0_.refs_1_, ...), custom_call_target="tpu_custom_call" | custom-call | flops 1 | bytes 1 | tf_op jit(solution)/shard_map/attend_back_blocks/pallas_call | solution.py:489
  399.4 6.0 %collective-permute-done.61 = bf16[512,1024]{1,0:T(8,128)(2,1)} collective-permute-done((bf16[512,1024]{1,0:T(8,128)(2,1)}, bf16[512,1024]{1,0:T(8,128)(2,1)}, u32[]{:S(2)}, u32[]{:S(2)}) %collective-permute-start.61) | collective-permute-done | bytes 1048608 | tf_op jit(solution)/shard_map/ppermute | solution.py:29
  407.0 3.0 add_convert_fusion.2
  411.5 2.9 add_convert_fusion.28
  414.4 6.4 %collective-permute-done.64.refs_18_ = bf16[128,2048]{1,0:T(8,128)(2,1)} collective-permute-done((bf16[128,2048]{1,0:T(8,128)(2,1)S(1)}, bf16[128,2048]{1,0:T(8,128)(2,1)}, u32[]{:S(2)}, u32[]{:S(2)}) %collective-permute-start.64) | collective-permute-done | bytes 524320 | tf_op jit(solution)/shard_map/ppermute | solution.py:24
  424.3 15.2 %attend_back_blocks.3 = (bf16[1024,2048]{1,0:T(8,128)(2,1)}, f32[1024,256]{1,0:T(8,128)}, f32[1024,256]{1,0:T(8,128)}, bf16[256,256]{1,0:T(8,128)(2,1)}, bf16[256,256]{1,0:T(8,128)(2,1)}) custom-call(s32[4]{0:T(128)} %copy-done.2, ...), custom_call_target="tpu_custom_call", output_to_operand_aliasing={{0}: (21, {}), {1}: (22, {}), {2}: (23, {})} | custom-call | flops 1 | bytes 1 | tf_op jit(solution)/shard_map/attend_back_blocks/pallas_call | solution.py:489
  439.5 4.6 collective-permute-done.69
  444.1 10.0 %finish_blocks.1 = (bf16[256,768]{1,0:T(8,128)(2,1)}, bf16[256,768]{1,0:T(8,128)(2,1)}, bf16[256,768]{1,0:T(8,128)(2,1)}, bf16[256,768]{1,0:T(8,128)(2,1)}, f32[...) custom-call(bf16[256,256]{1,0:T(8,128)(2,1)} %get-tuple-element.409., ...), custom_call_target="tpu_custom_call" | custom-call | flops 1 | bytes 1 | tf_op jit(solution)/shard_map/finish_blocks/pallas_call | solution.py:553
  464.7 2.9 add_convert_fusion.24
  467.6 9.6 %weight_terms.7 = (bf16[512,1024]{1,0:T(8,128)(2,1)}, bf16[512,1024]{1,0:T(8,128)(2,1)}, bf16[512,1024]{1,0:T(8,128)(2,1)}, bf16[512,1024]{1,0:T(8,128)(2,1)}) custom-call(bf16[1024,2048]{1,0:T(8,128)(2,1)} %get-tuple-element.414.refs_24_.refs_25_.refs_26_.refs_27_.refs_0_, bf16[256,768]{1,0:T(8,128)(2,1)} %get-tuple-element.436.refs_1_, ...), custom_call_target="tpu_custom_call" | custom-call | flops 1 | bytes 1 | tf_op jit(solution)/shard_map/weight_terms/pallas_call | solution.py:592
  486.0 13.5 %collective-permute-done.79 = bf16[128,2048]{1,0:T(8,128)(2,1)S(1)} collective-permute-done((bf16[128,2048]{1,0:T(8,128)(2,1)S(1)}, bf16[128,2048]{1,0:T(8,128)(2,1)S(1)}, u32[]{:S(2)}, u32[]{:S(2)}) %collective-permute-start.79) | collective-permute-done | bytes 524320 | tf_op jit(solution)/shard_map/ppermute | solution.py:24
  500.3 4.0 collective-permute-done.85
  505.9 3.0 collective-permute-done.80
  517.2 3.3 collective-permute-start.90
  523.0 13.0 %collective-permute-done.88 = bf16[512,1024]{1,0:T(8,128)(2,1)S(1)} collective-permute-done((bf16[512,1024]{1,0:T(8,128)(2,1)S(1)}, bf16[512,1024]{1,0:T(8,128)(2,1)S(1)}, u32[]{:S(2)}, u32[]{:S(2)}) %collective-permute-start.88) | collective-permute-done | bytes 1048608 | tf_op jit(solution)/shard_map/ppermute | solution.py:29
  537.9 2.9 collective-permute-done.90
  553.8 9.3 %collective-permute-done.100 = bf16[128,1024]{1,0:T(8,128)(2,1)S(1)} collective-permute-done((bf16[128,1024]{1,0:T(8,128)(2,1)S(1)}, bf16[128,1024]{1,0:T(8,128)(2,1)S(1)}, u32[]{:S(2)}, u32[]{:S(2)}) %collective-permute-start.100) | collective-permute-done | bytes 262176 | tf_op jit(solution)/shard_map/ppermute | solution.py:24
  563.2 16.4 %collective-permute-start.94 = (f32[2,512]{1,0:T(2,128)S(1)}, f32[2,512]{1,0:T(2,128)S(1)}, u32[]{:S(2)}, u32[]{:S(2)}) collective-permute-start(f32[2,512]{1,0:T(2,128)S(1)} %fusion.11), channel_id=1, source_target_pairs={{0,1},{1,2},{2,3},{3,0},{4,5},{5,6},{6,7},{7,4},{8,9},{9,10},{10,1... | collective-permute-start | bytes 12296 | tf_op jit(solution)/shard_map/ppermute | solution.py:24
  579.9 3.2 collective-permute-start.95
  584.7 4.2 collective-permute-start.96
  (439 shorter events, 167.6 us)
Async XLA Ops:
  2.1 42.3 %collective-permute-start = (bf16[128,2048]{1,0:T(8,128)(2,1)S(1)}, bf16[128,2048]{1,0:T(8,128)(2,1)S(1)}, u32[]{:S(2)}, u32[]{:S(2)}) collective-permute-start(bf16[128,2048]{1,0:T(8,128)(2,1)S(1)} %get-tuple-element.482.refs_0_), channel_id=1, source_target_pairs={{0,4},{4,0},{1,5},{5,1},{2,6},{6,2},{3,7},{7,3},{8,12},{12,8},{9,1... | collective-permute-start | bytes 1572872 | tf_op jit(solution)/shard_map/ppermute | solution.py:29
  2.6 41.8 %collective-permute-start.1 = (bf16[128,2048]{1,0:T(8,128)(2,1)S(1)}, bf16[128,2048]{1,0:T(8,128)(2,1)}, u32[]{:S(2)}, u32[]{:S(2)}) collective-permute-start(bf16[128,2048]{1,0:T(8,128)(2,1)S(1)} %get-tuple-element.482.refs_0_), channel_id=1, source_target_pairs={{0,1},{1,2},{2,3},{3,0},{4,5},{5,6},{6,7},{7,4},{8,9},{9,10},{10,1... | collective-permute-start | bytes 1572872 | tf_op jit(solution)/shard_map/ppermute | solution.py:24
  7.6 35.8 %collective-permute-start.4 = (bf16[128,1024]{1,0:T(8,128)(2,1)}, bf16[128,1024]{1,0:T(8,128)(2,1)}, u32[]{:S(2)}, u32[]{:S(2)}) collective-permute-start(bf16[128,1024]{1,0:T(8,128)(2,1)} %pad_maximum_fusion.10), channel_id=1, source_target_pairs={{0,3},{1,0},{2,1},{3,2},{4,7},{5,4},{6,5},{7,6},{8,11},{9,8},{10,9... | collective-permute-start | bytes 786440 | tf_op jit(solution)/shard_map/ppermute | solution.py:24
  10.5 31.9 %collective-permute-start.3 = (bf16[128,1024]{1,0:T(8,128)(2,1)}, bf16[128,1024]{1,0:T(8,128)(2,1)}, u32[]{:S(2)}, u32[]{:S(2)}) collective-permute-start(bf16[128,1024]{1,0:T(8,128)(2,1)} %pad_maximum_fusion.9), channel_id=1, source_target_pairs={{0,2},{1,3},{2,0},{3,1},{4,6},{5,7},{6,4},{7,5},{8,10},{9,11},{10,... | collective-permute-start | bytes 786440 | tf_op jit(solution)/shard_map/ppermute | solution.py:24
  12.1 24.8 %collective-permute-start.2 = (bf16[128,1024]{1,0:T(8,128)(2,1)}, bf16[128,1024]{1,0:T(8,128)(2,1)}, u32[]{:S(2)}, u32[]{:S(2)}) collective-permute-start(bf16[128,1024]{1,0:T(8,128)(2,1)} %pad_maximum_fusion.8), channel_id=1, source_target_pairs={{0,1},{1,2},{2,3},{3,0},{4,5},{5,6},{6,7},{7,4},{8,9},{9,10},{10,1... | collective-permute-start | bytes 786440 | tf_op jit(solution)/shard_map/ppermute | solution.py:24
  45.2 29.7 %collective-permute-start.6 = (bf16[512,1024]{1,0:T(8,128)(2,1)S(1)}, bf16[512,1024]{1,0:T(8,128)(2,1)S(1)}, u32[]{:S(2)}, u32[]{:S(2)}) collective-permute-start(bf16[512,1024]{1,0:T(8,128)(2,1)S(1)} %constant_dynamic-update-slice_fusion.4.refs_8_.refs_4_.refs_12_.refs_20_), channel_id=1, source_target_pairs={{0,8},{8,0},{16,24},{24,16},{1,9},{9,1},{17,25},{25,17},{2,10},{10... | collective-permute-start | bytes 3145736 | tf_op jit(solution)/shard_map/ppermute | solution.py:29
  46.7 28.2 %collective-permute-start.7 = (bf16[512,1024]{1,0:T(8,128)(2,1)S(1)}, bf16[512,1024]{1,0:T(8,128)(2,1)S(1)}, u32[]{:S(2)}, u32[]{:S(2)}) collective-permute-start(bf16[512,1024]{1,0:T(8,128)(2,1)S(1)} %constant_dynamic-update-slice_fusion.4.refs_8_.refs_4_.refs_12_.refs_20_), channel_id=1, source_target_pairs={{0,16},{8,24},{16,0},{24,8},{1,17},{9,25},{17,1},{25,9},{2,18},{10... | collective-permute-start | bytes 3145736 | tf_op jit(solution)/shard_map/ppermute | solution.py:29
  48.2 26.7 %collective-permute-start.8 = (bf16[128,2048]{1,0:T(8,128)(2,1)}, bf16[128,2048]{1,0:T(8,128)(2,1)}, u32[]{:S(2)}, u32[]{:S(2)}) collective-permute-start(bf16[128,2048]{1,0:T(8,128)(2,1)} %pad_maximum_fusion.3), channel_id=1, source_target_pairs={{0,1},{1,2},{2,3},{3,0},{4,5},{5,6},{6,7},{7,4},{8,9},{9,10},{10,1... | collective-permute-start | bytes 1572872 | tf_op jit(solution)/shard_map/ppermute | solution.py:24
  74.9 26.3 %collective-permute-start.12 = (bf16[512,1024]{1,0:T(8,128)(2,1)S(1)}, bf16[512,1024]{1,0:T(8,128)(2,1)S(1)}, u32[]{:S(2)}, u32[]{:S(2)}) collective-permute-start(bf16[512,1024]{1,0:T(8,128)(2,1)S(1)} %collective-permute-done.6.refs_9_.refs_5_.refs_13_.refs_21_), channel_id=1, source_target_pairs={{0,16},{8,24},{16,0},{24,8},{1,17},{9,25},{17,1},{25,9},{2,18},{10... | collective-permute-start | bytes 3145736 | tf_op jit(solution)/shard_map/ppermute | solution.py:29
  75.5 25.7 %collective-permute-start.13 = (bf16[128,2048]{1,0:T(8,128)(2,1)S(1)}, bf16[128,2048]{1,0:T(8,128)(2,1)S(1)}, u32[]{:S(2)}, u32[]{:S(2)}) collective-permute-start(bf16[128,2048]{1,0:T(8,128)(2,1)S(1)} %copy-done.58), channel_id=1, source_target_pairs={{0,3},{1,0},{2,1},{3,2},{4,7},{5,4},{6,5},{7,6},{8,11},{9,8},{10,9... | collective-permute-start | bytes 1572872 | tf_op jit(solution)/shard_map/ppermute | solution.py:24
  102.5 26.3 %collective-permute-start.15 = (bf16[128,2048]{1,0:T(8,128)(2,1)}, bf16[128,2048]{1,0:T(8,128)(2,1)}, u32[]{:S(2)}, u32[]{:S(2)}) collective-permute-start(bf16[128,2048]{1,0:T(8,128)(2,1)} %pad_maximum_fusion.4), channel_id=1, source_target_pairs={{0,2},{1,3},{2,0},{3,1},{4,6},{5,7},{6,4},{7,5},{8,10},{9,11},{10,... | collective-permute-start | bytes 1572872 | tf_op jit(solution)/shard_map/ppermute | solution.py:24
  132.0 28.9 %collective-permute-start.19 = (bf16[512,1024]{1,0:T(8,128)(2,1)S(1)}, bf16[512,1024]{1,0:T(8,128)(2,1)S(1)}, u32[]{:S(2)}, u32[]{:S(2)}) collective-permute-start(bf16[512,1024]{1,0:T(8,128)(2,1)S(1)} %get-tuple-element.539.refs_4_), channel_id=1, source_target_pairs={{0,8},{8,0},{16,24},{24,16},{1,9},{9,1},{17,25},{25,17},{2,10},{10... | collective-permute-start | bytes 3145736 | tf_op jit(solution)/shard_map/ppermute | solution.py:29
  132.6 28.3 %collective-permute-start.20 = (bf16[512,1024]{1,0:T(8,128)(2,1)S(1)}, bf16[512,1024]{1,0:T(8,128)(2,1)S(1)}, u32[]{:S(2)}, u32[]{:S(2)}) collective-permute-start(bf16[512,1024]{1,0:T(8,128)(2,1)S(1)} %get-tuple-element.539.refs_4_), channel_id=1, source_target_pairs={{0,16},{8,24},{16,0},{24,8},{1,17},{9,25},{17,1},{25,9},{2,18},{10... | collective-permute-start | bytes 3145736 | tf_op jit(solution)/shard_map/ppermute | solution.py:29
  134.6 26.3 %collective-permute-start.21 = (bf16[128,1024]{1,0:T(8,128)(2,1)S(1)}, bf16[128,1024]{1,0:T(8,128)(2,1)S(1)}, u32[]{:S(2)}, u32[]{:S(2)}) collective-permute-start(bf16[128,1024]{1,0:T(8,128)(2,1)S(1)} %copy-done.72), channel_id=1, source_target_pairs={{0,2},{1,3},{2,0},{3,1},{4,6},{5,7},{6,4},{7,5},{8,10},{9,11},{10,... | collective-permute-start | bytes 786440 | tf_op jit(solution)/shard_map/ppermute | solution.py:24
  160.9 24.8 %collective-permute-start.24 = (bf16[512,1024]{1,0:T(8,128)(2,1)S(1)}, bf16[512,1024]{1,0:T(8,128)(2,1)}, u32[]{:S(2)}, u32[]{:S(2)}) collective-permute-start(bf16[512,1024]{1,0:T(8,128)(2,1)S(1)} %get-tuple-element.284.refs_8_), channel_id=1, source_target_pairs={{0,16},{8,24},{16,0},{24,8},{1,17},{9,25},{17,1},{25,9},{2,18},{10... | collective-permute-start | bytes 3145736 | tf_op jit(solution)/shard_map/ppermute | solution.py:29
  161.5 24.4 %collective-permute-start.25 = (bf16[512,1024]{1,0:T(8,128)(2,1)S(1)}, bf16[512,1024]{1,0:T(8,128)(2,1)}, u32[]{:S(2)}, u32[]{:S(2)}) collective-permute-start(bf16[512,1024]{1,0:T(8,128)(2,1)S(1)} %get-tuple-element.284.refs_8_), channel_id=1, source_target_pairs={{0,8},{8,0},{16,24},{24,16},{1,9},{9,1},{17,25},{25,17},{2,10},{10... | collective-permute-start | bytes 3145736 | tf_op jit(solution)/shard_map/ppermute | solution.py:29
  188.2 25.6 %collective-permute-start.31 = (bf16[512,1024]{1,0:T(8,128)(2,1)S(1)}, bf16[512,1024]{1,0:T(8,128)(2,1)S(1)}, u32[]{:S(2)}, u32[]{:S(2)}) collective-permute-start(bf16[512,1024]{1,0:T(8,128)(2,1)S(1)} %copy-done.17), channel_id=1, source_target_pairs={{0,16},{8,24},{16,0},{24,8},{1,17},{9,25},{17,1},{25,9},{2,18},{10... | collective-permute-start | bytes 3145736 | tf_op jit(solution)/shard_map/ppermute | solution.py:29
  189.8 26.2 %collective-permute-start.32 = (bf16[512,1024]{1,0:T(8,128)(2,1)}, bf16[512,1024]{1,0:T(8,128)(2,1)S(1)}, u32[]{:S(2)}, u32[]{:S(2)}) collective-permute-start(bf16[512,1024]{1,0:T(8,128)(2,1)} %collective-permute-done.24.refs_10_), channel_id=1, source_target_pairs={{0,8},{8,0},{16,24},{24,16},{1,9},{9,1},{17,25},{25,17},{2,10},{10... | collective-permute-start | bytes 3145736 | tf_op jit(solution)/shard_map/ppermute | solution.py:29
  205.2 24.9 %collective-permute-start.30 = (bf16[128,4096]{1,0:T(8,128)(2,1)S(1)}, bf16[128,4096]{1,0:T(8,128)(2,1)S(1)}, u32[]{:S(2)}, u32[]{:S(2)}) collective-permute-start(bf16[128,4096]{1,0:T(8,128)(2,1)S(1)} %pad_maximum_fusion.refs_0_), channel_id=1, source_target_pairs={{0,1},{1,2},{2,3},{3,0},{4,5},{5,6},{6,7},{7,4},{8,9},{9,10},{10,1... | collective-permute-start | bytes 3145736 | tf_op jit(solution)/shard_map/ppermute | solution.py:24
  207.0 30.7 %collective-permute-start.36 = (bf16[512,1024]{1,0:T(8,128)(2,1)S(1)}, bf16[512,1024]{1,0:T(8,128)(2,1)S(1)}, u32[]{:S(2)}, u32[]{:S(2)}) collective-permute-start(bf16[512,1024]{1,0:T(8,128)(2,1)S(1)} %constant_dynamic-update-slice_fusion.refs_12_), channel_id=1, source_target_pairs={{0,8},{8,0},{16,24},{24,16},{1,9},{9,1},{17,25},{25,17},{2,10},{10... | collective-permute-start | bytes 3145736 | tf_op jit(solution)/shard_map/ppermute | solution.py:29
  213.8 24.8 %collective-permute-start.37 = (bf16[512,1024]{1,0:T(8,128)(2,1)S(1)}, bf16[512,1024]{1,0:T(8,128)(2,1)S(1)}, u32[]{:S(2)}, u32[]{:S(2)}) collective-permute-start(bf16[512,1024]{1,0:T(8,128)(2,1)S(1)} %constant_dynamic-update-slice_fusion.refs_12_), channel_id=1, source_target_pairs={{0,16},{8,24},{16,0},{24,8},{1,17},{9,25},{17,1},{25,9},{2,18},{10... | collective-permute-start | bytes 3145736 | tf_op jit(solution)/shard_map/ppermute | solution.py:29
  230.0 24.1 %collective-permute-start.34 = (bf16[128,4096]{1,0:T(8,128)(2,1)S(1)}, bf16[128,4096]{1,0:T(8,128)(2,1)}, u32[]{:S(2)}, u32[]{:S(2)}) collective-permute-start(bf16[128,4096]{1,0:T(8,128)(2,1)S(1)} %collective-permute-done.30.refs_2_), channel_id=1, source_target_pairs={{0,1},{1,2},{2,3},{3,0},{4,5},{5,6},{6,7},{7,4},{8,9},{9,10},{10,1... | collective-permute-start | bytes 3145736 | tf_op jit(solution)/shard_map/ppermute | solution.py:24
  230.1 24.0 %collective-permute-start.35 = (bf16[128,4096]{1,0:T(8,128)(2,1)S(1)}, bf16[128,4096]{1,0:T(8,128)(2,1)S(1)}, u32[]{:S(2)}, u32[]{:S(2)}) collective-permute-start(bf16[128,4096]{1,0:T(8,128)(2,1)S(1)} %collective-permute-done.30.refs_2_), channel_id=1, source_target_pairs={{0,4},{4,0},{1,5},{5,1},{2,6},{6,2},{3,7},{7,3},{8,12},{12,8},{9,1... | collective-permute-start | bytes 3145736 | tf_op jit(solution)/shard_map/ppermute | solution.py:29
  254.1 25.9 %collective-permute-start.40 = (bf16[128,4096]{1,0:T(8,128)(2,1)}, bf16[128,4096]{1,0:T(8,128)(2,1)}, u32[]{:S(2)}, u32[]{:S(2)}) collective-permute-start(bf16[128,4096]{1,0:T(8,128)(2,1)} %collective-permute-done.34.refs_0_), channel_id=1, source_target_pairs={{0,1},{1,2},{2,3},{3,0},{4,5},{5,6},{6,7},{7,4},{8,9},{9,10},{10,1... | collective-permute-start | bytes 3145736 | tf_op jit(solution)/shard_map/ppermute | solution.py:24
  255.1 24.9 %collective-permute-start.41 = (bf16[128,4096]{1,0:T(8,128)(2,1)}, bf16[128,4096]{1,0:T(8,128)(2,1)}, u32[]{:S(2)}, u32[]{:S(2)}) collective-permute-start(bf16[128,4096]{1,0:T(8,128)(2,1)} %collective-permute-done.34.refs_0_), channel_id=1, source_target_pairs={{0,4},{4,0},{1,5},{5,1},{2,6},{6,2},{3,7},{7,3},{8,12},{12,8},{9,1... | collective-permute-start | bytes 3145736 | tf_op jit(solution)/shard_map/ppermute | solution.py:29
  283.3 25.4 %collective-permute-start.46 = (bf16[128,2048]{1,0:T(8,128)(2,1)S(1)}, bf16[128,2048]{1,0:T(8,128)(2,1)}, u32[]{:S(2)}, u32[]{:S(2)}) collective-permute-start(bf16[128,2048]{1,0:T(8,128)(2,1)S(1)} %add_convert_fusion.11), channel_id=1, source_target_pairs={{0,1},{1,2},{2,3},{3,0},{4,5},{5,6},{6,7},{7,4},{8,9},{9,10},{10,1... | collective-permute-start | bytes 1572872 | tf_op jit(solution)/shard_map/ppermute | solution.py:24
  285.4 25.1 %collective-permute-start.43 = (bf16[128,2048]{1,0:T(8,128)(2,1)}, bf16[128,2048]{1,0:T(8,128)(2,1)}, u32[]{:S(2)}, u32[]{:S(2)}) collective-permute-start(bf16[128,2048]{1,0:T(8,128)(2,1)} %add_convert_fusion.12), channel_id=1, source_target_pairs={{0,1},{1,2},{2,3},{3,0},{4,5},{5,6},{6,7},{7,4},{8,9},{9,10},{10,1... | collective-permute-start | bytes 1572872 | tf_op jit(solution)/shard_map/ppermute | solution.py:24
  317.6 24.4 %collective-permute-start.48 = (bf16[128,2048]{1,0:T(8,128)(2,1)}, bf16[128,2048]{1,0:T(8,128)(2,1)S(1)}, u32[]{:S(2)}, u32[]{:S(2)}) collective-permute-start(bf16[128,2048]{1,0:T(8,128)(2,1)} %add_convert_fusion.10), channel_id=1, source_target_pairs={{0,1},{1,2},{2,3},{3,0},{4,5},{5,6},{6,7},{7,4},{8,9},{9,10},{10,1... | collective-permute-start | bytes 1572872 | tf_op jit(solution)/shard_map/ppermute | solution.py:24
  344.5 28.4 %collective-permute-start.56 = (bf16[512,1024]{1,0:T(8,128)(2,1)}, bf16[512,1024]{1,0:T(8,128)(2,1)}, u32[]{:S(2)}, u32[]{:S(2)}) collective-permute-start(bf16[512,1024]{1,0:T(8,128)(2,1)} %get-tuple-element.362), channel_id=1, source_target_pairs={{0,8},{8,0},{16,24},{24,16},{1,9},{9,1},{17,25},{25,17},{2,10},{10... | collective-permute-start | bytes 3145736 | tf_op jit(solution)/shard_map/ppermute | solution.py:29
  346.0 26.8 %collective-permute-start.58 = (bf16[512,1024]{1,0:T(8,128)(2,1)}, bf16[512,1024]{1,0:T(8,128)(2,1)}, u32[]{:S(2)}, u32[]{:S(2)}) collective-permute-start(bf16[512,1024]{1,0:T(8,128)(2,1)} %get-tuple-element.366), channel_id=1, source_target_pairs={{0,16},{8,24},{16,0},{24,8},{1,17},{9,25},{17,1},{25,9},{2,18},{10... | collective-permute-start | bytes 3145736 | tf_op jit(solution)/shard_map/ppermute | solution.py:29
  380.4 25.0 %collective-permute-start.61 = (bf16[512,1024]{1,0:T(8,128)(2,1)}, bf16[512,1024]{1,0:T(8,128)(2,1)}, u32[]{:S(2)}, u32[]{:S(2)}) collective-permute-start(bf16[512,1024]{1,0:T(8,128)(2,1)} %add_convert_fusion.3), channel_id=1, source_target_pairs={{0,16},{8,24},{16,0},{24,8},{1,17},{9,25},{17,1},{25,9},{2,18},{10... | collective-permute-start | bytes 3145736 | tf_op jit(solution)/shard_map/ppermute | solution.py:29
  380.7 24.7 %collective-permute-start.62 = (bf16[512,1024]{1,0:T(8,128)(2,1)}, bf16[512,1024]{1,0:T(8,128)(2,1)}, u32[]{:S(2)}, u32[]{:S(2)}) collective-permute-start(bf16[512,1024]{1,0:T(8,128)(2,1)} %get-tuple-element.379), channel_id=1, source_target_pairs={{0,8},{8,0},{16,24},{24,16},{1,9},{9,1},{17,25},{25,17},{2,10},{10... | collective-permute-start | bytes 3145736 | tf_op jit(solution)/shard_map/ppermute | solution.py:29
  382.2 32.3 %collective-permute-start.59 = (bf16[128,2048]{1,0:T(8,128)(2,1)}, bf16[128,2048]{1,0:T(8,128)(2,1)}, u32[]{:S(2)}, u32[]{:S(2)}) collective-permute-start(bf16[128,2048]{1,0:T(8,128)(2,1)} %add_convert_fusion.7), channel_id=1, source_target_pairs={{0,1},{1,2},{2,3},{3,0},{4,5},{5,6},{6,7},{7,4},{8,9},{9,10},{10,1... | collective-permute-start | bytes 1572872 | tf_op jit(solution)/shard_map/ppermute | solution.py:24
  405.4 38.7 %collective-permute-start.67 = (bf16[512,1024]{1,0:T(8,128)(2,1)}, bf16[512,1024]{1,0:T(8,128)(2,1)}, u32[]{:S(2)}, u32[]{:S(2)}) collective-permute-start(bf16[512,1024]{1,0:T(8,128)(2,1)} %get-tuple-element.406), channel_id=1, source_target_pairs={{0,8},{8,0},{16,24},{24,16},{1,9},{9,1},{17,25},{25,17},{2,10},{10... | collective-permute-start | bytes 3145736 | tf_op jit(solution)/shard_map/ppermute | solution.py:29
  420.9 33.3 %collective-permute-start.71 = (bf16[512,1024]{1,0:T(8,128)(2,1)}, bf16[512,1024]{1,0:T(8,128)(2,1)}, u32[]{:S(2)}, u32[]{:S(2)}) collective-permute-start(bf16[512,1024]{1,0:T(8,128)(2,1)} %add_convert_fusion.2), channel_id=1, source_target_pairs={{0,8},{8,0},{16,24},{24,16},{1,9},{9,1},{17,25},{25,17},{2,10},{10... | collective-permute-start | bytes 3145736 | tf_op jit(solution)/shard_map/ppermute | solution.py:29
  421.4 32.8 %collective-permute-start.72 = (bf16[512,1024]{1,0:T(8,128)(2,1)}, bf16[512,1024]{1,0:T(8,128)(2,1)}, u32[]{:S(2)}, u32[]{:S(2)}) collective-permute-start(bf16[512,1024]{1,0:T(8,128)(2,1)} %get-tuple-element.424), channel_id=1, source_target_pairs={{0,16},{8,24},{16,0},{24,8},{1,17},{9,25},{17,1},{25,9},{2,18},{10... | collective-permute-start | bytes 3145736 | tf_op jit(solution)/shard_map/ppermute | solution.py:29
  456.0 27.0 %collective-permute-start.70 = (bf16[128,2048]{1,0:T(8,128)(2,1)}, bf16[128,2048]{1,0:T(8,128)(2,1)}, u32[]{:S(2)}, u32[]{:S(2)}) collective-permute-start(bf16[128,2048]{1,0:T(8,128)(2,1)} %get-tuple-element.408), channel_id=1, source_target_pairs={{0,4},{4,0},{1,5},{5,1},{2,6},{6,2},{3,7},{7,3},{8,12},{12,8},{9,1... | collective-permute-start | bytes 1572872 | tf_op jit(solution)/shard_map/ppermute | solution.py:29
  461.1 51.4 %collective-permute-start.81 = (bf16[512,1024]{1,0:T(8,128)(2,1)}, bf16[512,1024]{1,0:T(8,128)(2,1)}, u32[]{:S(2)}, u32[]{:S(2)}) collective-permute-start(bf16[512,1024]{1,0:T(8,128)(2,1)} %add_convert_fusion), channel_id=1, source_target_pairs={{0,16},{8,24},{16,0},{24,8},{1,17},{9,25},{17,1},{25,9},{2,18},{10... | collective-permute-start | bytes 3145736 | tf_op jit(solution)/shard_map/ppermute | solution.py:29
  479.1 33.4 %collective-permute-start.82 = (bf16[512,1024]{1,0:T(8,128)(2,1)}, bf16[512,1024]{1,0:T(8,128)(2,1)S(1)}, u32[]{:S(2)}, u32[]{:S(2)}) collective-permute-start(bf16[512,1024]{1,0:T(8,128)(2,1)} %get-tuple-element.456), channel_id=1, source_target_pairs={{0,8},{8,0},{16,24},{24,16},{1,9},{9,1},{17,25},{25,17},{2,10},{10... | collective-permute-start | bytes 3145736 | tf_op jit(solution)/shard_map/ppermute | solution.py:29
  482.3 26.6 %collective-permute-start.80 = (bf16[512,1024]{1,0:T(8,128)(2,1)S(1)}, bf16[512,1024]{1,0:T(8,128)(2,1)S(1)}, u32[]{:S(2)}, u32[]{:S(2)}) collective-permute-start(bf16[512,1024]{1,0:T(8,128)(2,1)S(1)} %copy-done.78), channel_id=1, source_target_pairs={{0,16},{8,24},{16,0},{24,8},{1,17},{9,25},{17,1},{25,9},{2,18},{10... | collective-permute-start | bytes 3145736 | tf_op jit(solution)/shard_map/ppermute | solution.py:29
  484.6 27.9 %collective-permute-start.83 = (bf16[128,1024]{1,0:T(8,128)(2,1)}, bf16[128,1024]{1,0:T(8,128)(2,1)S(1)}, u32[]{:S(2)}, u32[]{:S(2)}) collective-permute-start(bf16[128,1024]{1,0:T(8,128)(2,1)} %get-tuple-element.451), channel_id=1, source_target_pairs={{0,1},{1,2},{2,3},{3,0},{4,5},{5,6},{6,7},{7,4},{8,9},{9,10},{10,1... | collective-permute-start | bytes 786440 | tf_op jit(solution)/shard_map/ppermute | solution.py:24
  516.1 24.6 %collective-permute-start.87 = (bf16[128,2048]{1,0:T(8,128)(2,1)S(1)}, bf16[128,2048]{1,0:T(8,128)(2,1)S(1)}, u32[]{:S(2)}, u32[]{:S(2)}) collective-permute-start(bf16[128,2048]{1,0:T(8,128)(2,1)S(1)} %add_convert_fusion.4), channel_id=1, source_target_pairs={{0,1},{1,2},{2,3},{3,0},{4,5},{5,6},{6,7},{7,4},{8,9},{9,10},{10,1... | collective-permute-start | bytes 1572872 | tf_op jit(solution)/shard_map/ppermute | solution.py:24
  517.2 23.5 %collective-permute-start.90 = (bf16[128,1024]{1,0:T(8,128)(2,1)S(1)}, bf16[128,1024]{1,0:T(8,128)(2,1)S(1)}, u32[]{:S(2)}, u32[]{:S(2)}) collective-permute-start(bf16[128,1024]{1,0:T(8,128)(2,1)S(1)} %get-tuple-element.466), channel_id=1, source_target_pairs={{0,2},{1,3},{2,0},{3,1},{4,6},{5,7},{6,4},{7,5},{8,10},{9,11},{10,... | collective-permute-start | bytes 786440 | tf_op jit(solution)/shard_map/ppermute | solution.py:24
  544.6 35.4 %collective-permute-start.97 = (bf16[128,1024]{1,0:T(8,128)(2,1)S(1)}, bf16[128,1024]{1,0:T(8,128)(2,1)S(1)}, u32[]{:S(2)}, u32[]{:S(2)}) collective-permute-start(bf16[128,1024]{1,0:T(8,128)(2,1)S(1)} %get-tuple-element.472), channel_id=1, source_target_pairs={{0,1},{1,2},{2,3},{3,0},{4,5},{5,6},{6,7},{7,4},{8,9},{9,10},{10,1... | collective-permute-start | bytes 786440 | tf_op jit(solution)/shard_map/ppermute | solution.py:24
  549.2 35.5 %collective-permute-start.98 = (bf16[128,1024]{1,0:T(8,128)(2,1)S(1)}, bf16[128,1024]{1,0:T(8,128)(2,1)S(1)}, u32[]{:S(2)}, u32[]{:S(2)}) collective-permute-start(bf16[128,1024]{1,0:T(8,128)(2,1)S(1)} %get-tuple-element.473), channel_id=1, source_target_pairs={{0,2},{1,3},{2,0},{3,1},{4,6},{5,7},{6,4},{7,5},{8,10},{9,11},{10,... | collective-permute-start | bytes 786440 | tf_op jit(solution)/shard_map/ppermute | solution.py:24
  551.8 37.3 %collective-permute-start.99 = (bf16[128,1024]{1,0:T(8,128)(2,1)S(1)}, bf16[128,1024]{1,0:T(8,128)(2,1)S(1)}, u32[]{:S(2)}, u32[]{:S(2)}) collective-permute-start(bf16[128,1024]{1,0:T(8,128)(2,1)S(1)} %get-tuple-element.474), channel_id=1, source_target_pairs={{0,3},{1,0},{2,1},{3,2},{4,7},{5,4},{6,5},{7,6},{8,11},{9,8},{10,9... | collective-permute-start | bytes 786440 | tf_op jit(solution)/shard_map/ppermute | solution.py:24
  563.1 28.2 %collective-permute-start.91 = (bf16[128,2048]{1,0:T(8,128)(2,1)S(1)}, bf16[128,2048]{1,0:T(8,128)(2,1)S(1)}, u32[]{:S(2)}, u32[]{:S(2)}) collective-permute-start(bf16[128,2048]{1,0:T(8,128)(2,1)S(1)} %copy-done.79), channel_id=1, source_target_pairs={{0,4},{4,0},{1,5},{5,1},{2,6},{6,2},{3,7},{7,3},{8,12},{12,8},{9,1... | collective-permute-start | bytes 1572872 | tf_op jit(solution)/shard_map/ppermute | solution.py:29
  563.2 26.1 %collective-permute-start.94 = (f32[2,512]{1,0:T(2,128)S(1)}, f32[2,512]{1,0:T(2,128)S(1)}, u32[]{:S(2)}, u32[]{:S(2)}) collective-permute-start(f32[2,512]{1,0:T(2,128)S(1)} %fusion.11), channel_id=1, source_target_pairs={{0,1},{1,2},{2,3},{3,0},{4,5},{5,6},{6,7},{7,4},{8,9},{9,10},{10,1... | collective-permute-start | bytes 12296 | tf_op jit(solution)/shard_map/ppermute | solution.py:24
  (135 other events, 1819.5 us)

commit v5 on v4

--- a/solution.py
+++ b/solution.py
@@ -638,28 +638,27 @@
         return [ks] if block * len(ks) <= most else [[k] for k in ks]
 
     token_blocks = [None] * blks
-    ahead = turn(own_tokens, "blk", 1)
     attn_out.send(1, 2, 3)
     token_blocks[0] = seq_gather(own_tokens)
-    phase.end(ahead, attn_out.got, token_blocks[0])
-
-    moving, part_attn, pair_out.pieces = phase.take(ahead, attn_out.by_rank(), pair_out.pieces)
-    ahead = turn(moving, "blk", 1)
+    phase.end(attn_out.got, token_blocks[0])
+
+    part_attn, moving = phase.take(attn_out.by_rank(), own_tokens)
+    second = turn(moving, "blk", 1)
+    ahead = turn(second, "blk", 1)
     near_x, near_y = swap(part_attn, "slot", 1), swap(part_attn, "slot", 2)
-    pair_out.send(1)
-    phase.end(ahead, near_x, near_y, pair_out.got, pair_out.pieces, down_out.pieces, cos_wide, sin_wide)
-
-    second, moving, near_x, pair_out.pieces = phase.take(moving, ahead, near_x, pair_out.pieces)
+    phase.end(second, ahead, near_x, near_y, pair_out.pieces, down_out.pieces, cos_wide, sin_wide)
+
+    second, moving, near_x, pair_out.pieces = phase.take(second, ahead, near_x, pair_out.pieces)
     ahead = turn(moving, "blk", 1)
     far = swap(near_x, "slot", 2)
-    pair_out.send(3)
+    pair_out.send(1)
     token_blocks[1], token_blocks[2] = seq_gather(second), seq_gather(moving)
     full_attn = [part_attn, near_x, near_y, far]
     phase.end(ahead, far, token_blocks[1:3], pair_out.got)
 
     moving, pair_out.pieces = phase.take(ahead, pair_out.pieces)
     token_blocks[3] = seq_gather(moving)
-    pair_out.send(2)
+    pair_out.send(2, 3)
     got = []
     for ks in [list(range(blks))] if total <= 1024 else [[k] for k in range(blks)]:
         here = slice(ks[0] * block, (ks[-1] + 1) * block)
@@ -742,22 +741,21 @@
     ahead = turn(moving, "blk", 1)
     blocks[2] = seq_gather(moving)
     held = feed(in_order[0], None)
-    phase.end(ahead, blocks[2], held)
+    grads_of[1], outs_of[1] = seq_reduce(grads_of[1]), seq_reduce(outs_of[1])
+    phase.end(ahead, blocks[2], held, grads_of[1], outs_of[1])
 
     moving, blocks[2], grads_of[:2], outs_of[:2] = phase.take(ahead, blocks[2], grads_of[:2], outs_of[:2])
-    grads_of[1] = seq_reduce(grads_of[1])
     blocks[3] = seq_gather(moving)
     grad = turn(add_up(grads_of[1]).astype(LOW), "blk", 1)
-    outs_of[1] = seq_reduce(outs_of[1])
     out = turn(add_up(outs_of[1]).astype(LOW), "blk", 1)
     held = feed(in_order[1], held)
-    phase.end(grad, out, held)
+    grads_of[2], outs_of[2] = seq_reduce(grads_of[2]), seq_reduce(outs_of[2])
+    phase.end(grad, out, held, grads_of[2], outs_of[2])
     hidden_mlp, all_cot, activation, *grad_pair = held
 
     grad, grads_of[2], outs_of[2], out, activation, grad_pair[1] = phase.take(
         grad, grads_of[2], outs_of[2], out, activation, grad_pair[1]
     )
-    grads_of[2], outs_of[2] = seq_reduce(grads_of[2]), seq_reduce(outs_of[2])
     grad = turn(add_up([grad, *grads_of[2]]).astype(LOW), "blk", 1)
     out = turn(add_up([out, *outs_of[2]]).astype(LOW), "blk", 1)
     down_terms = weight_terms((all_cot, [activation]))

time: 599 us -> 597 us (level)
  waiting for transfers between devices: 256 us -> 244 us
  starting transfers between devices: 106 us -> 112 us
    ppermute x45, waiting for transfers between devices: 190 us -> 172 us  [turn(): lax.ppermute(value, axis, [(i, (i + by) % count) for i in range(count)])]
    ppermute x45, starting transfers between devices: 69 us -> 77.6 us  [turn(): lax.ppermute(value, axis, [(i, (i + by) % count) for i in range(count)])]
  transfers between devices with their start and end apart: 102 -> 102, of which waited for: 49 -> 51; matrix products, arithmetic and copies ran while one was open for 10% -> 10% of each run, Pallas kernels for 26% -> 26%
where the time goes in v5:
time: 597 us; the launch traced here: 591 us
  waiting for transfers between devices  244 us (41%)
  Pallas kernels  156 us (26%)
  starting transfers between devices  112 us (19%)
  other arithmetic  55.7 us (9%)
  local copies, waits for them, and re-layouts  20.8 us (3%)
    ppermute x45, waiting for transfers between devices, turn(): lax.ppermute(value, axis, [(i, (i + by) % count) for i in range(count)])  172 us
    ppermute x45, starting transfers between devices, turn(): lax.ppermute(value, axis, [(i, (i + by) % count) for i in range(count)])  77.6 us
    ppermute x57, waiting for transfers between devices, swap(): return lax.ppermute(value, axis, [(i, i ^ mask) for i in range(count)])  72 us
    pallas_call x2, Pallas kernels, mlp_blocks(): pl.pallas_call(partial(mlp_kernel, count), grid=(1,), in_specs=[vmem((siz...  43.1 us
    pallas_call x4, Pallas kernels, weight_terms(): pl.pallas_call(partial(weight_kernel, [len(rights) for _, rights in pairs...  35 us
    ppermute x57, starting transfers between devices, swap(): return lax.ppermute(value, axis, [(i, i ^ mask) for i in range(count)])  34.1 us
    pallas_call x2, Pallas kernels, attend_back_blocks(): pl.pallas_call(partial(attend_back_kernel, (total, blks, seqs, size), ks,...  29.7 us
    pallas_call x2, Pallas kernels, attend_blocks(): pl.pallas_call(partial(attend_kernel, (total, blks, seqs, size), ks, widt...  24.7 us
  transfers between devices with their start and end apart: 102, of which 51 were waited for; matrix products, arithmetic and copies ran while one was open for 10% of the time, Pallas kernels for 26%

profile of v5, /device:TPU:0, one launch (start us, length us, event | category | flops | bytes accessed | tf_op | source)
XLA Modules:
  0.0 591.4 jit_solution(11797088629386416331)
XLA Ops:
  3.8 5.0 collective-permute-start.3
  15.0 12.0 %collective-permute-done.1 = bf16[128,1024]{1,0:T(8,128)(2,1)} collective-permute-done((bf16[128,1024]{1,0:T(8,128)(2,1)}, bf16[128,1024]{1,0:T(8,128)(2,1)}, u32[]{:S(2)}, u32[]{:S(2)}) %collective-permute-start.1) | collective-permute-done | bytes 262176 | tf_op jit(solution)/shard_map/ppermute | solution.py:24
  28.0 3.5 collective-permute-done.2
  32.5 2.8 collective-permute-start.4
  42.4 5.0 collective-permute-done.4.refs_2_
  51.7 2.8 rotary_tables.1
  56.3 6.3 %collective-permute-done.5.refs_4_ = bf16[128,2048]{1,0:T(8,128)(2,1)S(1)} collective-permute-done((bf16[128,2048]{1,0:T(8,128)(2,1)S(1)}, bf16[128,2048]{1,0:T(8,128)(2,1)S(1)}, u32[]{:S(2)}, u32[]{:S(2)}) %collective-permute-start.5) | collective-permute-done | bytes 524320 | tf_op jit(solution)/shard_map/ppermute | solution.py:24
  67.0 13.9 %collective-permute-done.10.refs_6_ = bf16[128,2048]{1,0:T(8,128)(2,1)S(1)} collective-permute-done((bf16[128,2048]{1,0:T(8,128)(2,1)S(1)}, bf16[128,2048]{1,0:T(8,128)(2,1)S(1)}, u32[]{:S(2)}, u32[]{:S(2)}) %collective-permute-start.10) | collective-permute-done | bytes 524320 | tf_op jit(solution)/shard_map/ppermute | solution.py:24
  80.8 8.5 %collective-permute-done.12 = bf16[128,2048]{1,0:T(8,128)(2,1)S(1)} collective-permute-done((bf16[128,2048]{1,0:T(8,128)(2,1)S(1)}, bf16[128,2048]{1,0:T(8,128)(2,1)S(1)}, u32[]{:S(2)}, u32[]{:S(2)}) %collective-permute-start.12) | collective-permute-done | bytes 524320 | tf_op jit(solution)/shard_map/ppermute | solution.py:24
  91.6 10.9 %project_qkv.1 = (bf16[1024,2048]{1,0:T(8,128)(2,1)}, bf16[1024,256]{1,0:T(8,128)(2,1)}, bf16[1024,256]{1,0:T(8,128)(2,1)}, bf16[1024,256]{1,0:T(8,128)(2,1)}) custom-call(bf16[128,2048]{1,0:T(8,128)(2,1)} %get-tuple-element.243.refs_0_, bf16[128,2048]{1,0:T(8,128)(2,1)} %copy-done.37, bf16[128,2048]{1,0:T(8,128)(2,1)} %copy-done.38, ...), custom_call_target="tpu_custom_call" | custom-call | flops 1 | bytes 1 | tf_op jit(solution)/shard_map/project_qkv/pallas_call | solution.py:252
  102.4 12.4 %attend_blocks.2 = (bf16[256,256]{1,0:T(8,128)(2,1)}, bf16[256,256]{1,0:T(8,128)(2,1)}, f32[256,128]{1,0:T(8,128)}, f32[256,128]{1,0:T(8,128)}, bf16[128,2048]{1...) custom-call(s32[4]{0:T(128)} %copy-done.2, ...), custom_call_target="tpu_custom_call" | custom-call | flops 1 | bytes 1 | tf_op jit(solution)/shard_map/attend_blocks/pallas_call | solution.py:349
  120.6 10.5 %collective-permute-start.17 = (bf16[128,2048]{1,0:T(8,128)(2,1)S(1)}, bf16[128,2048]{1,0:T(8,128)(2,1)S(1)}, u32[]{:S(2)}, u32[]{:S(2)}) collective-permute-start(bf16[128,2048]{1,0:T(8,128)(2,1)S(1)} %add_convert_fusion.15), channel_id=1, source_target_pairs={{0,1},{1,2},{2,3},{3,0},{4,5},{5,6},{6,7},{7,4},{8,9},{9,10},{10,1... | collective-permute-start | bytes 1572872 | tf_op jit(solution)/shard_map/ppermute | solution.py:24
  133.1 12.4 %attend_blocks.3 = (bf16[256,256]{1,0:T(8,128)(2,1)}, bf16[256,256]{1,0:T(8,128)(2,1)}, f32[256,128]{1,0:T(8,128)}, f32[256,128]{1,0:T(8,128)}, bf16[128,2048]{1...) custom-call(s32[4]{0:T(128)} %copy-done.2, ...), custom_call_target="tpu_custom_call" | custom-call | flops 1 | bytes 1 | tf_op jit(solution)/shard_map/attend_blocks/pallas_call | solution.py:349
  146.5 9.8 %collective-permute-done.21 = bf16[128,1024]{1,0:T(8,128)(2,1)S(1)} collective-permute-done((bf16[128,1024]{1,0:T(8,128)(2,1)S(1)}, bf16[128,1024]{1,0:T(8,128)(2,1)S(1)}, u32[]{:S(2)}, u32[]{:S(2)}) %collective-permute-start.21) | collective-permute-done | bytes 262176 | tf_op jit(solution)/shard_map/ppermute | solution.py:24
  159.9 15.5 %collective-permute-done.22 = bf16[128,2048]{1,0:T(8,128)(2,1)S(1)} collective-permute-done((bf16[128,2048]{1,0:T(8,128)(2,1)}, bf16[128,2048]{1,0:T(8,128)(2,1)S(1)}, u32[]{:S(2)}, u32[]{:S(2)}) %collective-permute-start.22) | collective-permute-done | bytes 524320 | tf_op jit(solution)/shard_map/ppermute | solution.py:24
  176.6 2.8 collective-permute-done.26
  187.6 13.7 %collective-permute-done.29 = bf16[128,1024]{1,0:T(8,128)(2,1)S(1)} collective-permute-done((bf16[128,1024]{1,0:T(8,128)(2,1)S(1)}, bf16[128,1024]{1,0:T(8,128)(2,1)S(1)}, u32[]{:S(2)}, u32[]{:S(2)}) %collective-permute-start.29) | collective-permute-done | bytes 262176 | tf_op jit(solution)/shard_map/ppermute | solution.py:24
  205.4 7.0 %collective-permute-done.31.refs_7_ = bf16[512,1024]{1,0:T(8,128)(2,1)S(1)} collective-permute-done((bf16[512,1024]{1,0:T(8,128)(2,1)}, bf16[512,1024]{1,0:T(8,128)(2,1)S(1)}, u32[]{:S(2)}, u32[]{:S(2)}) %collective-permute-start.31) | collective-permute-done | bytes 1048608 | tf_op jit(solution)/shard_map/ppermute | solution.py:29
  213.3 13.9 %collective-permute-done.30.refs_2_ = bf16[128,4096]{1,0:T(8,128)(2,1)S(1)} collective-permute-done((bf16[128,4096]{1,0:T(8,128)(2,1)S(1)}, bf16[128,4096]{1,0:T(8,128)(2,1)S(1)}, u32[]{:S(2)}, u32[]{:S(2)}) %collective-permute-start.30) | collective-permute-done | bytes 1048608 | tf_op jit(solution)/shard_map/ppermute | solution.py:24
  227.6 7.5 %collective-permute-done.36.refs_13_ = bf16[512,1024]{1,0:T(8,128)(2,1)S(1)} collective-permute-done((bf16[512,1024]{1,0:T(8,128)(2,1)}, bf16[512,1024]{1,0:T(8,128)(2,1)S(1)}, u32[]{:S(2)}, u32[]{:S(2)}) %collective-permute-start.36) | collective-permute-done | bytes 1048608 | tf_op jit(solution)/shard_map/ppermute | solution.py:29
  238.1 10.6 %collective-permute-done.38.refs_15_ = bf16[512,512]{1,0:T(8,128)(2,1)S(1)} collective-permute-done((bf16[512,512]{1,0:T(8,128)(2,1)S(1)}, bf16[512,512]{1,0:T(8,128)(2,1)S(1)}, u32[]{:S(2)}, u32[]{:S(2)}) %collective-permute-start.38) | collective-permute-done | bytes 524320 | tf_op jit(solution)/shard_map/ppermute | solution.py:29
  252.9 21.6 %mlp_blocks.2 = (bf16[1024,2048]{1,0:T(8,128)(2,1)}, bf16[1024,2048]{1,0:T(8,128)(2,1)}, bf16[1024,1024]{1,0:T(8,128)(2,1)}, bf16[1024,1024]{1,0:T(8,128)(2,1)},...) custom-call(bf16[128,4096]{1,0:T(8,128)(2,1)} %copy-done.15, ...), custom_call_target="tpu_custom_call" | custom-call | flops 1 | bytes 1 | tf_op jit(solution)/shard_map/mlp_blocks/pallas_call | solution.py:408
  284.0 21.4 %mlp_blocks.3 = (bf16[1024,2048]{1,0:T(8,128)(2,1)}, bf16[1024,2048]{1,0:T(8,128)(2,1)}, bf16[1024,1024]{1,0:T(8,128)(2,1)}, bf16[1024,1024]{1,0:T(8,128)(2,1)},...) custom-call(bf16[128,4096]{1,0:T(8,128)(2,1)} %collective-permute-do, ...), custom_call_target="tpu_custom_call", output_to_operand_aliasing={{0}: (17, {}), {1}: (18, {}), {2}: (19, {}), {3}: (20, {}),... | custom-call | flops 1 | bytes 1 | tf_op jit(solution)/shard_map/mlp_blocks/pallas_call | solution.py:408
  314.8 8.5 %weight_terms.5 = (bf16[512,1024]{1,0:T(8,128)(2,1)}, bf16[512,1024]{1,0:T(8,128)(2,1)}, bf16[512,1024]{1,0:T(8,128)(2,1)}, bf16[512,1024]{1,0:T(8,128)(2,1)}) custom-call(bf16[1024,2048]{1,0:T(8,128)(2,1)} %get-tuple-element.327.refs_0_, bf16[1024,1024]{1,0:T(8,128)(2,1)} %get-tuple-element.339.refs_1_), custom_call_target="tpu_custom_call" | custom-call | flops 1 | bytes 1 | tf_op jit(solution)/shard_map/weight_terms/pallas_call | solution.py:592
  323.3 8.4 %weight_terms.4 = (bf16[512,1024]{1,0:T(8,128)(2,1)}, bf16[512,1024]{1,0:T(8,128)(2,1)}, bf16[512,1024]{1,0:T(8,128)(2,1)}, bf16[512,1024]{1,0:T(8,128)(2,1)}) custom-call(bf16[1024,2048]{1,0:T(8,128)(2,1)} %get-tuple-element.328.refs_0_, bf16[1024,1024]{1,0:T(8,128)(2,1)} %get-tuple-element.337.refs_1_), custom_call_target="tpu_custom_call" | custom-call | flops 1 | bytes 1 | tf_op jit(solution)/shard_map/weight_terms/pallas_call | solution.py:592
  331.7 5.2 collective-permute-done.49
  341.2 13.9 %collective-permute-done.52 = bf16[128,2048]{1,0:T(8,128)(2,1)S(1)} collective-permute-done((bf16[128,2048]{1,0:T(8,128)(2,1)S(1)}, bf16[128,2048]{1,0:T(8,128)(2,1)S(1)}, u32[]{:S(2)}, u32[]{:S(2)}) %collective-permute-start.52) | collective-permute-done | bytes 524320 | tf_op jit(solution)/shard_map/ppermute | solution.py:24
  356.9 8.4 %weight_terms.6 = (bf16[512,1024]{1,0:T(8,128)(2,1)}, bf16[512,1024]{1,0:T(8,128)(2,1)}, bf16[512,1024]{1,0:T(8,128)(2,1)}, bf16[512,1024]{1,0:T(8,128)(2,1)}) custom-call(bf16[1024,2048]{1,0:T(8,128)(2,1)} %get-tuple-element.327.refs_0_, bf16[1024,1024]{1,0:T(8,128)(2,1)} %get-tuple-element.365.refs_1_), custom_call_target="tpu_custom_call" | custom-call | flops 1 | bytes 1 | tf_op jit(solution)/shard_map/weight_terms/pallas_call | solution.py:592
  367.8 4.7 collective-permute-done.54.refs_18_
  379.5 14.5 %attend_back_blocks.2 = (bf16[1024,2048]{1,0:T(8,128)(2,1)}, f32[1024,256]{1,0:T(8,128)}, f32[1024,256]{1,0:T(8,128)}, bf16[256,256]{1,0:T(8,128)(2,1)}, bf16[256,256]{1,0:T(8,128)(2,1)}) custom-call(s32[4]{0:T(128)} %copy-done.2, bf16[1024,256]{1,0:T(8,128)(2,1)} %get-tuple-element.274.refs_0_.refs_1_, ...), custom_call_target="tpu_custom_call" | custom-call | flops 1 | bytes 1 | tf_op jit(solution)/shard_map/attend_back_blocks/pallas_call | solution.py:489
  394.0 5.8 collective-permute-done.61
  401.6 2.9 add_convert_fusion.2
  406.0 2.9 add_convert_fusion.28
  408.9 6.5 %collective-permute-done.64.refs_18_ = bf16[128,2048]{1,0:T(8,128)(2,1)} collective-permute-done((bf16[128,2048]{1,0:T(8,128)(2,1)}, bf16[128,2048]{1,0:T(8,128)(2,1)}, u32[]{:S(2)}, u32[]{:S(2)}) %collective-permute-start.64) | collective-permute-done | bytes 524320 | tf_op jit(solution)/shard_map/ppermute | solution.py:24
  418.9 15.2 %attend_back_blocks.3 = (bf16[1024,2048]{1,0:T(8,128)(2,1)}, f32[1024,256]{1,0:T(8,128)}, f32[1024,256]{1,0:T(8,128)}, bf16[256,256]{1,0:T(8,128)(2,1)}, bf16[256,256]{1,0:T(8,128)(2,1)}) custom-call(s32[4]{0:T(128)} %copy-done.2, ...), custom_call_target="tpu_custom_call", output_to_operand_aliasing={{0}: (21, {}), {1}: (22, {}), {2}: (23, {})} | custom-call | flops 1 | bytes 1 | tf_op jit(solution)/shard_map/attend_back_blocks/pallas_call | solution.py:489
  434.1 4.7 collective-permute-done.69
  438.8 10.0 %finish_blocks.1 = (bf16[256,768]{1,0:T(8,128)(2,1)}, bf16[256,768]{1,0:T(8,128)(2,1)}, bf16[256,768]{1,0:T(8,128)(2,1)}, bf16[256,768]{1,0:T(8,128)(2,1)}, f32[...) custom-call(bf16[256,256]{1,0:T(8,128)(2,1)} %get-tuple-element.407., ...), custom_call_target="tpu_custom_call" | custom-call | flops 1 | bytes 1 | tf_op jit(solution)/shard_map/finish_blocks/pallas_call | solution.py:553
  460.7 2.9 add_convert_fusion.24
  463.6 9.7 %weight_terms.7 = (bf16[512,1024]{1,0:T(8,128)(2,1)}, bf16[512,1024]{1,0:T(8,128)(2,1)}, bf16[512,1024]{1,0:T(8,128)(2,1)}, bf16[512,1024]{1,0:T(8,128)(2,1)}) custom-call(bf16[1024,2048]{1,0:T(8,128)(2,1)} %get-tuple-element.412.refs_24_.refs_25_.refs_26_.refs_27_.refs_0_, bf16[256,768]{1,0:T(8,128)(2,1)} %get-tuple-element.434.refs_1_, ...), custom_call_target="tpu_custom_call" | custom-call | flops 1 | bytes 1 | tf_op jit(solution)/shard_map/weight_terms/pallas_call | solution.py:592
  482.1 13.4 %collective-permute-done.79 = bf16[128,2048]{1,0:T(8,128)(2,1)S(1)} collective-permute-done((bf16[128,2048]{1,0:T(8,128)(2,1)S(1)}, bf16[128,2048]{1,0:T(8,128)(2,1)S(1)}, u32[]{:S(2)}, u32[]{:S(2)}) %collective-permute-start.79) | collective-permute-done | bytes 524320 | tf_op jit(solution)/shard_map/ppermute | solution.py:24
  496.7 3.8 collective-permute-done.85
  502.1 3.0 collective-permute-done.80
  513.4 2.8 collective-permute-start.90
  517.5 14.8 %collective-permute-done.88 = bf16[512,1024]{1,0:T(8,128)(2,1)S(1)} collective-permute-done((bf16[512,1024]{1,0:T(8,128)(2,1)S(1)}, bf16[512,1024]{1,0:T(8,128)(2,1)S(1)}, u32[]{:S(2)}, u32[]{:S(2)}) %collective-permute-start.88) | collective-permute-done | bytes 1048608 | tf_op jit(solution)/shard_map/ppermute | solution.py:29
  549.5 9.3 %collective-permute-done.100 = bf16[128,1024]{1,0:T(8,128)(2,1)S(1)} collective-permute-done((bf16[128,1024]{1,0:T(8,128)(2,1)S(1)}, bf16[128,1024]{1,0:T(8,128)(2,1)S(1)}, u32[]{:S(2)}, u32[]{:S(2)}) %collective-permute-start.100) | collective-permute-done | bytes 262176 | tf_op jit(solution)/shard_map/ppermute | solution.py:24
  558.9 16.4 %collective-permute-start.94 = (f32[2,512]{1,0:T(2,128)S(1)}, f32[2,512]{1,0:T(2,128)S(1)}, u32[]{:S(2)}, u32[]{:S(2)}) collective-permute-start(f32[2,512]{1,0:T(2,128)S(1)} %fusion.11), channel_id=1, source_target_pairs={{0,1},{1,2},{2,3},{3,0},{4,5},{5,6},{6,7},{7,4},{8,9},{9,10},{10,1... | collective-permute-start | bytes 12296 | tf_op jit(solution)/shard_map/ppermute | solution.py:24
  575.7 3.2 collective-permute-start.95
  580.4 4.2 collective-permute-start.96
  (441 shorter events, 163.4 us)
Async XLA Ops:
  3.8 28.6 %collective-permute-start.3 = (bf16[128,1024]{1,0:T(8,128)(2,1)}, bf16[128,1024]{1,0:T(8,128)(2,1)S(1)}, u32[]{:S(2)}, u32[]{:S(2)}) collective-permute-start(bf16[128,1024]{1,0:T(8,128)(2,1)} %pad_maximum_fusion.10), channel_id=1, source_target_pairs={{0,3},{1,0},{2,1},{3,2},{4,7},{5,4},{6,5},{7,6},{8,11},{9,8},{10,9... | collective-permute-start | bytes 786440 | tf_op jit(solution)/shard_map/ppermute | solution.py:24
  35.4 27.2 %collective-permute-start.6 = (bf16[512,1024]{1,0:T(8,128)(2,1)S(1)}, bf16[512,1024]{1,0:T(8,128)(2,1)S(1)}, u32[]{:S(2)}, u32[]{:S(2)}) collective-permute-start(bf16[512,1024]{1,0:T(8,128)(2,1)S(1)} %constant_dynamic-update-slice_fusion.4.refs_8_.refs_4_.refs_12_.refs_20_), channel_id=1, source_target_pairs={{0,8},{8,0},{16,24},{24,16},{1,9},{9,1},{17,25},{25,17},{2,10},{10... | collective-permute-start | bytes 3145736 | tf_op jit(solution)/shard_map/ppermute | solution.py:29
  36.9 25.7 %collective-permute-start.7 = (bf16[512,1024]{1,0:T(8,128)(2,1)S(1)}, bf16[512,1024]{1,0:T(8,128)(2,1)S(1)}, u32[]{:S(2)}, u32[]{:S(2)}) collective-permute-start(bf16[512,1024]{1,0:T(8,128)(2,1)S(1)} %constant_dynamic-update-slice_fusion.4.refs_8_.refs_4_.refs_12_.refs_20_), channel_id=1, source_target_pairs={{0,16},{8,24},{16,0},{24,8},{1,17},{9,25},{17,1},{25,9},{2,18},{10... | collective-permute-start | bytes 3145736 | tf_op jit(solution)/shard_map/ppermute | solution.py:29
  62.6 26.8 %collective-permute-start.11 = (bf16[512,1024]{1,0:T(8,128)(2,1)S(1)}, bf16[512,1024]{1,0:T(8,128)(2,1)S(1)}, u32[]{:S(2)}, u32[]{:S(2)}) collective-permute-start(bf16[512,1024]{1,0:T(8,128)(2,1)S(1)} %collective-permute-done.6.refs_9_.refs_5_.refs_13_.refs_21_), channel_id=1, source_target_pairs={{0,16},{8,24},{16,0},{24,8},{1,17},{9,25},{17,1},{25,9},{2,18},{10... | collective-permute-start | bytes 3145736 | tf_op jit(solution)/shard_map/ppermute | solution.py:29
  65.4 24.0 %collective-permute-start.12 = (bf16[128,2048]{1,0:T(8,128)(2,1)S(1)}, bf16[128,2048]{1,0:T(8,128)(2,1)S(1)}, u32[]{:S(2)}, u32[]{:S(2)}) collective-permute-start(bf16[128,2048]{1,0:T(8,128)(2,1)S(1)} %pad_maximum_fusion.3), channel_id=1, source_target_pairs={{0,1},{1,2},{2,3},{3,0},{4,5},{5,6},{6,7},{7,4},{8,9},{9,10},{10,1... | collective-permute-start | bytes 1572872 | tf_op jit(solution)/shard_map/ppermute | solution.py:24
  89.5 25.7 %collective-permute-start.14 = (bf16[128,2048]{1,0:T(8,128)(2,1)}, bf16[128,2048]{1,0:T(8,128)(2,1)}, u32[]{:S(2)}, u32[]{:S(2)}) collective-permute-start(bf16[128,2048]{1,0:T(8,128)(2,1)} %pad_maximum_fusion.4), channel_id=1, source_target_pairs={{0,2},{1,3},{2,0},{3,1},{4,6},{5,7},{6,4},{7,5},{8,10},{9,11},{10,... | collective-permute-start | bytes 1572872 | tf_op jit(solution)/shard_map/ppermute | solution.py:24
  90.2 25.4 %collective-permute-start.15 = (bf16[128,2048]{1,0:T(8,128)(2,1)}, bf16[128,2048]{1,0:T(8,128)(2,1)}, u32[]{:S(2)}, u32[]{:S(2)}) collective-permute-start(bf16[128,2048]{1,0:T(8,128)(2,1)} %pad_maximum_fusion.5), channel_id=1, source_target_pairs={{0,3},{1,0},{2,1},{3,2},{4,7},{5,4},{6,5},{7,6},{8,11},{9,8},{10,9... | collective-permute-start | bytes 1572872 | tf_op jit(solution)/shard_map/ppermute | solution.py:24
  118.4 37.9 %collective-permute-start.19 = (bf16[512,1024]{1,0:T(8,128)(2,1)S(1)}, bf16[512,1024]{1,0:T(8,128)(2,1)}, u32[]{:S(2)}, u32[]{:S(2)}) collective-permute-start(bf16[512,1024]{1,0:T(8,128)(2,1)S(1)} %get-tuple-element.537.refs_4_), channel_id=1, source_target_pairs={{0,8},{8,0},{16,24},{24,16},{1,9},{9,1},{17,25},{25,17},{2,10},{10... | collective-permute-start | bytes 3145736 | tf_op jit(solution)/shard_map/ppermute | solution.py:29
  120.0 36.4 %collective-permute-start.20 = (bf16[512,1024]{1,0:T(8,128)(2,1)S(1)}, bf16[512,1024]{1,0:T(8,128)(2,1)S(1)}, u32[]{:S(2)}, u32[]{:S(2)}) collective-permute-start(bf16[512,1024]{1,0:T(8,128)(2,1)S(1)} %get-tuple-element.537.refs_4_), channel_id=1, source_target_pairs={{0,16},{8,24},{16,0},{24,8},{1,17},{9,25},{17,1},{25,9},{2,18},{10... | collective-permute-start | bytes 3145736 | tf_op jit(solution)/shard_map/ppermute | solution.py:29
  120.5 25.0 %collective-permute-start.18 = (bf16[128,2048]{1,0:T(8,128)(2,1)S(1)}, bf16[128,2048]{1,0:T(8,128)(2,1)S(1)}, u32[]{:S(2)}, u32[]{:S(2)}) collective-permute-start(bf16[128,2048]{1,0:T(8,128)(2,1)S(1)} %copy-done.80), channel_id=1, source_target_pairs={{0,4},{4,0},{1,5},{5,1},{2,6},{6,2},{3,7},{7,3},{8,12},{12,8},{9,1... | collective-permute-start | bytes 1572872 | tf_op jit(solution)/shard_map/ppermute | solution.py:29
  120.6 24.8 %collective-permute-start.17 = (bf16[128,2048]{1,0:T(8,128)(2,1)S(1)}, bf16[128,2048]{1,0:T(8,128)(2,1)S(1)}, u32[]{:S(2)}, u32[]{:S(2)}) collective-permute-start(bf16[128,2048]{1,0:T(8,128)(2,1)S(1)} %add_convert_fusion.15), channel_id=1, source_target_pairs={{0,1},{1,2},{2,3},{3,0},{4,5},{5,6},{6,7},{7,4},{8,9},{9,10},{10,1... | collective-permute-start | bytes 1572872 | tf_op jit(solution)/shard_map/ppermute | solution.py:24
  131.2 25.1 %collective-permute-start.21 = (bf16[128,1024]{1,0:T(8,128)(2,1)S(1)}, bf16[128,1024]{1,0:T(8,128)(2,1)S(1)}, u32[]{:S(2)}, u32[]{:S(2)}) collective-permute-start(bf16[128,1024]{1,0:T(8,128)(2,1)S(1)} %copy-done.70), channel_id=1, source_target_pairs={{0,2},{1,3},{2,0},{3,1},{4,6},{5,7},{6,4},{7,5},{8,10},{9,11},{10,... | collective-permute-start | bytes 786440 | tf_op jit(solution)/shard_map/ppermute | solution.py:24
  156.3 25.3 %collective-permute-start.24 = (bf16[512,1024]{1,0:T(8,128)(2,1)S(1)}, bf16[512,1024]{1,0:T(8,128)(2,1)}, u32[]{:S(2)}, u32[]{:S(2)}) collective-permute-start(bf16[512,1024]{1,0:T(8,128)(2,1)S(1)} %get-tuple-element.282.refs_8_), channel_id=1, source_target_pairs={{0,16},{8,24},{16,0},{24,8},{1,17},{9,25},{17,1},{25,9},{2,18},{10... | collective-permute-start | bytes 3145736 | tf_op jit(solution)/shard_map/ppermute | solution.py:29
  157.9 24.8 %collective-permute-start.25 = (bf16[512,1024]{1,0:T(8,128)(2,1)S(1)}, bf16[512,1024]{1,0:T(8,128)(2,1)S(1)}, u32[]{:S(2)}, u32[]{:S(2)}) collective-permute-start(bf16[512,1024]{1,0:T(8,128)(2,1)S(1)} %get-tuple-element.282.refs_8_), channel_id=1, source_target_pairs={{0,8},{8,0},{16,24},{24,16},{1,9},{9,1},{17,25},{25,17},{2,10},{10... | collective-permute-start | bytes 3145736 | tf_op jit(solution)/shard_map/ppermute | solution.py:29
  186.6 25.8 %collective-permute-start.31 = (bf16[512,1024]{1,0:T(8,128)(2,1)}, bf16[512,1024]{1,0:T(8,128)(2,1)S(1)}, u32[]{:S(2)}, u32[]{:S(2)}) collective-permute-start(bf16[512,1024]{1,0:T(8,128)(2,1)} %collective-permute-done.19.refs_5_), channel_id=1, source_target_pairs={{0,16},{8,24},{16,0},{24,8},{1,17},{9,25},{17,1},{25,9},{2,18},{10... | collective-permute-start | bytes 3145736 | tf_op jit(solution)/shard_map/ppermute | solution.py:29
  187.1 26.2 %collective-permute-start.32 = (bf16[512,1024]{1,0:T(8,128)(2,1)}, bf16[512,1024]{1,0:T(8,128)(2,1)S(1)}, u32[]{:S(2)}, u32[]{:S(2)}) collective-permute-start(bf16[512,1024]{1,0:T(8,128)(2,1)} %collective-permute-done.24.refs_10_), channel_id=1, source_target_pairs={{0,8},{8,0},{16,24},{24,16},{1,9},{9,1},{17,25},{25,17},{2,10},{10... | collective-permute-start | bytes 3145736 | tf_op jit(solution)/shard_map/ppermute | solution.py:29
  203.8 23.4 %collective-permute-start.30 = (bf16[128,4096]{1,0:T(8,128)(2,1)S(1)}, bf16[128,4096]{1,0:T(8,128)(2,1)S(1)}, u32[]{:S(2)}, u32[]{:S(2)}) collective-permute-start(bf16[128,4096]{1,0:T(8,128)(2,1)S(1)} %pad_maximum_fusion.refs_0_), channel_id=1, source_target_pairs={{0,1},{1,2},{2,3},{3,0},{4,5},{5,6},{6,7},{7,4},{8,9},{9,10},{10,1... | collective-permute-start | bytes 3145736 | tf_op jit(solution)/shard_map/ppermute | solution.py:24
  204.0 23.2 %collective-permute-start.33 = (bf16[128,4096]{1,0:T(8,128)(2,1)S(1)}, bf16[128,4096]{1,0:T(8,128)(2,1)S(1)}, u32[]{:S(2)}, u32[]{:S(2)}) collective-permute-start(bf16[128,4096]{1,0:T(8,128)(2,1)S(1)} %pad_maximum_fusion.refs_0_), channel_id=1, source_target_pairs={{0,4},{4,0},{1,5},{5,1},{2,6},{6,2},{3,7},{7,3},{8,12},{12,8},{9,1... | collective-permute-start | bytes 3145736 | tf_op jit(solution)/shard_map/ppermute | solution.py:29
  204.0 31.1 %collective-permute-start.36 = (bf16[512,1024]{1,0:T(8,128)(2,1)}, bf16[512,1024]{1,0:T(8,128)(2,1)S(1)}, u32[]{:S(2)}, u32[]{:S(2)}) collective-permute-start(bf16[512,1024]{1,0:T(8,128)(2,1)} %constant_dynamic-update-slice_fusion.refs_12_), channel_id=1, source_target_pairs={{0,8},{8,0},{16,24},{24,16},{1,9},{9,1},{17,25},{25,17},{2,10},{10... | collective-permute-start | bytes 3145736 | tf_op jit(solution)/shard_map/ppermute | solution.py:29
  212.4 25.0 %collective-permute-start.37 = (bf16[512,1024]{1,0:T(8,128)(2,1)}, bf16[512,1024]{1,0:T(8,128)(2,1)S(1)}, u32[]{:S(2)}, u32[]{:S(2)}) collective-permute-start(bf16[512,1024]{1,0:T(8,128)(2,1)} %constant_dynamic-update-slice_fusion.refs_12_), channel_id=1, source_target_pairs={{0,16},{8,24},{16,0},{24,8},{1,17},{9,25},{17,1},{25,9},{2,18},{10... | collective-permute-start | bytes 3145736 | tf_op jit(solution)/shard_map/ppermute | solution.py:29
  227.2 24.7 %collective-permute-start.34 = (bf16[128,4096]{1,0:T(8,128)(2,1)S(1)}, bf16[128,4096]{1,0:T(8,128)(2,1)}, u32[]{:S(2)}, u32[]{:S(2)}) collective-permute-start(bf16[128,4096]{1,0:T(8,128)(2,1)S(1)} %collective-permute-done.30.refs_2_), channel_id=1, source_target_pairs={{0,1},{1,2},{2,3},{3,0},{4,5},{5,6},{6,7},{7,4},{8,9},{9,10},{10,1... | collective-permute-start | bytes 3145736 | tf_op jit(solution)/shard_map/ppermute | solution.py:24
  227.6 24.3 %collective-permute-start.35 = (bf16[128,4096]{1,0:T(8,128)(2,1)S(1)}, bf16[128,4096]{1,0:T(8,128)(2,1)S(1)}, u32[]{:S(2)}, u32[]{:S(2)}) collective-permute-start(bf16[128,4096]{1,0:T(8,128)(2,1)S(1)} %collective-permute-done.30.refs_2_), channel_id=1, source_target_pairs={{0,4},{4,0},{1,5},{5,1},{2,6},{6,2},{3,7},{7,3},{8,12},{12,8},{9,1... | collective-permute-start | bytes 3145736 | tf_op jit(solution)/shard_map/ppermute | solution.py:29
  251.9 25.6 %collective-permute-start.40 = (bf16[128,4096]{1,0:T(8,128)(2,1)}, bf16[128,4096]{1,0:T(8,128)(2,1)}, u32[]{:S(2)}, u32[]{:S(2)}) collective-permute-start(bf16[128,4096]{1,0:T(8,128)(2,1)} %collective-permute-done.34.refs_0_), channel_id=1, source_target_pairs={{0,1},{1,2},{2,3},{3,0},{4,5},{5,6},{6,7},{7,4},{8,9},{9,10},{10,1... | collective-permute-start | bytes 3145736 | tf_op jit(solution)/shard_map/ppermute | solution.py:24
  252.9 24.6 %collective-permute-start.41 = (bf16[128,4096]{1,0:T(8,128)(2,1)}, bf16[128,4096]{1,0:T(8,128)(2,1)}, u32[]{:S(2)}, u32[]{:S(2)}) collective-permute-start(bf16[128,4096]{1,0:T(8,128)(2,1)} %collective-permute-done.34.refs_0_), channel_id=1, source_target_pairs={{0,4},{4,0},{1,5},{5,1},{2,6},{6,2},{3,7},{7,3},{8,12},{12,8},{9,1... | collective-permute-start | bytes 3145736 | tf_op jit(solution)/shard_map/ppermute | solution.py:29
  279.1 27.0 %collective-permute-start.48 = (bf16[128,2048]{1,0:T(8,128)(2,1)S(1)}, bf16[128,2048]{1,0:T(8,128)(2,1)}, u32[]{:S(2)}, u32[]{:S(2)}) collective-permute-start(bf16[128,2048]{1,0:T(8,128)(2,1)S(1)} %add_convert_fusion.11), channel_id=1, source_target_pairs={{0,1},{1,2},{2,3},{3,0},{4,5},{5,6},{6,7},{7,4},{8,9},{9,10},{10,1... | collective-permute-start | bytes 1572872 | tf_op jit(solution)/shard_map/ppermute | solution.py:24
  281.6 24.6 %collective-permute-start.44 = (bf16[128,2048]{1,0:T(8,128)(2,1)S(1)}, bf16[128,2048]{1,0:T(8,128)(2,1)}, u32[]{:S(2)}, u32[]{:S(2)}) collective-permute-start(bf16[128,2048]{1,0:T(8,128)(2,1)S(1)} %add_convert_fusion.12), channel_id=1, source_target_pairs={{0,1},{1,2},{2,3},{3,0},{4,5},{5,6},{6,7},{7,4},{8,9},{9,10},{10,1... | collective-permute-start | bytes 1572872 | tf_op jit(solution)/shard_map/ppermute | solution.py:24
  313.8 23.1 %collective-permute-start.49 = (bf16[128,2048]{1,0:T(8,128)(2,1)}, bf16[128,2048]{1,0:T(8,128)(2,1)S(1)}, u32[]{:S(2)}, u32[]{:S(2)}) collective-permute-start(bf16[128,2048]{1,0:T(8,128)(2,1)} %add_convert_fusion.10), channel_id=1, source_target_pairs={{0,1},{1,2},{2,3},{3,0},{4,5},{5,6},{6,7},{7,4},{8,9},{9,10},{10,1... | collective-permute-start | bytes 1572872 | tf_op jit(solution)/shard_map/ppermute | solution.py:24
  339.3 28.4 %collective-permute-start.56 = (bf16[512,1024]{1,0:T(8,128)(2,1)}, bf16[512,1024]{1,0:T(8,128)(2,1)}, u32[]{:S(2)}, u32[]{:S(2)}) collective-permute-start(bf16[512,1024]{1,0:T(8,128)(2,1)} %get-tuple-element.360), channel_id=1, source_target_pairs={{0,8},{8,0},{16,24},{24,16},{1,9},{9,1},{17,25},{25,17},{2,10},{10... | collective-permute-start | bytes 3145736 | tf_op jit(solution)/shard_map/ppermute | solution.py:29
  340.6 27.1 %collective-permute-start.58 = (bf16[512,1024]{1,0:T(8,128)(2,1)}, bf16[512,1024]{1,0:T(8,128)(2,1)}, u32[]{:S(2)}, u32[]{:S(2)}) collective-permute-start(bf16[512,1024]{1,0:T(8,128)(2,1)} %get-tuple-element.364), channel_id=1, source_target_pairs={{0,16},{8,24},{16,0},{24,8},{1,17},{9,25},{17,1},{25,9},{2,18},{10... | collective-permute-start | bytes 3145736 | tf_op jit(solution)/shard_map/ppermute | solution.py:29
  374.9 24.9 %collective-permute-start.61 = (bf16[512,1024]{1,0:T(8,128)(2,1)S(1)}, bf16[512,1024]{1,0:T(8,128)(2,1)}, u32[]{:S(2)}, u32[]{:S(2)}) collective-permute-start(bf16[512,1024]{1,0:T(8,128)(2,1)S(1)} %add_convert_fusion.3), channel_id=1, source_target_pairs={{0,16},{8,24},{16,0},{24,8},{1,17},{9,25},{17,1},{25,9},{2,18},{10... | collective-permute-start | bytes 3145736 | tf_op jit(solution)/shard_map/ppermute | solution.py:29
  375.7 24.7 %collective-permute-start.62 = (bf16[512,1024]{1,0:T(8,128)(2,1)}, bf16[512,1024]{1,0:T(8,128)(2,1)}, u32[]{:S(2)}, u32[]{:S(2)}) collective-permute-start(bf16[512,1024]{1,0:T(8,128)(2,1)} %get-tuple-element.377), channel_id=1, source_target_pairs={{0,8},{8,0},{16,24},{24,16},{1,9},{9,1},{17,25},{25,17},{2,10},{10... | collective-permute-start | bytes 3145736 | tf_op jit(solution)/shard_map/ppermute | solution.py:29
  376.8 32.2 %collective-permute-start.59 = (bf16[128,2048]{1,0:T(8,128)(2,1)}, bf16[128,2048]{1,0:T(8,128)(2,1)}, u32[]{:S(2)}, u32[]{:S(2)}) collective-permute-start(bf16[128,2048]{1,0:T(8,128)(2,1)} %add_convert_fusion.7), channel_id=1, source_target_pairs={{0,1},{1,2},{2,3},{3,0},{4,5},{5,6},{6,7},{7,4},{8,9},{9,10},{10,1... | collective-permute-start | bytes 1572872 | tf_op jit(solution)/shard_map/ppermute | solution.py:24
  400.5 38.3 %collective-permute-start.67 = (bf16[512,1024]{1,0:T(8,128)(2,1)}, bf16[512,1024]{1,0:T(8,128)(2,1)S(1)}, u32[]{:S(2)}, u32[]{:S(2)}) collective-permute-start(bf16[512,1024]{1,0:T(8,128)(2,1)} %get-tuple-element.404), channel_id=1, source_target_pairs={{0,8},{8,0},{16,24},{24,16},{1,9},{9,1},{17,25},{25,17},{2,10},{10... | collective-permute-start | bytes 3145736 | tf_op jit(solution)/shard_map/ppermute | solution.py:29
  415.5 33.4 %collective-permute-start.71 = (bf16[512,1024]{1,0:T(8,128)(2,1)}, bf16[512,1024]{1,0:T(8,128)(2,1)}, u32[]{:S(2)}, u32[]{:S(2)}) collective-permute-start(bf16[512,1024]{1,0:T(8,128)(2,1)} %add_convert_fusion.2), channel_id=1, source_target_pairs={{0,8},{8,0},{16,24},{24,16},{1,9},{9,1},{17,25},{25,17},{2,10},{10... | collective-permute-start | bytes 3145736 | tf_op jit(solution)/shard_map/ppermute | solution.py:29
  416.5 32.5 %collective-permute-start.72 = (bf16[512,1024]{1,0:T(8,128)(2,1)}, bf16[512,1024]{1,0:T(8,128)(2,1)}, u32[]{:S(2)}, u32[]{:S(2)}) collective-permute-start(bf16[512,1024]{1,0:T(8,128)(2,1)} %get-tuple-element.422), channel_id=1, source_target_pairs={{0,16},{8,24},{16,0},{24,8},{1,17},{9,25},{17,1},{25,9},{2,18},{10... | collective-permute-start | bytes 3145736 | tf_op jit(solution)/shard_map/ppermute | solution.py:29
  452.7 26.4 %collective-permute-start.70 = (bf16[128,2048]{1,0:T(8,128)(2,1)}, bf16[128,2048]{1,0:T(8,128)(2,1)}, u32[]{:S(2)}, u32[]{:S(2)}) collective-permute-start(bf16[128,2048]{1,0:T(8,128)(2,1)} %get-tuple-element.406), channel_id=1, source_target_pairs={{0,4},{4,0},{1,5},{5,1},{2,6},{6,2},{3,7},{7,3},{8,12},{12,8},{9,1... | collective-permute-start | bytes 1572872 | tf_op jit(solution)/shard_map/ppermute | solution.py:29
  457.2 51.5 %collective-permute-start.81 = (bf16[512,1024]{1,0:T(8,128)(2,1)}, bf16[512,1024]{1,0:T(8,128)(2,1)S(1)}, u32[]{:S(2)}, u32[]{:S(2)}) collective-permute-start(bf16[512,1024]{1,0:T(8,128)(2,1)} %add_convert_fusion), channel_id=1, source_target_pairs={{0,16},{8,24},{16,0},{24,8},{1,17},{9,25},{17,1},{25,9},{2,18},{10... | collective-permute-start | bytes 3145736 | tf_op jit(solution)/shard_map/ppermute | solution.py:29
  475.3 33.4 %collective-permute-start.82 = (bf16[512,1024]{1,0:T(8,128)(2,1)}, bf16[512,1024]{1,0:T(8,128)(2,1)S(1)}, u32[]{:S(2)}, u32[]{:S(2)}) collective-permute-start(bf16[512,1024]{1,0:T(8,128)(2,1)} %get-tuple-element.454), channel_id=1, source_target_pairs={{0,8},{8,0},{16,24},{24,16},{1,9},{9,1},{17,25},{25,17},{2,10},{10... | collective-permute-start | bytes 3145736 | tf_op jit(solution)/shard_map/ppermute | solution.py:29
  478.2 26.9 %collective-permute-start.80 = (bf16[512,1024]{1,0:T(8,128)(2,1)S(1)}, bf16[512,1024]{1,0:T(8,128)(2,1)S(1)}, u32[]{:S(2)}, u32[]{:S(2)}) collective-permute-start(bf16[512,1024]{1,0:T(8,128)(2,1)S(1)} %copy-done.77), channel_id=1, source_target_pairs={{0,16},{8,24},{16,0},{24,8},{1,17},{9,25},{17,1},{25,9},{2,18},{10... | collective-permute-start | bytes 3145736 | tf_op jit(solution)/shard_map/ppermute | solution.py:29
  480.7 28.0 %collective-permute-start.83 = (bf16[128,1024]{1,0:T(8,128)(2,1)}, bf16[128,1024]{1,0:T(8,128)(2,1)S(1)}, u32[]{:S(2)}, u32[]{:S(2)}) collective-permute-start(bf16[128,1024]{1,0:T(8,128)(2,1)} %get-tuple-element.449), channel_id=1, source_target_pairs={{0,1},{1,2},{2,3},{3,0},{4,5},{5,6},{6,7},{7,4},{8,9},{9,10},{10,1... | collective-permute-start | bytes 786440 | tf_op jit(solution)/shard_map/ppermute | solution.py:24
  508.7 23.6 %collective-permute-start.88 = (bf16[512,1024]{1,0:T(8,128)(2,1)S(1)}, bf16[512,1024]{1,0:T(8,128)(2,1)S(1)}, u32[]{:S(2)}, u32[]{:S(2)}) collective-permute-start(bf16[512,1024]{1,0:T(8,128)(2,1)S(1)} %add_convert_fusion.1), channel_id=1, source_target_pairs={{0,8},{8,0},{16,24},{24,16},{1,9},{9,1},{17,25},{25,17},{2,10},{10... | collective-permute-start | bytes 3145736 | tf_op jit(solution)/shard_map/ppermute | solution.py:29
  510.0 23.2 %collective-permute-start.89 = (bf16[512,1024]{1,0:T(8,128)(2,1)S(1)}, bf16[512,1024]{1,0:T(8,128)(2,1)S(1)}, u32[]{:S(2)}, u32[]{:S(2)}) collective-permute-start(bf16[512,1024]{1,0:T(8,128)(2,1)S(1)} %copy-done.76), channel_id=1, source_target_pairs={{0,16},{8,24},{16,0},{24,8},{1,17},{9,25},{17,1},{25,9},{2,18},{10... | collective-permute-start | bytes 3145736 | tf_op jit(solution)/shard_map/ppermute | solution.py:29
  511.8 24.6 %collective-permute-start.87 = (bf16[128,2048]{1,0:T(8,128)(2,1)S(1)}, bf16[128,2048]{1,0:T(8,128)(2,1)S(1)}, u32[]{:S(2)}, u32[]{:S(2)}) collective-permute-start(bf16[128,2048]{1,0:T(8,128)(2,1)S(1)} %add_convert_fusion.4), channel_id=1, source_target_pairs={{0,1},{1,2},{2,3},{3,0},{4,5},{5,6},{6,7},{7,4},{8,9},{9,10},{10,1... | collective-permute-start | bytes 1572872 | tf_op jit(solution)/shard_map/ppermute | solution.py:24
  540.3 35.4 %collective-permute-start.97 = (bf16[128,1024]{1,0:T(8,128)(2,1)S(1)}, bf16[128,1024]{1,0:T(8,128)(2,1)S(1)}, u32[]{:S(2)}, u32[]{:S(2)}) collective-permute-start(bf16[128,1024]{1,0:T(8,128)(2,1)S(1)} %get-tuple-element.470), channel_id=1, source_target_pairs={{0,1},{1,2},{2,3},{3,0},{4,5},{5,6},{6,7},{7,4},{8,9},{9,10},{10,1... | collective-permute-start | bytes 786440 | tf_op jit(solution)/shard_map/ppermute | solution.py:24
  544.9 35.5 %collective-permute-start.98 = (bf16[128,1024]{1,0:T(8,128)(2,1)S(1)}, bf16[128,1024]{1,0:T(8,128)(2,1)S(1)}, u32[]{:S(2)}, u32[]{:S(2)}) collective-permute-start(bf16[128,1024]{1,0:T(8,128)(2,1)S(1)} %get-tuple-element.471), channel_id=1, source_target_pairs={{0,2},{1,3},{2,0},{3,1},{4,6},{5,7},{6,4},{7,5},{8,10},{9,11},{10,... | collective-permute-start | bytes 786440 | tf_op jit(solution)/shard_map/ppermute | solution.py:24
  547.6 37.3 %collective-permute-start.99 = (bf16[128,1024]{1,0:T(8,128)(2,1)S(1)}, bf16[128,1024]{1,0:T(8,128)(2,1)S(1)}, u32[]{:S(2)}, u32[]{:S(2)}) collective-permute-start(bf16[128,1024]{1,0:T(8,128)(2,1)S(1)} %get-tuple-element.472), channel_id=1, source_target_pairs={{0,3},{1,0},{2,1},{3,2},{4,7},{5,4},{6,5},{7,6},{8,11},{9,8},{10,9... | collective-permute-start | bytes 786440 | tf_op jit(solution)/shard_map/ppermute | solution.py:24
  558.8 28.2 %collective-permute-start.91 = (bf16[128,2048]{1,0:T(8,128)(2,1)S(1)}, bf16[128,2048]{1,0:T(8,128)(2,1)S(1)}, u32[]{:S(2)}, u32[]{:S(2)}) collective-permute-start(bf16[128,2048]{1,0:T(8,128)(2,1)S(1)} %copy-done.78), channel_id=1, source_target_pairs={{0,4},{4,0},{1,5},{5,1},{2,6},{6,2},{3,7},{7,3},{8,12},{12,8},{9,1... | collective-permute-start | bytes 1572872 | tf_op jit(solution)/shard_map/ppermute | solution.py:29
  558.9 26.1 %collective-permute-start.94 = (f32[2,512]{1,0:T(2,128)S(1)}, f32[2,512]{1,0:T(2,128)S(1)}, u32[]{:S(2)}, u32[]{:S(2)}) collective-permute-start(f32[2,512]{1,0:T(2,128)S(1)} %fusion.11), channel_id=1, source_target_pairs={{0,1},{1,2},{2,3},{3,0},{4,5},{5,6},{6,7},{7,4},{8,9},{9,10},{10,1... | collective-permute-start | bytes 12296 | tf_op jit(solution)/shard_map/ppermute | solution.py:24
  (136 other events, 1714.1 us)

commit v6 on v5

--- a/solution.py
+++ b/solution.py
@@ -683,7 +683,7 @@
     near_x, near_y = [swap(half_a, "slot", 1)], [swap(half_a, "slot", 2)]
     terms[1] = seq_reduce(terms[1])
     moving = turn(add_up(terms[1]).astype(LOW), "blk", 1)
-    down_out.send(2)
+    down_out.send(1)
     terms[2] = seq_reduce(terms[2])
     attend(in_turn[1], queries)
     phase.end(moving, terms, near_x, near_y, down_out.got)
@@ -694,7 +694,7 @@
     )
     near_x, near_y = near_x + [swap(half_b, "slot", 1)], near_y + [swap(half_b, "slot", 2)]
     moving = turn(moving, "blk", 1)
-    down_out.send(1)
+    down_out.send(2)
     terms[3] = seq_reduce(terms[3])
     phase.end(moving, terms[3], near_x, near_y, down_out.got)
 

time: 597 us -> 597 us (level)
  waiting for transfers between devices: 244 us -> 238 us
  transfers between devices with their start and end apart: 102 -> 102, of which waited for: 51 -> 50; matrix products, arithmetic and copies ran while one was open for 10% -> 10% of each run, Pallas kernels for 26% -> 26%
where the time goes in v6:
time: 597 us; the launch traced here: 591 us
  waiting for transfers between devices  238 us (40%)
  Pallas kernels  156 us (26%)
  starting transfers between devices  117 us (20%)
  other arithmetic  55.7 us (9%)
  local copies, waits for them, and re-layouts  20.9 us (4%)
    ppermute x45, waiting for transfers between devices, turn(): lax.ppermute(value, axis, [(i, (i + by) % count) for i in range(count)])  171 us
    ppermute x45, starting transfers between devices, turn(): lax.ppermute(value, axis, [(i, (i + by) % count) for i in range(count)])  80.6 us
    ppermute x57, waiting for transfers between devices, swap(): return lax.ppermute(value, axis, [(i, i ^ mask) for i in range(count)])  67.1 us
    pallas_call x2, Pallas kernels, mlp_blocks(): pl.pallas_call(partial(mlp_kernel, count), grid=(1,), in_specs=[vmem((siz...  43 us
    ppermute x57, starting transfers between devices, swap(): return lax.ppermute(value, axis, [(i, i ^ mask) for i in range(count)])  36.7 us
    pallas_call x4, Pallas kernels, weight_terms(): pl.pallas_call(partial(weight_kernel, [len(rights) for _, rights in pairs...  35 us
    pallas_call x2, Pallas kernels, attend_back_blocks(): pl.pallas_call(partial(attend_back_kernel, (total, blks, seqs, size), ks,...  29.7 us
    pallas_call x2, Pallas kernels, attend_blocks(): pl.pallas_call(partial(attend_kernel, (total, blks, seqs, size), ks, widt...  24.7 us
  transfers between devices with their start and end apart: 102, of which 50 were waited for; matrix products, arithmetic and copies ran while one was open for 10% of the time, Pallas kernels for 26%

profile of v6, /device:TPU:0, one launch (start us, length us, event | category | flops | bytes accessed | tf_op | source)
XLA Modules:
  0.0 591.3 jit_solution(10927642035985763589)
XLA Ops:
  3.8 5.0 collective-permute-start.3
  15.0 12.0 %collective-permute-done.1 = bf16[128,1024]{1,0:T(8,128)(2,1)} collective-permute-done((bf16[128,1024]{1,0:T(8,128)(2,1)}, bf16[128,1024]{1,0:T(8,128)(2,1)}, u32[]{:S(2)}, u32[]{:S(2)}) %collective-permute-start.1) | collective-permute-done | bytes 262176 | tf_op jit(solution)/shard_map/ppermute | solution.py:24
  28.0 3.5 collective-permute-done.2
  42.4 5.0 collective-permute-done.4.refs_2_
  51.7 2.8 rotary_tables.1
  56.3 6.3 %collective-permute-done.5.refs_4_ = bf16[128,2048]{1,0:T(8,128)(2,1)S(1)} collective-permute-done((bf16[128,2048]{1,0:T(8,128)(2,1)S(1)}, bf16[128,2048]{1,0:T(8,128)(2,1)S(1)}, u32[]{:S(2)}, u32[]{:S(2)}) %collective-permute-start.5) | collective-permute-done | bytes 524320 | tf_op jit(solution)/shard_map/ppermute | solution.py:24
  67.0 13.9 %collective-permute-done.10.refs_6_ = bf16[128,2048]{1,0:T(8,128)(2,1)S(1)} collective-permute-done((bf16[128,2048]{1,0:T(8,128)(2,1)S(1)}, bf16[128,2048]{1,0:T(8,128)(2,1)S(1)}, u32[]{:S(2)}, u32[]{:S(2)}) %collective-permute-start.10) | collective-permute-done | bytes 524320 | tf_op jit(solution)/shard_map/ppermute | solution.py:24
  80.8 8.5 %collective-permute-done.12 = bf16[128,2048]{1,0:T(8,128)(2,1)S(1)} collective-permute-done((bf16[128,2048]{1,0:T(8,128)(2,1)S(1)}, bf16[128,2048]{1,0:T(8,128)(2,1)S(1)}, u32[]{:S(2)}, u32[]{:S(2)}) %collective-permute-start.12) | collective-permute-done | bytes 524320 | tf_op jit(solution)/shard_map/ppermute | solution.py:24
  91.6 10.9 %project_qkv.1 = (bf16[1024,2048]{1,0:T(8,128)(2,1)}, bf16[1024,256]{1,0:T(8,128)(2,1)}, bf16[1024,256]{1,0:T(8,128)(2,1)}, bf16[1024,256]{1,0:T(8,128)(2,1)}) custom-call(bf16[128,2048]{1,0:T(8,128)(2,1)} %get-tuple-element.243.refs_0_, bf16[128,2048]{1,0:T(8,128)(2,1)} %copy-done.37, bf16[128,2048]{1,0:T(8,128)(2,1)} %copy-done.38, ...), custom_call_target="tpu_custom_call" | custom-call | flops 1 | bytes 1 | tf_op jit(solution)/shard_map/project_qkv/pallas_call | solution.py:252
  102.4 12.4 %attend_blocks.2 = (bf16[256,256]{1,0:T(8,128)(2,1)}, bf16[256,256]{1,0:T(8,128)(2,1)}, f32[256,128]{1,0:T(8,128)}, f32[256,128]{1,0:T(8,128)}, bf16[128,2048]{1...) custom-call(s32[4]{0:T(128)} %copy-done.2, ...), custom_call_target="tpu_custom_call" | custom-call | flops 1 | bytes 1 | tf_op jit(solution)/shard_map/attend_blocks/pallas_call | solution.py:349
  120.6 10.5 %collective-permute-start.17 = (bf16[128,2048]{1,0:T(8,128)(2,1)S(1)}, bf16[128,2048]{1,0:T(8,128)(2,1)S(1)}, u32[]{:S(2)}, u32[]{:S(2)}) collective-permute-start(bf16[128,2048]{1,0:T(8,128)(2,1)S(1)} %add_convert_fusion.15), channel_id=1, source_target_pairs={{0,1},{1,2},{2,3},{3,0},{4,5},{5,6},{6,7},{7,4},{8,9},{9,10},{10,1... | collective-permute-start | bytes 1572872 | tf_op jit(solution)/shard_map/ppermute | solution.py:24
  131.3 12.4 %attend_blocks.3 = (bf16[256,256]{1,0:T(8,128)(2,1)}, bf16[256,256]{1,0:T(8,128)(2,1)}, f32[256,128]{1,0:T(8,128)}, f32[256,128]{1,0:T(8,128)}, bf16[128,2048]{1...) custom-call(s32[4]{0:T(128)} %copy-done.2, ...), custom_call_target="tpu_custom_call" | custom-call | flops 1 | bytes 1 | tf_op jit(solution)/shard_map/attend_blocks/pallas_call | solution.py:349
  146.3 4.4 collective-permute-done.21
  152.8 4.7 collective-permute-start.22
  159.9 11.3 %collective-permute-done.22 = bf16[128,2048]{1,0:T(8,128)(2,1)S(1)} collective-permute-done((bf16[128,2048]{1,0:T(8,128)(2,1)}, bf16[128,2048]{1,0:T(8,128)(2,1)S(1)}, u32[]{:S(2)}, u32[]{:S(2)}) %collective-permute-start.22) | collective-permute-done | bytes 524320 | tf_op jit(solution)/shard_map/ppermute | solution.py:24
  172.5 8.4 %collective-permute-done.26 = bf16[128,1024]{1,0:T(8,128)(2,1)S(1)} collective-permute-done((bf16[128,1024]{1,0:T(8,128)(2,1)}, bf16[128,1024]{1,0:T(8,128)(2,1)S(1)}, u32[]{:S(2)}, u32[]{:S(2)}) %collective-permute-start.26) | collective-permute-done | bytes 262176 | tf_op jit(solution)/shard_map/ppermute | solution.py:24
  187.3 13.4 %collective-permute-done.29 = bf16[128,1024]{1,0:T(8,128)(2,1)S(1)} collective-permute-done((bf16[128,1024]{1,0:T(8,128)(2,1)S(1)}, bf16[128,1024]{1,0:T(8,128)(2,1)S(1)}, u32[]{:S(2)}, u32[]{:S(2)}) %collective-permute-start.29) | collective-permute-done | bytes 262176 | tf_op jit(solution)/shard_map/ppermute | solution.py:24
  204.3 6.2 %collective-permute-done.31.refs_7_ = bf16[512,1024]{1,0:T(8,128)(2,1)S(1)} collective-permute-done((bf16[512,1024]{1,0:T(8,128)(2,1)}, bf16[512,1024]{1,0:T(8,128)(2,1)S(1)}, u32[]{:S(2)}, u32[]{:S(2)}) %collective-permute-start.31) | collective-permute-done | bytes 1048608 | tf_op jit(solution)/shard_map/ppermute | solution.py:29
  212.2 15.1 %collective-permute-done.30.refs_2_ = bf16[128,4096]{1,0:T(8,128)(2,1)S(1)} collective-permute-done((bf16[128,4096]{1,0:T(8,128)(2,1)S(1)}, bf16[128,4096]{1,0:T(8,128)(2,1)S(1)}, u32[]{:S(2)}, u32[]{:S(2)}) %collective-permute-start.30) | collective-permute-done | bytes 1048608 | tf_op jit(solution)/shard_map/ppermute | solution.py:24
  227.4 6.5 %collective-permute-done.36.refs_13_ = bf16[512,1024]{1,0:T(8,128)(2,1)S(1)} collective-permute-done((bf16[512,1024]{1,0:T(8,128)(2,1)}, bf16[512,1024]{1,0:T(8,128)(2,1)S(1)}, u32[]{:S(2)}, u32[]{:S(2)}) %collective-permute-start.36) | collective-permute-done | bytes 1048608 | tf_op jit(solution)/shard_map/ppermute | solution.py:29
  236.7 10.7 %collective-permute-done.38.refs_15_ = bf16[512,512]{1,0:T(8,128)(2,1)S(1)} collective-permute-done((bf16[512,512]{1,0:T(8,128)(2,1)S(1)}, bf16[512,512]{1,0:T(8,128)(2,1)S(1)}, u32[]{:S(2)}, u32[]{:S(2)}) %collective-permute-start.38) | collective-permute-done | bytes 524320 | tf_op jit(solution)/shard_map/ppermute | solution.py:29
  252.2 21.6 %mlp_blocks.2 = (bf16[1024,2048]{1,0:T(8,128)(2,1)}, bf16[1024,2048]{1,0:T(8,128)(2,1)}, bf16[1024,1024]{1,0:T(8,128)(2,1)}, bf16[1024,1024]{1,0:T(8,128)(2,1)},...) custom-call(bf16[128,4096]{1,0:T(8,128)(2,1)} %copy-done.15, ...), custom_call_target="tpu_custom_call" | custom-call | flops 1 | bytes 1 | tf_op jit(solution)/shard_map/mlp_blocks/pallas_call | solution.py:408
  283.5 21.4 %mlp_blocks.3 = (bf16[1024,2048]{1,0:T(8,128)(2,1)}, bf16[1024,2048]{1,0:T(8,128)(2,1)}, bf16[1024,1024]{1,0:T(8,128)(2,1)}, bf16[1024,1024]{1,0:T(8,128)(2,1)},...) custom-call(bf16[128,4096]{1,0:T(8,128)(2,1)} %collective-permute-do, ...), custom_call_target="tpu_custom_call", output_to_operand_aliasing={{0}: (17, {}), {1}: (18, {}), {2}: (19, {}), {3}: (20, {}),... | custom-call | flops 1 | bytes 1 | tf_op jit(solution)/shard_map/mlp_blocks/pallas_call | solution.py:408
  314.1 8.5 %weight_terms.5 = (bf16[512,1024]{1,0:T(8,128)(2,1)}, bf16[512,1024]{1,0:T(8,128)(2,1)}, bf16[512,1024]{1,0:T(8,128)(2,1)}, bf16[512,1024]{1,0:T(8,128)(2,1)}) custom-call(bf16[1024,2048]{1,0:T(8,128)(2,1)} %get-tuple-element.327.refs_0_, bf16[1024,1024]{1,0:T(8,128)(2,1)} %get-tuple-element.339.refs_1_), custom_call_target="tpu_custom_call" | custom-call | flops 1 | bytes 1 | tf_op jit(solution)/shard_map/weight_terms/pallas_call | solution.py:592
  322.5 8.4 %weight_terms.4 = (bf16[512,1024]{1,0:T(8,128)(2,1)}, bf16[512,1024]{1,0:T(8,128)(2,1)}, bf16[512,1024]{1,0:T(8,128)(2,1)}, bf16[512,1024]{1,0:T(8,128)(2,1)}) custom-call(bf16[1024,2048]{1,0:T(8,128)(2,1)} %get-tuple-element.328.refs_0_, bf16[1024,1024]{1,0:T(8,128)(2,1)} %get-tuple-element.337.refs_1_), custom_call_target="tpu_custom_call" | custom-call | flops 1 | bytes 1 | tf_op jit(solution)/shard_map/weight_terms/pallas_call | solution.py:592
  331.0 5.4 collective-permute-done.49
  341.5 13.1 %collective-permute-done.52 = bf16[128,2048]{1,0:T(8,128)(2,1)S(1)} collective-permute-done((bf16[128,2048]{1,0:T(8,128)(2,1)S(1)}, bf16[128,2048]{1,0:T(8,128)(2,1)S(1)}, u32[]{:S(2)}, u32[]{:S(2)}) %collective-permute-start.52) | collective-permute-done | bytes 524320 | tf_op jit(solution)/shard_map/ppermute | solution.py:24
  356.4 8.4 %weight_terms.6 = (bf16[512,1024]{1,0:T(8,128)(2,1)}, bf16[512,1024]{1,0:T(8,128)(2,1)}, bf16[512,1024]{1,0:T(8,128)(2,1)}, bf16[512,1024]{1,0:T(8,128)(2,1)}) custom-call(bf16[1024,2048]{1,0:T(8,128)(2,1)} %get-tuple-element.327.refs_0_, bf16[1024,1024]{1,0:T(8,128)(2,1)} %get-tuple-element.365.refs_1_), custom_call_target="tpu_custom_call" | custom-call | flops 1 | bytes 1 | tf_op jit(solution)/shard_map/weight_terms/pallas_call | solution.py:592
  367.3 4.7 collective-permute-done.54.refs_18_
  379.7 14.5 %attend_back_blocks.2 = (bf16[1024,2048]{1,0:T(8,128)(2,1)}, f32[1024,256]{1,0:T(8,128)}, f32[1024,256]{1,0:T(8,128)}, bf16[256,256]{1,0:T(8,128)(2,1)}, bf16[256,256]{1,0:T(8,128)(2,1)}) custom-call(s32[4]{0:T(128)} %copy-done.2, bf16[1024,256]{1,0:T(8,128)(2,1)} %get-tuple-element.274.refs_0_.refs_1_, ...), custom_call_target="tpu_custom_call" | custom-call | flops 1 | bytes 1 | tf_op jit(solution)/shard_map/attend_back_blocks/pallas_call | solution.py:489
  394.2 5.0 collective-permute-done.61
  401.8 2.9 add_convert_fusion.2
  406.3 2.9 add_convert_fusion.28
  409.2 6.5 %collective-permute-done.64.refs_18_ = bf16[128,2048]{1,0:T(8,128)(2,1)} collective-permute-done((bf16[128,2048]{1,0:T(8,128)(2,1)}, bf16[128,2048]{1,0:T(8,128)(2,1)}, u32[]{:S(2)}, u32[]{:S(2)}) %collective-permute-start.64) | collective-permute-done | bytes 524320 | tf_op jit(solution)/shard_map/ppermute | solution.py:24
  418.6 15.2 %attend_back_blocks.3 = (bf16[1024,2048]{1,0:T(8,128)(2,1)}, f32[1024,256]{1,0:T(8,128)}, f32[1024,256]{1,0:T(8,128)}, bf16[256,256]{1,0:T(8,128)(2,1)}, bf16[256,256]{1,0:T(8,128)(2,1)}) custom-call(s32[4]{0:T(128)} %copy-done.2, ...), custom_call_target="tpu_custom_call", output_to_operand_aliasing={{0}: (21, {}), {1}: (22, {}), {2}: (23, {})} | custom-call | flops 1 | bytes 1 | tf_op jit(solution)/shard_map/attend_back_blocks/pallas_call | solution.py:489
  433.8 4.8 collective-permute-done.69
  438.6 10.1 %finish_blocks.1 = (bf16[256,768]{1,0:T(8,128)(2,1)}, bf16[256,768]{1,0:T(8,128)(2,1)}, bf16[256,768]{1,0:T(8,128)(2,1)}, bf16[256,768]{1,0:T(8,128)(2,1)}, f32[...) custom-call(bf16[256,256]{1,0:T(8,128)(2,1)} %get-tuple-element.407., ...), custom_call_target="tpu_custom_call" | custom-call | flops 1 | bytes 1 | tf_op jit(solution)/shard_map/finish_blocks/pallas_call | solution.py:553
  460.4 2.9 add_convert_fusion.24
  463.3 9.7 %weight_terms.7 = (bf16[512,1024]{1,0:T(8,128)(2,1)}, bf16[512,1024]{1,0:T(8,128)(2,1)}, bf16[512,1024]{1,0:T(8,128)(2,1)}, bf16[512,1024]{1,0:T(8,128)(2,1)}) custom-call(bf16[1024,2048]{1,0:T(8,128)(2,1)} %get-tuple-element.412.refs_24_.refs_25_.refs_26_.refs_27_.refs_0_, bf16[256,768]{1,0:T(8,128)(2,1)} %get-tuple-element.434.refs_1_, ...), custom_call_target="tpu_custom_call" | custom-call | flops 1 | bytes 1 | tf_op jit(solution)/shard_map/weight_terms/pallas_call | solution.py:592
  482.4 13.3 %collective-permute-done.79 = bf16[128,2048]{1,0:T(8,128)(2,1)S(1)} collective-permute-done((bf16[128,2048]{1,0:T(8,128)(2,1)S(1)}, bf16[128,2048]{1,0:T(8,128)(2,1)S(1)}, u32[]{:S(2)}, u32[]{:S(2)}) %collective-permute-start.79) | collective-permute-done | bytes 524320 | tf_op jit(solution)/shard_map/ppermute | solution.py:24
  496.7 3.3 collective-permute-done.85
  501.6 3.3 collective-permute-done.80
  516.8 15.3 %collective-permute-done.88 = bf16[512,1024]{1,0:T(8,128)(2,1)S(1)} collective-permute-done((bf16[512,1024]{1,0:T(8,128)(2,1)S(1)}, bf16[512,1024]{1,0:T(8,128)(2,1)S(1)}, u32[]{:S(2)}, u32[]{:S(2)}) %collective-permute-start.88) | collective-permute-done | bytes 1048608 | tf_op jit(solution)/shard_map/ppermute | solution.py:29
  533.5 2.9 collective-permute-done.90
  549.5 9.3 %collective-permute-done.100 = bf16[128,1024]{1,0:T(8,128)(2,1)S(1)} collective-permute-done((bf16[128,1024]{1,0:T(8,128)(2,1)S(1)}, bf16[128,1024]{1,0:T(8,128)(2,1)S(1)}, u32[]{:S(2)}, u32[]{:S(2)}) %collective-permute-start.100) | collective-permute-done | bytes 262176 | tf_op jit(solution)/shard_map/ppermute | solution.py:24
  558.9 16.4 %collective-permute-start.94 = (f32[2,512]{1,0:T(2,128)S(1)}, f32[2,512]{1,0:T(2,128)S(1)}, u32[]{:S(2)}, u32[]{:S(2)}) collective-permute-start(f32[2,512]{1,0:T(2,128)S(1)} %fusion.11), channel_id=1, source_target_pairs={{0,1},{1,2},{2,3},{3,0},{4,5},{5,6},{6,7},{7,4},{8,9},{9,10},{10,1... | collective-permute-start | bytes 12296 | tf_op jit(solution)/shard_map/ppermute | solution.py:24
  575.6 3.2 collective-permute-start.95
  580.4 4.2 collective-permute-start.96
  (441 shorter events, 166.9 us)
Async XLA Ops:
  3.8 28.6 %collective-permute-start.3 = (bf16[128,1024]{1,0:T(8,128)(2,1)}, bf16[128,1024]{1,0:T(8,128)(2,1)S(1)}, u32[]{:S(2)}, u32[]{:S(2)}) collective-permute-start(bf16[128,1024]{1,0:T(8,128)(2,1)} %pad_maximum_fusion.10), channel_id=1, source_target_pairs={{0,3},{1,0},{2,1},{3,2},{4,7},{5,4},{6,5},{7,6},{8,11},{9,8},{10,9... | collective-permute-start | bytes 786440 | tf_op jit(solution)/shard_map/ppermute | solution.py:24
  35.4 27.2 %collective-permute-start.6 = (bf16[512,1024]{1,0:T(8,128)(2,1)S(1)}, bf16[512,1024]{1,0:T(8,128)(2,1)S(1)}, u32[]{:S(2)}, u32[]{:S(2)}) collective-permute-start(bf16[512,1024]{1,0:T(8,128)(2,1)S(1)} %constant_dynamic-update-slice_fusion.4.refs_8_.refs_4_.refs_12_.refs_20_), channel_id=1, source_target_pairs={{0,8},{8,0},{16,24},{24,16},{1,9},{9,1},{17,25},{25,17},{2,10},{10... | collective-permute-start | bytes 3145736 | tf_op jit(solution)/shard_map/ppermute | solution.py:29
  36.9 25.7 %collective-permute-start.7 = (bf16[512,1024]{1,0:T(8,128)(2,1)S(1)}, bf16[512,1024]{1,0:T(8,128)(2,1)S(1)}, u32[]{:S(2)}, u32[]{:S(2)}) collective-permute-start(bf16[512,1024]{1,0:T(8,128)(2,1)S(1)} %constant_dynamic-update-slice_fusion.4.refs_8_.refs_4_.refs_12_.refs_20_), channel_id=1, source_target_pairs={{0,16},{8,24},{16,0},{24,8},{1,17},{9,25},{17,1},{25,9},{2,18},{10... | collective-permute-start | bytes 3145736 | tf_op jit(solution)/shard_map/ppermute | solution.py:29
  62.6 26.8 %collective-permute-start.11 = (bf16[512,1024]{1,0:T(8,128)(2,1)S(1)}, bf16[512,1024]{1,0:T(8,128)(2,1)S(1)}, u32[]{:S(2)}, u32[]{:S(2)}) collective-permute-start(bf16[512,1024]{1,0:T(8,128)(2,1)S(1)} %collective-permute-done.6.refs_9_.refs_5_.refs_13_.refs_21_), channel_id=1, source_target_pairs={{0,16},{8,24},{16,0},{24,8},{1,17},{9,25},{17,1},{25,9},{2,18},{10... | collective-permute-start | bytes 3145736 | tf_op jit(solution)/shard_map/ppermute | solution.py:29
  65.4 24.0 %collective-permute-start.12 = (bf16[128,2048]{1,0:T(8,128)(2,1)S(1)}, bf16[128,2048]{1,0:T(8,128)(2,1)S(1)}, u32[]{:S(2)}, u32[]{:S(2)}) collective-permute-start(bf16[128,2048]{1,0:T(8,128)(2,1)S(1)} %pad_maximum_fusion.3), channel_id=1, source_target_pairs={{0,1},{1,2},{2,3},{3,0},{4,5},{5,6},{6,7},{7,4},{8,9},{9,10},{10,1... | collective-permute-start | bytes 1572872 | tf_op jit(solution)/shard_map/ppermute | solution.py:24
  66.5 22.9 %collective-permute-start.9 = (bf16[128,2048]{1,0:T(8,128)(2,1)S(1)}, bf16[128,2048]{1,0:T(8,128)(2,1)S(1)}, u32[]{:S(2)}, u32[]{:S(2)}) collective-permute-start(bf16[128,2048]{1,0:T(8,128)(2,1)S(1)} %collective-permute-done.5.refs_4_), channel_id=1, source_target_pairs={{0,4},{4,0},{1,5},{5,1},{2,6},{6,2},{3,7},{7,3},{8,12},{12,8},{9,1... | collective-permute-start | bytes 1572872 | tf_op jit(solution)/shard_map/ppermute | solution.py:29
  89.5 25.7 %collective-permute-start.14 = (bf16[128,2048]{1,0:T(8,128)(2,1)}, bf16[128,2048]{1,0:T(8,128)(2,1)}, u32[]{:S(2)}, u32[]{:S(2)}) collective-permute-start(bf16[128,2048]{1,0:T(8,128)(2,1)} %pad_maximum_fusion.4), channel_id=1, source_target_pairs={{0,2},{1,3},{2,0},{3,1},{4,6},{5,7},{6,4},{7,5},{8,10},{9,11},{10,... | collective-permute-start | bytes 1572872 | tf_op jit(solution)/shard_map/ppermute | solution.py:24
  90.2 25.4 %collective-permute-start.15 = (bf16[128,2048]{1,0:T(8,128)(2,1)}, bf16[128,2048]{1,0:T(8,128)(2,1)}, u32[]{:S(2)}, u32[]{:S(2)}) collective-permute-start(bf16[128,2048]{1,0:T(8,128)(2,1)} %pad_maximum_fusion.5), channel_id=1, source_target_pairs={{0,3},{1,0},{2,1},{3,2},{4,7},{5,4},{6,5},{7,6},{8,11},{9,8},{10,9... | collective-permute-start | bytes 1572872 | tf_op jit(solution)/shard_map/ppermute | solution.py:24
  118.4 32.3 %collective-permute-start.19 = (bf16[512,1024]{1,0:T(8,128)(2,1)S(1)}, bf16[512,1024]{1,0:T(8,128)(2,1)}, u32[]{:S(2)}, u32[]{:S(2)}) collective-permute-start(bf16[512,1024]{1,0:T(8,128)(2,1)S(1)} %get-tuple-element.537.refs_4_), channel_id=1, source_target_pairs={{0,8},{8,0},{16,24},{24,16},{1,9},{9,1},{17,25},{25,17},{2,10},{10... | collective-permute-start | bytes 3145736 | tf_op jit(solution)/shard_map/ppermute | solution.py:29
  120.0 30.7 %collective-permute-start.20 = (bf16[512,1024]{1,0:T(8,128)(2,1)S(1)}, bf16[512,1024]{1,0:T(8,128)(2,1)S(1)}, u32[]{:S(2)}, u32[]{:S(2)}) collective-permute-start(bf16[512,1024]{1,0:T(8,128)(2,1)S(1)} %get-tuple-element.537.refs_4_), channel_id=1, source_target_pairs={{0,16},{8,24},{16,0},{24,8},{1,17},{9,25},{17,1},{25,9},{2,18},{10... | collective-permute-start | bytes 3145736 | tf_op jit(solution)/shard_map/ppermute | solution.py:29
  120.5 23.1 %collective-permute-start.18 = (bf16[128,2048]{1,0:T(8,128)(2,1)S(1)}, bf16[128,2048]{1,0:T(8,128)(2,1)S(1)}, u32[]{:S(2)}, u32[]{:S(2)}) collective-permute-start(bf16[128,2048]{1,0:T(8,128)(2,1)S(1)} %copy-done.80), channel_id=1, source_target_pairs={{0,4},{4,0},{1,5},{5,1},{2,6},{6,2},{3,7},{7,3},{8,12},{12,8},{9,1... | collective-permute-start | bytes 1572872 | tf_op jit(solution)/shard_map/ppermute | solution.py:29
  120.6 24.6 %collective-permute-start.17 = (bf16[128,2048]{1,0:T(8,128)(2,1)S(1)}, bf16[128,2048]{1,0:T(8,128)(2,1)S(1)}, u32[]{:S(2)}, u32[]{:S(2)}) collective-permute-start(bf16[128,2048]{1,0:T(8,128)(2,1)S(1)} %add_convert_fusion.15), channel_id=1, source_target_pairs={{0,1},{1,2},{2,3},{3,0},{4,5},{5,6},{6,7},{7,4},{8,9},{9,10},{10,1... | collective-permute-start | bytes 1572872 | tf_op jit(solution)/shard_map/ppermute | solution.py:24
  150.7 30.1 %collective-permute-start.24 = (bf16[512,1024]{1,0:T(8,128)(2,1)S(1)}, bf16[512,1024]{1,0:T(8,128)(2,1)}, u32[]{:S(2)}, u32[]{:S(2)}) collective-permute-start(bf16[512,1024]{1,0:T(8,128)(2,1)S(1)} %get-tuple-element.282.refs_8_), channel_id=1, source_target_pairs={{0,16},{8,24},{16,0},{24,8},{1,17},{9,25},{17,1},{25,9},{2,18},{10... | collective-permute-start | bytes 3145736 | tf_op jit(solution)/shard_map/ppermute | solution.py:29
  152.3 28.5 %collective-permute-start.25 = (bf16[512,1024]{1,0:T(8,128)(2,1)S(1)}, bf16[512,1024]{1,0:T(8,128)(2,1)S(1)}, u32[]{:S(2)}, u32[]{:S(2)}) collective-permute-start(bf16[512,1024]{1,0:T(8,128)(2,1)S(1)} %get-tuple-element.282.refs_8_), channel_id=1, source_target_pairs={{0,8},{8,0},{16,24},{24,16},{1,9},{9,1},{17,25},{25,17},{2,10},{10... | collective-permute-start | bytes 3145736 | tf_op jit(solution)/shard_map/ppermute | solution.py:29
  184.8 25.8 %collective-permute-start.31 = (bf16[512,1024]{1,0:T(8,128)(2,1)}, bf16[512,1024]{1,0:T(8,128)(2,1)S(1)}, u32[]{:S(2)}, u32[]{:S(2)}) collective-permute-start(bf16[512,1024]{1,0:T(8,128)(2,1)} %collective-permute-done.19.refs_5_), channel_id=1, source_target_pairs={{0,16},{8,24},{16,0},{24,8},{1,17},{9,25},{17,1},{25,9},{2,18},{10... | collective-permute-start | bytes 3145736 | tf_op jit(solution)/shard_map/ppermute | solution.py:29
  186.0 26.2 %collective-permute-start.32 = (bf16[512,1024]{1,0:T(8,128)(2,1)}, bf16[512,1024]{1,0:T(8,128)(2,1)S(1)}, u32[]{:S(2)}, u32[]{:S(2)}) collective-permute-start(bf16[512,1024]{1,0:T(8,128)(2,1)} %collective-permute-done.24.refs_10_), channel_id=1, source_target_pairs={{0,8},{8,0},{16,24},{24,16},{1,9},{9,1},{17,25},{25,17},{2,10},{10... | collective-permute-start | bytes 3145736 | tf_op jit(solution)/shard_map/ppermute | solution.py:29
  203.1 24.2 %collective-permute-start.30 = (bf16[128,4096]{1,0:T(8,128)(2,1)S(1)}, bf16[128,4096]{1,0:T(8,128)(2,1)S(1)}, u32[]{:S(2)}, u32[]{:S(2)}) collective-permute-start(bf16[128,4096]{1,0:T(8,128)(2,1)S(1)} %pad_maximum_fusion.refs_0_), channel_id=1, source_target_pairs={{0,1},{1,2},{2,3},{3,0},{4,5},{5,6},{6,7},{7,4},{8,9},{9,10},{10,1... | collective-permute-start | bytes 3145736 | tf_op jit(solution)/shard_map/ppermute | solution.py:24
  203.2 24.1 %collective-permute-start.33 = (bf16[128,4096]{1,0:T(8,128)(2,1)S(1)}, bf16[128,4096]{1,0:T(8,128)(2,1)S(1)}, u32[]{:S(2)}, u32[]{:S(2)}) collective-permute-start(bf16[128,4096]{1,0:T(8,128)(2,1)S(1)} %pad_maximum_fusion.refs_0_), channel_id=1, source_target_pairs={{0,4},{4,0},{1,5},{5,1},{2,6},{6,2},{3,7},{7,3},{8,12},{12,8},{9,1... | collective-permute-start | bytes 3145736 | tf_op jit(solution)/shard_map/ppermute | solution.py:29
  203.2 30.7 %collective-permute-start.36 = (bf16[512,1024]{1,0:T(8,128)(2,1)}, bf16[512,1024]{1,0:T(8,128)(2,1)S(1)}, u32[]{:S(2)}, u32[]{:S(2)}) collective-permute-start(bf16[512,1024]{1,0:T(8,128)(2,1)} %constant_dynamic-update-slice_fusion.refs_12_), channel_id=1, source_target_pairs={{0,8},{8,0},{16,24},{24,16},{1,9},{9,1},{17,25},{25,17},{2,10},{10... | collective-permute-start | bytes 3145736 | tf_op jit(solution)/shard_map/ppermute | solution.py:29
  210.5 25.0 %collective-permute-start.37 = (bf16[512,1024]{1,0:T(8,128)(2,1)}, bf16[512,1024]{1,0:T(8,128)(2,1)S(1)}, u32[]{:S(2)}, u32[]{:S(2)}) collective-permute-start(bf16[512,1024]{1,0:T(8,128)(2,1)} %constant_dynamic-update-slice_fusion.refs_12_), channel_id=1, source_target_pairs={{0,16},{8,24},{16,0},{24,8},{1,17},{9,25},{17,1},{25,9},{2,18},{10... | collective-permute-start | bytes 3145736 | tf_op jit(solution)/shard_map/ppermute | solution.py:29
  227.3 23.9 %collective-permute-start.34 = (bf16[128,4096]{1,0:T(8,128)(2,1)S(1)}, bf16[128,4096]{1,0:T(8,128)(2,1)}, u32[]{:S(2)}, u32[]{:S(2)}) collective-permute-start(bf16[128,4096]{1,0:T(8,128)(2,1)S(1)} %collective-permute-done.30.refs_2_), channel_id=1, source_target_pairs={{0,1},{1,2},{2,3},{3,0},{4,5},{5,6},{6,7},{7,4},{8,9},{9,10},{10,1... | collective-permute-start | bytes 3145736 | tf_op jit(solution)/shard_map/ppermute | solution.py:24
  227.4 23.8 %collective-permute-start.35 = (bf16[128,4096]{1,0:T(8,128)(2,1)S(1)}, bf16[128,4096]{1,0:T(8,128)(2,1)S(1)}, u32[]{:S(2)}, u32[]{:S(2)}) collective-permute-start(bf16[128,4096]{1,0:T(8,128)(2,1)S(1)} %collective-permute-done.30.refs_2_), channel_id=1, source_target_pairs={{0,4},{4,0},{1,5},{5,1},{2,6},{6,2},{3,7},{7,3},{8,12},{12,8},{9,1... | collective-permute-start | bytes 3145736 | tf_op jit(solution)/shard_map/ppermute | solution.py:29
  251.2 25.6 %collective-permute-start.40 = (bf16[128,4096]{1,0:T(8,128)(2,1)}, bf16[128,4096]{1,0:T(8,128)(2,1)}, u32[]{:S(2)}, u32[]{:S(2)}) collective-permute-start(bf16[128,4096]{1,0:T(8,128)(2,1)} %collective-permute-done.34.refs_0_), channel_id=1, source_target_pairs={{0,1},{1,2},{2,3},{3,0},{4,5},{5,6},{6,7},{7,4},{8,9},{9,10},{10,1... | collective-permute-start | bytes 3145736 | tf_op jit(solution)/shard_map/ppermute | solution.py:24
  252.2 24.6 %collective-permute-start.41 = (bf16[128,4096]{1,0:T(8,128)(2,1)}, bf16[128,4096]{1,0:T(8,128)(2,1)}, u32[]{:S(2)}, u32[]{:S(2)}) collective-permute-start(bf16[128,4096]{1,0:T(8,128)(2,1)} %collective-permute-done.34.refs_0_), channel_id=1, source_target_pairs={{0,4},{4,0},{1,5},{5,1},{2,6},{6,2},{3,7},{7,3},{8,12},{12,8},{9,1... | collective-permute-start | bytes 3145736 | tf_op jit(solution)/shard_map/ppermute | solution.py:29
  278.4 27.2 %collective-permute-start.48 = (bf16[128,2048]{1,0:T(8,128)(2,1)S(1)}, bf16[128,2048]{1,0:T(8,128)(2,1)}, u32[]{:S(2)}, u32[]{:S(2)}) collective-permute-start(bf16[128,2048]{1,0:T(8,128)(2,1)S(1)} %add_convert_fusion.11), channel_id=1, source_target_pairs={{0,1},{1,2},{2,3},{3,0},{4,5},{5,6},{6,7},{7,4},{8,9},{9,10},{10,1... | collective-permute-start | bytes 1572872 | tf_op jit(solution)/shard_map/ppermute | solution.py:24
  281.2 24.4 %collective-permute-start.44 = (bf16[128,2048]{1,0:T(8,128)(2,1)S(1)}, bf16[128,2048]{1,0:T(8,128)(2,1)}, u32[]{:S(2)}, u32[]{:S(2)}) collective-permute-start(bf16[128,2048]{1,0:T(8,128)(2,1)S(1)} %add_convert_fusion.12), channel_id=1, source_target_pairs={{0,1},{1,2},{2,3},{3,0},{4,5},{5,6},{6,7},{7,4},{8,9},{9,10},{10,1... | collective-permute-start | bytes 1572872 | tf_op jit(solution)/shard_map/ppermute | solution.py:24
  313.0 23.4 %collective-permute-start.49 = (bf16[128,2048]{1,0:T(8,128)(2,1)}, bf16[128,2048]{1,0:T(8,128)(2,1)S(1)}, u32[]{:S(2)}, u32[]{:S(2)}) collective-permute-start(bf16[128,2048]{1,0:T(8,128)(2,1)} %add_convert_fusion.10), channel_id=1, source_target_pairs={{0,1},{1,2},{2,3},{3,0},{4,5},{5,6},{6,7},{7,4},{8,9},{9,10},{10,1... | collective-permute-start | bytes 1572872 | tf_op jit(solution)/shard_map/ppermute | solution.py:24
  338.8 28.4 %collective-permute-start.56 = (bf16[512,1024]{1,0:T(8,128)(2,1)}, bf16[512,1024]{1,0:T(8,128)(2,1)}, u32[]{:S(2)}, u32[]{:S(2)}) collective-permute-start(bf16[512,1024]{1,0:T(8,128)(2,1)} %get-tuple-element.360), channel_id=1, source_target_pairs={{0,8},{8,0},{16,24},{24,16},{1,9},{9,1},{17,25},{25,17},{2,10},{10... | collective-permute-start | bytes 3145736 | tf_op jit(solution)/shard_map/ppermute | solution.py:29
  339.9 27.4 %collective-permute-start.58 = (bf16[512,1024]{1,0:T(8,128)(2,1)}, bf16[512,1024]{1,0:T(8,128)(2,1)}, u32[]{:S(2)}, u32[]{:S(2)}) collective-permute-start(bf16[512,1024]{1,0:T(8,128)(2,1)} %get-tuple-element.364), channel_id=1, source_target_pairs={{0,16},{8,24},{16,0},{24,8},{1,17},{9,25},{17,1},{25,9},{2,18},{10... | collective-permute-start | bytes 3145736 | tf_op jit(solution)/shard_map/ppermute | solution.py:29
  374.4 24.9 %collective-permute-start.61 = (bf16[512,1024]{1,0:T(8,128)(2,1)S(1)}, bf16[512,1024]{1,0:T(8,128)(2,1)}, u32[]{:S(2)}, u32[]{:S(2)}) collective-permute-start(bf16[512,1024]{1,0:T(8,128)(2,1)S(1)} %add_convert_fusion.3), channel_id=1, source_target_pairs={{0,16},{8,24},{16,0},{24,8},{1,17},{9,25},{17,1},{25,9},{2,18},{10... | collective-permute-start | bytes 3145736 | tf_op jit(solution)/shard_map/ppermute | solution.py:29
  375.7 24.7 %collective-permute-start.62 = (bf16[512,1024]{1,0:T(8,128)(2,1)}, bf16[512,1024]{1,0:T(8,128)(2,1)}, u32[]{:S(2)}, u32[]{:S(2)}) collective-permute-start(bf16[512,1024]{1,0:T(8,128)(2,1)} %get-tuple-element.377), channel_id=1, source_target_pairs={{0,8},{8,0},{16,24},{24,16},{1,9},{9,1},{17,25},{25,17},{2,10},{10... | collective-permute-start | bytes 3145736 | tf_op jit(solution)/shard_map/ppermute | solution.py:29
  377.0 32.2 %collective-permute-start.59 = (bf16[128,2048]{1,0:T(8,128)(2,1)}, bf16[128,2048]{1,0:T(8,128)(2,1)}, u32[]{:S(2)}, u32[]{:S(2)}) collective-permute-start(bf16[128,2048]{1,0:T(8,128)(2,1)} %add_convert_fusion.7), channel_id=1, source_target_pairs={{0,1},{1,2},{2,3},{3,0},{4,5},{5,6},{6,7},{7,4},{8,9},{9,10},{10,1... | collective-permute-start | bytes 1572872 | tf_op jit(solution)/shard_map/ppermute | solution.py:24
  400.4 38.2 %collective-permute-start.67 = (bf16[512,1024]{1,0:T(8,128)(2,1)}, bf16[512,1024]{1,0:T(8,128)(2,1)S(1)}, u32[]{:S(2)}, u32[]{:S(2)}) collective-permute-start(bf16[512,1024]{1,0:T(8,128)(2,1)} %get-tuple-element.404), channel_id=1, source_target_pairs={{0,8},{8,0},{16,24},{24,16},{1,9},{9,1},{17,25},{25,17},{2,10},{10... | collective-permute-start | bytes 3145736 | tf_op jit(solution)/shard_map/ppermute | solution.py:29
  415.7 33.1 %collective-permute-start.71 = (bf16[512,1024]{1,0:T(8,128)(2,1)}, bf16[512,1024]{1,0:T(8,128)(2,1)}, u32[]{:S(2)}, u32[]{:S(2)}) collective-permute-start(bf16[512,1024]{1,0:T(8,128)(2,1)} %add_convert_fusion.2), channel_id=1, source_target_pairs={{0,8},{8,0},{16,24},{24,16},{1,9},{9,1},{17,25},{25,17},{2,10},{10... | collective-permute-start | bytes 3145736 | tf_op jit(solution)/shard_map/ppermute | solution.py:29
  416.4 32.4 %collective-permute-start.72 = (bf16[512,1024]{1,0:T(8,128)(2,1)}, bf16[512,1024]{1,0:T(8,128)(2,1)}, u32[]{:S(2)}, u32[]{:S(2)}) collective-permute-start(bf16[512,1024]{1,0:T(8,128)(2,1)} %get-tuple-element.422), channel_id=1, source_target_pairs={{0,16},{8,24},{16,0},{24,8},{1,17},{9,25},{17,1},{25,9},{2,18},{10... | collective-permute-start | bytes 3145736 | tf_op jit(solution)/shard_map/ppermute | solution.py:29
  452.5 26.5 %collective-permute-start.70 = (bf16[128,2048]{1,0:T(8,128)(2,1)}, bf16[128,2048]{1,0:T(8,128)(2,1)}, u32[]{:S(2)}, u32[]{:S(2)}) collective-permute-start(bf16[128,2048]{1,0:T(8,128)(2,1)} %get-tuple-element.406), channel_id=1, source_target_pairs={{0,4},{4,0},{1,5},{5,1},{2,6},{6,2},{3,7},{7,3},{8,12},{12,8},{9,1... | collective-permute-start | bytes 1572872 | tf_op jit(solution)/shard_map/ppermute | solution.py:29
  457.0 51.5 %collective-permute-start.81 = (bf16[512,1024]{1,0:T(8,128)(2,1)}, bf16[512,1024]{1,0:T(8,128)(2,1)S(1)}, u32[]{:S(2)}, u32[]{:S(2)}) collective-permute-start(bf16[512,1024]{1,0:T(8,128)(2,1)} %add_convert_fusion), channel_id=1, source_target_pairs={{0,16},{8,24},{16,0},{24,8},{1,17},{9,25},{17,1},{25,9},{2,18},{10... | collective-permute-start | bytes 3145736 | tf_op jit(solution)/shard_map/ppermute | solution.py:29
  474.8 33.7 %collective-permute-start.82 = (bf16[512,1024]{1,0:T(8,128)(2,1)}, bf16[512,1024]{1,0:T(8,128)(2,1)S(1)}, u32[]{:S(2)}, u32[]{:S(2)}) collective-permute-start(bf16[512,1024]{1,0:T(8,128)(2,1)} %get-tuple-element.454), channel_id=1, source_target_pairs={{0,8},{8,0},{16,24},{24,16},{1,9},{9,1},{17,25},{25,17},{2,10},{10... | collective-permute-start | bytes 3145736 | tf_op jit(solution)/shard_map/ppermute | solution.py:29
  477.6 27.3 %collective-permute-start.80 = (bf16[512,1024]{1,0:T(8,128)(2,1)S(1)}, bf16[512,1024]{1,0:T(8,128)(2,1)S(1)}, u32[]{:S(2)}, u32[]{:S(2)}) collective-permute-start(bf16[512,1024]{1,0:T(8,128)(2,1)S(1)} %copy-done.77), channel_id=1, source_target_pairs={{0,16},{8,24},{16,0},{24,8},{1,17},{9,25},{17,1},{25,9},{2,18},{10... | collective-permute-start | bytes 3145736 | tf_op jit(solution)/shard_map/ppermute | solution.py:29
  480.7 27.9 %collective-permute-start.83 = (bf16[128,1024]{1,0:T(8,128)(2,1)}, bf16[128,1024]{1,0:T(8,128)(2,1)S(1)}, u32[]{:S(2)}, u32[]{:S(2)}) collective-permute-start(bf16[128,1024]{1,0:T(8,128)(2,1)} %get-tuple-element.449), channel_id=1, source_target_pairs={{0,1},{1,2},{2,3},{3,0},{4,5},{5,6},{6,7},{7,4},{8,9},{9,10},{10,1... | collective-permute-start | bytes 786440 | tf_op jit(solution)/shard_map/ppermute | solution.py:24
  508.5 23.6 %collective-permute-start.88 = (bf16[512,1024]{1,0:T(8,128)(2,1)S(1)}, bf16[512,1024]{1,0:T(8,128)(2,1)S(1)}, u32[]{:S(2)}, u32[]{:S(2)}) collective-permute-start(bf16[512,1024]{1,0:T(8,128)(2,1)S(1)} %add_convert_fusion.1), channel_id=1, source_target_pairs={{0,8},{8,0},{16,24},{24,16},{1,9},{9,1},{17,25},{25,17},{2,10},{10... | collective-permute-start | bytes 3145736 | tf_op jit(solution)/shard_map/ppermute | solution.py:29
  509.8 23.1 %collective-permute-start.89 = (bf16[512,1024]{1,0:T(8,128)(2,1)S(1)}, bf16[512,1024]{1,0:T(8,128)(2,1)S(1)}, u32[]{:S(2)}, u32[]{:S(2)}) collective-permute-start(bf16[512,1024]{1,0:T(8,128)(2,1)S(1)} %copy-done.76), channel_id=1, source_target_pairs={{0,16},{8,24},{16,0},{24,8},{1,17},{9,25},{17,1},{25,9},{2,18},{10... | collective-permute-start | bytes 3145736 | tf_op jit(solution)/shard_map/ppermute | solution.py:29
  511.7 24.7 %collective-permute-start.87 = (bf16[128,2048]{1,0:T(8,128)(2,1)S(1)}, bf16[128,2048]{1,0:T(8,128)(2,1)S(1)}, u32[]{:S(2)}, u32[]{:S(2)}) collective-permute-start(bf16[128,2048]{1,0:T(8,128)(2,1)S(1)} %add_convert_fusion.4), channel_id=1, source_target_pairs={{0,1},{1,2},{2,3},{3,0},{4,5},{5,6},{6,7},{7,4},{8,9},{9,10},{10,1... | collective-permute-start | bytes 1572872 | tf_op jit(solution)/shard_map/ppermute | solution.py:24
  540.2 35.4 %collective-permute-start.97 = (bf16[128,1024]{1,0:T(8,128)(2,1)S(1)}, bf16[128,1024]{1,0:T(8,128)(2,1)S(1)}, u32[]{:S(2)}, u32[]{:S(2)}) collective-permute-start(bf16[128,1024]{1,0:T(8,128)(2,1)S(1)} %get-tuple-element.470), channel_id=1, source_target_pairs={{0,1},{1,2},{2,3},{3,0},{4,5},{5,6},{6,7},{7,4},{8,9},{9,10},{10,1... | collective-permute-start | bytes 786440 | tf_op jit(solution)/shard_map/ppermute | solution.py:24
  544.9 35.5 %collective-permute-start.98 = (bf16[128,1024]{1,0:T(8,128)(2,1)S(1)}, bf16[128,1024]{1,0:T(8,128)(2,1)S(1)}, u32[]{:S(2)}, u32[]{:S(2)}) collective-permute-start(bf16[128,1024]{1,0:T(8,128)(2,1)S(1)} %get-tuple-element.471), channel_id=1, source_target_pairs={{0,2},{1,3},{2,0},{3,1},{4,6},{5,7},{6,4},{7,5},{8,10},{9,11},{10,... | collective-permute-start | bytes 786440 | tf_op jit(solution)/shard_map/ppermute | solution.py:24
  547.5 37.3 %collective-permute-start.99 = (bf16[128,1024]{1,0:T(8,128)(2,1)S(1)}, bf16[128,1024]{1,0:T(8,128)(2,1)S(1)}, u32[]{:S(2)}, u32[]{:S(2)}) collective-permute-start(bf16[128,1024]{1,0:T(8,128)(2,1)S(1)} %get-tuple-element.472), channel_id=1, source_target_pairs={{0,3},{1,0},{2,1},{3,2},{4,7},{5,4},{6,5},{7,6},{8,11},{9,8},{10,9... | collective-permute-start | bytes 786440 | tf_op jit(solution)/shard_map/ppermute | solution.py:24
  558.7 28.2 %collective-permute-start.91 = (bf16[128,2048]{1,0:T(8,128)(2,1)S(1)}, bf16[128,2048]{1,0:T(8,128)(2,1)S(1)}, u32[]{:S(2)}, u32[]{:S(2)}) collective-permute-start(bf16[128,2048]{1,0:T(8,128)(2,1)S(1)} %copy-done.78), channel_id=1, source_target_pairs={{0,4},{4,0},{1,5},{5,1},{2,6},{6,2},{3,7},{7,3},{8,12},{12,8},{9,1... | collective-permute-start | bytes 1572872 | tf_op jit(solution)/shard_map/ppermute | solution.py:29
  558.9 26.1 %collective-permute-start.94 = (f32[2,512]{1,0:T(2,128)S(1)}, f32[2,512]{1,0:T(2,128)S(1)}, u32[]{:S(2)}, u32[]{:S(2)}) collective-permute-start(f32[2,512]{1,0:T(2,128)S(1)} %fusion.11), channel_id=1, source_target_pairs={{0,1},{1,2},{2,3},{3,0},{4,5},{5,6},{6,7},{7,4},{8,9},{9,10},{10,1... | collective-permute-start | bytes 12296 | tf_op jit(solution)/shard_map/ppermute | solution.py:24
  (136 other events, 1705.5 us)
